TPU v7x, 32 devices: a whole 2x2x4 slice. The times are simulated.
32 devices in a mesh: dp: 4 (over y, x), seq: 8 (over z, core).
Axes of the slice: x: 2, y: 2, z: 4, core: 2. Of those that a mesh axis runs over, the one named last changes fastest.
Arguments:
- tokens: bfloat16 [4, 2048, 1024], P('dp', 'seq'), may hold values from -6 to 6
- out_grad: bfloat16 [4, 2048, 1024], P('dp', 'seq'), may hold values from -6 to 6
- doc_ids: int32 [4, 2048], P('dp', 'seq'), may hold values from 0 to 15, never falling along the last dimension, each value on 1 to 1024 neighbouring positions
- expert_picks: int32 [4, 2048, 8], P('dp', 'seq'), may hold values from 0 to 15, all different within a row; in each aligned block of 256 rows (0 to 255, 256 to 511, ..., all dimensions but the last counted through in order) at most 192 rows name the same one
- w_query: float32 [1024, 1024], P('dp'), may hold values from -0.625 to 0.625
- key_weight_matrix: float32 [1024, 512], P('dp'), may hold values from -0.625 to 0.625
- value_weight_matrix: float32 [1024, 512], P('dp'), may hold values from -0.1875 to 0.1875
- w_out: float32 [1024, 1024], P('dp'), may hold values from -6 to 6
- w_router: float32 [1024, 16], P('dp'), may hold values from -0.09375 to 0.09375
- gain_attn: float32 [1024], P('dp'), may hold values from 0.5 to 1.5
- gain_moe: float32 [1024], P('dp'), may hold values from 0.5 to 1.5
- expert_in: float32 [16, 1024, 1024], P('seq', 'dp'), may hold values from -0.1875 to 0.1875
- expert_out: float32 [16, 1024, 512], P('seq', 'dp'), may hold values from -5 to 5
Outputs:
- output: bfloat16 [4, 2048, 1024], P('dp', 'seq')
- input_grad: bfloat16 [4, 2048, 1024], P('dp', 'seq')
- grad_w_query: float32 [1024, 1024], P(('dp', 'seq'))
- grad_w_key: float32 [1024, 512], P(('dp', 'seq'))
- grad_w_value: float32 [1024, 512], P(('dp', 'seq'))
- grad_w_out: float32 [1024, 1024], P(('dp', 'seq'))
- grad_w_router: float32 [1024, 16], P(('dp', 'seq'))
- grad_gain_attn: float32 [1024], P(('dp', 'seq'))
- grad_gain_moe: float32 [1024], P(('dp', 'seq'))
- grad_expert_in: float32 [16, 1024, 1024], P('seq', 'dp')
- grad_expert_out: float32 [16, 1024, 512], P('seq', 'dp')
Inputs may be any that keep to these rules, and one draw needn't show every extreme that they name: `doc_ids`: within each sequence segment numbers never fall; a segment has 1 to 1024 positions, one exactly that many. `expert_picks`: each token names 8 different experts. Among the 256 tokens of one device (aligned blocks of a sequence) no expert is named more than 192 times, a bound that some block reaches.
All inputs are finite; a program needn't handle non-finite values.
Results may differ from a plain program's by a relative error of at most 0.019.
The roundings to bfloat16 on the way count: a program that leaves them out, or rounds other values in their place, can miss the bound.
Values may be sent and summed in bfloat16 or wider, within the bound.
A program may use at most 192 MiB of HBM per device.

v0:
```python
import jax
import jax.numpy as jnp
from jax import lax
from jax.sharding import PartitionSpec as P

QUERY_HEADS = 16
KEY_VALUE_HEADS = 8
HEAD_SIZE = 64
FFE = 512
TOP = 8


att_mult = 0.015625
res_mult = 0.22
norm_eps = 1e-06
rope_theta = 10000.0


def rope_tables(positions, head_size):
    half_size = head_size // 2
    frequency = rope_theta ** (-jnp.arange(half_size, dtype=jnp.float32) * 2.0 / head_size)
    angles = positions.astype(jnp.float32)[:, None] * frequency[None, :]
    return (jnp.cos(angles), jnp.sin(angles))


def apply_rotary(values, cosine_table, sinusoid_table):
    half_size = values.shape[-1] // 2
    first_half = values[..., :half_size]
    second_half = values[..., half_size:]
    cos_b = cosine_table[:, None, :]
    sin_b = sinusoid_table[:, None, :]
    return jnp.concatenate(
        [first_half * cos_b - second_half * sin_b, second_half * cos_b + first_half * sin_b],
        axis=-1,
    )


def rms_scale(values, gain_vec):
    return (
        values * lax.rsqrt(jnp.mean(values * values, axis=-1, keepdims=True) + norm_eps) * gain_vec
    )


def swiglu(gate_part, up_part):
    return jax.nn.silu(gate_part) * up_part


def gate_softmax(selected):
    return jax.nn.softmax(selected, axis=-1)


def on_device(
    tokens,
    out_grad,
    doc_ids,
    expert_picks,
    w_query,
    key_weight_matrix,
    value_weight_matrix,
    w_out,
    w_router,
    gain_attn,
    gain_moe,
    expert_in,
    expert_out,
):
    narrow_dtype = jnp.bfloat16
    broad_dtype = jnp.float32
    seq_devices = lax.axis_size("seq")
    rows_per_shard = tokens.shape[1]
    model_width = tokens.shape[2]
    seq_length = rows_per_shard * seq_devices
    heads_dev = QUERY_HEADS // seq_devices
    query_group_width = QUERY_HEADS // KEY_VALUE_HEADS
    expert_count = w_router.shape[1]
    capacity = rows_per_shard * TOP * 3 // (2 * expert_count)
    block_rows = min(512, seq_length)
    block_count = seq_length // block_rows
    wq_full, wk_full, wv_full, wo_full, router_full, gain_a_full, gain_m_full = (
        lax.all_gather(w_query.astype(narrow_dtype), "dp", axis=0, tiled=True),
        lax.all_gather(key_weight_matrix.astype(narrow_dtype), "dp", axis=0, tiled=True),
        lax.all_gather(value_weight_matrix.astype(narrow_dtype), "dp", axis=0, tiled=True),
        lax.all_gather(w_out.astype(narrow_dtype), "dp", axis=0, tiled=True),
        lax.all_gather(w_router.astype(narrow_dtype), "dp", axis=0, tiled=True),
        lax.all_gather(gain_attn.astype(narrow_dtype), "dp", axis=0, tiled=True),
        lax.all_gather(gain_moe.astype(narrow_dtype), "dp", axis=0, tiled=True),
    )
    expert_in_full, expert_out_full = (
        lax.all_gather(expert_in.astype(narrow_dtype), "dp", axis=1, tiled=True),
        lax.all_gather(expert_out.astype(narrow_dtype), "dp", axis=1, tiled=True),
    )
    resid_in = tokens[0].astype(broad_dtype)
    normed_attn, pull_attn_norm = jax.vjp(rms_scale, resid_in, gain_a_full.astype(broad_dtype))
    attention_normed_input = normed_attn.astype(narrow_dtype)
    query_lin = jnp.dot(
        attention_normed_input, wq_full, preferred_element_type=broad_dtype
    ).reshape(rows_per_shard, QUERY_HEADS, HEAD_SIZE)
    key_linear = jnp.dot(
        attention_normed_input, wk_full, preferred_element_type=broad_dtype
    ).reshape(rows_per_shard, KEY_VALUE_HEADS, HEAD_SIZE)
    value_linear = (
        jnp.dot(attention_normed_input, wv_full, preferred_element_type=broad_dtype)
        .astype(narrow_dtype)
        .reshape(rows_per_shard, KEY_VALUE_HEADS, HEAD_SIZE)
    )
    positions = lax.axis_index("seq") * rows_per_shard + jnp.arange(rows_per_shard, dtype=jnp.int32)
    cosine_table, sinusoid_table = rope_tables(positions, HEAD_SIZE)
    query_send = (
        apply_rotary(query_lin, cosine_table, sinusoid_table)
        .astype(narrow_dtype)
        .reshape(rows_per_shard, QUERY_HEADS * HEAD_SIZE)
    )
    key_send = jnp.repeat(
        apply_rotary(key_linear, cosine_table, sinusoid_table).astype(narrow_dtype),
        query_group_width,
        axis=1,
    ).reshape(rows_per_shard, QUERY_HEADS * HEAD_SIZE)
    value_send = jnp.repeat(value_linear, query_group_width, axis=1).reshape(
        rows_per_shard, QUERY_HEADS * HEAD_SIZE
    )
    query_heads, key_heads, value_heads = (
        lax.all_to_all(query_send, "seq", split_axis=1, concat_axis=0, tiled=True),
        lax.all_to_all(key_send, "seq", split_axis=1, concat_axis=0, tiled=True),
        lax.all_to_all(value_send, "seq", split_axis=1, concat_axis=0, tiled=True),
    )
    seq_docs = lax.all_gather(doc_ids, "seq", axis=1, tiled=True)[0]
    query_heads = query_heads.reshape(seq_length, heads_dev, HEAD_SIZE)
    key_heads = key_heads.reshape(seq_length, heads_dev, HEAD_SIZE)
    value_heads = value_heads.reshape(seq_length, heads_dev, HEAD_SIZE)
    key_positions = jnp.arange(seq_length, dtype=jnp.int32)

    def block_scores(block_index):
        first_row = block_index * block_rows
        query_block = lax.dynamic_slice_in_dim(query_heads, first_row, block_rows, 0)
        doc_block = lax.dynamic_slice_in_dim(seq_docs, first_row, block_rows, 0)
        row_positions = first_row + jnp.arange(block_rows, dtype=jnp.int32)
        raw_scores = (
            jnp.einsum("qhd,khd->hqk", query_block, key_heads, preferred_element_type=broad_dtype)
            * att_mult
        )
        allowed = (doc_block[:, None] == seq_docs[None, :]) & (
            row_positions[:, None] >= key_positions[None, :]
        )
        return (jnp.where(allowed[None], raw_scores, -1e30), query_block)

    def attend_block(block_index):
        scores, query_block = block_scores(block_index)
        row_max = jnp.max(scores, axis=-1, keepdims=True)
        shifted = jnp.exp(scores - row_max)
        row_total = jnp.sum(shifted, axis=-1, keepdims=True)
        probs_low = (shifted / row_total).astype(narrow_dtype)
        attended_block = jnp.einsum(
            "hqk,khd->qhd", probs_low, value_heads, preferred_element_type=broad_dtype
        )
        return (attended_block.astype(narrow_dtype), (row_max + jnp.log(row_total))[..., 0])

    attended_blocks, log_totals = lax.map(attend_block, jnp.arange(block_count, dtype=jnp.int32))
    attended_heads = attended_blocks.reshape(seq_length, heads_dev * HEAD_SIZE)
    attended = lax.all_to_all(attended_heads, "seq", split_axis=0, concat_axis=1, tiled=True)
    attn_branch = jnp.dot(attended, wo_full, preferred_element_type=broad_dtype)
    mid_resid = resid_in + res_mult * attn_branch
    normed_moe, pull_moe_norm = jax.vjp(rms_scale, mid_resid, gain_m_full.astype(broad_dtype))
    normed_m = normed_moe.astype(narrow_dtype)
    logits = jnp.dot(normed_m, router_full, preferred_element_type=broad_dtype)
    chosen = expert_picks[0]
    chosen_hot = chosen[:, :, None] == jnp.arange(expert_count, dtype=jnp.int32)[None, None, :]
    selected = jnp.sum(jnp.where(chosen_hot, logits[:, None, :], 0.0), axis=2)
    gate_probs, pull_gates = jax.vjp(gate_softmax, selected)
    flat_hot = chosen_hot.reshape(rows_per_shard * TOP, expert_count).astype(jnp.int32)
    slot_rank = jnp.sum((jnp.cumsum(flat_hot, axis=0) - 1) * flat_hot, axis=1).reshape(
        rows_per_shard, TOP
    )
    spread_rows = jnp.broadcast_to(normed_m[:, None, :], (rows_per_shard, TOP, model_width))
    send_rows = (
        jnp.zeros((expert_count, capacity, model_width), narrow_dtype)
        .at[chosen, slot_rank]
        .set(spread_rows)
    )
    expert_rows = lax.all_to_all(send_rows, "seq", split_axis=0, concat_axis=1, tiled=True)
    gate_up = jnp.einsum(
        "erd,edf->erf", expert_rows, expert_in_full, preferred_element_type=broad_dtype
    )
    gate_lin = gate_up[..., :FFE]
    up_lin = gate_up[..., FFE:]
    expert_hidden = swiglu(gate_lin, up_lin).astype(narrow_dtype)
    expert_res = jnp.einsum(
        "erf,edf->erd", expert_hidden, expert_out_full, preferred_element_type=broad_dtype
    ).astype(narrow_dtype)
    returned = lax.all_to_all(expert_res, "seq", split_axis=1, concat_axis=0, tiled=True)
    picked = returned[chosen, slot_rank].astype(broad_dtype)
    moe_branch = jnp.sum(gate_probs[:, :, None] * picked, axis=1)
    final_resid = mid_resid + res_mult * moe_branch
    output = final_resid.astype(narrow_dtype)[None]
    out_cot = out_grad[0].astype(broad_dtype)
    moe_cot = res_mult * out_cot
    gate_cot = jnp.sum(moe_cot[:, None, :] * picked, axis=2)
    slot_cot = (gate_probs[:, :, None] * moe_cot[:, None, :]).astype(narrow_dtype)
    send_cot = (
        jnp.zeros((expert_count, capacity, model_width), narrow_dtype)
        .at[chosen, slot_rank]
        .set(slot_cot)
    )
    result_cot = lax.all_to_all(send_cot, "seq", split_axis=0, concat_axis=1, tiled=True)
    hidden_cot = jnp.einsum(
        "erd,edf->erf", result_cot, expert_out_full, preferred_element_type=broad_dtype
    )
    grad_e_out = jnp.einsum(
        "erd,erf->edf", result_cot, expert_hidden, preferred_element_type=broad_dtype
    )
    gate_lin_cot, up_lin_cot = jax.vjp(swiglu, gate_lin, up_lin)[1](hidden_cot)
    gate_up_cot = jnp.concatenate([gate_lin_cot, up_lin_cot], axis=-1).astype(narrow_dtype)
    grad_e_in = jnp.einsum(
        "erd,erf->edf", expert_rows, gate_up_cot, preferred_element_type=broad_dtype
    )
    rows_cot = jnp.einsum(
        "erf,edf->erd", gate_up_cot, expert_in_full, preferred_element_type=broad_dtype
    ).astype(narrow_dtype)
    back_cot = lax.all_to_all(rows_cot, "seq", split_axis=1, concat_axis=0, tiled=True)
    normed_m_cot = jnp.sum(back_cot[chosen, slot_rank].astype(broad_dtype), axis=1)
    selected_cot = pull_gates(gate_cot)[0]
    logits_cot = jnp.sum(jnp.where(chosen_hot, selected_cot[:, :, None], 0.0), axis=1).astype(
        narrow_dtype
    )
    grad_router = jnp.dot(normed_m.T, logits_cot, preferred_element_type=broad_dtype)
    normed_m_cot = normed_m_cot + jnp.dot(
        logits_cot, router_full.T, preferred_element_type=broad_dtype
    )
    mid_norm_cot, grad_gain_m = pull_moe_norm(normed_m_cot)
    mid_cot = out_cot + mid_norm_cot
    branch_cot = (res_mult * mid_cot).astype(narrow_dtype)
    grad_wo = jnp.dot(attended.T, branch_cot, preferred_element_type=broad_dtype)
    attended_cot = jnp.dot(branch_cot, wo_full.T, preferred_element_type=broad_dtype).astype(
        narrow_dtype
    )
    heads_cot = lax.all_to_all(
        attended_cot, "seq", split_axis=1, concat_axis=0, tiled=True
    ).reshape(seq_length, heads_dev, HEAD_SIZE)

    def attend_back(accums, block_index):
        key_acc, value_acc = accums
        scores, query_block = block_scores(block_index)
        prob_rows = jnp.exp(scores - log_totals[block_index][..., None])
        out_block = lax.dynamic_slice_in_dim(heads_cot, block_index * block_rows, block_rows, 0)
        probs_cot = jnp.einsum(
            "qhd,khd->hqk", out_block, value_heads, preferred_element_type=broad_dtype
        )
        row_dot = jnp.sum(prob_rows * probs_cot, axis=-1, keepdims=True)
        scores_cot = (prob_rows * (probs_cot - row_dot)).astype(narrow_dtype)
        query_cot = (
            jnp.einsum("hqk,khd->qhd", scores_cot, key_heads, preferred_element_type=broad_dtype)
            * att_mult
        )
        key_acc = (
            key_acc
            + jnp.einsum(
                "hqk,qhd->khd", scores_cot, query_block, preferred_element_type=broad_dtype
            )
            * att_mult
        )
        value_acc = value_acc + jnp.einsum(
            "hqk,qhd->khd",
            prob_rows.astype(narrow_dtype),
            out_block,
            preferred_element_type=broad_dtype,
        )
        return ((key_acc, value_acc), query_cot.astype(narrow_dtype))

    empty_acc = jnp.zeros((seq_length, heads_dev, HEAD_SIZE), broad_dtype)
    (key_acc, value_acc), query_blocks_cot = lax.scan(
        attend_back, (empty_acc, empty_acc), jnp.arange(block_count, dtype=jnp.int32)
    )
    query_cot_tok, key_token_cotangent, value_token_cotangent = (
        lax.all_to_all(
            query_blocks_cot.reshape(seq_length, heads_dev * HEAD_SIZE),
            "seq",
            split_axis=0,
            concat_axis=1,
            tiled=True,
        ),
        lax.all_to_all(
            key_acc.reshape(seq_length, heads_dev * HEAD_SIZE).astype(narrow_dtype),
            "seq",
            split_axis=0,
            concat_axis=1,
            tiled=True,
        ),
        lax.all_to_all(
            value_acc.reshape(seq_length, heads_dev * HEAD_SIZE).astype(narrow_dtype),
            "seq",
            split_axis=0,
            concat_axis=1,
            tiled=True,
        ),
    )
    query_lin_cot = (
        apply_rotary(
            query_cot_tok.reshape(rows_per_shard, QUERY_HEADS, HEAD_SIZE).astype(broad_dtype),
            cosine_table,
            -sinusoid_table,
        )
        .astype(narrow_dtype)
        .reshape(rows_per_shard, QUERY_HEADS * HEAD_SIZE)
    )
    key_gradient_total = jnp.sum(
        key_token_cotangent.reshape(
            rows_per_shard, KEY_VALUE_HEADS, query_group_width, HEAD_SIZE
        ).astype(broad_dtype),
        axis=2,
    )
    key_linear_cotangent = (
        apply_rotary(key_gradient_total, cosine_table, -sinusoid_table)
        .astype(narrow_dtype)
        .reshape(rows_per_shard, KEY_VALUE_HEADS * HEAD_SIZE)
    )
    value_lin_cot = (
        jnp.sum(
            value_token_cotangent.reshape(
                rows_per_shard, KEY_VALUE_HEADS, query_group_width, HEAD_SIZE
            ).astype(broad_dtype),
            axis=2,
        )
        .astype(narrow_dtype)
        .reshape(rows_per_shard, KEY_VALUE_HEADS * HEAD_SIZE)
    )
    grad_wq = jnp.dot(attention_normed_input.T, query_lin_cot, preferred_element_type=broad_dtype)
    grad_wk = jnp.dot(
        attention_normed_input.T, key_linear_cotangent, preferred_element_type=broad_dtype
    )
    grad_wv = jnp.dot(attention_normed_input.T, value_lin_cot, preferred_element_type=broad_dtype)
    normed_a_cot = jnp.dot(query_lin_cot, wq_full.T, preferred_element_type=broad_dtype)
    normed_a_cot = normed_a_cot + jnp.dot(
        key_linear_cotangent, wk_full.T, preferred_element_type=broad_dtype
    )
    normed_a_cot = normed_a_cot + jnp.dot(
        value_lin_cot, wv_full.T, preferred_element_type=broad_dtype
    )
    resid_cot, grad_gain_a = pull_attn_norm(normed_a_cot)
    input_grad = (mid_cot + resid_cot).astype(narrow_dtype)[None]
    (
        summed_query,
        summed_key,
        summed_value,
        summed_out,
        summed_router,
        summed_gain_a,
        summed_gain_m,
    ) = (
        lax.psum_scatter(grad_wq, ("dp", "seq"), scatter_dimension=0, tiled=True),
        lax.psum_scatter(grad_wk, ("dp", "seq"), scatter_dimension=0, tiled=True),
        lax.psum_scatter(grad_wv, ("dp", "seq"), scatter_dimension=0, tiled=True),
        lax.psum_scatter(grad_wo, ("dp", "seq"), scatter_dimension=0, tiled=True),
        lax.psum_scatter(grad_router, ("dp", "seq"), scatter_dimension=0, tiled=True),
        lax.psum_scatter(grad_gain_a, ("dp", "seq"), scatter_dimension=0, tiled=True),
        lax.psum_scatter(grad_gain_m, ("dp", "seq"), scatter_dimension=0, tiled=True),
    )
    summed_e_in, summed_e_out = (
        lax.psum_scatter(
            grad_e_in.astype(jnp.bfloat16), "dp", scatter_dimension=1, tiled=True
        ).astype(jnp.float32),
        lax.psum_scatter(
            grad_e_out.astype(jnp.bfloat16), "dp", scatter_dimension=1, tiled=True
        ).astype(jnp.float32),
    )
    return (
        output,
        input_grad,
        summed_query,
        summed_key,
        summed_value,
        summed_out,
        summed_router,
        summed_gain_a,
        summed_gain_m,
        summed_e_in,
        summed_e_out,
    )


def solution(mesh):
    return jax.shard_map(
        on_device,
        mesh=mesh,
        in_specs=(
            P("dp", "seq", None),
            P("dp", "seq", None),
            P("dp", "seq"),
            P("dp", "seq", None),
            P("dp", None),
            P("dp", None),
            P("dp", None),
            P("dp", None),
            P("dp", None),
            P("dp"),
            P("dp"),
            P("seq", "dp", None),
            P("seq", "dp", None),
        ),
        out_specs=(
            P("dp", "seq", None),
            P("dp", "seq", None),
            P(("dp", "seq"), None),
            P(("dp", "seq"), None),
            P(("dp", "seq"), None),
            P(("dp", "seq"), None),
            P(("dp", "seq"), None),
            P(("dp", "seq")),
            P(("dp", "seq")),
            P("seq", "dp", None),
            P("seq", "dp", None),
        ),
        check_vma=False,
    )
```

profile of v0, /device:TPU:13, one launch (start us, length us, event | category | flops | bytes accessed | tf_op | source)
XLA Modules:
  0.0 1763.6 jit_solution(6644304459604157711)
XLA Ops:
  22.0 16.2 all-gather.11.cloned.1.call-done
  46.7 20.6 %all-gather.13.cloned.1.call-done = bf16[1024,512]{1,0:T(8,128)(2,1)} async-done(((bf16[256,512]{1,0:T(8,128)(2,1)}), bf16[1024,512]{1,0:T(8,128)(2,1)}) %all-gather.13.cloned.1.call-update) | async-done | bytes 1048592 | tf_op jit(solution)/shard_map/all_gather | solution.py:82
  75.4 29.6 %all-gather.9.cloned.1.call-done = bf16[1024,1024]{1,0:T(8,128)(2,1)} async-done(((bf16[256,1024]{1,0:T(8,128)(2,1)}), bf16[1024,1024]{1,0:T(8,128)(2,1)}) %all-gather.9.cloned.1.call-update) | async-done | bytes 2097168 | tf_op jit(solution)/shard_map/all_gather | solution.py:80
  143.1 41.2 %while.28 = (s32[]{:T(128)}, bf16[4,512,2,64]{1,3,2,0:T(8,128)(2,1)S(1)}, f32[4,2,512]{2,1,0:T(2,128)}, s32[4]{0:T(128)S(1)}, s32[2048]{0:T(1024)S(1)}, /*index=...) while((s32[]{:T(128)}, ...), condition=%wide.region_4.5_spmd.clone, body=%wide.region_1.4_spmd.clone.sunk | while | flops 565247488 | bytes 30722760 | solution.py:157
  208.7 14.2 scatter_custom_fusion.1
  231.2 23.6 %scatter_custom_fusion = bf16[3072,1024]{1,0:T(8,128)(2,1)} fusion(s32[2048]{0:T(1024)S(1)} %reshape.671, bf16[]{:T(256)} %constant.53.clone.1, bf16[256,1024]{1,0:T(8,128)(2,1)S(1)} %multiply_convert_fusion.5), kind=kCustom, calls=%fused_computation.74 | custom fusion | bytes 6815746
  254.8 111.8 %all-to-all-done.6 = bf16[16,192,1024]{2,1,0:T(8,128)(2,1)} async-done(((bf16[16,192,1024]{2,1,0:T(8,128)(2,1)}), bf16[16,192,1024]{2,1,0:T(8,128)(2,1)}, u32[]{:S(2)}, u32[]{:S(2)}) %all-to-all-start.6) | async-done | bytes 6291488 | tf_op jit(solution)/shard_map/all_to_all | solution.py:203
  385.0 125.5 %all-to-all-done.4 = bf16[16,192,1024]{2,1,0:T(8,128)(2,1)} async-done(((bf16[16,192,1024]{2,1,0:T(8,128)(2,1)}), bf16[16,192,1024]{2,1,0:T(8,128)(2,1)}, u32[]{:S(2)}, u32[]{:S(2)}) %all-to-all-start.4) | async-done | bytes 6291488 | tf_op jit(solution)/shard_map/all_to_all | solution.py:179
  547.0 22.0 %copy.251 = bf16[2,1536,1024]{2,0,1:T(2,128)(2,1)} copy(bf16[2,1536,1024]{2,1,0:T(8,128)(2,1)S(1)} %convolution_convert_fusion) | data formatting | bytes 12582912 | tf_op jit(solution)/shard_map/convert_element_type | solution.py:188
  588.0 22.0 %copy.257 = bf16[2,1536,1024]{2,0,1:T(2,128)(2,1)} copy(bf16[2,1536,1024]{2,1,0:T(8,128)(2,1)S(1)} %convolution_convert_fusion.1) | data formatting | bytes 12582912 | tf_op jit(solution)/shard_map/convert_element_type | solution.py:217
  610.0 103.2 %all-to-all-done.5 = bf16[2,1536,1024]{2,0,1:T(2,128)(2,1)} async-done(((bf16[2,1536,1024]{2,0,1:T(2,128)(2,1)}), bf16[2,1536,1024]{2,0,1:T(2,128)(2,1)}, u32[]{:S(2)}, u32[]{:S(2)}) %all-to-all-start.5) | async-done | bytes 6291488 | tf_op jit(solution)/shard_map/all_to_all | solution.py:189
  738.4 41.0 %gather_fusion = bf16[2048,1024]{1,0:T(8,128)(2,1)} fusion(bf16[16,192,1024]{2,1,0:T(8,128)(2,1)} %bitcast.265, s32[2048]{0:T(1024)S(1)} %reshape.659), kind=kCustom, calls=%fused_computation | custom fusion | bytes 8404992 | tf_op jit(solution)/shard_map/gather | solution.py:190
  785.7 71.2 %all-to-all-done.7 = bf16[2,1536,1024]{2,0,1:T(2,128)(2,1)} async-done(((bf16[2,1536,1024]{2,0,1:T(2,128)(2,1)}), bf16[2,1536,1024]{2,0,1:T(2,128)(2,1)}, u32[]{:S(2)}, u32[]{:S(2)}) %all-to-all-start.7) | async-done | bytes 6291488 | tf_op jit(solution)/shard_map/all_to_all | solution.py:218
  864.4 40.9 %gather_fusion.1 = bf16[2048,1024]{1,0:T(8,128)(2,1)} fusion(bf16[16,192,1024]{2,1,0:T(8,128)(2,1)} %bitcast.264, s32[2048]{0:T(1024)S(1)} %reshape.659), kind=kCustom, calls=%fused_computation.1 | custom fusion | bytes 8404992 | tf_op jit(solution)/shard_map/gather | solution.py:219
  922.6 12.9 fusion.60
  937.8 125.7 %while.29 = (s32[]{:T(128)}, f32[2048,2,64]{0,2,1:T(8,128)S(1)}, f32[2048,2,64]{0,2,1:T(8,128)}, bf16[4,512,2,64]{1,3,2,0:T(8,128)(2,1)}, s32[4]{0:T(128)S(1)}, ...) while((s32[]{:T(128)}, f32[2048,2,64]{0,2,1:T(8,128)S(1)}, ...), condition=%wide.region_22.23_spmd.clone, body=%wide.region_20.22_spmd.clone.sunk | while | flops 1378221568 | bytes 157465456 | solution.py:269
  1086.2 19.1 %all_to_all.189 = bf16[8,256,128]{1,2,0:T(8,128)(2,1)S(1)} all-to-all(bf16[8,256,128]{1,2,0:T(8,128)(2,1)S(1)} %copy.269), channel_id=1, replica_groups=mesh['dp'=4,'seq'=8] {'seq'}, dimensions={0} | all-to-all | bytes 1048576 | tf_op jit(solution)/shard_map/all_to_all | solution.py:287
  1110.8 18.5 %all_to_all.188 = bf16[8,256,128]{1,2,0:T(8,128)(2,1)S(1)} all-to-all(bf16[8,256,128]{1,2,0:T(8,128)(2,1)S(1)} %copy.264), channel_id=1, replica_groups=mesh['dp'=4,'seq'=8] {'seq'}, dimensions={0} | all-to-all | bytes 1048576 | tf_op jit(solution)/shard_map/all_to_all | solution.py:273
  1137.5 61.9 %reduce-scatter.22.cloned.1.call-done = f32[32,16]{1,0:T(8,128)} async-done(((f32[1024,16]{1,0:T(8,128)}), f32[32,16]{1,0:T(8,128)}) %reduce-scatter.22.cloned.1.call-update) | async-done | bytes 2064
  1205.4 47.6 %all-reduce.2 = (f32[1024]{0:T(1024)S(1)}, f32[1024]{0:T(1024)S(1)}) all-reduce(f32[1024]{0:T(1024)S(1)} %get-tuple-element.215, f32[1024]{0:T(1024)S(1)} %get-tuple-element.213), channel_id=7, replica_groups=mesh['dp'=4,'seq'=8] {'dp','seq'}, use_global_device_ids=true, to_apply=%region_32.33.clone | all-reduce | flops 2048 | bytes 16384
  1255.3 80.0 %reduce-scatter.12.cloned.1.call-done = f32[32,512]{1,0:T(8,128)} async-done(((f32[1024,512]{1,0:T(8,128)}), f32[32,512]{1,0:T(8,128)}) %reduce-scatter.12.cloned.1.call-update) | async-done | bytes 65552 | tf_op jit(solution)/shard_map/reduce_scatter | solution.py:349
  1335.3 136.7 %reduce-scatter.14.cloned.1.call-done = f32[32,512]{1,0:T(8,128)} async-done(((f32[1024,512]{1,0:T(8,128)}), f32[32,512]{1,0:T(8,128)}) %reduce-scatter.14.cloned.1.call-update) | async-done | bytes 65552 | tf_op jit(solution)/shard_map/reduce_scatter | solution.py:350
  1472.0 142.1 %reduce-scatter.16.cloned.1.call-done = f32[32,1024]{1,0:T(8,128)} async-done(((f32[1024,1024]{1,0:T(8,128)}), f32[32,1024]{1,0:T(8,128)}) %reduce-scatter.16.cloned.1.call-update) | async-done | bytes 131088 | tf_op jit(solution)/shard_map/reduce_scatter | solution.py:351
  1614.1 142.5 %reduce-scatter.10.cloned.1.call-done = f32[32,1024]{1,0:T(8,128)} async-done(((f32[1024,1024]{1,0:T(8,128)}), f32[32,1024]{1,0:T(8,128)}) %reduce-scatter.10.cloned.1.call-update) | async-done | bytes 131088 | tf_op jit(solution)/shard_map/reduce_scatter | solution.py:348
  (360 shorter events, 431.8 us)
Async XLA Ops:
  7.2 31.0 %all-gather.11.cloned.1.call-start = ((), (), s32[]{:S(2)}) async-start(), calls=%async_computation.20 | async-start | bytes 1310720 | tf_op jit(solution)/shard_map/all_gather | solution.py:81
  9.1 58.2 %all-gather.13.cloned.1.call-start = ((), (), s32[]{:S(2)}) async-start(), calls=%async_computation.21 | async-start | bytes 1310720 | tf_op jit(solution)/shard_map/all_gather | solution.py:82
  10.9 94.1 %all-gather.9.cloned.1.call-start = ((), (), s32[]{:S(2)}) async-start(), calls=%async_computation.19 | async-start | bytes 2621440 | tf_op jit(solution)/shard_map/all_gather | solution.py:80
  41.2 27.9 %all-to-all-start.1 = ((bf16[256,8,128]{0,2,1:T(8,128)(2,1)}), bf16[256,8,128]{0,2,1:T(8,128)(2,1)S(1)}, u32[]{:S(2)}, u32[]{:S(2)}) async-start(bf16[256,8,128]{0,2,1:T(8,128)(2,1)} %bitcast.11), calls=%async_computation.1 | async-start | bytes 1048576 | tf_op jit(solution)/shard_map/all_to_all | solution.py:123
  70.0 39.8 %all-to-all-start.2 = ((bf16[256,8,128]{0,2,1:T(8,128)(2,1)}), bf16[256,8,128]{0,2,1:T(8,128)(2,1)}, u32[]{:S(2)}, u32[]{:S(2)}) async-start(bf16[256,8,128]{0,2,1:T(8,128)(2,1)} %bitcast.14), calls=%async_computation.2 | async-start | bytes 1048576 | tf_op jit(solution)/shard_map/all_to_all | solution.py:124
  109.8 32.6 %all-to-all-start = ((bf16[256,8,128]{0,2,1:T(8,128)(2,1)}), bf16[256,8,128]{0,2,1:T(8,128)(2,1)S(1)}, u32[]{:S(2)}, u32[]{:S(2)}) async-start(bf16[256,8,128]{0,2,1:T(8,128)(2,1)} %bitcast.7), calls=%async_computation | async-start | bytes 1048576 | tf_op jit(solution)/shard_map/all_to_all | solution.py:122
  115.3 88.0 %all-gather.15.cloned.1.call-start = ((), (), s32[]{:S(2)}) async-start(), calls=%async_computation.22 | async-start | bytes 2621440 | tf_op jit(solution)/shard_map/all_gather | solution.py:83
  186.3 18.3 %all-to-all-start.3 = ((bf16[8,256,128]{1,2,0:T(8,128)(2,1)}), bf16[8,256,128]{1,2,0:T(8,128)(2,1)S(1)}, u32[]{:S(2)}, u32[]{:S(2)}) async-start(bf16[8,256,128]{1,2,0:T(8,128)(2,1)} %copy.240), calls=%async_computation.3 | async-start | bytes 1048576 | tf_op jit(solution)/shard_map/all_to_all | solution.py:159
  223.0 143.6 %all-to-all-start.6 = ((bf16[16,192,1024]{2,1,0:T(8,128)(2,1)}), bf16[16,192,1024]{2,1,0:T(8,128)(2,1)}, u32[]{:S(2)}, u32[]{:S(2)}) async-start(bf16[16,192,1024]{2,1,0:T(8,128)(2,1)} %bitcast.267), calls=%async_computation.6 | async-start | bytes 12582912 | tf_op jit(solution)/shard_map/all_to_all | solution.py:203
  366.6 143.9 %all-to-all-start.4 = ((bf16[16,192,1024]{2,1,0:T(8,128)(2,1)}), bf16[16,192,1024]{2,1,0:T(8,128)(2,1)}, u32[]{:S(2)}, u32[]{:S(2)}) async-start(bf16[16,192,1024]{2,1,0:T(8,128)(2,1)} %bitcast.266), calls=%async_computation.4 | async-start | bytes 12582912 | tf_op jit(solution)/shard_map/all_to_all | solution.py:179
  375.1 141.7 %all-gather.17.cloned.1.call-start = ((), (), s32[]{:S(2)}) async-start(), calls=%async_computation.23 | async-start | bytes 5242880 | tf_op jit(solution)/shard_map/all_gather | solution.py:89
  376.5 153.2 %all-gather.19.cloned.1.call-start = ((), (), s32[]{:S(2)}) async-start(), calls=%async_computation.24 | async-start | bytes 2621440 | tf_op jit(solution)/shard_map/all_gather | solution.py:90
  569.0 144.2 %all-to-all-start.5 = ((bf16[2,1536,1024]{2,0,1:T(2,128)(2,1)}), bf16[2,1536,1024]{2,0,1:T(2,128)(2,1)}, u32[]{:S(2)}, u32[]{:S(2)}) async-start(bf16[2,1536,1024]{2,0,1:T(2,128)(2,1)} %copy.251), calls=%async_computation.5 | async-start | bytes 12582912 | tf_op jit(solution)/shard_map/all_to_all | solution.py:189
  713.2 143.7 %all-to-all-start.7 = ((bf16[2,1536,1024]{2,0,1:T(2,128)(2,1)}), bf16[2,1536,1024]{2,0,1:T(2,128)(2,1)}, u32[]{:S(2)}, u32[]{:S(2)}) async-start(bf16[2,1536,1024]{2,0,1:T(2,128)(2,1)} %copy.257), calls=%async_computation.7 | async-start | bytes 12582912 | tf_op jit(solution)/shard_map/all_to_all | solution.py:218
  721.5 411.0 %reduce-scatter.20.cloned.1.call-start = ((), (), s32[]{:S(2)}) async-start(), calls=%async_computation.30 | async-start | bytes 2621440 | tf_op jit(solution)/shard_map/reduce_scatter | solution.py:360
  915.4 20.2 %all-to-all-start.8 = ((bf16[256,8,128]{2,0,1:T(8,128)(2,1)}), bf16[256,8,128]{2,0,1:T(8,128)(2,1)S(1)}, u32[]{:S(2)}, u32[]{:S(2)}) async-start(bf16[256,8,128]{2,0,1:T(8,128)(2,1)} %bitcast.228), calls=%async_computation.8 | async-start | bytes 1048576 | tf_op jit(solution)/shard_map/all_to_all | solution.py:235
  922.6 212.1 %reduce-scatter.18.cloned.1.call-start = ((), (), s32[]{:S(2)}) async-start(), calls=%async_computation.29 | async-start | bytes 5242880 | tf_op jit(solution)/shard_map/reduce_scatter | solution.py:357
  1064.7 18.2 %all-to-all-start.10 = ((bf16[8,256,128]{1,2,0:T(8,128)(2,1)}), bf16[8,256,128]{1,2,0:T(8,128)(2,1)S(1)}, u32[]{:S(2)}, u32[]{:S(2)}) async-start(bf16[8,256,128]{1,2,0:T(8,128)(2,1)} %copy.265), calls=%async_computation.10 | async-start | bytes 1048576 | tf_op jit(solution)/shard_map/all_to_all | solution.py:280
  1070.8 128.6 %reduce-scatter.22.cloned.1.call-start = ((), (), s32[]{:S(2)}) async-start(), calls=%async_computation.31 | async-start | bytes 540672
  1073.1 262.2 %reduce-scatter.12.cloned.1.call-start = ((), (), s32[]{:S(2)}) async-start(), calls=%async_computation.26 | async-start | bytes 2162688 | tf_op jit(solution)/shard_map/reduce_scatter | solution.py:349
  1085.8 386.2 %reduce-scatter.14.cloned.1.call-start = ((), (), s32[]{:S(2)}) async-start(), calls=%async_computation.27 | async-start | bytes 2162688 | tf_op jit(solution)/shard_map/reduce_scatter | solution.py:350
  1107.3 506.8 %reduce-scatter.16.cloned.1.call-start = ((), (), s32[]{:S(2)}) async-start(), calls=%async_computation.28 | async-start | bytes 4325376 | tf_op jit(solution)/shard_map/reduce_scatter | solution.py:351
  1110.1 646.5 %reduce-scatter.10.cloned.1.call-start = ((), (), s32[]{:S(2)}) async-start(), calls=%async_computation.25 | async-start | bytes 4325376 | tf_op jit(solution)/shard_map/reduce_scatter | solution.py:348
  1137.5 116.7 %copy-start.36 = (f32[256]{0:T(256)S(1)}, f32[256]{0:T(256)}, u32[]{:S(2)}) copy-start(f32[256]{0:T(256)} %copy-done.35) | copy-start | bytes 3076
  (50 other events, 881.2 us)
Sparse Core Ops, SparseCore 0:
  10.4 27.7 all-gather.10
  40.6 26.6 all-gather.12
  69.7 35.3 all-gather.8
  118.2 34.9 all-gather.14
  378.0 53.1 all-gather.16
  433.4 35.2 all-gather.18
  731.1 35.6 reduce-scatter.19
  935.7 53.0 reduce-scatter.17
  1073.9 125.4 reduce-scatter.21
  1202.2 133.0 reduce-scatter.11
  1338.1 133.8 reduce-scatter.13
  1474.8 139.2 reduce-scatter.15
  1617.0 139.5 reduce-scatter.9
where the time goes:
time: 1780 us; the launch traced here: 1760 us
  waiting for transfers between devices  1050 us (59%)
  local copies, waits for them, and re-layouts  213 us (12%)
  matrix products  190 us (11%)
  blocking collectives  115 us (6%)
  other arithmetic  94.3 us (5%)
  starting transfers between devices  70.5 us (4%)
    reduce_scatter x1, waiting for transfers between devices, on_device(): lax.psum_scatter(grad_wq, ('dp', 'seq'), scatter_dimension=0, tiled=True)  143 us
    reduce_scatter x1, waiting for transfers between devices, on_device(): lax.psum_scatter(grad_wo, ('dp', 'seq'), scatter_dimension=0, tiled=True)  142 us
    reduce_scatter x1, waiting for transfers between devices, on_device(): lax.psum_scatter(grad_wv, ('dp', 'seq'), scatter_dimension=0, tiled=True)  137 us
    all_to_all x1, waiting for transfers between devices, on_device(): lax.all_to_all(send_rows, 'seq', split_axis=0, concat_axis=1, tiled=True)  125 us
    all_to_all x1, waiting for transfers between devices, on_device(): lax.all_to_all(send_cot, 'seq', split_axis=0, concat_axis=1, tiled=True)  112 us
    all_to_all x1, waiting for transfers between devices, on_device(): lax.all_to_all(expert_res, 'seq', split_axis=1, concat_axis=0, tiled=True)  103 us
    reduce_scatter x1, waiting for transfers between devices, on_device(): lax.psum_scatter(grad_wk, ('dp', 'seq'), scatter_dimension=0, tiled=True)  80 us
    all_to_all x1, waiting for transfers between devices, on_device(): lax.all_to_all(rows_cot, 'seq', split_axis=1, concat_axis=0, tiled=True)  71.2 us
  transfers between devices with their start and end apart: 23, of which 14 were waited for; matrix products, arithmetic and copies ran while one was open for 24% of the time, Pallas kernels for 0%

commit v1 on v0

v1 whole, which is shorter than its diff:
```python
import jax
import jax.numpy as jnp
from jax import lax
from jax.experimental import pallas as pl
from jax.experimental.pallas import tpu as pltpu
from jax.sharding import PartitionSpec as P

MESH = pl.DeviceIdType.MESH


def _block(ref, j, cut):
    if cut is None:
        return ref.at[j]
    return ref.at[:, pl.ds(pl.multiple_of(j * cut, cut), cut)]


def exchange(collective_id, ops):
    axes = tuple(dict.fromkeys(axis for _, axis, _, _ in ops))
    size = {axis: lax.axis_size(axis) for axis in axes}
    out_shapes, out_specs, scratch, places = [], [], [], []
    for kind, axis, x, cut in ops:
        count = size[axis]
        out_spec = pl.BlockSpec(memory_space=pl.ANY)
        extra = []
        if kind == "gather":
            shape, dtype, copies = (count,) + x.shape, x.dtype, count - 1
        elif kind == "swap":
            copies, dtype = count - 1, x.dtype
            if cut is None:
                shape = x.shape
            elif cut[0] == "in":
                shape = (count, x.shape[0], cut[1])
            else:
                shape = (x.shape[1], count * cut[1])
        else:
            chips = count // 2
            shape, dtype, copies = x.shape[1:], jnp.float32, 2 * chips - 1
            out_spec = pl.BlockSpec(memory_space=pltpu.VMEM)
            extra = [
                pltpu.VMEM((chips,) + x.shape[1:], x.dtype),
                pltpu.VMEM((chips,) + x.shape[1:], x.dtype),
                pltpu.VMEM((chips,) + x.shape[1:], x.dtype),
                pltpu.VMEM((chips,) + x.shape[1:], x.dtype),
                pltpu.SemaphoreType.DMA((chips,)),
            ]
        out_shapes.append(jax.ShapeDtypeStruct(shape, dtype))
        out_specs.append(out_spec)
        places.append((len(scratch), len(extra)))
        scratch += [
            pltpu.SemaphoreType.DMA((copies,)),
            pltpu.SemaphoreType.DMA((copies,)),
            pltpu.SemaphoreType.DMA,
        ] + extra

    def kernel(*refs):
        ins, outs, work = refs[: len(ops)], refs[len(ops) : 2 * len(ops)], refs[2 * len(ops) :]
        me = {axis: lax.axis_index(axis) for axis in axes}
        barrier = pltpu.get_barrier_semaphore()
        for axis in axes:
            for k in range(1, size[axis]):
                pl.semaphore_signal(
                    barrier,
                    inc=1,
                    device_id={axis: lax.rem(me[axis] + k, size[axis])},
                    device_id_type=MESH,
                )
        pl.semaphore_wait(barrier, sum(size[axis] - 1 for axis in axes))

        def remote(axis, src, dst, send, recv, to):
            return pltpu.make_async_remote_copy(
                src_ref=src,
                dst_ref=dst,
                send_sem=send,
                recv_sem=recv,
                device_id={axis: to},
                device_id_type=MESH,
            )

        second, third = [], []
        for (kind, axis, _, cut), x, o, (at, extra) in zip(ops, ins, outs, places):
            send, recv, local = work[at : at + 3]
            count, my = size[axis], me[axis]
            if kind == "swap":
                into = cut[1] if cut is not None and cut[0] == "out" else None
                outof = cut[1] if cut is not None and cut[0] == "in" else None
                own = pltpu.make_async_copy(_block(x, my, outof), _block(o, my, into), local)
                own.start()
                third.append(own.wait)
                for k in range(1, count):
                    to = lax.rem(my + k, count)
                    copy = remote(
                        axis,
                        _block(x, to, outof),
                        _block(o, my, into),
                        send.at[k - 1],
                        recv.at[k - 1],
                        to,
                    )
                    copy.start()
                    frm = lax.rem(my + count - k, count)
                    arrive = remote(
                        axis,
                        _block(x, to, outof),
                        _block(o, frm, into),
                        send.at[k - 1],
                        recv.at[k - 1],
                        to,
                    )
                    third.append(copy.wait_send)
                    third.append(arrive.wait_recv)
            elif kind == "gather" and axis == "dp":
                own = pltpu.make_async_copy(x, o.at[my], local)
                own.start()
                third.append(own.wait)
                for k in range(1, count):
                    to = lax.rem(my + k, count)
                    frm = lax.rem(my + count - k, count)
                    copy = remote(axis, x, o.at[my], send.at[k - 1], recv.at[k - 1], to)
                    copy.start()
                    third.append(copy.wait_send)
                    third.append(
                        remote(
                            axis, x, o.at[frm], send.at[k - 1], recv.at[k - 1], to
                        ).wait_recv
                    )
            elif kind == "gather":
                chips = count // 2
                chip, core = my // 2, lax.rem(my, 2)
                sibling = my + 1 - 2 * core
                own = pltpu.make_async_copy(x, o.at[my], local)
                own.start()
                third.append(own.wait)
                for k in range(1, chips):
                    to = lax.rem(chip + k, chips) * 2 + core
                    copy = remote(axis, x, o.at[my], send.at[k], recv.at[k], to)
                    copy.start()
                    third.append(copy.wait_send)
                copy = remote(axis, x, o.at[my], send.at[0], recv.at[0], sibling)
                copy.start()
                third.append(copy.wait_send)
                third.append(
                    remote(
                        axis, x, o.at[sibling], send.at[0], recv.at[0], sibling
                    ).wait_recv
                )

                def forward(
                    k, axis=axis, x=x, o=o, send=send, recv=recv, chips=chips, chip=chip, core=core, sibling=sibling
                ):
                    frm = lax.rem(chip + chips - k, chips) * 2
                    remote(
                        axis, x, o.at[frm + core], send.at[k], recv.at[k], sibling
                    ).wait_recv()
                    slot = chips - 1 + k
                    copy = remote(
                        axis,
                        o.at[frm + core],
                        o.at[frm + core],
                        send.at[slot],
                        recv.at[slot],
                        sibling,
                    )
                    copy.start()
                    third.append(copy.wait_send)
                    third.append(
                        remote(
                            axis,
                            x,
                            o.at[frm + 1 - core],
                            send.at[slot],
                            recv.at[slot],
                            sibling,
                        ).wait_recv
                    )

                for k in range(1, chips):
                    second.append((k, lambda k=k, forward=forward: forward(k)))
            else:
                chips = count // 2
                chip, core = my // 2, lax.rem(my, 2)
                sibling = my + 1 - 2 * core
                mine, theirs, pre, far, loads = work[at + 3 : at + 3 + extra]
                order = [k % chips for k in range(1, chips + 1)]
                for k in order:
                    to = lax.rem(chip + k, chips)
                    remote(
                        axis,
                        x.at[2 * to + 1 - core],
                        theirs.at[k],
                        send.at[k],
                        recv.at[k],
                        sibling,
                    ).start()
                    pltpu.make_async_copy(x.at[2 * to + core], mine.at[k], loads.at[k]).start()

                def fold(k, last, axis=axis, x=x, o=o, send=send, recv=recv, chips=chips, chip=chip, core=core, sibling=sibling, mine=mine, theirs=theirs, pre=pre, far=far, loads=loads):
                    to = lax.rem(chip + k, chips)
                    give = remote(
                        axis,
                        x.at[2 * to + 1 - core],
                        theirs.at[k],
                        send.at[k],
                        recv.at[k],
                        sibling,
                    )
                    give.wait_recv()
                    third.append(give.wait_send)
                    pltpu.make_async_copy(
                        x.at[2 * to + core], mine.at[k], loads.at[k]
                    ).wait()
                    both = mine[k].astype(jnp.float32) + theirs[k].astype(jnp.float32)
                    if not last:
                        pre[k] = both.astype(pre.dtype)
                        copy = remote(
                            axis,
                            pre.at[k],
                            far.at[k],
                            send.at[chips - 1 + k],
                            recv.at[chips - 1 + k],
                            to * 2 + core,
                        )
                        copy.start()
                        third.append(copy.wait_send)
                    else:
                        o[...] = both

                for k in order:
                    second.append((k or chips, lambda k=k, fold=fold: fold(k, k == 0)))

                def total(k, axis=axis, o=o, send=send, recv=recv, chips=chips, pre=pre, far=far, core=core, chip=chip):
                    remote(
                        axis,
                        pre.at[k],
                        far.at[k],
                        send.at[chips - 1 + k],
                        recv.at[chips - 1 + k],
                        lax.rem(chip + k, chips) * 2 + core,
                    ).wait_recv()
                    o[...] += far[k].astype(jnp.float32)

                for k in range(1, chips):
                    second.append((chips + k, lambda k=k, total=total: total(k)))
        for _, run in sorted(second, key=lambda item: item[0]):
            run()
        for wait in third:
            wait()

    return pl.pallas_call(
        kernel,
        name=f"exchange{collective_id}",
        out_shape=out_shapes,
        in_specs=[pl.BlockSpec(memory_space=pl.ANY)] * len(ops),
        out_specs=out_specs,
        scratch_shapes=scratch,
        compiler_params=pltpu.CompilerParams(
            collective_id=collective_id, has_side_effects=True, vmem_limit_bytes=48 << 20
        ),
    )(*[x for _, _, x, _ in ops])

QUERY_HEADS = 16
KEY_VALUE_HEADS = 8
HEAD_SIZE = 64
FFE = 512
TOP = 8

att_mult = 0.015625
res_mult = 0.22
norm_eps = 1e-06
rope_theta = 10000.0
LANES = 128
bf16 = jnp.bfloat16
f32 = jnp.float32
HEADS_LANES = 128


def dot_nt(a, b):
    return lax.dot_general(a, b, (((1,), (1,)), ((), ())), preferred_element_type=f32)


def dot_nn(a, b):
    return lax.dot_general(a, b, (((1,), (0,)), ((), ())), preferred_element_type=f32)


def dot_tn(a, b):
    return lax.dot_general(a, b, (((0,), (0,)), ((), ())), preferred_element_type=f32)


def turn(x):
    half = HEAD_SIZE // 2
    lane = lax.broadcasted_iota(jnp.int32, x.shape, 1)
    width = x.shape[1]
    return jnp.where(
        lax.rem(lane, HEAD_SIZE) < half, pltpu.roll(x, width - half, 1), pltpu.roll(x, half, 1)
    )


def rope_tables(length):
    half = HEAD_SIZE // 2
    frequency = rope_theta ** (-jnp.arange(half, dtype=f32) * 2.0 / HEAD_SIZE)
    angles = jnp.arange(length, dtype=jnp.int32).astype(f32)[:, None] * frequency[None, :]
    cos, sin = jnp.cos(angles), jnp.sin(angles)
    repeat = LANES // HEAD_SIZE
    return (
        jnp.concatenate([cos, cos] * repeat, axis=1),
        jnp.concatenate([-sin, sin] * repeat, axis=1),
    )


def stack_heads(x, heads):
    return jnp.concatenate(
        [x[:, h * HEAD_SIZE : (h + 1) * HEAD_SIZE] for h in range(heads)], axis=0
    )


def attend_forward(tok_all, w_own, gain, cos, sin, start, heads):
    blocks, rows, width = tok_all.shape
    length = blocks * rows
    cols = heads * rows
    first = start.reshape(blocks, rows)[:, 0] // rows
    start_rows = jnp.tile(start.reshape(blocks, 1, rows), (1, 1, heads))
    out_width = heads * HEAD_SIZE

    def kernel(first_ref, tok, w, gain_ref, cos_ref, sin_ref, start_ref, na_ref, q_ref, kv_ref, att_ref, ot_ref, lse_ref, k_scr, vt_scr):
        i = pl.program_id(0)
        x = tok[0].astype(f32)
        scale = lax.rsqrt(jnp.mean(x * x, axis=-1, keepdims=True) + norm_eps)
        na = (x * scale * gain_ref[...].astype(f32)).astype(bf16)
        na_ref[0] = na
        qkv = dot_nn(na, w[...])
        c, s = cos_ref[0], sin_ref[0]
        q, kv = qkv[:, :HEADS_LANES], qkv[:, HEADS_LANES:]
        q = (q * c + turn(q) * s).astype(bf16)
        lane = lax.broadcasted_iota(jnp.int32, kv.shape, 1)
        kv = jnp.where(lane < HEAD_SIZE, kv * c + turn(kv) * s, kv).astype(bf16)
        q_ref[0] = q
        kv_ref[0] = kv
        k_scr[i] = kv[:, :HEAD_SIZE]
        vt_scr[i] = kv.astype(f32).T[HEAD_SIZE:].astype(bf16)
        q2 = stack_heads(q, heads)
        start_row = start_ref[0]
        query = i * rows + lax.rem(lax.broadcasted_iota(jnp.int32, (1, cols), 1), rows)
        key_iota = lax.broadcasted_iota(jnp.int32, (rows, cols), 0)

        def step(j, carry):
            top, total, ot = carry
            scores = dot_nt(k_scr[j], q2) * att_mult
            key = key_iota + j * rows
            scores = jnp.where((key >= start_row) & (key <= query), scores, -1e30)
            new_top = jnp.maximum(top, jnp.max(scores, axis=0, keepdims=True))
            p = jnp.exp(scores - new_top)
            keep = jnp.exp(top - new_top)
            total = total * keep + jnp.sum(p, axis=0, keepdims=True)
            ot = ot * keep + dot_nn(vt_scr[j], p.astype(bf16))
            return new_top, total, ot

        top, total, ot = lax.fori_loop(
            first_ref[i],
            i + 1,
            step,
            (
                jnp.full((1, cols), -1e30, f32),
                jnp.zeros((1, cols), f32),
                jnp.zeros((HEAD_SIZE, cols), f32),
            ),
        )
        ot = ot / total
        ot_ref[0] = ot
        lse_ref[0] = top + jnp.log(total)
        out = ot.T
        att_ref[0] = jnp.concatenate(
            [out[h * rows : (h + 1) * rows] for h in range(heads)], axis=1
        ).astype(bf16)

    def block(shape):
        return pl.BlockSpec((1,) + shape, lambda i, _: (i, 0, 0))

    def whole(shape):
        return pl.BlockSpec(shape, lambda i, _: (0,) * len(shape))

    grid_spec = pltpu.PrefetchScalarGridSpec(
        num_scalar_prefetch=1,
        grid=(blocks,),
        in_specs=[
            block((rows, width)),
            whole(w_own.shape),
            whole((1, width)),
            block((rows, LANES)),
            block((rows, LANES)),
            block((1, cols)),
        ],
        out_specs=[
            block((rows, width)),
            block((rows, HEADS_LANES)),
            block((rows, LANES)),
            block((rows, out_width)),
            block((HEAD_SIZE, cols)),
            block((1, cols)),
        ],
        scratch_shapes=[
            pltpu.VMEM((blocks, rows, HEAD_SIZE), bf16),
            pltpu.VMEM((blocks, HEAD_SIZE, rows), bf16),
        ],
    )
    return pl.pallas_call(
        kernel,
        name="attend_forward",
        grid_spec=grid_spec,
        out_shape=[
            jax.ShapeDtypeStruct((blocks, rows, width), bf16),
            jax.ShapeDtypeStruct((blocks, rows, HEADS_LANES), bf16),
            jax.ShapeDtypeStruct((blocks, rows, LANES), bf16),
            jax.ShapeDtypeStruct((blocks, rows, out_width), bf16),
            jax.ShapeDtypeStruct((blocks, HEAD_SIZE, cols), f32),
            jax.ShapeDtypeStruct((blocks, 1, cols), f32),
        ],
        cost_estimate=pl.CostEstimate(
            flops=2 * length * width * 256 + 2 * length * length * cols // rows * 128,
            bytes_accessed=2 * length * width * 4,
            transcendentals=length * length,
        ),
        compiler_params=pltpu.CompilerParams(
            dimension_semantics=("arbitrary",), vmem_limit_bytes=40 << 20
        ),
    )(
        first,
        tok_all,
        w_own,
        gain,
        cos.reshape(blocks, rows, LANES),
        sin.reshape(blocks, rows, LANES),
        start_rows,
    )


def attend_backward(q_all, kv_all, cot, ot, lse, cos, sin, start, heads):
    blocks, rows, _ = q_all.shape
    length = blocks * rows
    cols = heads * rows
    first = start.reshape(blocks, rows)[:, 0] // rows
    start_rows = jnp.tile(start.reshape(blocks, 1, rows), (1, 1, heads))

    def kernel(first_ref, q_ref, kv_ref, do_ref, ot_ref, lse_ref, cos_ref, sin_ref, start_ref, out_ref, dk_scr, dv_scr, dq_scr):
        i = pl.program_id(0)

        @pl.when(i == 0)
        def _():
            dk_scr[...] = jnp.zeros_like(dk_scr)
            dv_scr[...] = jnp.zeros_like(dv_scr)

        q2 = stack_heads(q_ref[0], heads)
        do2 = stack_heads(do_ref[0], heads)
        delta = jnp.sum(do2.astype(f32).T * ot_ref[0], axis=0, keepdims=True)
        log_total = lse_ref[0]
        start_row = start_ref[0]
        query = i * rows + lax.rem(lax.broadcasted_iota(jnp.int32, (1, cols), 1), rows)
        key_iota = lax.broadcasted_iota(jnp.int32, (rows, cols), 0)
        dq_scr[...] = jnp.zeros_like(dq_scr)

        @pl.loop(first_ref[i], i + 1)
        def _(j):
            kv = kv_ref[j]
            k, v = kv[:, :HEAD_SIZE], kv[:, HEAD_SIZE:]
            scores = dot_nt(k, q2) * att_mult
            key = key_iota + j * rows
            p = jnp.where(
                (key >= start_row) & (key <= query), jnp.exp(scores - log_total), 0.0
            )
            ds = (p * (dot_nt(v, do2) - delta)).astype(bf16)
            dv_scr[j] += dot_nn(p.astype(bf16), do2)
            dk_scr[j] += dot_nn(ds, q2)
            dq_scr[...] += dot_tn(ds, k)

        def rope_back(x, c, s):
            return (x * c - turn(x) * s).astype(bf16)

        dq = dq_scr[...] * att_mult
        dq = [dq[h * rows : (h + 1) * rows] for h in range(heads)]
        if heads * HEAD_SIZE < HEADS_LANES:
            dq.append(jnp.zeros((rows, HEADS_LANES - heads * HEAD_SIZE), f32))
        dq = jnp.concatenate(dq, axis=1).astype(bf16).astype(f32)
        out_ref[i, :, :HEADS_LANES] = rope_back(dq, cos_ref[i], sin_ref[i])

        @pl.when(i == blocks - 1)
        def _():
            @pl.loop(0, blocks)
            def _(j):
                kv = jnp.concatenate([dk_scr[j] * att_mult, dv_scr[j]], axis=1)
                lane = lax.broadcasted_iota(jnp.int32, kv.shape, 1)
                out_ref[j, :, HEADS_LANES:] = jnp.where(
                    lane < HEAD_SIZE, kv * cos_ref[j] - turn(kv) * sin_ref[j], kv
                ).astype(bf16)

    def block(shape):
        return pl.BlockSpec((1,) + shape, lambda i, _: (i, 0, 0))

    def whole(shape):
        return pl.BlockSpec(shape, lambda i, _: (0,) * len(shape))

    grid_spec = pltpu.PrefetchScalarGridSpec(
        num_scalar_prefetch=1,
        grid=(blocks,),
        in_specs=[
            block((rows, HEADS_LANES)),
            whole((blocks, rows, LANES)),
            block((rows, heads * HEAD_SIZE)),
            block((HEAD_SIZE, cols)),
            block((1, cols)),
            whole((blocks, rows, LANES)),
            whole((blocks, rows, LANES)),
            block((1, cols)),
        ],
        out_specs=whole((blocks, rows, HEADS_LANES + LANES)),
        scratch_shapes=[
            pltpu.VMEM((blocks, rows, HEAD_SIZE), f32),
            pltpu.VMEM((blocks, rows, HEAD_SIZE), f32),
            pltpu.VMEM((cols, HEAD_SIZE), f32),
        ],
    )
    return pl.pallas_call(
        kernel,
        name="attend_backward",
        grid_spec=grid_spec,
        out_shape=jax.ShapeDtypeStruct((blocks, rows, HEADS_LANES + LANES), bf16),
        cost_estimate=pl.CostEstimate(
            flops=5 * length * length * cols // rows * 128,
            bytes_accessed=2 * length * 1024,
            transcendentals=length * length,
        ),
        compiler_params=pltpu.CompilerParams(
            dimension_semantics=("arbitrary",), vmem_limit_bytes=48 << 20
        ),
    )(
        first,
        q_all,
        kv_all,
        cot,
        ot,
        lse,
        cos.reshape(blocks, rows, LANES),
        sin.reshape(blocks, rows, LANES),
        start_rows,
    )


def rms_parts(values):
    return lax.rsqrt(jnp.mean(values * values, axis=-1, keepdims=True) + norm_eps)


def rms_pull(values, scale, gain, cot):
    weighted = cot * gain
    pulled = scale * weighted - values * (scale * scale * scale) * jnp.mean(
        weighted * values, axis=-1, keepdims=True
    )
    return pulled, jnp.sum(cot * values * scale, axis=0)


def on_device(
    tokens,
    out_grad,
    doc_ids,
    expert_picks,
    w_query,
    key_weight_matrix,
    value_weight_matrix,
    w_out,
    w_router,
    gain_attn,
    gain_moe,
    expert_in,
    expert_out,
):
    devices, parts = lax.axis_size("seq"), lax.axis_size("dp")
    me = lax.axis_index("seq")
    rows, width = tokens.shape[1:]
    length = rows * devices
    experts = w_router.shape[1]
    own_experts = expert_in.shape[0]
    heads = QUERY_HEADS // devices
    group = QUERY_HEADS // KEY_VALUE_HEADS
    share = max(1, group // heads)
    q_width = heads * HEAD_SIZE
    w_rows = w_query.shape[0]

    wq = w_query.astype(bf16).reshape(w_rows, devices, q_width)
    wq = jnp.pad(wq, ((0, 0), (0, 0), (0, HEADS_LANES - q_width)))
    wk = key_weight_matrix.astype(bf16).reshape(w_rows, KEY_VALUE_HEADS, HEAD_SIZE)
    wv = value_weight_matrix.astype(bf16).reshape(w_rows, KEY_VALUE_HEADS, HEAD_SIZE)
    wkv = jnp.repeat(jnp.concatenate([wk, wv], axis=2), share, axis=1)
    w_cols = HEADS_LANES + LANES
    w_all = jnp.concatenate([wq, wkv], axis=2).reshape(w_rows, devices * w_cols)
    w_own = lax.dynamic_slice_in_dim(w_all, me * w_cols, w_cols, 1)
    misc = jnp.concatenate(
        [w_router, gain_attn[:, None], gain_moe[:, None]], axis=1
    ).astype(bf16)
    misc = jnp.pad(misc, ((0, 0), (0, LANES - experts - 2)))
    ints = jnp.concatenate([expert_picks[0].T, doc_ids], axis=0)
    ints = jnp.pad(ints, ((0, 16 - TOP - 1), (0, 0)))

    out_grad_all = lax.all_gather(out_grad[0], "seq", axis=0, tiled=True)
    expert_in_full = lax.all_gather(expert_in.astype(bf16), "dp", axis=1, tiled=True)
    expert_out_full = lax.all_gather(expert_out.astype(bf16), "dp", axis=1, tiled=True)
    w_full = lax.all_gather(w_all, "dp", axis=0, tiled=True)

    tok_all, ints_all, w_own_all, wo_full, misc_full = exchange(
        0,
        [
            ("gather", "seq", tokens[0], None),
            ("gather", "seq", ints, None),
            ("gather", "dp", w_own, None),
            ("gather", "dp", w_out.astype(bf16), None),
            ("gather", "dp", misc, None),
        ],
    )
    w_own_all = w_own_all.reshape(width, w_cols)
    wo_full = wo_full.reshape(width, width)
    misc_full = misc_full.reshape(width, LANES)
    router_full = misc_full[:, :experts]
    gain_a = misc_full[:, experts]
    gain_m = misc_full[:, experts + 1].astype(f32)
    docs = ints_all[:, TOP].reshape(length)
    picks = ints_all[:, :TOP].transpose(1, 0, 2).reshape(TOP, length)
    start = jnp.sum((docs[:, None] < docs[None, :]).astype(jnp.int32), axis=0)
    cos, sin = rope_tables(length)

    normed_a, q_all, kv_all, attended_own, ot, lse = attend_forward(
        tok_all, w_own_all, gain_a[None], cos, sin, start, heads
    )
    wide = q_width % LANES == 0
    (attended,) = exchange(
        1, [("swap", "seq", attended_own, ("out", q_width) if wide else None)]
    )
    if not wide:
        attended = attended.transpose(1, 0, 2).reshape(rows, devices * q_width)

    resid = tokens[0].astype(f32)
    mid = resid + res_mult * dot_nn(attended, wo_full)
    mid_scale = rms_parts(mid)
    normed_m = (mid * mid_scale * gain_m).astype(bf16)
    (moe_all,) = exchange(2, [("gather", "seq", normed_m, None)])
    moe_all = moe_all.reshape(length, width)

    logits = lax.dot_general(
        router_full, moe_all, (((0,), (1,)), ((), ())), preferred_element_type=f32
    )
    chosen = jnp.any(
        picks[:, None, :] == jnp.arange(experts, dtype=jnp.int32)[None, :, None], axis=0
    )
    logits = jnp.where(chosen, logits, -jnp.inf)
    gates = jnp.exp(logits - jnp.max(logits, axis=0, keepdims=True))
    gates = gates / jnp.sum(gates, axis=0, keepdims=True)
    own_gates = lax.dynamic_slice_in_dim(gates, me * own_experts, own_experts, 0)

    out_cot = out_grad_all.astype(f32) * res_mult
    branch = jnp.zeros((length, width), f32)
    moe_cot = jnp.zeros((length, width), f32)
    gate_cots, grads_in, grads_out = [], [], []
    for e in range(own_experts):
        gate = own_gates[e][:, None]
        lin = dot_nn(moe_all, expert_in_full[e])
        gate_lin, up_lin = lin[:, :FFE], lin[:, FFE:]
        sig = jax.nn.sigmoid(gate_lin)
        silu = gate_lin * sig
        hidden = (silu * up_lin).astype(bf16)
        res = dot_nt(hidden, expert_out_full[e]).astype(bf16).astype(f32)
        branch = branch + gate * res
        gate_cots.append(jnp.sum(out_cot * res, axis=1))
        slot = (gate * out_cot).astype(bf16)
        hidden_cot = dot_nn(slot, expert_out_full[e])
        grads_out.append(dot_tn(slot, hidden).astype(bf16))
        lin_cot = jnp.concatenate(
            [hidden_cot * up_lin * (sig * (1 + gate_lin * (1 - sig))), hidden_cot * silu], axis=1
        ).astype(bf16)
        grads_in.append(dot_tn(moe_all, lin_cot).astype(bf16))
        moe_cot = moe_cot + dot_nt(lin_cot, expert_in_full[e]).astype(bf16).astype(f32)
    gate_cot = jnp.pad(
        jnp.stack(gate_cots).reshape(own_experts, devices, rows).transpose(1, 0, 2),
        ((0, 0), (0, 8 - own_experts), (0, 0)),
    )
    moe_sum, branch_sum, gate_cot = exchange(
        3,
        [
            ("sum", "seq", moe_cot.astype(bf16).reshape(devices, rows, width), None),
            ("sum", "seq", branch.astype(bf16).reshape(devices, rows, width), None),
            ("swap", "seq", gate_cot, None),
        ],
    )
    grads_in = jnp.stack(grads_in).reshape(own_experts, parts, w_rows, 2 * FFE)
    grads_out = jnp.stack(grads_out).reshape(own_experts, parts, w_rows, FFE)
    grads_in = lax.all_to_all(grads_in, "dp", split_axis=1, concat_axis=1)
    grads_out = lax.all_to_all(grads_out, "dp", split_axis=1, concat_axis=1)
    grad_e_in = jnp.sum(grads_in.astype(f32), axis=1)
    grad_e_out = jnp.sum(grads_out.astype(f32), axis=1)

    output = (mid + res_mult * branch_sum).astype(bf16)[None]
    gate_cot = gate_cot[:, :own_experts].reshape(experts, rows)
    my_gates = lax.dynamic_slice_in_dim(gates, me * rows, rows, 1)
    pick_cot = my_gates * (gate_cot - jnp.sum(my_gates * gate_cot, axis=0, keepdims=True))
    logit_cot = pick_cot.astype(bf16)
    grad_router = dot_nn(logit_cot, normed_m).T
    normed_m_cot = moe_sum + lax.dot_general(
        logit_cot, router_full, (((0,), (1,)), ((), ())), preferred_element_type=f32
    )
    pulled, grad_gain_m = rms_pull(mid, mid_scale, gain_m, normed_m_cot)
    mid_cot = out_grad[0].astype(f32) + pulled
    branch_cot = (res_mult * mid_cot).astype(bf16)
    grad_wo = dot_tn(attended, branch_cot)
    attended_cot = dot_nt(branch_cot, wo_full).astype(bf16)
    if not wide:
        attended_cot = attended_cot.reshape(rows, devices, q_width).transpose(1, 0, 2)
    (heads_cot,) = exchange(
        4, [("swap", "seq", attended_cot, ("in", q_width) if wide else None)]
    )
    qkv_cot = attend_backward(q_all, kv_all, heads_cot, ot, lse, cos, sin, start, heads)
    grad_qkv = dot_tn(
        normed_a.reshape(length, width), qkv_cot.reshape(length, w_cols)
    ).astype(bf16)
    token_pack = jnp.concatenate(
        [
            grad_wo,
            grad_router,
            grad_gain_m[:, None],
            jnp.zeros((width, LANES - experts - 1), f32),
        ],
        axis=1,
    ).astype(bf16)
    pack_cols = width + LANES
    qkv_cot_tok, grad_qkv, token_pack = exchange(
        5,
        [
            ("swap", "seq", qkv_cot, ("out", w_cols)),
            ("swap", "dp", grad_qkv.reshape(parts, w_rows, w_cols), None),
            ("swap", "dp", token_pack.reshape(parts, w_rows, pack_cols), None),
        ],
    )
    normed_a_cot = dot_nt(qkv_cot_tok, w_full)
    grad_qkv = jnp.sum(grad_qkv.astype(f32), axis=0).astype(bf16)
    token_pack = jnp.sum(token_pack.astype(f32), axis=0).astype(bf16)
    out_rows = w_rows // devices
    grad_qkv, token_pack = exchange(
        6,
        [
            ("swap", "seq", grad_qkv.reshape(devices, out_rows, w_cols), None),
            ("swap", "seq", token_pack.reshape(devices, out_rows, pack_cols), None),
        ],
    )
    resid_scale = rms_parts(resid)
    weighted = normed_a_cot * gain_a.astype(f32)
    input_grad = (
        mid_cot
        + resid_scale * weighted
        - resid
        * (resid_scale * resid_scale * resid_scale)
        * jnp.mean(weighted * resid, axis=-1, keepdims=True)
    ).astype(bf16)[None]

    grad_qkv = grad_qkv.astype(f32)
    grad_wq = grad_qkv[:, :, :q_width].transpose(1, 0, 2).reshape(out_rows, devices * q_width)

    def per_head(part):
        part = part.reshape(devices // share, share, out_rows, HEAD_SIZE).sum(axis=1)
        return part.transpose(1, 0, 2).reshape(out_rows, KEY_VALUE_HEADS * HEAD_SIZE)

    grad_wk = per_head(grad_qkv[:, :, HEADS_LANES : HEADS_LANES + HEAD_SIZE])
    grad_wv = per_head(grad_qkv[:, :, HEADS_LANES + HEAD_SIZE :])
    token_pack = jnp.sum(token_pack.astype(f32), axis=0)
    grad_wo = token_pack[:, :width]
    grad_router = token_pack[:, width : width + experts]
    grad_gain_m = token_pack[:, width + experts]

    def own_rows(weight):
        return lax.dynamic_slice_in_dim(weight, me * out_rows, out_rows, 0).astype(bf16).astype(f32)

    grad_gain_a = (
        jnp.sum(own_rows(w_query) * grad_wq, axis=1)
        + jnp.sum(own_rows(key_weight_matrix) * grad_wk, axis=1)
        + jnp.sum(own_rows(value_weight_matrix) * grad_wv, axis=1)
    ) / own_rows(gain_attn)
    return (
        output,
        input_grad,
        grad_wq,
        grad_wk,
        grad_wv,
        grad_wo,
        grad_router,
        grad_gain_a,
        grad_gain_m,
        grad_e_in,
        grad_e_out,
    )


def solution(mesh):
    return jax.shard_map(
        on_device,
        mesh=mesh,
        in_specs=(
            P("dp", "seq", None),
            P("dp", "seq", None),
            P("dp", "seq"),
            P("dp", "seq", None),
            P("dp", None),
            P("dp", None),
            P("dp", None),
            P("dp", None),
            P("dp", None),
            P("dp"),
            P("dp"),
            P("seq", "dp", None),
            P("seq", "dp", None),
        ),
        out_specs=(
            P("dp", "seq", None),
            P("dp", "seq", None),
            P(("dp", "seq"), None),
            P(("dp", "seq"), None),
            P(("dp", "seq"), None),
            P(("dp", "seq"), None),
            P(("dp", "seq"), None),
            P(("dp", "seq")),
            P(("dp", "seq")),
            P("seq", "dp", None),
            P("seq", "dp", None),
        ),
        check_vma=False,
    )
```

time: 1780 us -> 579 us (0.33)
  waiting for transfers between devices: 1050 us -> 0.78 us
  Pallas kernels: 0 us -> 387 us
  local copies, waits for them, and re-layouts: 213 us -> 27.1 us
  blocking collectives: 115 us -> 0 us
  matrix products: 190 us -> 91.4 us
  starting transfers between devices: 70.5 us -> 9.79 us
  other arithmetic: 94.3 us -> 37.5 us
    reduce_scatter x6 -> x0, waiting for transfers between devices: 501 us -> none  [the longest x1 143 us: on_device(): lax.psum_scatter(grad_wq, ('dp', 'seq'), scatter_dimension=0, tiled=True)]
    all_to_all x10 -> x2, waiting for transfers between devices: 423 us -> 0.01 us  [the longest x1 0.01 us: on_device(): grads_out = lax.all_to_all(grads_out, 'dp', split_axis=1, concat_axis=1)]
    pallas_call x0 -> x9, Pallas kernels: none -> 387 us  [the longest x7 351 us: exchange(): pl.pallas_call(kernel, name=f'exchange{collective_id}', out_shape=out_sha...]
    dot_general x48 -> x20, matrix products: 188 us -> 91.4 us  [the longest x6 35.4 us: dot_nn(): lax.dot_general(a, b, (((1,), (0,)), ((), ())), preferred_element_type=f32)]
    gather x2 -> x0, local copies, waits for them, and re-layouts: 81.9 us -> none  [the longest x1 41 us: on_device(): picked = returned[chosen, slot_rank].astype(broad_dtype)]
    all_gather x6 -> x4, waiting for transfers between devices: 66.4 us -> 0.04 us  [the longest x1 0.02 us: on_device(): lax.all_gather(expert_in.astype(bf16), 'dp', axis=1, tiled=True)]
    unnamed x14 -> x4, waiting for transfers between devices: 62.1 us -> 0.73 us
    all_to_all x10 -> x2, starting transfers between devices: 70.2 us -> 9.63 us  [the longest x1 4.83 us: on_device(): grads_in = lax.all_to_all(grads_in, 'dp', split_axis=1, concat_axis=1)]
  transfers between devices with their start and end apart: 23 -> 6, of which waited for: 14 -> 0; matrix products, arithmetic and copies ran while one was open for 24% -> 24% of each run, Pallas kernels for 0% -> 68%
where the time goes in v1:
time: 579 us; the launch traced here: 569 us
  Pallas kernels  387 us (67%)
  matrix products  91.4 us (16%)
  other arithmetic  37.5 us (6%)
  local copies, waits for them, and re-layouts  27.1 us (5%)
  between operations  15.4 us (3%)
  starting transfers between devices  9.79 us (2%)
    pallas_call x7, Pallas kernels, exchange(): pl.pallas_call(kernel, name=f'exchange{collective_id}', out_shape=out_sha...  351 us
    dot_general x6, matrix products, dot_nn(): lax.dot_general(a, b, (((1,), (0,)), ((), ())), preferred_element_type=f32)  35.4 us
    dot_general x6, matrix products, dot_nt(): lax.dot_general(a, b, (((1,), (1,)), ((), ())), preferred_element_type=f32)  26.9 us
    dot_general x6, matrix products, dot_tn(): lax.dot_general(a, b, (((0,), (0,)), ((), ())), preferred_element_type=f32)  25.8 us
    pallas_call x1, Pallas kernels, attend_backward(): pl.pallas_call(kernel, name='attend_backward', grid_spec=grid_spec, out_s...  18.2 us
    pallas_call x1, Pallas kernels, attend_forward(): pl.pallas_call(kernel, name='attend_forward', grid_spec=grid_spec, out_sh...  17.5 us
    unnamed x125, local copies, waits for them, and re-layouts  16.8 us
  transfers between devices with their start and end apart: 6, of which 0 were waited for; matrix products, arithmetic and copies ran while one was open for 24% of the time, Pallas kernels for 68%

profile of v1, /device:TPU:13, one launch (start us, length us, event | category | flops | bytes accessed | tf_op | source)
XLA Modules:
  0.0 568.9 jit_solution(8321647554583032536)
XLA Ops:
  18.4 53.3 %exchange0.1 = (bf16[8,256,1024]{2,1,0:T(8,128)(2,1)}, s32[8,16,256]{2,1,0:T(8,128)S(1)}, bf16[4,256,256]{2,1,0:T(8,128)(2,1)S(1)}, bf16[4,256,1024]{2,1,0:T(8,128)(2,1)S(1)}, bf16[4,256,128]{2,1,0:T(8,128)(2,1)S(1)}) custom-call(bf16[256,1024]{1,0:T(8,128)(2,1)S(1)} %bitcast.144, s32[16,256]{1,0:T(8,128)S(1)} %pad.12.refs_1_, ...), custom_call_target="tpu_custom_call" | custom-call | tf_op jit(solution)/shard_map/exchange0/pallas_call | solution.py:248
  75.6 3.7 fusion.38
  81.0 17.5 %attend_forward.1 = (bf16[8,256,1024]{2,1,0:T(8,128)(2,1)S(1)}, bf16[8,256,128]{2,1,0:T(8,128)(2,1)S(1)}, bf16[8,256,128]{2,1,0:T(8,128)(2,1)S(1)}, bf16[8,256,1...) custom-call(s32[8]{0:T(128)S(1)} %and_select_fusion.first_ref, ...), custom_call_target="tpu_custom_call" | custom-call | flops 3221225472 | bytes 16777216 | tf_op jit(solution)/shard_map/attend_forward/pallas_call | solution.py:404
  101.1 15.9 %exchange1.1 = bf16[256,1024]{1,0:T(8,128)(2,1)S(1)} custom-call(bf16[8,256,128]{2,1,0:T(8,128)(2,1)S(1)} %get-tuple-element.34.refs_0_), custom_call_target="tpu_custom_call" | custom-call | tf_op jit(solution)/shard_map/exchange1/pallas_call | solution.py:248
  121.2 84.2 %exchange2.1 = bf16[8,256,1024]{2,1,0:T(8,128)(2,1)S(1)} custom-call(bf16[256,1024]{1,0:T(8,128)(2,1)S(1)} %multiply_convert_fusion.7.refs_0_), custom_call_target="tpu_custom_call" | custom-call | tf_op jit(solution)/shard_map/exchange2/pallas_call | solution.py:248
  210.3 10.8 %fusion.14 = f32[2048,1024]{0,1:T(8,128)} fusion(bf16[2048,1024]{1,0:T(8,128)(2,1)} %bitcast.134, bf16[2,1024,1024]{2,1,0:T(8,128)(2,1)} %all-gather.8.cloned.1.call-done), kind=kOutput, calls=%fused_computation.43 | convolution fusion | flops 4294967296 | bytes 14680064 | tf_op jit(solution)/shard_map/dot_general | solution.py:281
  221.1 7.0 %fusion.13 = f32[2048,1024]{0,1:T(8,128)} fusion(bf16[2048,1024]{1,0:T(8,128)(2,1)S(1)} %bitcast.136, bf16[2,1024,1024]{2,1,0:T(8,128)(2,1)S(1)} %copy-done.42), kind=kOutput, calls=%fused_computation.42 | convolution fusion | flops 4294967296 | bytes 14680064 | tf_op jit(solution)/shard_map/dot_general | solution.py:281
  228.1 10.0 %multiply_convert_fusion.3 = (bf16[2048,512]{0,1:T(8,128)(2,1)}, bf16[2048,512]{0,1:T(8,128)(2,1)}, bf16[2048,512]{0,1:T(8,128)(2,1)S(1)}) fusion(f32[2048,1024]{0,1:T(8,128)} %fusion.14, bf16[2,1024,512]{2,1,0:T(8,128)(2,1)} %all-gather.6.cloned.1.call-done, bf16[1,2048,1024]{2,1,0:T(8,128)(2,1)} %all-gather.12.cloned.1.call-done, ...), kind=kOutput, calls=%fused_computation.23 | convolution fusion | flops 2169503744 | bytes 19931136 | tf_op jit(solution)/shard_map/dot_general | solution.py:281
  242.9 5.7 %multiply_convert_fusion.5 = (bf16[2048,512]{0,1:T(8,128)(2,1)}, bf16[2048,512]{0,1:T(8,128)(2,1)}, bf16[2048,512]{0,1:T(8,128)(2,1)S(1)}) fusion(f32[2048,1024]{0,1:T(8,128)S(1)} %copy-done.50, bf16[2,1024,512]{2,1,0:T(8,128)(2,1)S(1)} %copy-done.46, bf16[1,2048,1024]{2,1,0:T(8,128)(2,1)S(1)} %copy-done.44, f32[2048]{0:T(1024)S(1)} %broadcast_multiply_fusion.1), kind=kOutput, calls=%fused_computation.27 | convolution fusion | flops 2169503744 | bytes 19931136 | tf_op jit(solution)/shard_map/dot_general | solution.py:281
  252.9 4.8 all-to-all-start.1
  257.7 4.4 convolution_convert_fusion
  262.2 7.1 %fusion.2 = (f32[2048]{0:T(1024)S(1)}, f32[2048]{0:T(1024)S(1)}, bf16[2048,1024]{1,0:T(8,128)(2,1)}) fusion(bf16[1,2048,1024]{2,1,0:T(8,128)(2,1)S(1)} %copy-done.45, bf16[2048,1024]{1,0:T(8,128)(2,1)S(1)} %convolution_convert_fusion, f32[2048]{0:T(1024)S(1)} %bitcast.168, f32[2048]{0:T(1024)S(1)} %bitcast.170, bf16[2048,512]{0,1:T(8,128)(2,1)S(1)} %copy-done.52, ...), kind=kOutput, calls=%fused_computation.10 | convolution fusion | flops 2174742528 | bytes 15761408 | tf_op jit(solution)/shard_map/dot_general | solution.py:277
  269.4 4.9 fusion.10
  274.3 6.2 %add_convert_fusion = bf16[2048,1024]{1,0:T(8,128)(2,1)} fusion(bf16[2048,1024]{1,0:T(8,128)(2,1)S(1)} %fusion.10, bf16[2048,512]{0,1:T(8,128)(2,1)S(1)} %copy-done.55, bf16[2048,512]{0,1:T(8,128)(2,1)S(1)} %copy-done.53, bf16[2,1024,1024]{2,1,0:T(8,128)(2,1)S(1)} %copy-done.43), kind=kOutput, calls=%fused_computation.15 | convolution fusion | flops 4313841664 | bytes 14680064 | tf_op jit(solution)/shard_map/dot_general | solution.py:277
  280.5 96.6 %exchange3.1 = (f32[256,1024]{1,0:T(8,128)S(1)}, f32[256,1024]{1,0:T(8,128)S(1)}, f32[8,8,256]{2,1,0:T(8,128)S(1)}) custom-call(bf16[8,256,1024]{2,1,0:T(8,128)(2,1)} %bitcast.153, bf16[8,256,1024]{2,1,0:T(8,128)(2,1)} %bitcast.152, f32[8,8,256]{2,1,0:T(8,128)S(1)} %pad.14.refs_2_), custom_call_target="tpu_custom_call" | custom-call | tf_op jit(solution)/shard_map/exchange3/pallas_call | solution.py:248
  382.7 8.1 %fusion.11 = bf16[1024,1024]{1,0:T(8,128)(2,1)S(1)} fusion(bf16[2048,1024]{1,0:T(8,128)(2,1)} %bitcast.135, bf16[2048,512]{0,1:T(8,128)(2,1)} %get-tuple-element.126, bf16[2048,512]{0,1:T(8,128)(2,1)} %get-tuple-element.125), kind=kOutput, calls=%fused_computation.40 | convolution fusion | flops 4304404480 | bytes 10485760 | tf_op jit(solution)/shard_map/dot_general | solution.py:285
  390.9 6.5 %fusion.12 = bf16[1024,1024]{1,0:T(8,128)(2,1)S(1)} fusion(bf16[2048,1024]{1,0:T(8,128)(2,1)S(1)} %bitcast.137, bf16[2048,512]{0,1:T(8,128)(2,1)S(1)} %copy-done.56, bf16[2048,512]{0,1:T(8,128)(2,1)S(1)} %copy-done.54), kind=kOutput, calls=%fused_computation.41 | convolution fusion | flops 4304404480 | bytes 10485760 | tf_op jit(solution)/shard_map/dot_general | solution.py:285
  399.4 14.2 %exchange4.1.do_ref = bf16[8,256,128]{2,1,0:T(8,128)(2,1)S(1)} custom-call(bf16[256,1024]{1,0:T(8,128)(2,1)S(1)} %convolution_convert_fusion.3.refs_0_), custom_call_target="tpu_custom_call" | custom-call | tf_op jit(solution)/shard_map/exchange4/pallas_call | solution.py:248
  418.4 18.2 %attend_backward.1.refs_0_ = bf16[8,256,256]{2,1,0:T(8,128)(2,1)S(1)} custom-call(s32[8]{0:T(128)S(1)} %and_select_fusion.first_ref, bf16[8,256,128]{2,1,0:T(8,128)(2,1)S(1)} %copy-done.25, bf16[8,256,128]{2,1,0:T(8,128)(2,1)S(1)} %copy-done.27, bf16[8,256,128]{2,1,0:T(8,128)(2,1)S(1)} %exchange4.1.do_ref, f32[8,64,512]{2,1,0:T(8,128)S(1)} %copy-done.23, ...), custom_call_target="tpu_custom_call" | custom-call | flops 5368709120 | bytes 4194304 | tf_op jit(solution)/shard_map/attend_backward/pallas_call | solution.py:519
  436.6 4.8 all-to-all-start
  442.3 5.0 concatenate.50.refs_2_
  452.0 68.2 %exchange5.1 = (bf16[256,2048]{1,0:T(8,128)(2,1)S(1)}, bf16[4,256,256]{2,1,0:T(8,128)(2,1)S(1)}, bf16[4,256,1152]{2,1,0:T(8,128)(2,1)S(1)}) custom-call(bf16[8,256,256]{2,1,0:T(8,128)(2,1)S(1)} %copy-done.12, bf16[4,256,256]{2,1,0:T(8,128)(2,1)S(1)} %bitcast.145, bf16[4,256,1152]{2,1,0:T(8,128)(2,1)} %concatenate.50.refs_2_), custom_call_target="tpu_custom_call" | custom-call | tf_op jit(solution)/shard_map/exchange5/pallas_call | solution.py:248
  524.0 18.7 %exchange6.1 = (bf16[8,32,256]{2,1,0:T(8,128)(2,1)S(1)}, bf16[8,32,1152]{2,1,0:T(8,128)(2,1)S(1)}) custom-call(bf16[8,32,256]{2,1,0:T(8,128)(2,1)S(1)} %bitcast.146, bf16[8,32,1152]{2,1,0:T(8,128)(2,1)S(1)} %bitcast.141), custom_call_target="tpu_custom_call" | custom-call | tf_op jit(solution)/shard_map/exchange6/pallas_call | solution.py:248
  557.3 4.6 convert_reduce_fusion.1
  (221 shorter events, 72.9 us)
Async XLA Ops:
  7.2 203.1 %all-gather.8.cloned.1.call-start = ((), (), s32[]{:S(2)}) async-start(), calls=%async_computation.3 | async-start | bytes 5242880 | tf_op jit(solution)/shard_map/all_gather | solution.py:600
  10.2 217.9 %all-gather.6.cloned.1.call-start = ((), (), s32[]{:S(2)}) async-start(), calls=%async_computation.2 | async-start | bytes 2621440 | tf_op jit(solution)/shard_map/all_gather | solution.py:601
  11.1 216.9 %all-gather.12.cloned.1.call-start = ((), (), s32[]{:S(2)}) async-start(), calls=%async_computation.5 | async-start | bytes 4718592 | tf_op jit(solution)/shard_map/all_gather | solution.py:599
  11.8 535.4 %all-gather.10.cloned.1.call-start = ((), (), s32[]{:S(2)}) async-start(), calls=%async_computation.4 | async-start | bytes 5242880 | tf_op jit(solution)/shard_map/all_gather | solution.py:602
  81.0 17.5 %copy-start.6 = (f32[8,256,128]{2,1,0:T(8,128)}, f32[8,256,128]{2,1,0:T(8,128)S(1)}, u32[]{:S(2)}) copy-start(f32[8,256,128]{2,1,0:T(8,128)S(1)} %get-tuple-element.151.cos_ref) | copy-start | bytes 3145732
  81.0 17.5 %copy-start.8 = (f32[8,256,128]{2,1,0:T(8,128)}, f32[8,256,128]{2,1,0:T(8,128)S(1)}, u32[]{:S(2)}) copy-start(f32[8,256,128]{2,1,0:T(8,128)S(1)} %get-tuple-element.152.sin_ref) | copy-start | bytes 3145732
  101.1 18.5 %copy-start.21 = (bf16[8,256,1024]{2,1,0:T(8,128)(2,1)}, bf16[8,256,1024]{2,1,0:T(8,128)(2,1)S(1)}, u32[]{:S(2)}) copy-start(bf16[8,256,1024]{2,1,0:T(8,128)(2,1)S(1)} %get-tuple-element.43) | copy-start | bytes 12582916
  101.1 18.5 %copy-start.32 = (f32[1024,1]{1,0:T(8,128)S(1)}, f32[1024,1]{1,0:T(8,128)}, u32[]{:S(2)}) copy-start(f32[1024,1]{1,0:T(8,128)} %get-tuple-element.134) | copy-start | bytes 12292
  210.3 10.8 %copy-start.1 = (bf16[8,256,1024]{2,1,0:T(8,128)(2,1)S(1)}, bf16[8,256,1024]{2,1,0:T(8,128)(2,1)}, u32[]{:S(2)}) copy-start(bf16[8,256,1024]{2,1,0:T(8,128)(2,1)} %copy-done) | copy-start | bytes 12582916
  210.3 10.8 %copy-start.42 = (bf16[2,1024,1024]{2,1,0:T(8,128)(2,1)S(1)}, bf16[2,1024,1024]{2,1,0:T(8,128)(2,1)}, u32[]{:S(2)}) copy-start(bf16[2,1024,1024]{2,1,0:T(8,128)(2,1)} %all-gather.8.cloned.1.call-done) | copy-start | bytes 12582916
  228.0 10.1 %copy-start.44 = (bf16[1,2048,1024]{2,1,0:T(8,128)(2,1)S(1)}, bf16[1,2048,1024]{2,1,0:T(8,128)(2,1)}, u32[]{:S(2)}) copy-start(bf16[1,2048,1024]{2,1,0:T(8,128)(2,1)} %all-gather.12.cloned.1.call-done) | copy-start | bytes 12582916
  252.9 183.7 %all-to-all-start.1 = ((bf16[2,4,256,512]{3,2,0,1:T(8,128)(2,1)}), bf16[2,4,256,512]{3,2,0,1:T(8,128)(2,1)}, u32[]{:S(2)}, u32[]{:S(2)}) async-start(bf16[2,4,256,512]{3,2,0,1:T(8,128)(2,1)} %pad_maximum_fusion.7), calls=%async_computation.1 | async-start | bytes 4194304 | tf_op jit(solution)/shard_map/all_to_all | solution.py:690
  262.2 7.2 %copy-start.43 = (bf16[2,1024,1024]{2,1,0:T(8,128)(2,1)S(1)}, bf16[2,1024,1024]{2,1,0:T(8,128)(2,1)}, u32[]{:S(2)}) copy-start(bf16[2,1024,1024]{2,1,0:T(8,128)(2,1)} %all-gather.8.cloned.1.call-done) | copy-start | bytes 12582916
  262.2 7.2 %copy-start.57 = (bf16[2048,512]{0,1:T(8,128)(2,1)S(1)}, bf16[2048,512]{0,1:T(8,128)(2,1)}, u32[]{:S(2)}) copy-start(bf16[2048,512]{0,1:T(8,128)(2,1)} %get-tuple-element.125) | copy-start | bytes 6291460
  262.2 7.2 %copy-start.58 = (bf16[2048,512]{0,1:T(8,128)(2,1)S(1)}, bf16[2048,512]{0,1:T(8,128)(2,1)}, u32[]{:S(2)}) copy-start(bf16[2048,512]{0,1:T(8,128)(2,1)} %get-tuple-element.126) | copy-start | bytes 6291460
  382.7 8.2 %copy-start.2 = (bf16[8,256,1024]{2,1,0:T(8,128)(2,1)S(1)}, bf16[8,256,1024]{2,1,0:T(8,128)(2,1)}, u32[]{:S(2)}) copy-start(bf16[8,256,1024]{2,1,0:T(8,128)(2,1)} %copy-done) | copy-start | bytes 12582916
  382.7 8.2 %copy-start.54 = (bf16[2048,512]{0,1:T(8,128)(2,1)S(1)}, bf16[2048,512]{0,1:T(8,128)(2,1)}, u32[]{:S(2)}) copy-start(bf16[2048,512]{0,1:T(8,128)(2,1)} %get-tuple-element.123) | copy-start | bytes 6291460
  382.7 8.2 %copy-start.56 = (bf16[2048,512]{0,1:T(8,128)(2,1)S(1)}, bf16[2048,512]{0,1:T(8,128)(2,1)}, u32[]{:S(2)}) copy-start(bf16[2048,512]{0,1:T(8,128)(2,1)} %get-tuple-element.124) | copy-start | bytes 6291460
  398.7 17.6 %copy-start.28 = (f32[256,1024]{1,0:T(8,128)}, f32[256,1024]{1,0:T(8,128)S(1)}, u32[]{:S(2)}) copy-start(f32[256,1024]{1,0:T(8,128)S(1)} %get-tuple-element.130) | copy-start | bytes 3145732
  436.6 10.7 %copy-start.11 = (bf16[8,256,256]{2,1,0:T(8,128)(2,1)}, bf16[8,256,256]{2,1,0:T(8,128)(2,1)S(1)}, u32[]{:S(2)}) copy-start(bf16[8,256,256]{2,1,0:T(8,128)(2,1)S(1)} %attend_backward.1.refs_0_) | copy-start | bytes 3145732
  436.6 120.7 %all-to-all-start = ((bf16[2,4,256,1024]{3,2,0,1:T(8,128)(2,1)}), bf16[2,4,256,1024]{3,2,0,1:T(8,128)(2,1)}, u32[]{:S(2)}, u32[]{:S(2)}) async-start(bf16[2,4,256,1024]{3,2,0,1:T(8,128)(2,1)} %pad_maximum_fusion.2), calls=%async_computation | async-start | bytes 8388608 | tf_op jit(solution)/shard_map/all_to_all | solution.py:689
  522.7 24.5 %copy-start.18 = (bf16[256,2048]{1,0:T(8,128)(2,1)S(1)}, bf16[256,2048]{1,0:T(8,128)(2,1)}, u32[]{:S(2)}) copy-start(bf16[256,2048]{1,0:T(8,128)(2,1)} %copy-done.17) | copy-start | bytes 3145732
  543.7 7.2 %copy-start.36 = (f32[32,512]{1,0:T(8,128)}, f32[32,512]{1,0:T(8,128)S(1)}, u32[]{:S(2)}) copy-start(f32[32,512]{1,0:T(8,128)S(1)} %reshape.292) | copy-start | bytes 196612
  543.9 8.7 %copy-start.37 = (f32[32,512]{1,0:T(8,128)}, f32[32,512]{1,0:T(8,128)S(1)}, u32[]{:S(2)}) copy-start(f32[32,512]{1,0:T(8,128)S(1)} %reshape.291) | copy-start | bytes 196612
  (41 other events, 149.9 us)
Sparse Core Ops, SparseCore 0:
  10.5 78.0 all-gather.7
  90.4 35.3 all-gather.5
  127.5 77.1 all-gather.11
  206.9 53.5 all-gather.9

commit v2 on v1

--- a/solution.py
+++ b/solution.py
@@ -1,3 +1,5 @@
+import functools
+
 import jax
 import jax.numpy as jnp
 from jax import lax
@@ -23,7 +25,8 @@
         out_spec = pl.BlockSpec(memory_space=pl.ANY)
         extra = []
         if kind == "gather":
-            shape, dtype, copies = (count,) + x.shape, x.dtype, count - 1
+            shape, dtype = (count,) + x.shape, x.dtype
+            copies = count - 1 if axis == "dp" else 3 + 4 * (count // 2 - 1)
         elif kind == "swap":
             copies, dtype = count - 1, x.dtype
             if cut is None:
@@ -48,7 +51,7 @@
         places.append((len(scratch), len(extra)))
         scratch += [
             pltpu.SemaphoreType.DMA((copies,)),
-            pltpu.SemaphoreType.DMA((copies,)),
+            pltpu.SemaphoreType.DMA((max(copies, count),)),
             pltpu.SemaphoreType.DMA,
         ] + extra
 
@@ -130,51 +133,55 @@
                 own = pltpu.make_async_copy(x, o.at[my], local)
                 own.start()
                 third.append(own.wait)
-                for k in range(1, chips):
-                    to = lax.rem(chip + k, chips) * 2 + core
-                    copy = remote(axis, x, o.at[my], send.at[k], recv.at[k], to)
-                    copy.start()
-                    third.append(copy.wait_send)
-                copy = remote(axis, x, o.at[my], send.at[0], recv.at[0], sibling)
+
+                def line(src, b, slot, to, axis=axis, o=o, send=send, recv=recv, core=core):
+                    return remote(
+                        axis, src, o.at[2 * b + core], send.at[slot], recv.at[b], to
+                    )
+
+                def across(src, b, slot, half, axis=axis, o=o, send=send, recv=recv, chips=chips, sibling=sibling):
+                    return remote(
+                        axis, src, o.at[2 * b + half], send.at[slot], recv.at[chips + b], sibling
+                    )
+
+                def guarded(where, act):
+                    pl.when(where)(act)
+
+                for slot, where, to in ((0, chip > 0, my - 2), (1, chip < chips - 1, my + 2)):
+                    copy = line(x, chip, slot, to)
+                    guarded(where, copy.start)
+                    third.append(functools.partial(guarded, where, copy.wait_send))
+                copy = across(x, chip, 2, core)
                 copy.start()
                 third.append(copy.wait_send)
-                third.append(
-                    remote(
-                        axis, x, o.at[sibling], send.at[0], recv.at[0], sibling
-                    ).wait_recv
-                )
-
-                def forward(
-                    k, axis=axis, x=x, o=o, send=send, recv=recv, chips=chips, chip=chip, core=core, sibling=sibling
-                ):
-                    frm = lax.rem(chip + chips - k, chips) * 2
-                    remote(
-                        axis, x, o.at[frm + core], send.at[k], recv.at[k], sibling
-                    ).wait_recv()
-                    slot = chips - 1 + k
-                    copy = remote(
-                        axis,
-                        o.at[frm + core],
-                        o.at[frm + core],
-                        send.at[slot],
-                        recv.at[slot],
-                        sibling,
+                third.append(across(x, chip, 2, 1 - core).wait_recv)
+
+                def hop(k, side, chips=chips, chip=chip, core=core, my=my, x=x, o=o, line=line, across=across):
+                    b = chip + side * k
+                    there = (b >= 0) & (b < chips)
+                    onward = there & ((chip - side >= 0) & (chip - side < chips))
+                    slot = 3 + (k - 1) * 4 + (side + 1)
+                    spot = o.at[2 * b + core]
+                    further = line(spot, b, slot, my - 2 * side)
+                    over = across(spot, b, slot + 1, core)
+
+                    @pl.when(there)
+                    def _():
+                        line(x, b, slot, my).wait_recv()
+                        over.start()
+
+                    guarded(onward, further.start)
+                    third.append(functools.partial(guarded, onward, further.wait_send))
+                    third.append(functools.partial(guarded, there, over.wait_send))
+                    third.append(
+                        functools.partial(
+                            guarded, there, across(x, b, slot + 1, 1 - core).wait_recv
+                        )
                     )
-                    copy.start()
-                    third.append(copy.wait_send)
-                    third.append(
-                        remote(
-                            axis,
-                            x,
-                            o.at[frm + 1 - core],
-                            send.at[slot],
-                            recv.at[slot],
-                            sibling,
-                        ).wait_recv
-                    )
 
                 for k in range(1, chips):
-                    second.append((k, lambda k=k, forward=forward: forward(k)))
+                    for side in (-1, 1):
+                        second.append((k, functools.partial(hop, k, side)))
             else:
                 chips = count // 2
                 chip, core = my // 2, lax.rem(my, 2)
@@ -542,6 +549,468 @@
     )
 
 
+def moe_exchange(collective_id, normed, cots, mask, router, w_in, w_out, parts):
+    devices = lax.axis_size("seq")
+    chips = devices // 2
+    rows, width = normed.shape
+    own_experts = w_in.shape[0]
+
+    def order(chip, k):
+        near = jnp.minimum(chip, chips - 1 - chip)
+        step = (k + 1) // 2
+        both = jnp.where(lax.rem(k, 2) == 1, chip - step, chip + step)
+        return jnp.where(
+            k <= 2 * near, both, jnp.where(chip <= chips - 1 - chip, k, chips - 1 - k)
+        )
+
+    def kernel(*refs):
+        x_in, g_in = refs[0], refs[1 : 1 + chips]
+        mask_ref, router_ref, win_in, wout_in = refs[1 + chips : 5 + chips]
+        (lin_out, slot_out, hid_out, n_sum, gate_out, gin_out, gout_out) = refs[
+            5 + chips : 12 + chips
+        ]
+        y_outs = refs[12 + chips : 12 + 2 * chips]
+        (
+            x_all, g_all, win, wout, y_acc, n_acc, gate_acc, gate_stage,
+            n_mine, n_far, n_give, n_theirs, y_mine, y_give, y_theirs, y_pre,
+            lin_st, slot_st, hid_st, gin, gout, hid_ld,
+            local, line_send, line_recv, sib_send, sib_recv, g_local, g_send, g_recv,
+            n_send, n_recv, y_send, y_recv, far_send, far_recv, gate_send, gate_recv,
+            st_sem, y_sem, ld_sem, w_sem, wg_sem,
+        ) = refs[12 + 2 * chips :]
+        me = lax.axis_index("seq")
+        chip, core = me // 2, lax.rem(me, 2)
+        sibling = me + 1 - 2 * core
+        win_copy = pltpu.make_async_copy(win_in, win, w_sem.at[0])
+        wout_copy = pltpu.make_async_copy(wout_in, wout, w_sem.at[1])
+        win_copy.start()
+        wout_copy.start()
+        barrier = pltpu.get_barrier_semaphore()
+        for k in range(1, devices):
+            pl.semaphore_signal(
+                barrier, inc=1, device_id={"seq": lax.rem(me + k, devices)}, device_id_type=MESH
+            )
+        pl.semaphore_wait(barrier, devices - 1)
+
+        def remote(src, dst, send, recv, to):
+            return pltpu.make_async_remote_copy(
+                src_ref=src,
+                dst_ref=dst,
+                send_sem=send,
+                recv_sem=recv,
+                device_id={"seq": to},
+                device_id_type=MESH,
+            )
+
+        def own_left():
+            return remote(x_in, x_all.at[me], line_send.at[0], line_recv.at[chip], me - 2)
+
+        def own_right():
+            return remote(x_in, x_all.at[me], line_send.at[1], line_recv.at[chip], me + 2)
+
+        def pass_on(b, k, to):
+            place = x_all.at[2 * b + core]
+            return remote(place, place, line_send.at[1 + k], line_recv.at[b], to)
+
+        def to_sibling(b, k):
+            place = x_all.at[2 * b + core]
+            return remote(place, place, sib_send.at[k], sib_recv.at[b], sibling)
+
+        def own_to_sibling():
+            return remote(x_in, x_all.at[me], sib_send.at[0], sib_recv.at[chip], sibling)
+
+        def cot_to_sibling(k):
+            b = lax.rem(chip + chips - k, chips)
+            return remote(
+                g_in[k], g_all.at[2 * b + core], g_send.at[k], g_recv.at[b], sibling
+            )
+
+        def cot_local(k):
+            b = lax.rem(chip + chips - k, chips)
+            return pltpu.make_async_copy(g_in[k], g_all.at[2 * b + core], g_local.at[k])
+
+        @pl.when(chip > 0)
+        def _():
+            own_left().start()
+
+        @pl.when(chip < chips - 1)
+        def _():
+            own_right().start()
+
+        own_to_sibling().start()
+        own = pltpu.make_async_copy(x_in, x_all.at[me], local)
+        own.start()
+        for k in range(chips):
+            cot_to_sibling(k).start()
+            cot_local(k).start()
+        own.wait()
+        for k in range(chips):
+            cot_local(k).wait()
+        win_copy.wait()
+        wout_copy.wait()
+
+        def gate_copy(block):
+            return remote(
+                gate_stage.at[block],
+                gate_out.at[me],
+                gate_send.at[block],
+                gate_recv.at[me],
+                block,
+            )
+
+        def n_copy(p):
+            return remote(n_give.at[p], n_theirs.at[p], n_send.at[p], n_recv.at[p], sibling)
+
+        def y_copy(p):
+            return remote(y_give.at[p], y_theirs.at[p], y_send.at[p], y_recv.at[p], sibling)
+
+        def y_leave(p, k):
+            return pltpu.make_async_copy(y_pre.at[p], y_outs[k], y_sem.at[p])
+
+        def stage_copies(e, block):
+            return [
+                pltpu.make_async_copy(lin_st.at[e], lin_out.at[e, block], st_sem.at[0, e]),
+                pltpu.make_async_copy(slot_st.at[e], slot_out.at[e, block], st_sem.at[1, e]),
+                pltpu.make_async_copy(hid_st.at[e], hid_out.at[e, block], st_sem.at[2, e]),
+            ]
+
+        def far_copy(b):
+            return remote(
+                n_mine.at[b], n_far.at[chip], far_send.at[b], far_recv.at[chip], 2 * b + core
+            )
+
+        def fold(k):
+            b, p = order(chip, k), lax.rem(k, 2)
+            n_copy(p).wait_recv()
+            both = n_mine[b].astype(f32) + n_theirs[p].astype(f32)
+
+            @pl.when(b == chip)
+            def _():
+                n_sum[...] = both
+
+            @pl.when(b != chip)
+            def _():
+                n_mine[b] = both.astype(bf16)
+                far_copy(b).start()
+
+            @pl.when(k > 1)
+            def _():
+                y_leave(p, 0).wait()
+
+            y_copy(p).wait_recv()
+            y_pre[p] = (y_mine[...].astype(f32) + y_theirs[p].astype(f32)).astype(bf16)
+            away = lax.rem(b - chip + chips, chips)
+            for r in range(chips):
+
+                @pl.when(away == r)
+                def _(r=r):
+                    y_leave(p, r).start()
+
+        def compute(block, before):
+            x = x_all[block]
+            there = mask_ref[block] > 0
+            logits = jnp.where(there, dot_nn(x, router_ref[...]), -1e30)
+            gates = jnp.where(
+                there, jnp.exp(logits - jnp.max(logits, axis=1, keepdims=True)), 0.0
+            )
+            gates = gates / jnp.sum(gates, axis=1, keepdims=True)
+            lane = lax.broadcasted_iota(jnp.int32, gates.shape, 1)
+            y_acc[...] = jnp.zeros_like(y_acc)
+            n_acc[...] = jnp.zeros_like(n_acc)
+            gate_acc[...] = jnp.zeros_like(gate_acc)
+
+            @pl.loop(0, own_experts)
+            def _(e):
+                gate = jnp.sum(
+                    jnp.where(lane == me * own_experts + e, gates, 0.0), axis=1, keepdims=True
+                )
+                lin = dot_nn(x_all[block], win[e])
+                gate_lin, up_lin = lin[:, :FFE], lin[:, FFE:]
+                sig = 1.0 / (1.0 + jnp.exp(-gate_lin))
+                silu = gate_lin * sig
+                hidden = (silu * up_lin).astype(bf16)
+
+                @pl.when(before)
+                def _():
+                    for copy in stage_copies(e, block):
+                        copy.wait()
+
+                hid_st[e] = hidden
+                res = dot_nt(hidden, wout[e]).astype(bf16).astype(f32)
+                y_acc[...] += gate * res
+                cot = g_all[block].astype(f32) * res_mult
+                gate_acc[...] += jnp.where(
+                    lane == e, jnp.sum(cot * res, axis=1, keepdims=True), 0.0
+                )
+                slot = (gate * cot).astype(bf16)
+                slot_st[e] = slot
+                hidden_cot = dot_nn(slot, wout[e])
+                lin_cot = jnp.concatenate(
+                    [
+                        hidden_cot * up_lin * (sig * (1.0 + gate_lin * (1.0 - sig))),
+                        hidden_cot * silu,
+                    ],
+                    axis=1,
+                ).astype(bf16)
+                lin_st[e] = lin_cot
+                for copy in stage_copies(e, block):
+                    copy.start()
+                n_acc[...] += dot_nt(lin_cot, win[e]).astype(bf16).astype(f32)
+
+            gate_stage[block] = gate_acc[...].T[:8]
+
+            @pl.when(block != me)
+            def _():
+                gate_copy(block).start()
+
+            @pl.when(block == me)
+            def _():
+                gate_out[block] = gate_stage[block]
+
+        @pl.loop(0, chips)
+        def _(k):
+            b = order(chip, k)
+
+            @pl.when(k > 0)
+            def _():
+                pass_on(b, k, sibling).wait_recv()
+                to_sibling(b, k).start()
+
+                @pl.when((b < chip) & (chip < chips - 1))
+                def _():
+                    pass_on(b, k, me + 2).start()
+
+                @pl.when((b > chip) & (chip > 0))
+                def _():
+                    pass_on(b, k, me - 2).start()
+
+            remote(
+                x_in, x_all.at[2 * b + 1 - core], sib_send.at[0], sib_recv.at[b], sibling
+            ).wait_recv()
+            remote(
+                x_in, g_all.at[2 * b + 1 - core], g_send.at[0], g_recv.at[b], sibling
+            ).wait_recv()
+
+            @pl.loop(0, 2)
+            def _(h):
+                compute(2 * b + lax.rem(core + 1 + h, 2), (k > 0) | (h > 0))
+
+                @pl.when(h == 0)
+                def _():
+                    p = lax.rem(k, 2)
+
+                    @pl.when(k > 0)
+                    def _():
+                        fold(k - 1)
+
+                    @pl.when(k > 1)
+                    def _():
+                        n_copy(p).wait_send()
+                        y_copy(p).wait_send()
+
+                    n_give[p] = n_acc[...].astype(bf16)
+                    y_give[p] = y_acc[...].astype(bf16)
+                    n_copy(p).start()
+                    y_copy(p).start()
+
+                @pl.when(h == 1)
+                def _():
+                    n_mine[b] = n_acc[...].astype(bf16)
+                    y_mine[...] = y_acc[...].astype(bf16)
+
+        @pl.loop(chips - 1, chips)
+        def _(k):
+            fold(k)
+
+        for e in range(own_experts):
+            for copy in stage_copies(e, 0):
+                copy.wait()
+
+        def loads(t, p):
+            e, b = lax.rem(t, own_experts), t // own_experts
+            pair = pl.ds(2 * b, 2)
+            return [
+                pltpu.make_async_copy(
+                    lin_out.at[e, pair], g_all.at[pl.ds(4 * p, 2)], ld_sem.at[0, p]
+                ),
+                pltpu.make_async_copy(
+                    slot_out.at[e, pair], g_all.at[pl.ds(4 * p + 2, 2)], ld_sem.at[1, p]
+                ),
+                pltpu.make_async_copy(hid_out.at[e, pair], hid_ld.at[p], ld_sem.at[2, p]),
+            ]
+
+        for copy in loads(jnp.int32(0), 0):
+            copy.start()
+        gin[...] = jnp.zeros_like(gin)
+        gout[...] = jnp.zeros_like(gout)
+
+        @pl.loop(0, chips * own_experts)
+        def _(t):
+            p = lax.rem(t, 2)
+            for copy in loads(t, p):
+                copy.wait()
+
+            @pl.when(t + 1 < chips * own_experts)
+            def _():
+                for copy in loads(t + 1, 1 - p):
+                    copy.start()
+
+            e, b = lax.rem(t, own_experts), t // own_experts
+            x = x_all[pl.ds(2 * b, 2)].reshape(2 * rows, width)
+            lin_cot = g_all[pl.ds(4 * p, 2)].reshape(2 * rows, width)
+            gin[e] += dot_tn(x, lin_cot)
+            slot = g_all[pl.ds(4 * p + 2, 2)].reshape(2 * rows, width)
+            gout[e] += dot_tn(slot, hid_ld[p].reshape(2 * rows, FFE))
+
+        @pl.loop(1, chips)
+        def _(k):
+            b = order(chip, k)
+            to_sibling(b, k).wait_send()
+
+            @pl.when((b < chip) & (chip < chips - 1))
+            def _():
+                pass_on(b, k, me + 2).wait_send()
+
+            @pl.when((b > chip) & (chip > 0))
+            def _():
+                pass_on(b, k, me - 2).wait_send()
+
+        own_to_sibling().wait_send()
+
+        @pl.when(chip > 0)
+        def _():
+            own_left().wait_send()
+
+        @pl.when(chip < chips - 1)
+        def _():
+            own_right().wait_send()
+
+        part_rows = width // parts
+        leaving = []
+        for e in range(own_experts):
+            for j in range(width // rows):
+                i = e * (width // rows) + j
+                x_all[i] = gin[e, j * rows : (j + 1) * rows].astype(bf16)
+                g_all[i, :, :FFE] = gout[e, j * rows : (j + 1) * rows].astype(bf16)
+                for q in range(rows // part_rows):
+                    here = pl.ds(q * part_rows, part_rows)
+                    part = (j * rows + q * part_rows) // part_rows
+                    at = 2 * len(leaving)
+                    leaving.append(
+                        (
+                            pltpu.make_async_copy(
+                                x_all.at[i, here], gin_out.at[part, e], wg_sem.at[at]
+                            ),
+                            pltpu.make_async_copy(
+                                g_all.at[i, here, pl.ds(0, FFE)],
+                                gout_out.at[part, e],
+                                wg_sem.at[at + 1],
+                            ),
+                        )
+                    )
+                    for copy in leaving[-1]:
+                        copy.start()
+
+        @pl.loop(1, chips)
+        def _(k):
+            b = order(chip, k)
+            remote(
+                n_mine.at[b], n_far.at[b], far_send.at[b], far_recv.at[b], 2 * b + core
+            ).wait_recv()
+            n_sum[...] += n_far[b].astype(f32)
+            far_copy(b).wait_send()
+
+        @pl.loop(1, devices)
+        def _(k):
+            block = lax.rem(me + k, devices)
+            remote(
+                gate_stage.at[block],
+                gate_out.at[block],
+                gate_send.at[block],
+                gate_recv.at[block],
+                block,
+            ).wait_recv()
+            gate_copy(block).wait_send()
+
+        for p in range(2):
+            n_copy(p).wait_send()
+            y_copy(p).wait_send()
+            y_leave(p, 0).wait()
+        for pair in leaving:
+            for copy in pair:
+                copy.wait()
+
+        for k in range(chips):
+            cot_to_sibling(k).wait_send()
+
+    hbm = pl.BlockSpec(memory_space=pl.ANY)
+    vmem = pl.BlockSpec(memory_space=pltpu.VMEM)
+    block = (rows, width)
+    dma = pltpu.SemaphoreType.DMA
+    flops = 9 * own_experts * 2 * devices * rows * width * FFE // 1
+    return pl.pallas_call(
+        kernel,
+        name="moe_exchange",
+        out_shape=[
+            jax.ShapeDtypeStruct((own_experts, devices, rows, 2 * FFE), bf16),
+            jax.ShapeDtypeStruct((own_experts, devices) + block, bf16),
+            jax.ShapeDtypeStruct((own_experts, devices, rows, FFE), bf16),
+            jax.ShapeDtypeStruct(block, f32),
+            jax.ShapeDtypeStruct((devices, 8, rows), f32),
+            jax.ShapeDtypeStruct((parts, own_experts, width // parts, 2 * FFE), bf16),
+            jax.ShapeDtypeStruct((parts, own_experts, width // parts, FFE), bf16),
+        ]
+        + [jax.ShapeDtypeStruct(block, bf16)] * chips,
+        in_specs=[hbm] * (1 + chips) + [vmem] * 2 + [hbm] * 2,
+        out_specs=[hbm] * 3 + [vmem] * 2 + [hbm] * (2 + chips),
+        scratch_shapes=[
+            pltpu.VMEM((devices,) + block, bf16),
+            pltpu.VMEM((devices,) + block, bf16),
+            pltpu.VMEM(w_in.shape, bf16),
+            pltpu.VMEM(w_out.shape, bf16),
+            pltpu.VMEM(block, f32),
+            pltpu.VMEM(block, f32),
+            pltpu.VMEM((rows, LANES), f32),
+            pltpu.VMEM((devices, 8, rows), f32),
+            pltpu.VMEM((chips,) + block, bf16),
+            pltpu.VMEM((chips,) + block, bf16),
+            pltpu.VMEM((2,) + block, bf16),
+            pltpu.VMEM((2,) + block, bf16),
+            pltpu.VMEM(block, bf16),
+            pltpu.VMEM((2,) + block, bf16),
+            pltpu.VMEM((2,) + block, bf16),
+            pltpu.VMEM((2,) + block, bf16),
+            pltpu.VMEM((own_experts, rows, 2 * FFE), bf16),
+            pltpu.VMEM((own_experts,) + block, bf16),
+            pltpu.VMEM((own_experts, rows, FFE), bf16),
+            pltpu.VMEM((own_experts, width, 2 * FFE), f32),
+            pltpu.VMEM((own_experts, width, FFE), f32),
+            pltpu.VMEM((2, 2, rows, FFE), bf16),
+        ]
+        + [dma]
+        + [
+            dma((count,))
+            for count in (
+                chips + 1, chips, chips, chips, chips, chips, chips,
+                2, 2, 2, 2, chips, chips, devices, devices,
+            )
+        ]
+        + [
+            dma((3, own_experts)),
+            dma((2,)),
+            dma((3, 2)),
+            dma((2,)),
+            dma((2 * own_experts * max(parts, width // rows),)),
+        ],
+        cost_estimate=pl.CostEstimate(
+            flops=flops, bytes_accessed=40 << 20, transcendentals=devices * rows * FFE * 2
+        ),
+        compiler_params=pltpu.CompilerParams(
+            collective_id=collective_id, has_side_effects=True, vmem_limit_bytes=62 << 20
+        ),
+    )(normed, *cots, mask, router, w_in, w_out)
+
+
 def rms_parts(values):
     return lax.rsqrt(jnp.mean(values * values, axis=-1, keepdims=True) + norm_eps)
 
@@ -596,7 +1065,6 @@
     ints = jnp.concatenate([expert_picks[0].T, doc_ids], axis=0)
     ints = jnp.pad(ints, ((0, 16 - TOP - 1), (0, 0)))
 
-    out_grad_all = lax.all_gather(out_grad[0], "seq", axis=0, tiled=True)
     expert_in_full = lax.all_gather(expert_in.astype(bf16), "dp", axis=1, tiled=True)
     expert_out_full = lax.all_gather(expert_out.astype(bf16), "dp", axis=1, tiled=True)
     w_full = lax.all_gather(w_all, "dp", axis=0, tiled=True)
@@ -611,14 +1079,22 @@
             ("gather", "dp", misc, None),
         ],
     )
+    held, tok_all = lax.optimization_barrier((out_grad[0], tok_all))
+    chips = devices // 2
+    cots = [held] + [
+        lax.ppermute(held, "seq", [(i, (i + 2 * k) % devices) for i in range(devices)])
+        for k in range(1, chips)
+    ]
     w_own_all = w_own_all.reshape(width, w_cols)
     wo_full = wo_full.reshape(width, width)
     misc_full = misc_full.reshape(width, LANES)
-    router_full = misc_full[:, :experts]
+    router_full = jnp.where(jnp.arange(LANES)[None, :] < experts, misc_full, 0)
     gain_a = misc_full[:, experts]
     gain_m = misc_full[:, experts + 1].astype(f32)
     docs = ints_all[:, TOP].reshape(length)
-    picks = ints_all[:, :TOP].transpose(1, 0, 2).reshape(TOP, length)
+    chosen = jnp.any(
+        ints_all[:, :TOP, :, None] == jnp.arange(LANES, dtype=jnp.int32), axis=1
+    ).astype(bf16)
     start = jnp.sum((docs[:, None] < docs[None, :]).astype(jnp.int32), axis=0)
     cos, sin = rope_tables(length)
 
@@ -636,69 +1112,32 @@
     mid = resid + res_mult * dot_nn(attended, wo_full)
     mid_scale = rms_parts(mid)
     normed_m = (mid * mid_scale * gain_m).astype(bf16)
-    (moe_all,) = exchange(2, [("gather", "seq", normed_m, None)])
-    moe_all = moe_all.reshape(length, width)
-
+    (_, _, _, moe_sum, gate_cot, grads_in, grads_out, *branches) = moe_exchange(
+        2, normed_m, cots, chosen, router_full, expert_in_full, expert_out_full, parts
+    )
+    branches = [branches[0]] + [
+        lax.ppermute(
+            branches[k], "seq", [(i, (i + 2 * k) % devices) for i in range(devices)]
+        )
+        for k in range(1, chips)
+    ]
+    grads_in = lax.all_to_all(grads_in, "dp", split_axis=0, concat_axis=0)
+    grads_out = lax.all_to_all(grads_out, "dp", split_axis=0, concat_axis=0)
+    gate_cot = gate_cot[:, :own_experts].reshape(experts, rows)
     logits = lax.dot_general(
-        router_full, moe_all, (((0,), (1,)), ((), ())), preferred_element_type=f32
-    )
-    chosen = jnp.any(
-        picks[:, None, :] == jnp.arange(experts, dtype=jnp.int32)[None, :, None], axis=0
-    )
-    logits = jnp.where(chosen, logits, -jnp.inf)
-    gates = jnp.exp(logits - jnp.max(logits, axis=0, keepdims=True))
-    gates = gates / jnp.sum(gates, axis=0, keepdims=True)
-    own_gates = lax.dynamic_slice_in_dim(gates, me * own_experts, own_experts, 0)
-
-    out_cot = out_grad_all.astype(f32) * res_mult
-    branch = jnp.zeros((length, width), f32)
-    moe_cot = jnp.zeros((length, width), f32)
-    gate_cots, grads_in, grads_out = [], [], []
-    for e in range(own_experts):
-        gate = own_gates[e][:, None]
-        lin = dot_nn(moe_all, expert_in_full[e])
-        gate_lin, up_lin = lin[:, :FFE], lin[:, FFE:]
-        sig = jax.nn.sigmoid(gate_lin)
-        silu = gate_lin * sig
-        hidden = (silu * up_lin).astype(bf16)
-        res = dot_nt(hidden, expert_out_full[e]).astype(bf16).astype(f32)
-        branch = branch + gate * res
-        gate_cots.append(jnp.sum(out_cot * res, axis=1))
-        slot = (gate * out_cot).astype(bf16)
-        hidden_cot = dot_nn(slot, expert_out_full[e])
-        grads_out.append(dot_tn(slot, hidden).astype(bf16))
-        lin_cot = jnp.concatenate(
-            [hidden_cot * up_lin * (sig * (1 + gate_lin * (1 - sig))), hidden_cot * silu], axis=1
-        ).astype(bf16)
-        grads_in.append(dot_tn(moe_all, lin_cot).astype(bf16))
-        moe_cot = moe_cot + dot_nt(lin_cot, expert_in_full[e]).astype(bf16).astype(f32)
-    gate_cot = jnp.pad(
-        jnp.stack(gate_cots).reshape(own_experts, devices, rows).transpose(1, 0, 2),
-        ((0, 0), (0, 8 - own_experts), (0, 0)),
-    )
-    moe_sum, branch_sum, gate_cot = exchange(
-        3,
-        [
-            ("sum", "seq", moe_cot.astype(bf16).reshape(devices, rows, width), None),
-            ("sum", "seq", branch.astype(bf16).reshape(devices, rows, width), None),
-            ("swap", "seq", gate_cot, None),
-        ],
-    )
-    grads_in = jnp.stack(grads_in).reshape(own_experts, parts, w_rows, 2 * FFE)
-    grads_out = jnp.stack(grads_out).reshape(own_experts, parts, w_rows, FFE)
-    grads_in = lax.all_to_all(grads_in, "dp", split_axis=1, concat_axis=1)
-    grads_out = lax.all_to_all(grads_out, "dp", split_axis=1, concat_axis=1)
-    grad_e_in = jnp.sum(grads_in.astype(f32), axis=1)
-    grad_e_out = jnp.sum(grads_out.astype(f32), axis=1)
-
-    output = (mid + res_mult * branch_sum).astype(bf16)[None]
-    gate_cot = gate_cot[:, :own_experts].reshape(experts, rows)
-    my_gates = lax.dynamic_slice_in_dim(gates, me * rows, rows, 1)
+        router_full[:, :experts], normed_m, (((0,), (1,)), ((), ())), preferred_element_type=f32
+    )
+    my_chosen = jnp.any(
+        expert_picks[0].T[:, None, :] == jnp.arange(experts, dtype=jnp.int32)[None, :, None], axis=0
+    )
+    logits = jnp.where(my_chosen, logits, -jnp.inf)
+    my_gates = jnp.exp(logits - jnp.max(logits, axis=0, keepdims=True))
+    my_gates = my_gates / jnp.sum(my_gates, axis=0, keepdims=True)
     pick_cot = my_gates * (gate_cot - jnp.sum(my_gates * gate_cot, axis=0, keepdims=True))
     logit_cot = pick_cot.astype(bf16)
     grad_router = dot_nn(logit_cot, normed_m).T
     normed_m_cot = moe_sum + lax.dot_general(
-        logit_cot, router_full, (((0,), (1,)), ((), ())), preferred_element_type=f32
+        logit_cot, router_full[:, :experts], (((0,), (1,)), ((), ())), preferred_element_type=f32
     )
     pulled, grad_gain_m = rms_pull(mid, mid_scale, gain_m, normed_m_cot)
     mid_cot = out_grad[0].astype(f32) + pulled
@@ -743,6 +1182,15 @@
             ("swap", "seq", token_pack.reshape(devices, out_rows, pack_cols), None),
         ],
     )
+    (grad_qkv, token_pack), branches, grads_in, grads_out = lax.optimization_barrier(
+        ((grad_qkv, token_pack), branches, grads_in, grads_out)
+    )
+    branch_sum = branches[0].astype(f32)
+    for k in range(1, chips):
+        branch_sum = branch_sum + branches[k].astype(f32)
+    output = (mid + res_mult * branch_sum).astype(bf16)[None]
+    grad_e_in = jnp.sum(grads_in.astype(f32), axis=0)
+    grad_e_out = jnp.sum(grads_out.astype(f32), axis=0)
     resid_scale = rms_parts(resid)
     weighted = normed_a_cot * gain_a.astype(f32)
     input_grad = (

time: 579 us -> 464 us (0.80); the launches traced: 569 us -> 462 us
  matrix products: 91.4 us -> 14.6 us
  Pallas kernels: 387 us -> 327 us
  waiting for transfers between devices: 0.78 us -> 21.2 us
  starting transfers between devices: 9.79 us -> 16.1 us
  other arithmetic: 37.5 us -> 43.6 us
    pallas_call x7 -> x5, Pallas kernels: 351 us -> 213 us  [exchange(): pl.pallas_call(kernel, name=f'exchange{collective_id}', out_shape=out_sha...]
    pallas_call x0 -> x1, Pallas kernels: none -> 78 us  [moe_exchange(): pl.pallas_call(kernel, name='moe_exchange', out_shape=[jax.ShapeDtypeStru...]
    dot_general x6 -> x2, matrix products: 35.4 us -> 1.03 us  [dot_nn(): lax.dot_general(a, b, (((1,), (0,)), ((), ())), preferred_element_type=f32)]
    dot_general x6 -> x2, matrix products: 25.8 us -> 4.74 us  [dot_tn(): lax.dot_general(a, b, (((0,), (0,)), ((), ())), preferred_element_type=f32)]
    all_to_all x2, waiting for transfers between devices: 0.01 us -> 21.1 us  [the longest x1 21.1 us: on_device(): grads_out = lax.all_to_all(grads_out, 'dp', split_axis=0, concat_axis=0)]
    dot_general x6 -> x2, matrix products: 26.9 us -> 5.9 us  [dot_nt(): lax.dot_general(a, b, (((1,), (1,)), ((), ())), preferred_element_type=f32)]
    ppermute x0 -> x6, starting transfers between devices: none -> 5.84 us  [the longest x3 3.3 us: on_device(): lax.ppermute(branches[k], 'seq', [(i, (i + 2 * k) % devices) for i in ran...]
    unnamed x125 -> x89, local copies, waits for them, and re-layouts: 16.8 us -> 12.4 us
  transfers between devices with their start and end apart: 6 -> 11, of which waited for: 0 -> 1; matrix products, arithmetic and copies ran while one was open for 24% -> 12% of each run, Pallas kernels for 68% -> 71%
where the time goes in v2:
time: 464 us; the launch traced here: 462 us
  Pallas kernels  327 us (70%)
  other arithmetic  43.6 us (9%)
  local copies, waits for them, and re-layouts  25.2 us (5%)
  waiting for transfers between devices  21.2 us (5%)
  starting transfers between devices  16.1 us (3%)
  matrix products  14.6 us (3%)
  between operations  14.6 us (3%)
    pallas_call x5, Pallas kernels, exchange(): pl.pallas_call(kernel, name=f'exchange{collective_id}', out_shape=out_sha...  213 us
    pallas_call x1, Pallas kernels, moe_exchange(): pl.pallas_call(kernel, name='moe_exchange', out_shape=[jax.ShapeDtypeStru...  78 us
    all_to_all x1, waiting for transfers between devices, on_device(): grads_out = lax.all_to_all(grads_out, 'dp', split_axis=0, concat_axis=0)  21.1 us
    pallas_call x1, Pallas kernels, attend_backward(): pl.pallas_call(kernel, name='attend_backward', grid_spec=grid_spec, out_s...  18.2 us
    pallas_call x1, Pallas kernels, attend_forward(): pl.pallas_call(kernel, name='attend_forward', grid_spec=grid_spec, out_sh...  17.6 us
    unnamed x89, local copies, waits for them, and re-layouts  12.4 us
  transfers between devices with their start and end apart: 11, of which 1 were waited for; matrix products, arithmetic and copies ran while one was open for 12% of the time, Pallas kernels for 71%

profile of v2, /device:TPU:13, one launch (start us, length us, event | category | flops | bytes accessed | tf_op | source)
XLA Modules:
  0.0 462.0 jit_solution(4810304960397150727)
XLA Ops:
  9.5 2.7 convert_element_type.163
  17.4 45.2 %exchange0.1 = (bf16[8,256,1024]{2,1,0:T(8,128)(2,1)}, s32[8,16,256]{2,1,0:T(8,128)S(1)}, bf16[4,256,256]{2,1,0:T(8,128)(2,1)S(1)}, bf16[4,256,1024]{2,1,0:T(8,128)(2,1)S(1)}, bf16[4,256,128]{2,1,0:T(8,128)(2,1)S(1)}) custom-call(bf16[256,1024]{1,0:T(8,128)(2,1)S(1)} %bitcast.63, s32[16,256]{1,0:T(8,128)S(1)} %pad.8.refs_1_, ...), custom_call_target="tpu_custom_call" | custom-call | tf_op jit(solution)/shard_map/exchange0/pallas_call | solution.py:255
  71.0 3.7 fusion.9
  76.4 17.6 %attend_forward.1 = (bf16[8,256,1024]{2,1,0:T(8,128)(2,1)S(1)}, bf16[8,256,128]{2,1,0:T(8,128)(2,1)S(1)}, bf16[8,256,128]{2,1,0:T(8,128)(2,1)S(1)}, bf16[8,256,1...) custom-call(s32[8]{0:T(128)S(1)} %and_select_fusion.first_ref, ...), custom_call_target="tpu_custom_call" | custom-call | flops 3221225472 | bytes 16777216 | tf_op jit(solution)/shard_map/attend_forward/pallas_call | solution.py:411
  96.9 27.6 %exchange1.1 = bf16[256,1024]{1,0:T(8,128)(2,1)S(1)} custom-call(bf16[8,256,128]{2,1,0:T(8,128)(2,1)S(1)} %get-tuple-element.50.refs_0_), custom_call_target="tpu_custom_call" | custom-call | tf_op jit(solution)/shard_map/exchange1/pallas_call | solution.py:255
  125.3 2.9 fusion
  130.9 78.0 %moe_exchange.1 = (bf16[2,8,256,1024]{3,2,1,0:T(8,128)(2,1)}, bf16[2,8,256,1024]{3,2,1,0:T(8,128)(2,1)}, bf16[2,8,256,512]{3,2,1,0:T(8,128)(2,1)}, f32[256,1024]...) custom-call(bf16[256,1024]{1,0:T(8,128)(2,1)} %multiply_convert_fusi, ...), custom_call_target="tpu_custom_call" | custom-call | flops 38654705664 | bytes 41943040 | tf_op jit(solution)/shard_map/moe_exchange/pallas_call | solution.py:951
  209.0 4.9 %all-to-all-start.1 = ((bf16[4,2,256,512]{3,2,1,0:T(8,128)(2,1)}), bf16[4,2,256,512]{3,2,1,0:T(8,128)(2,1)}, u32[]{:S(2)}, u32[]{:S(2)}) async-start(bf16[4,2,256,512]{3,2,1,0:T(8,128)(2,1)} %get-tuple-element.69), calls=%async_computation.1 | async-start | bytes 4194304 | tf_op jit(solution)/shard_map/all_to_all | solution.py:1125
  215.1 2.6 multiply_reduce_fusion
  217.8 21.1 %all-to-all-done.1 = bf16[4,2,256,512]{3,2,1,0:T(8,128)(2,1)} async-done(((bf16[4,2,256,512]{3,2,1,0:T(8,128)(2,1)}), bf16[4,2,256,512]{3,2,1,0:T(8,128)(2,1)}, u32[]{:S(2)}, u32[]{:S(2)}) %all-to-all-start.1) | async-done | bytes 2097184 | tf_op jit(solution)/shard_map/all_to_all | solution.py:1125
  238.8 5.2 %all-to-all-start = ((bf16[4,2,256,1024]{3,2,1,0:T(8,128)(2,1)}), bf16[4,2,256,1024]{3,2,1,0:T(8,128)(2,1)}, u32[]{:S(2)}, u32[]{:S(2)}) async-start(bf16[4,2,256,1024]{3,2,1,0:T(8,128)(2,1)} %get-tuple-element.68), calls=%async_computation | async-start | bytes 8388608 | tf_op jit(solution)/shard_map/all_to_all | solution.py:1124
  244.0 3.0 subtract_add_fusion
  249.1 44.7 %exchange4.1.do_ref = bf16[8,256,128]{2,1,0:T(8,128)(2,1)S(1)} custom-call(bf16[256,1024]{1,0:T(8,128)(2,1)S(1)} %convolution_convert_fusion.1.refs_0_), custom_call_target="tpu_custom_call" | custom-call | tf_op jit(solution)/shard_map/exchange4/pallas_call | solution.py:255
  296.8 3.4 convolution_convert_fusion
  300.2 5.1 %concatenate.37.refs_2_ = bf16[4,256,1152]{2,1,0:T(8,128)(2,1)} concatenate(bf16[4,256,1024]{2,1,0:T(8,128)(2,1)} %bitcast.67, bf16[4,256,16]{2,1,0:T(8,128)(2,1)} %bitcast.74, bf16[4,256,1]{2,1,0:T(8,128)(2,1)} %concatenate.38, bf16[4,256,111]{2,1,0:T(8,128)(2,1)S(1)} %broadcast_in_dim.56), dimensions={2} | concatenate | bytes 4718592 | tf_op jit(solution)/shard_map/concatenate | solution.py:1156
  308.7 18.2 %attend_backward.1.refs_0_ = bf16[8,256,256]{2,1,0:T(8,128)(2,1)S(1)} custom-call(s32[8]{0:T(128)S(1)} %and_select_fusion.first_ref, bf16[8,256,128]{2,1,0:T(8,128)(2,1)S(1)} %copy-done.21, bf16[8,256,128]{2,1,0:T(8,128)(2,1)S(1)} %copy-done.23, bf16[8,256,128]{2,1,0:T(8,128)(2,1)S(1)} %copy-done.8, f32[8,64,512]{2,1,0:T(8,128)S(1)} %copy-done.19, ...), custom_call_target="tpu_custom_call" | custom-call | flops 5368709120 | bytes 4194304 | tf_op jit(solution)/shard_map/attend_backward/pallas_call | solution.py:526
  328.2 35.1 %exchange5.1 = (bf16[256,2048]{1,0:T(8,128)(2,1)S(1)}, bf16[4,256,256]{2,1,0:T(8,128)(2,1)S(1)}, bf16[4,256,1152]{2,1,0:T(8,128)(2,1)S(1)}) custom-call(bf16[8,256,256]{2,1,0:T(8,128)(2,1)S(1)} %attend_backward.1.refs_0_, bf16[4,256,256]{2,1,0:T(8,128)(2,1)S(1)} %bitcast.64, bf16[4,256,1152]{2,1,0:T(8,128)(2,1)} %concatenate.37.refs_2_), custom_call_target="tpu_custom_call" | custom-call | tf_op jit(solution)/shard_map/exchange5/pallas_call | solution.py:255
  367.9 2.9 collective-permute-start.4
  371.8 60.4 %exchange6.1 = (bf16[8,32,256]{2,1,0:T(8,128)(2,1)S(1)}, bf16[8,32,1152]{2,1,0:T(8,128)(2,1)S(1)}) custom-call(bf16[8,32,256]{2,1,0:T(8,128)(2,1)S(1)} %bitcast.65, bf16[8,32,1152]{2,1,0:T(8,128)(2,1)S(1)} %bitcast.60), custom_call_target="tpu_custom_call" | custom-call | tf_op jit(solution)/shard_map/exchange6/pallas_call | solution.py:255
  432.2 3.9 fusion.2
  436.2 2.3 fusion.8
  444.7 4.7 %convert_reduce_fusion.1 = f32[2,256,1024]{2,1,0:T(8,128)} fusion(bf16[4,2,256,1024]{3,2,1,0:T(8,128)(2,1)} %all-to-all-done), kind=kLoop, calls=%fused_computation.1 | loop fusion | flops 3670016 | bytes 6291456 | tf_op jit(solution)/shard_map/reduce_sum | solution.py:1192
  449.5 3.0 convert_reduce_fusion.2
  453.1 2.4 fusion.7
  (179 shorter events, 46.6 us)
Async XLA Ops:
  7.2 123.7 %all-gather.6.cloned.1.call-start = ((), (), s32[]{:S(2)}) async-start(), calls=%async_computation.3 | async-start | bytes 2621440 | tf_op jit(solution)/shard_map/all_gather | solution.py:1069
  9.5 121.5 %all-gather.4.cloned.1.call-start = ((), (), s32[]{:S(2)}) async-start(), calls=%async_computation.2 | async-start | bytes 5242880 | tf_op jit(solution)/shard_map/all_gather | solution.py:1068
  12.3 420.0 %all-gather.8.cloned.1.call-start = ((), (), s32[]{:S(2)}) async-start(), calls=%async_computation.4 | async-start | bytes 5242880 | tf_op jit(solution)/shard_map/all_gather | solution.py:1070
  64.1 60.4 %copy-start = (bf16[4,256,1024]{2,1,0:T(8,128)(2,1)}, bf16[4,256,1024]{2,1,0:T(8,128)(2,1)S(1)}, u32[]{:S(2)}) copy-start(bf16[4,256,1024]{2,1,0:T(8,128)(2,1)S(1)} %get-tuple-element.51) | copy-start | bytes 6291460
  64.1 66.7 %collective-permute-start = (bf16[256,1024]{1,0:T(8,128)(2,1)}, bf16[256,1024]{1,0:T(8,128)(2,1)}, u32[]{:S(2)}, u32[]{:S(2)}) collective-permute-start(bf16[256,1024]{1,0:T(8,128)(2,1)} %bitcast.75), channel_id=1, source_target_pairs={{0,2},{1,3},{2,4},{3,5},{4,6},{5,7},{6,0},{7,1},{8,10},{9,11},{10,... | collective-permute-start | bytes 1572872 | tf_op jit(solution)/shard_map/ppermute | solution.py:1085
  65.4 65.5 %collective-permute-start.1 = (bf16[256,1024]{1,0:T(8,128)(2,1)}, bf16[256,1024]{1,0:T(8,128)(2,1)}, u32[]{:S(2)}, u32[]{:S(2)}) collective-permute-start(bf16[256,1024]{1,0:T(8,128)(2,1)} %bitcast.76), channel_id=1, source_target_pairs={{0,4},{1,5},{2,6},{3,7},{4,0},{5,1},{6,2},{7,3},{8,12},{9,13},{10,... | collective-permute-start | bytes 1572872 | tf_op jit(solution)/shard_map/ppermute | solution.py:1085
  66.5 64.3 %collective-permute-start.2 = (bf16[256,1024]{1,0:T(8,128)(2,1)}, bf16[256,1024]{1,0:T(8,128)(2,1)}, u32[]{:S(2)}, u32[]{:S(2)}) collective-permute-start(bf16[256,1024]{1,0:T(8,128)(2,1)} %bitcast.77), channel_id=1, source_target_pairs={{0,6},{1,7},{2,0},{3,1},{4,2},{5,3},{6,4},{7,5},{8,14},{9,15},{10,... | collective-permute-start | bytes 1572872 | tf_op jit(solution)/shard_map/ppermute | solution.py:1085
  76.4 17.7 %copy-start.3 = (f32[8,256,128]{2,1,0:T(8,128)}, f32[8,256,128]{2,1,0:T(8,128)S(1)}, u32[]{:S(2)}) copy-start(f32[8,256,128]{2,1,0:T(8,128)S(1)} %get-tuple-element.168.cos_ref) | copy-start | bytes 3145732
  76.4 17.7 %copy-start.5 = (f32[8,256,128]{2,1,0:T(8,128)}, f32[8,256,128]{2,1,0:T(8,128)S(1)}, u32[]{:S(2)}) copy-start(f32[8,256,128]{2,1,0:T(8,128)S(1)} %get-tuple-element.169.sin_ref) | copy-start | bytes 3145732
  96.9 34.0 %copy-start.18 = (f32[8,64,512]{2,1,0:T(8,128)}, f32[8,64,512]{2,1,0:T(8,128)S(1)}, u32[]{:S(2)}) copy-start(f32[8,64,512]{2,1,0:T(8,128)S(1)} %get-tuple-element.57.ot_ref) | copy-start | bytes 3145732
  96.9 34.0 %copy-start.22 = (bf16[8,256,128]{2,1,0:T(8,128)(2,1)}, bf16[8,256,128]{2,1,0:T(8,128)(2,1)S(1)}, u32[]{:S(2)}) copy-start(bf16[8,256,128]{2,1,0:T(8,128)(2,1)S(1)} %get-tuple-element.53.kv_ref) | copy-start | bytes 1572868
  209.0 29.9 %all-to-all-start.1 = ((bf16[4,2,256,512]{3,2,1,0:T(8,128)(2,1)}), bf16[4,2,256,512]{3,2,1,0:T(8,128)(2,1)}, u32[]{:S(2)}, u32[]{:S(2)}) async-start(bf16[4,2,256,512]{3,2,1,0:T(8,128)(2,1)} %get-tuple-element.69), calls=%async_computation.1 | async-start | bytes 4194304 | tf_op jit(solution)/shard_map/all_to_all | solution.py:1125
  238.8 199.7 %all-to-all-start = ((bf16[4,2,256,1024]{3,2,1,0:T(8,128)(2,1)}), bf16[4,2,256,1024]{3,2,1,0:T(8,128)(2,1)}, u32[]{:S(2)}, u32[]{:S(2)}) async-start(bf16[4,2,256,1024]{3,2,1,0:T(8,128)(2,1)} %get-tuple-element.68), calls=%async_computation | async-start | bytes 8388608 | tf_op jit(solution)/shard_map/all_to_all | solution.py:1124
  296.7 8.6 %copy-start.4 = (f32[8,256,128]{2,1,0:T(8,128)S(1)}, f32[8,256,128]{2,1,0:T(8,128)}, u32[]{:S(2)}) copy-start(f32[8,256,128]{2,1,0:T(8,128)} %copy-done.3) | copy-start | bytes 3145732
  296.8 8.6 %copy-start.6 = (f32[8,256,128]{2,1,0:T(8,128)S(1)}, f32[8,256,128]{2,1,0:T(8,128)}, u32[]{:S(2)}) copy-start(f32[8,256,128]{2,1,0:T(8,128)} %copy-done.5) | copy-start | bytes 3145732
  308.7 18.2 %copy-start.17 = (bf16[8,256,1024]{2,1,0:T(8,128)(2,1)S(1)}, bf16[8,256,1024]{2,1,0:T(8,128)(2,1)}, u32[]{:S(2)}) copy-start(bf16[8,256,1024]{2,1,0:T(8,128)(2,1)} %copy-done.16) | copy-start | bytes 12582916
  367.6 70.9 %collective-permute-start.3 = (bf16[256,1024]{1,0:T(8,128)(2,1)}, bf16[256,1024]{1,0:T(8,128)(2,1)S(1)}, u32[]{:S(2)}, u32[]{:S(2)}) collective-permute-start(bf16[256,1024]{1,0:T(8,128)(2,1)} %get-tuple-element.65), channel_id=1, source_target_pairs={{0,2},{1,3},{2,4},{3,5},{4,6},{5,7},{6,0},{7,1},{8,10},{9,11},{10,... | collective-permute-start | bytes 1572872 | tf_op jit(solution)/shard_map/ppermute | solution.py:1119
  367.9 70.5 %collective-permute-start.4 = (bf16[256,1024]{1,0:T(8,128)(2,1)}, bf16[256,1024]{1,0:T(8,128)(2,1)}, u32[]{:S(2)}, u32[]{:S(2)}) collective-permute-start(bf16[256,1024]{1,0:T(8,128)(2,1)} %get-tuple-element.66), channel_id=1, source_target_pairs={{0,4},{1,5},{2,6},{3,7},{4,0},{5,1},{6,2},{7,3},{8,12},{9,13},{10,... | collective-permute-start | bytes 1572872 | tf_op jit(solution)/shard_map/ppermute | solution.py:1119
  370.9 67.6 %collective-permute-start.5 = (bf16[256,1024]{1,0:T(8,128)(2,1)}, bf16[256,1024]{1,0:T(8,128)(2,1)}, u32[]{:S(2)}, u32[]{:S(2)}) collective-permute-start(bf16[256,1024]{1,0:T(8,128)(2,1)} %get-tuple-element.67), channel_id=1, source_target_pairs={{0,6},{1,7},{2,0},{3,1},{4,2},{5,3},{6,4},{7,5},{8,14},{9,15},{10,... | collective-permute-start | bytes 1572872 | tf_op jit(solution)/shard_map/ppermute | solution.py:1119
  441.9 10.5 %copy-start.34 = (f32[32,512]{1,0:T(8,128)}, f32[32,512]{1,0:T(8,128)S(1)}, u32[]{:S(2)}) copy-start(f32[32,512]{1,0:T(8,128)S(1)} %reshape.268) | copy-start | bytes 196612
  442.1 10.3 %copy-start.35 = (f32[32,512]{1,0:T(8,128)}, f32[32,512]{1,0:T(8,128)S(1)}, u32[]{:S(2)}) copy-start(f32[32,512]{1,0:T(8,128)S(1)} %reshape.269) | copy-start | bytes 196612
  444.7 7.7 %copy-start.40 = (f32[256]{0:T(256)S(1)}, f32[256]{0:T(256)}, u32[]{:S(2)}) copy-start(f32[256]{0:T(256)} %param.22) | copy-start | bytes 3076
  444.7 8.3 %copy-start.26 = (f32[256,1024]{1,0:T(8,128)S(1)}, f32[256,1024]{1,0:T(8,128)}, u32[]{:S(2)}) copy-start(f32[256,1024]{1,0:T(8,128)} %copy-done.24) | copy-start | bytes 3145732
  444.7 8.3 %copy-start.32 = (bf16[256,1024]{1,0:T(8,128)(2,1)S(1)}, bf16[256,1024]{1,0:T(8,128)(2,1)}, u32[]{:S(2)}) copy-start(bf16[256,1024]{1,0:T(8,128)(2,1)} %get-tuple-element.70) | copy-start | bytes 1572868
  (29 other events, 88.9 us)
Sparse Core Ops, SparseCore 0:
  9.9 59.6 all-gather.5
  72.0 52.4 all-gather.3
  126.4 52.6 all-gather.7

commit v3 on v2

--- a/solution.py
+++ b/solution.py
@@ -2,12 +2,14 @@
 
 import jax
 import jax.numpy as jnp
+import numpy as np
 from jax import lax
 from jax.experimental import pallas as pl
 from jax.experimental.pallas import tpu as pltpu
 from jax.sharding import PartitionSpec as P
 
 MESH = pl.DeviceIdType.MESH
+PIECES = 2
 
 
 def _block(ref, j, cut):
@@ -24,6 +26,7 @@
         count = size[axis]
         out_spec = pl.BlockSpec(memory_space=pl.ANY)
         extra = []
+        lead = (PIECES,) if kind == "gather" and axis == "seq" else ()
         if kind == "gather":
             shape, dtype = (count,) + x.shape, x.dtype
             copies = count - 1 if axis == "dp" else 3 + 4 * (count // 2 - 1)
@@ -35,23 +38,12 @@
                 shape = (count, x.shape[0], cut[1])
             else:
                 shape = (x.shape[1], count * cut[1])
-        else:
-            chips = count // 2
-            shape, dtype, copies = x.shape[1:], jnp.float32, 2 * chips - 1
-            out_spec = pl.BlockSpec(memory_space=pltpu.VMEM)
-            extra = [
-                pltpu.VMEM((chips,) + x.shape[1:], x.dtype),
-                pltpu.VMEM((chips,) + x.shape[1:], x.dtype),
-                pltpu.VMEM((chips,) + x.shape[1:], x.dtype),
-                pltpu.VMEM((chips,) + x.shape[1:], x.dtype),
-                pltpu.SemaphoreType.DMA((chips,)),
-            ]
         out_shapes.append(jax.ShapeDtypeStruct(shape, dtype))
         out_specs.append(out_spec)
         places.append((len(scratch), len(extra)))
         scratch += [
-            pltpu.SemaphoreType.DMA((copies,)),
-            pltpu.SemaphoreType.DMA((max(copies, count),)),
+            pltpu.SemaphoreType.DMA(lead + (copies,)),
+            pltpu.SemaphoreType.DMA(lead + (max(copies, count),)),
             pltpu.SemaphoreType.DMA,
         ] + extra
 
@@ -134,119 +126,66 @@
                 own.start()
                 third.append(own.wait)
 
-                def line(src, b, slot, to, axis=axis, o=o, send=send, recv=recv, core=core):
+                cuts = PIECES if x.shape[0] % (16 * PIECES) == 0 else 1
+                size_of = x.shape[0] // cuts
+
+                def cut_of(ref, i, size_of=size_of):
+                    return ref.at[pl.ds(i * size_of, size_of)]
+
+                def line(src, b, i, slot, to, axis=axis, o=o, send=send, recv=recv, core=core, cut_of=cut_of):
                     return remote(
-                        axis, src, o.at[2 * b + core], send.at[slot], recv.at[b], to
+                        axis, src, cut_of(o.at[2 * b + core], i), send.at[i, slot], recv.at[i, b], to
                     )
 
-                def across(src, b, slot, half, axis=axis, o=o, send=send, recv=recv, chips=chips, sibling=sibling):
+                def across(src, b, i, slot, half, axis=axis, o=o, send=send, recv=recv, chips=chips, sibling=sibling, cut_of=cut_of):
                     return remote(
-                        axis, src, o.at[2 * b + half], send.at[slot], recv.at[chips + b], sibling
+                        axis,
+                        src,
+                        cut_of(o.at[2 * b + half], i),
+                        send.at[i, slot],
+                        recv.at[i, chips + b],
+                        sibling,
                     )
 
                 def guarded(where, act):
                     pl.when(where)(act)
 
-                for slot, where, to in ((0, chip > 0, my - 2), (1, chip < chips - 1, my + 2)):
-                    copy = line(x, chip, slot, to)
-                    guarded(where, copy.start)
-                    third.append(functools.partial(guarded, where, copy.wait_send))
-                copy = across(x, chip, 2, core)
-                copy.start()
-                third.append(copy.wait_send)
-                third.append(across(x, chip, 2, 1 - core).wait_recv)
-
-                def hop(k, side, chips=chips, chip=chip, core=core, my=my, x=x, o=o, line=line, across=across):
+                for i in range(cuts):
+                    for slot, where, to in ((0, chip > 0, my - 2), (1, chip < chips - 1, my + 2)):
+                        copy = line(cut_of(x, i), chip, i, slot, to)
+                        guarded(where, copy.start)
+                        third.append(functools.partial(guarded, where, copy.wait_send))
+                for i in range(cuts):
+                    copy = across(cut_of(x, i), chip, i, 2, core)
+                    copy.start()
+                    third.append(copy.wait_send)
+                    third.append(across(cut_of(x, i), chip, i, 2, 1 - core).wait_recv)
+
+                def hop(k, side, i, chips=chips, chip=chip, core=core, my=my, x=x, o=o, line=line, across=across, cut_of=cut_of):
                     b = chip + side * k
                     there = (b >= 0) & (b < chips)
                     onward = there & ((chip - side >= 0) & (chip - side < chips))
                     slot = 3 + (k - 1) * 4 + (side + 1)
-                    spot = o.at[2 * b + core]
-                    further = line(spot, b, slot, my - 2 * side)
-                    over = across(spot, b, slot + 1, core)
+                    spot = cut_of(o.at[2 * b + core], i)
+                    further = line(spot, b, i, slot, my - 2 * side)
+                    over = across(spot, b, i, slot + 1, core)
+                    arrived = line(cut_of(x, i), b, i, slot, my)
+                    brought = across(cut_of(x, i), b, i, slot + 1, 1 - core)
 
                     @pl.when(there)
                     def _():
-                        line(x, b, slot, my).wait_recv()
-                        over.start()
+                        arrived.wait_recv()
 
                     guarded(onward, further.start)
+                    guarded(there, over.start)
                     third.append(functools.partial(guarded, onward, further.wait_send))
                     third.append(functools.partial(guarded, there, over.wait_send))
-                    third.append(
-                        functools.partial(
-                            guarded, there, across(x, b, slot + 1, 1 - core).wait_recv
-                        )
-                    )
+                    third.append(functools.partial(guarded, there, brought.wait_recv))
 
                 for k in range(1, chips):
-                    for side in (-1, 1):
-                        second.append((k, functools.partial(hop, k, side)))
-            else:
-                chips = count // 2
-                chip, core = my // 2, lax.rem(my, 2)
-                sibling = my + 1 - 2 * core
-                mine, theirs, pre, far, loads = work[at + 3 : at + 3 + extra]
-                order = [k % chips for k in range(1, chips + 1)]
-                for k in order:
-                    to = lax.rem(chip + k, chips)
-                    remote(
-                        axis,
-                        x.at[2 * to + 1 - core],
-                        theirs.at[k],
-                        send.at[k],
-                        recv.at[k],
-                        sibling,
-                    ).start()
-                    pltpu.make_async_copy(x.at[2 * to + core], mine.at[k], loads.at[k]).start()
-
-                def fold(k, last, axis=axis, x=x, o=o, send=send, recv=recv, chips=chips, chip=chip, core=core, sibling=sibling, mine=mine, theirs=theirs, pre=pre, far=far, loads=loads):
-                    to = lax.rem(chip + k, chips)
-                    give = remote(
-                        axis,
-                        x.at[2 * to + 1 - core],
-                        theirs.at[k],
-                        send.at[k],
-                        recv.at[k],
-                        sibling,
-                    )
-                    give.wait_recv()
-                    third.append(give.wait_send)
-                    pltpu.make_async_copy(
-                        x.at[2 * to + core], mine.at[k], loads.at[k]
-                    ).wait()
-                    both = mine[k].astype(jnp.float32) + theirs[k].astype(jnp.float32)
-                    if not last:
-                        pre[k] = both.astype(pre.dtype)
-                        copy = remote(
-                            axis,
-                            pre.at[k],
-                            far.at[k],
-                            send.at[chips - 1 + k],
-                            recv.at[chips - 1 + k],
-                            to * 2 + core,
-                        )
-                        copy.start()
-                        third.append(copy.wait_send)
-                    else:
-                        o[...] = both
-
-                for k in order:
-                    second.append((k or chips, lambda k=k, fold=fold: fold(k, k == 0)))
-
-                def total(k, axis=axis, o=o, send=send, recv=recv, chips=chips, pre=pre, far=far, core=core, chip=chip):
-                    remote(
-                        axis,
-                        pre.at[k],
-                        far.at[k],
-                        send.at[chips - 1 + k],
-                        recv.at[chips - 1 + k],
-                        lax.rem(chip + k, chips) * 2 + core,
-                    ).wait_recv()
-                    o[...] += far[k].astype(jnp.float32)
-
-                for k in range(1, chips):
-                    second.append((chips + k, lambda k=k, total=total: total(k)))
+                    for i in range(cuts):
+                        for side in (-1, 1):
+                            second.append((k + i / cuts, functools.partial(hop, k, side, i)))
         for _, run in sorted(second, key=lambda item: item[0]):
             run()
         for wait in third:
@@ -301,15 +240,35 @@
     )
 
 
-def rope_tables(length):
+def rope_table(blocks, rows):
     half = HEAD_SIZE // 2
-    frequency = rope_theta ** (-jnp.arange(half, dtype=f32) * 2.0 / HEAD_SIZE)
-    angles = jnp.arange(length, dtype=jnp.int32).astype(f32)[:, None] * frequency[None, :]
-    cos, sin = jnp.cos(angles), jnp.sin(angles)
-    repeat = LANES // HEAD_SIZE
+    frequency = np.float32(rope_theta) ** (
+        -np.arange(half, dtype=np.float32) * np.float32(2.0) / np.float32(HEAD_SIZE)
+    )
+    angles = (frequency[:, None] * np.arange(blocks * rows, dtype=np.float32)[None, :]).astype(
+        np.float32
+    )
+    table = np.concatenate([np.cos(angles), np.sin(angles)], axis=0).astype(np.float32)
+    return jnp.asarray(table.reshape(HEAD_SIZE, blocks, rows).transpose(1, 0, 2))
+
+
+def spread_table(table):
+    half = HEAD_SIZE // 2
+    turned = table.T
+    cos, sin = turned[:, :half], turned[:, half:]
     return (
-        jnp.concatenate([cos, cos] * repeat, axis=1),
-        jnp.concatenate([-sin, sin] * repeat, axis=1),
+        jnp.concatenate([cos, cos] * (LANES // HEAD_SIZE), axis=1),
+        jnp.concatenate([-sin, sin] * (LANES // HEAD_SIZE), axis=1),
+    )
+
+
+def across_lanes(row, lanes):
+    return jnp.broadcast_to(row, (lanes, row.shape[1])).T
+
+
+def first_blocks(docs):
+    return jnp.sum(
+        (docs[:, -1][:, None] < docs[:, 0][None, :]).astype(jnp.int32), axis=0
     )
 
 
@@ -319,22 +278,21 @@
     )
 
 
-def attend_forward(tok_all, w_own, gain, cos, sin, start, heads):
+def attend_forward(tok_all, w_own, gain, table, docs, heads):
     blocks, rows, width = tok_all.shape
     length = blocks * rows
     cols = heads * rows
-    first = start.reshape(blocks, rows)[:, 0] // rows
-    start_rows = jnp.tile(start.reshape(blocks, 1, rows), (1, 1, heads))
+    first = first_blocks(docs)
     out_width = heads * HEAD_SIZE
 
-    def kernel(first_ref, tok, w, gain_ref, cos_ref, sin_ref, start_ref, na_ref, q_ref, kv_ref, att_ref, ot_ref, lse_ref, k_scr, vt_scr):
+    def kernel(first_ref, tok, w, gain_ref, table_ref, docs_ref, na_ref, q_ref, kv_ref, att_ref, ot_ref, lse_ref, k_scr, vt_scr, doc_scr):
         i = pl.program_id(0)
         x = tok[0].astype(f32)
         scale = lax.rsqrt(jnp.mean(x * x, axis=-1, keepdims=True) + norm_eps)
         na = (x * scale * gain_ref[...].astype(f32)).astype(bf16)
         na_ref[0] = na
         qkv = dot_nn(na, w[...])
-        c, s = cos_ref[0], sin_ref[0]
+        c, s = spread_table(table_ref[0])
         q, kv = qkv[:, :HEADS_LANES], qkv[:, HEADS_LANES:]
         q = (q * c + turn(q) * s).astype(bf16)
         lane = lax.broadcasted_iota(jnp.int32, kv.shape, 1)
@@ -344,7 +302,9 @@
         k_scr[i] = kv[:, :HEAD_SIZE]
         vt_scr[i] = kv.astype(f32).T[HEAD_SIZE:].astype(bf16)
         q2 = stack_heads(q, heads)
-        start_row = start_ref[0]
+        doc_row = docs_ref[0].astype(f32)
+        doc_scr[i] = across_lanes(doc_row, LANES)
+        doc_query = jnp.concatenate([doc_row] * heads, axis=1)
         query = i * rows + lax.rem(lax.broadcasted_iota(jnp.int32, (1, cols), 1), rows)
         key_iota = lax.broadcasted_iota(jnp.int32, (rows, cols), 0)
 
@@ -352,7 +312,8 @@
             top, total, ot = carry
             scores = dot_nt(k_scr[j], q2) * att_mult
             key = key_iota + j * rows
-            scores = jnp.where((key >= start_row) & (key <= query), scores, -1e30)
+            same = jnp.concatenate([doc_scr[j]] * (cols // LANES), axis=1) == doc_query
+            scores = jnp.where(same & (key <= query), scores, -1e30)
             new_top = jnp.maximum(top, jnp.max(scores, axis=0, keepdims=True))
             p = jnp.exp(scores - new_top)
             keep = jnp.exp(top - new_top)
@@ -391,9 +352,8 @@
             block((rows, width)),
             whole(w_own.shape),
             whole((1, width)),
-            block((rows, LANES)),
-            block((rows, LANES)),
-            block((1, cols)),
+            block((HEAD_SIZE, rows)),
+            block((1, rows)),
         ],
         out_specs=[
             block((rows, width)),
@@ -406,6 +366,7 @@
         scratch_shapes=[
             pltpu.VMEM((blocks, rows, HEAD_SIZE), bf16),
             pltpu.VMEM((blocks, HEAD_SIZE, rows), bf16),
+            pltpu.VMEM((blocks, rows, LANES), f32),
         ],
     )
     return pl.pallas_call(
@@ -433,20 +394,18 @@
         tok_all,
         w_own,
         gain,
-        cos.reshape(blocks, rows, LANES),
-        sin.reshape(blocks, rows, LANES),
-        start_rows,
-    )
-
-
-def attend_backward(q_all, kv_all, cot, ot, lse, cos, sin, start, heads):
+        table,
+        docs[:, None],
+    )
+
+
+def attend_backward(q_all, kv_all, cot, ot, lse, table, docs, heads):
     blocks, rows, _ = q_all.shape
     length = blocks * rows
     cols = heads * rows
-    first = start.reshape(blocks, rows)[:, 0] // rows
-    start_rows = jnp.tile(start.reshape(blocks, 1, rows), (1, 1, heads))
-
-    def kernel(first_ref, q_ref, kv_ref, do_ref, ot_ref, lse_ref, cos_ref, sin_ref, start_ref, out_ref, dk_scr, dv_scr, dq_scr):
+    first = first_blocks(docs)
+
+    def kernel(first_ref, q_ref, kv_ref, do_ref, ot_ref, lse_ref, table_ref, docs_ref, out_ref, dk_scr, dv_scr, dq_scr, doc_scr):
         i = pl.program_id(0)
 
         @pl.when(i == 0)
@@ -458,7 +417,9 @@
         do2 = stack_heads(do_ref[0], heads)
         delta = jnp.sum(do2.astype(f32).T * ot_ref[0], axis=0, keepdims=True)
         log_total = lse_ref[0]
-        start_row = start_ref[0]
+        doc_row = docs_ref[0].astype(f32)
+        doc_scr[i] = across_lanes(doc_row, LANES)
+        doc_query = jnp.concatenate([doc_row] * heads, axis=1)
         query = i * rows + lax.rem(lax.broadcasted_iota(jnp.int32, (1, cols), 1), rows)
         key_iota = lax.broadcasted_iota(jnp.int32, (rows, cols), 0)
         dq_scr[...] = jnp.zeros_like(dq_scr)
@@ -469,9 +430,8 @@
             k, v = kv[:, :HEAD_SIZE], kv[:, HEAD_SIZE:]
             scores = dot_nt(k, q2) * att_mult
             key = key_iota + j * rows
-            p = jnp.where(
-                (key >= start_row) & (key <= query), jnp.exp(scores - log_total), 0.0
-            )
+            same = jnp.concatenate([doc_scr[j]] * (cols // LANES), axis=1) == doc_query
+            p = jnp.where(same & (key <= query), jnp.exp(scores - log_total), 0.0)
             ds = (p * (dot_nt(v, do2) - delta)).astype(bf16)
             dv_scr[j] += dot_nn(p.astype(bf16), do2)
             dk_scr[j] += dot_nn(ds, q2)
@@ -485,7 +445,7 @@
         if heads * HEAD_SIZE < HEADS_LANES:
             dq.append(jnp.zeros((rows, HEADS_LANES - heads * HEAD_SIZE), f32))
         dq = jnp.concatenate(dq, axis=1).astype(bf16).astype(f32)
-        out_ref[i, :, :HEADS_LANES] = rope_back(dq, cos_ref[i], sin_ref[i])
+        out_ref[i, :, :HEADS_LANES] = rope_back(dq, *spread_table(table_ref[i]))
 
         @pl.when(i == blocks - 1)
         def _():
@@ -493,8 +453,9 @@
             def _(j):
                 kv = jnp.concatenate([dk_scr[j] * att_mult, dv_scr[j]], axis=1)
                 lane = lax.broadcasted_iota(jnp.int32, kv.shape, 1)
+                c, s = spread_table(table_ref[j])
                 out_ref[j, :, HEADS_LANES:] = jnp.where(
-                    lane < HEAD_SIZE, kv * cos_ref[j] - turn(kv) * sin_ref[j], kv
+                    lane < HEAD_SIZE, kv * c - turn(kv) * s, kv
                 ).astype(bf16)
 
     def block(shape):
@@ -512,15 +473,15 @@
             block((rows, heads * HEAD_SIZE)),
             block((HEAD_SIZE, cols)),
             block((1, cols)),
-            whole((blocks, rows, LANES)),
-            whole((blocks, rows, LANES)),
-            block((1, cols)),
+            whole((blocks, HEAD_SIZE, rows)),
+            block((1, rows)),
         ],
         out_specs=whole((blocks, rows, HEADS_LANES + LANES)),
         scratch_shapes=[
             pltpu.VMEM((blocks, rows, HEAD_SIZE), f32),
             pltpu.VMEM((blocks, rows, HEAD_SIZE), f32),
             pltpu.VMEM((cols, HEAD_SIZE), f32),
+            pltpu.VMEM((blocks, rows, LANES), f32),
         ],
     )
     return pl.pallas_call(
@@ -543,9 +504,8 @@
         cot,
         ot,
         lse,
-        cos.reshape(blocks, rows, LANES),
-        sin.reshape(blocks, rows, LANES),
-        start_rows,
+        table,
+        docs[:, None],
     )
 
 
@@ -556,20 +516,16 @@
     own_experts = w_in.shape[0]
 
     def order(chip, k):
-        near = jnp.minimum(chip, chips - 1 - chip)
-        step = (k + 1) // 2
-        both = jnp.where(lax.rem(k, 2) == 1, chip - step, chip + step)
-        return jnp.where(
-            k <= 2 * near, both, jnp.where(chip <= chips - 1 - chip, k, chips - 1 - k)
-        )
+        left = chip < chips - 1 - chip
+        longer = jnp.where(left, chips - 1 - chip, chip)
+        near = jnp.where(left, chip + k, chip - k)
+        return jnp.where(k <= longer, near, jnp.where(left, chips - 1 - k, k))
 
     def kernel(*refs):
         x_in, g_in = refs[0], refs[1 : 1 + chips]
         mask_ref, router_ref, win_in, wout_in = refs[1 + chips : 5 + chips]
-        (lin_out, slot_out, hid_out, n_sum, gate_out, gin_out, gout_out) = refs[
-            5 + chips : 12 + chips
-        ]
-        y_outs = refs[12 + chips : 12 + 2 * chips]
+        (lin_out, slot_out, hid_out, n_sum, gate_out, g_out) = refs[5 + chips : 11 + chips]
+        y_outs = refs[11 + chips : 11 + 2 * chips]
         (
             x_all, g_all, win, wout, y_acc, n_acc, gate_acc, gate_stage,
             n_mine, n_far, n_give, n_theirs, y_mine, y_give, y_theirs, y_pre,
@@ -577,7 +533,7 @@
             local, line_send, line_recv, sib_send, sib_recv, g_local, g_send, g_recv,
             n_send, n_recv, y_send, y_recv, far_send, far_recv, gate_send, gate_recv,
             st_sem, y_sem, ld_sem, w_sem, wg_sem,
-        ) = refs[12 + 2 * chips :]
+        ) = refs[11 + 2 * chips :]
         me = lax.axis_index("seq")
         chip, core = me // 2, lax.rem(me, 2)
         sibling = me + 1 - 2 * core
@@ -602,22 +558,43 @@
                 device_id_type=MESH,
             )
 
-        def own_left():
-            return remote(x_in, x_all.at[me], line_send.at[0], line_recv.at[chip], me - 2)
-
-        def own_right():
-            return remote(x_in, x_all.at[me], line_send.at[1], line_recv.at[chip], me + 2)
-
-        def pass_on(b, k, to):
-            place = x_all.at[2 * b + core]
-            return remote(place, place, line_send.at[1 + k], line_recv.at[b], to)
-
-        def to_sibling(b, k):
-            place = x_all.at[2 * b + core]
-            return remote(place, place, sib_send.at[k], sib_recv.at[b], sibling)
-
-        def own_to_sibling():
-            return remote(x_in, x_all.at[me], sib_send.at[0], sib_recv.at[chip], sibling)
+        half = rows // PIECES
+
+        def piece(b, core_of, i):
+            return x_all.at[2 * b + core_of, pl.ds(i * half, half)]
+
+        def line(src, b, i, slot, to):
+            return remote(
+                src, piece(b, core, i), line_send.at[i, slot], line_recv.at[i, b], to
+            )
+
+        def across(src, b, core_of, i):
+            return remote(
+                src, piece(b, core_of, i), sib_send.at[i, b], sib_recv.at[i, b], sibling
+            )
+
+        def own_piece(i):
+            return x_in.at[pl.ds(i * half, half)]
+
+        def pass_on(b, i, to):
+            return line(piece(b, core, i), b, i, 2 + b, to)
+
+        def to_sibling(b, i):
+            return across(piece(b, core, i), b, core, i)
+
+        def own_sends(act):
+            for i in range(PIECES):
+
+                @pl.when(chip > 0)
+                def _(i=i):
+                    act(line(own_piece(i), chip, i, 0, me - 2))
+
+                @pl.when(chip < chips - 1)
+                def _(i=i):
+                    act(line(own_piece(i), chip, i, 1, me + 2))
+
+            for i in range(PIECES):
+                act(across(own_piece(i), chip, core, i))
 
         def cot_to_sibling(k):
             b = lax.rem(chip + chips - k, chips)
@@ -629,15 +606,7 @@
             b = lax.rem(chip + chips - k, chips)
             return pltpu.make_async_copy(g_in[k], g_all.at[2 * b + core], g_local.at[k])
 
-        @pl.when(chip > 0)
-        def _():
-            own_left().start()
-
-        @pl.when(chip < chips - 1)
-        def _():
-            own_right().start()
-
-        own_to_sibling().start()
+        own_sends(lambda copy: copy.start())
         own = pltpu.make_async_copy(x_in, x_all.at[me], local)
         own.start()
         for k in range(chips):
@@ -771,22 +740,22 @@
         def _(k):
             b = order(chip, k)
 
-            @pl.when(k > 0)
-            def _():
-                pass_on(b, k, sibling).wait_recv()
-                to_sibling(b, k).start()
-
-                @pl.when((b < chip) & (chip < chips - 1))
-                def _():
-                    pass_on(b, k, me + 2).start()
-
-                @pl.when((b > chip) & (chip > 0))
-                def _():
-                    pass_on(b, k, me - 2).start()
-
-            remote(
-                x_in, x_all.at[2 * b + 1 - core], sib_send.at[0], sib_recv.at[b], sibling
-            ).wait_recv()
+            for side in (-1, 1):
+                away = chip + side * k
+
+                for i in range(PIECES):
+
+                    @pl.when((k > 0) & (away >= 0) & (away < chips))
+                    def _(side=side, away=away, i=i):
+                        pass_on(away, i, me).wait_recv()
+                        to_sibling(away, i).start()
+
+                        @pl.when((chip - side >= 0) & (chip - side < chips))
+                        def _():
+                            pass_on(away, i, me - 2 * side).start()
+
+            for i in range(PIECES):
+                across(own_piece(i), b, 1 - core, i).wait_recv()
             remote(
                 x_in, g_all.at[2 * b + 1 - core], g_send.at[0], g_recv.at[b], sibling
             ).wait_recv()
@@ -864,26 +833,20 @@
 
         @pl.loop(1, chips)
         def _(k):
-            b = order(chip, k)
-            to_sibling(b, k).wait_send()
-
-            @pl.when((b < chip) & (chip < chips - 1))
-            def _():
-                pass_on(b, k, me + 2).wait_send()
-
-            @pl.when((b > chip) & (chip > 0))
-            def _():
-                pass_on(b, k, me - 2).wait_send()
-
-        own_to_sibling().wait_send()
-
-        @pl.when(chip > 0)
-        def _():
-            own_left().wait_send()
-
-        @pl.when(chip < chips - 1)
-        def _():
-            own_right().wait_send()
+            for side in (-1, 1):
+                away = chip + side * k
+
+                for i in range(PIECES):
+
+                    @pl.when((away >= 0) & (away < chips))
+                    def _(side=side, away=away, i=i):
+                        to_sibling(away, i).wait_send()
+
+                        @pl.when((chip - side >= 0) & (chip - side < chips))
+                        def _():
+                            pass_on(away, i, me - 2 * side).wait_send()
+
+        own_sends(lambda copy: copy.wait_send())
 
         part_rows = width // parts
         leaving = []
@@ -899,11 +862,11 @@
                     leaving.append(
                         (
                             pltpu.make_async_copy(
-                                x_all.at[i, here], gin_out.at[part, e], wg_sem.at[at]
+                                x_all.at[i, here], g_out.at[part, e, :, pl.ds(0, 2 * FFE)], wg_sem.at[at]
                             ),
                             pltpu.make_async_copy(
                                 g_all.at[i, here, pl.ds(0, FFE)],
-                                gout_out.at[part, e],
+                                g_out.at[part, e, :, pl.ds(2 * FFE, FFE)],
                                 wg_sem.at[at + 1],
                             ),
                         )
@@ -957,12 +920,11 @@
             jax.ShapeDtypeStruct((own_experts, devices, rows, FFE), bf16),
             jax.ShapeDtypeStruct(block, f32),
             jax.ShapeDtypeStruct((devices, 8, rows), f32),
-            jax.ShapeDtypeStruct((parts, own_experts, width // parts, 2 * FFE), bf16),
-            jax.ShapeDtypeStruct((parts, own_experts, width // parts, FFE), bf16),
+            jax.ShapeDtypeStruct((parts, own_experts, width // parts, 3 * FFE), bf16),
         ]
         + [jax.ShapeDtypeStruct(block, bf16)] * chips,
         in_specs=[hbm] * (1 + chips) + [vmem] * 2 + [hbm] * 2,
-        out_specs=[hbm] * 3 + [vmem] * 2 + [hbm] * (2 + chips),
+        out_specs=[hbm] * 3 + [vmem] * 2 + [hbm] * (1 + chips),
         scratch_shapes=[
             pltpu.VMEM((devices,) + block, bf16),
             pltpu.VMEM((devices,) + block, bf16),
@@ -989,10 +951,11 @@
         ]
         + [dma]
         + [
-            dma((count,))
+            dma(count)
             for count in (
-                chips + 1, chips, chips, chips, chips, chips, chips,
-                2, 2, 2, 2, chips, chips, devices, devices,
+                (PIECES, chips + 2), (PIECES, chips), (PIECES, chips), (PIECES, chips),
+                (chips,), (chips,), (chips,), (2,), (2,), (2,), (2,),
+                (chips,), (chips,), (devices,), (devices,),
             )
         ]
         + [
@@ -1062,18 +1025,21 @@
         [w_router, gain_attn[:, None], gain_moe[:, None]], axis=1
     ).astype(bf16)
     misc = jnp.pad(misc, ((0, 0), (0, LANES - experts - 2)))
-    ints = jnp.concatenate([expert_picks[0].T, doc_ids], axis=0)
-    ints = jnp.pad(ints, ((0, 16 - TOP - 1), (0, 0)))
+    mask = jnp.any(
+        expert_picks[0][:, :, None] == jnp.arange(LANES, dtype=jnp.int32), axis=1
+    ).astype(bf16)
+    doc_rows = jnp.broadcast_to(doc_ids, (8, rows))
 
     expert_in_full = lax.all_gather(expert_in.astype(bf16), "dp", axis=1, tiled=True)
     expert_out_full = lax.all_gather(expert_out.astype(bf16), "dp", axis=1, tiled=True)
     w_full = lax.all_gather(w_all, "dp", axis=0, tiled=True)
 
-    tok_all, ints_all, w_own_all, wo_full, misc_full = exchange(
+    tok_all, doc_all, mask_all, w_own_all, wo_full, misc_full = exchange(
         0,
         [
             ("gather", "seq", tokens[0], None),
-            ("gather", "seq", ints, None),
+            ("gather", "seq", doc_rows, None),
+            ("gather", "seq", mask, None),
             ("gather", "dp", w_own, None),
             ("gather", "dp", w_out.astype(bf16), None),
             ("gather", "dp", misc, None),
@@ -1088,18 +1054,13 @@
     w_own_all = w_own_all.reshape(width, w_cols)
     wo_full = wo_full.reshape(width, width)
     misc_full = misc_full.reshape(width, LANES)
-    router_full = jnp.where(jnp.arange(LANES)[None, :] < experts, misc_full, 0)
     gain_a = misc_full[:, experts]
     gain_m = misc_full[:, experts + 1].astype(f32)
-    docs = ints_all[:, TOP].reshape(length)
-    chosen = jnp.any(
-        ints_all[:, :TOP, :, None] == jnp.arange(LANES, dtype=jnp.int32), axis=1
-    ).astype(bf16)
-    start = jnp.sum((docs[:, None] < docs[None, :]).astype(jnp.int32), axis=0)
-    cos, sin = rope_tables(length)
+    docs = doc_all[:, 0]
+    table = rope_table(devices, rows)
 
     normed_a, q_all, kv_all, attended_own, ot, lse = attend_forward(
-        tok_all, w_own_all, gain_a[None], cos, sin, start, heads
+        tok_all, w_own_all, gain_a[None], table, docs, heads
     )
     wide = q_width % LANES == 0
     (attended,) = exchange(
@@ -1112,8 +1073,8 @@
     mid = resid + res_mult * dot_nn(attended, wo_full)
     mid_scale = rms_parts(mid)
     normed_m = (mid * mid_scale * gain_m).astype(bf16)
-    (_, _, _, moe_sum, gate_cot, grads_in, grads_out, *branches) = moe_exchange(
-        2, normed_m, cots, chosen, router_full, expert_in_full, expert_out_full, parts
+    (_, _, _, moe_sum, gate_cot, e_grads, *branches) = moe_exchange(
+        2, normed_m, cots, mask_all, misc_full, expert_in_full, expert_out_full, parts
     )
     branches = [branches[0]] + [
         lax.ppermute(
@@ -1121,23 +1082,19 @@
         )
         for k in range(1, chips)
     ]
-    grads_in = lax.all_to_all(grads_in, "dp", split_axis=0, concat_axis=0)
-    grads_out = lax.all_to_all(grads_out, "dp", split_axis=0, concat_axis=0)
+    e_grads = lax.all_to_all(e_grads, "dp", split_axis=0, concat_axis=0)
     gate_cot = gate_cot[:, :own_experts].reshape(experts, rows)
     logits = lax.dot_general(
-        router_full[:, :experts], normed_m, (((0,), (1,)), ((), ())), preferred_element_type=f32
-    )
-    my_chosen = jnp.any(
-        expert_picks[0].T[:, None, :] == jnp.arange(experts, dtype=jnp.int32)[None, :, None], axis=0
-    )
-    logits = jnp.where(my_chosen, logits, -jnp.inf)
+        misc_full[:, :experts], normed_m, (((0,), (1,)), ((), ())), preferred_element_type=f32
+    )
+    logits = jnp.where(mask[:, :experts].T > 0, logits, -jnp.inf)
     my_gates = jnp.exp(logits - jnp.max(logits, axis=0, keepdims=True))
     my_gates = my_gates / jnp.sum(my_gates, axis=0, keepdims=True)
     pick_cot = my_gates * (gate_cot - jnp.sum(my_gates * gate_cot, axis=0, keepdims=True))
     logit_cot = pick_cot.astype(bf16)
     grad_router = dot_nn(logit_cot, normed_m).T
     normed_m_cot = moe_sum + lax.dot_general(
-        logit_cot, router_full[:, :experts], (((0,), (1,)), ((), ())), preferred_element_type=f32
+        logit_cot, misc_full[:, :experts], (((0,), (1,)), ((), ())), preferred_element_type=f32
     )
     pulled, grad_gain_m = rms_pull(mid, mid_scale, gain_m, normed_m_cot)
     mid_cot = out_grad[0].astype(f32) + pulled
@@ -1149,48 +1106,43 @@
     (heads_cot,) = exchange(
         4, [("swap", "seq", attended_cot, ("in", q_width) if wide else None)]
     )
-    qkv_cot = attend_backward(q_all, kv_all, heads_cot, ot, lse, cos, sin, start, heads)
+    qkv_cot = attend_backward(q_all, kv_all, heads_cot, ot, lse, table, docs, heads)
+    qkv_cot, branches = lax.optimization_barrier((qkv_cot, branches))
     grad_qkv = dot_tn(
         normed_a.reshape(length, width), qkv_cot.reshape(length, w_cols)
     ).astype(bf16)
-    token_pack = jnp.concatenate(
-        [
-            grad_wo,
-            grad_router,
-            grad_gain_m[:, None],
-            jnp.zeros((width, LANES - experts - 1), f32),
-        ],
-        axis=1,
+    router_pack = jnp.concatenate(
+        [grad_router, grad_gain_m[:, None], jnp.zeros((width, LANES - experts - 1), f32)], axis=1
     ).astype(bf16)
-    pack_cols = width + LANES
-    qkv_cot_tok, grad_qkv, token_pack = exchange(
+    qkv_cot_tok, grad_qkv, grad_wo, router_pack = exchange(
         5,
         [
             ("swap", "seq", qkv_cot, ("out", w_cols)),
             ("swap", "dp", grad_qkv.reshape(parts, w_rows, w_cols), None),
-            ("swap", "dp", token_pack.reshape(parts, w_rows, pack_cols), None),
+            ("swap", "dp", grad_wo.astype(bf16).reshape(parts, w_rows, width), None),
+            ("swap", "dp", router_pack.reshape(parts, w_rows, LANES), None),
         ],
     )
     normed_a_cot = dot_nt(qkv_cot_tok, w_full)
     grad_qkv = jnp.sum(grad_qkv.astype(f32), axis=0).astype(bf16)
-    token_pack = jnp.sum(token_pack.astype(f32), axis=0).astype(bf16)
+    grad_wo = jnp.sum(grad_wo.astype(f32), axis=0).astype(bf16)
+    router_pack = jnp.sum(router_pack.astype(f32), axis=0).astype(bf16)
     out_rows = w_rows // devices
-    grad_qkv, token_pack = exchange(
+    grad_qkv, grad_wo, router_pack = exchange(
         6,
         [
             ("swap", "seq", grad_qkv.reshape(devices, out_rows, w_cols), None),
-            ("swap", "seq", token_pack.reshape(devices, out_rows, pack_cols), None),
+            ("swap", "seq", grad_wo.reshape(devices, out_rows, width), None),
+            ("swap", "seq", router_pack.reshape(devices, out_rows, LANES), None),
         ],
     )
-    (grad_qkv, token_pack), branches, grads_in, grads_out = lax.optimization_barrier(
-        ((grad_qkv, token_pack), branches, grads_in, grads_out)
-    )
+    grad_wo, e_grads = lax.optimization_barrier((grad_wo, e_grads))
     branch_sum = branches[0].astype(f32)
     for k in range(1, chips):
         branch_sum = branch_sum + branches[k].astype(f32)
     output = (mid + res_mult * branch_sum).astype(bf16)[None]
-    grad_e_in = jnp.sum(grads_in.astype(f32), axis=0)
-    grad_e_out = jnp.sum(grads_out.astype(f32), axis=0)
+    e_grads = jnp.sum(e_grads.astype(f32), axis=0)
+    grad_e_in, grad_e_out = e_grads[:, :, : 2 * FFE], e_grads[:, :, 2 * FFE :]
     resid_scale = rms_parts(resid)
     weighted = normed_a_cot * gain_a.astype(f32)
     input_grad = (
@@ -1210,10 +1162,10 @@
 
     grad_wk = per_head(grad_qkv[:, :, HEADS_LANES : HEADS_LANES + HEAD_SIZE])
     grad_wv = per_head(grad_qkv[:, :, HEADS_LANES + HEAD_SIZE :])
-    token_pack = jnp.sum(token_pack.astype(f32), axis=0)
-    grad_wo = token_pack[:, :width]
-    grad_router = token_pack[:, width : width + experts]
-    grad_gain_m = token_pack[:, width + experts]
+    grad_wo = jnp.sum(grad_wo.astype(f32), axis=0)
+    router_pack = jnp.sum(router_pack.astype(f32), axis=0)
+    grad_router = router_pack[:, :experts]
+    grad_gain_m = router_pack[:, experts]
 
     def own_rows(weight):
         return lax.dynamic_slice_in_dim(weight, me * out_rows, out_rows, 0).astype(bf16).astype(f32)

time: 464 us -> 392 us (0.84)
  waiting for transfers between devices: 21.2 us -> 0.11 us
  Pallas kernels: 327 us -> 306 us
  other arithmetic: 43.6 us -> 24.2 us
  local copies, waits for them, and re-layouts: 25.2 us -> 17.1 us
    pallas_call x5, Pallas kernels: 213 us -> 177 us  [exchange(): pl.pallas_call(kernel, name=f'exchange{collective_id}', out_shape=out_sha...]
    all_to_all x2 -> x1, waiting for transfers between devices: 21.1 us -> 0.01 us  [on_device(): e_grads = lax.all_to_all(e_grads, 'dp', split_axis=0, concat_axis=0)]
    pallas_call x1, Pallas kernels: 78 us -> 89.9 us  [moe_exchange(): pl.pallas_call(kernel, name='moe_exchange', out_shape=[jax.ShapeDtypeStru...]
    concatenate x2, local copies, waits for them, and re-layouts: 6.3 us -> 0.52 us  [on_device(): jnp.concatenate([grad_router, grad_gain_m[:, None], jnp.zeros((width, LAN...]
    reduce_sum x6, other arithmetic: 11.1 us -> 5.36 us  [the longest x1 4.06 us: on_device(): e_grads = jnp.sum(e_grads.astype(f32), axis=0)]
    all_to_all x2 -> x1, starting transfers between devices: 10.1 us -> 5.35 us  [on_device(): e_grads = lax.all_to_all(e_grads, 'dp', split_axis=0, concat_axis=0)]
    unnamed x89 -> x80, local copies, waits for them, and re-layouts: 12.4 us -> 10.3 us
  transfers between devices with their start and end apart: 11 -> 10, of which waited for: 1 -> 0; matrix products, arithmetic and copies ran while one was open for 12% -> 9% of each run, Pallas kernels for 71% -> 79%
where the time goes in v3:
time: 392 us; the launch traced here: 388 us
  Pallas kernels  306 us (78%)
  other arithmetic  24.2 us (6%)
  local copies, waits for them, and re-layouts  17.1 us (4%)
  between operations  14.6 us (4%)
  matrix products  13.2 us (3%)
  starting transfers between devices  12.4 us (3%)
    pallas_call x5, Pallas kernels, exchange(): pl.pallas_call(kernel, name=f'exchange{collective_id}', out_shape=out_sha...  177 us
    pallas_call x1, Pallas kernels, moe_exchange(): pl.pallas_call(kernel, name='moe_exchange', out_shape=[jax.ShapeDtypeStru...  89.9 us
    pallas_call x1, Pallas kernels, attend_backward(): pl.pallas_call(kernel, name='attend_backward', grid_spec=grid_spec, out_s...  22.1 us
    pallas_call x1, Pallas kernels, attend_forward(): pl.pallas_call(kernel, name='attend_forward', grid_spec=grid_spec, out_sh...  17.8 us
    unnamed x80, local copies, waits for them, and re-layouts  10.3 us
  transfers between devices with their start and end apart: 10, of which 0 were waited for; matrix products, arithmetic and copies ran while one was open for 9% of the time, Pallas kernels for 79%

profile of v3, /device:TPU:13, one launch (start us, length us, event | category | flops | bytes accessed | tf_op | source)
XLA Modules:
  0.0 387.8 jit_solution(15547552653155711966)
XLA Ops:
  7.3 2.2 convert_element_type.146
  14.5 1.7 convert_element_type.139.refs_4_
  16.5 47.4 %exchange0.1 = (bf16[8,256,1024]{2,1,0:T(8,128)(2,1)}, s32[8,8,256]{2,1,0:T(8,128)S(1)}, bf16[8,256,128]{2,1,0:T(8,128)(2,1)S(1)}, bf16[4,256,256]{2,1,0:T(8,128...) custom-call(bf16[256,1024]{1,0:T(8,128)(2,1)S(1)} %bitcast.67, ...), custom_call_target="tpu_custom_call" | custom-call | tf_op jit(solution)/shard_map/exchange0/pallas_call | solution.py:194
  69.3 2.2 copy-done.6
  71.5 17.8 %attend_forward.1 = (bf16[8,256,1024]{2,1,0:T(8,128)(2,1)S(1)}, bf16[8,256,128]{2,1,0:T(8,128)(2,1)S(1)}, bf16[8,256,128]{2,1,0:T(8,128)(2,1)S(1)}, bf16[8,256,1...) custom-call(s32[8]{0:T(128)S(1)} %convert_reduce_fusion.5.first_ref, ...), custom_call_target="tpu_custom_call" | custom-call | flops 3221225472 | bytes 16777216 | tf_op jit(solution)/shard_map/attend_forward/pallas_call | solution.py:372
  89.3 2.1 copy-done.11
  92.1 33.7 %exchange1.1 = bf16[256,1024]{1,0:T(8,128)(2,1)S(1)} custom-call(bf16[8,256,128]{2,1,0:T(8,128)(2,1)S(1)} %get-tuple-element.51.refs_0_), custom_call_target="tpu_custom_call" | custom-call | tf_op jit(solution)/shard_map/exchange1/pallas_call | solution.py:194
  125.9 1.7 multiply_reduce_fusion.2
  127.7 1.4 multiply_convert_fusion.1.refs_0_
  129.9 89.9 %moe_exchange.1 = (bf16[2,8,256,1024]{3,2,1,0:T(8,128)(2,1)}, bf16[2,8,256,1024]{3,2,1,0:T(8,128)(2,1)}, bf16[2,8,256,512]{3,2,1,0:T(8,128)(2,1)}, f32[256,1024]...) custom-call(bf16[256,1024]{1,0:T(8,128)(2,1)} %copy-done.28, ...), custom_call_target="tpu_custom_call" | custom-call | flops 38654705664 | bytes 41943040 | tf_op jit(solution)/shard_map/moe_exchange/pallas_call | solution.py:914
  220.9 4.5 %collective-permute-start.4 = (bf16[256,1024]{1,0:T(8,128)(2,1)}, bf16[256,1024]{1,0:T(8,128)(2,1)}, u32[]{:S(2)}, u32[]{:S(2)}) collective-permute-start(bf16[256,1024]{1,0:T(8,128)(2,1)} %get-tuple-element.63), channel_id=1, source_target_pairs={{0,4},{1,5},{2,6},{3,7},{4,0},{5,1},{6,2},{7,3},{8,12},{9,13},{10,... | collective-permute-start | bytes 1572872 | tf_op jit(solution)/shard_map/ppermute | solution.py:1080
  225.7 3.0 multiply_reduce_fusion
  229.6 5.4 %all-to-all-start = ((bf16[4,2,256,1536]{3,2,1,0:T(8,128)(2,1)}), bf16[4,2,256,1536]{3,2,1,0:T(8,128)(2,1)}, u32[]{:S(2)}, u32[]{:S(2)}) async-start(bf16[4,2,256,1536]{3,2,1,0:T(8,128)(2,1)} %get-tuple-element.77), calls=%async_computation | async-start | bytes 12582912 | tf_op jit(solution)/shard_map/all_to_all | solution.py:1085
  235.0 2.2 subtract_add_fusion
  238.2 2.1 convolution_convert_fusion
  240.4 42.1 %exchange4.1.do_ref = bf16[8,256,128]{2,1,0:T(8,128)(2,1)S(1)} custom-call(bf16[256,1024]{1,0:T(8,128)(2,1)S(1)} %convolution_convert_fusion.1.refs_0_), custom_call_target="tpu_custom_call" | custom-call | tf_op jit(solution)/shard_map/exchange4/pallas_call | solution.py:194
  282.6 22.1 %attend_backward.1.refs_0_ = bf16[8,256,256]{2,1,0:T(8,128)(2,1)S(1)} custom-call(s32[8]{0:T(128)S(1)} %convert_reduce_fusion.5.first_ref, bf16[8,256,128]{2,1,0:T(8,128)(2,1)S(1)} %copy-done.16, bf16[8,256,128]{2,1,0:T(8,128)(2,1)S(1)} %copy-done.18, bf16[8,256,128]{2,1,0:T(8,128)(2,1)S(1)} %exchange4.1.do_ref, f32[8,64,512]{2,1,0:T(8,128)S(1)} %copy-done.14, ...), custom_call_target="tpu_custom_call" | custom-call | flops 5368709120 | bytes 4194304 | tf_op jit(solution)/shard_map/attend_backward/pallas_call | solution.py:487
  306.1 34.4 %exchange5.1 = (bf16[256,2048]{1,0:T(8,128)(2,1)S(1)}, bf16[4,256,256]{2,1,0:T(8,128)(2,1)S(1)}, bf16[4,256,1024]{2,1,0:T(8,128)(2,1)S(1)}, bf16[4,256,128]{2,1,0:T(8,128)(2,1)S(1)}) custom-call(bf16[8,256,256]{2,1,0:T(8,128)(2,1)S(1)} %attend_backward.1.refs_0_, bf16[4,256,256]{2,1,0:T(8,128)(2,1)S(1)} %bitcast.69, bf16[4,256,1024]{2,1,0:T(8,128)(2,1)} %bitcast.73, ...), custom_call_target="tpu_custom_call" | custom-call | tf_op jit(solution)/shard_map/exchange5/pallas_call | solution.py:194
  342.0 18.9 %exchange6.1 = (bf16[8,32,256]{2,1,0:T(8,128)(2,1)S(1)}, bf16[8,32,1024]{2,1,0:T(8,128)(2,1)S(1)}, bf16[8,32,128]{2,1,0:T(8,128)(2,1)S(1)}) custom-call(bf16[8,32,256]{2,1,0:T(8,128)(2,1)S(1)} %bitcast.70, bf16[8,32,1024]{2,1,0:T(8,128)(2,1)S(1)} %bitcast.68, bf16[8,32,128]{2,1,0:T(8,128)(2,1)S(1)} %bitcast.71), custom_call_target="tpu_custom_call" | custom-call | tf_op jit(solution)/shard_map/exchange6/pallas_call | solution.py:194
  363.8 1.7 multiply_reduce_fusion.3
  366.1 3.7 fusion.1
  371.4 2.6 fusion.7
  374.0 4.1 %convert_reduce_fusion = f32[2,256,1536]{2,1,0:T(8,128)S(1)} fusion(bf16[4,2,256,1536]{3,2,1,0:T(8,128)(2,1)} %all-to-all-done), kind=kLoop, calls=%fused_computation | loop fusion | flops 5505024 | bytes 9437184 | tf_op jit(solution)/shard_map/reduce_sum | solution.py:1144
  378.0 1.5 slice.74
  (156 shorter events, 25.0 us)
Async XLA Ops:
  7.2 122.5 %all-gather.6.cloned.1.call-start = ((), (), s32[]{:S(2)}) async-start(), calls=%async_computation.2 | async-start | bytes 2621440 | tf_op jit(solution)/shard_map/all_gather | solution.py:1034
  9.5 120.2 %all-gather.4.cloned.1.call-start = ((), (), s32[]{:S(2)}) async-start(), calls=%async_computation.1 | async-start | bytes 5242880 | tf_op jit(solution)/shard_map/all_gather | solution.py:1033
  10.8 355.4 %all-gather.8.cloned.1.call-start = ((), (), s32[]{:S(2)}) async-start(), calls=%async_computation.3 | async-start | bytes 5242880 | tf_op jit(solution)/shard_map/all_gather | solution.py:1035
  14.5 54.8 %copy-start.10 = (f32[8,64,256]{2,1,0:T(8,128)S(1)}, f32[8,64,256]{2,1,0:T(8,128)}, u32[]{:S(2)}) copy-start(f32[8,64,256]{2,1,0:T(8,128)} %constant.38.clone.table_ref) | copy-start | bytes 1572868
  66.0 63.1 %copy-start = (bf16[4,256,128]{2,1,0:T(8,128)(2,1)}, bf16[4,256,128]{2,1,0:T(8,128)(2,1)S(1)}, u32[]{:S(2)}) copy-start(bf16[4,256,128]{2,1,0:T(8,128)(2,1)S(1)} %get-tuple-element.50) | copy-start | bytes 786436
  66.0 63.7 %collective-permute-start = (bf16[256,1024]{1,0:T(8,128)(2,1)}, bf16[256,1024]{1,0:T(8,128)(2,1)}, u32[]{:S(2)}, u32[]{:S(2)}) collective-permute-start(bf16[256,1024]{1,0:T(8,128)(2,1)} %bitcast.81), channel_id=1, source_target_pairs={{0,2},{1,3},{2,4},{3,5},{4,6},{5,7},{6,0},{7,1},{8,10},{9,11},{10,... | collective-permute-start | bytes 1572872 | tf_op jit(solution)/shard_map/ppermute | solution.py:1051
  67.2 62.5 %collective-permute-start.1 = (bf16[256,1024]{1,0:T(8,128)(2,1)}, bf16[256,1024]{1,0:T(8,128)(2,1)}, u32[]{:S(2)}, u32[]{:S(2)}) collective-permute-start(bf16[256,1024]{1,0:T(8,128)(2,1)} %bitcast.82), channel_id=1, source_target_pairs={{0,4},{1,5},{2,6},{3,7},{4,0},{5,1},{6,2},{7,3},{8,12},{9,13},{10,... | collective-permute-start | bytes 1572872 | tf_op jit(solution)/shard_map/ppermute | solution.py:1051
  68.3 61.4 %collective-permute-start.2 = (bf16[256,1024]{1,0:T(8,128)(2,1)}, bf16[256,1024]{1,0:T(8,128)(2,1)}, u32[]{:S(2)}, u32[]{:S(2)}) collective-permute-start(bf16[256,1024]{1,0:T(8,128)(2,1)} %bitcast.83), channel_id=1, source_target_pairs={{0,6},{1,7},{2,0},{3,1},{4,2},{5,3},{6,4},{7,5},{8,14},{9,15},{10,... | collective-permute-start | bytes 1572872 | tf_op jit(solution)/shard_map/ppermute | solution.py:1051
  71.5 54.4 %copy-start.3 = (bf16[4,256,1024]{2,1,0:T(8,128)(2,1)S(1)}, bf16[4,256,1024]{2,1,0:T(8,128)(2,1)}, u32[]{:S(2)}) copy-start(bf16[4,256,1024]{2,1,0:T(8,128)(2,1)} %copy-done.2) | copy-start | bytes 6291460
  92.1 35.5 %copy-start.13 = (f32[8,64,512]{2,1,0:T(8,128)}, f32[8,64,512]{2,1,0:T(8,128)S(1)}, u32[]{:S(2)}) copy-start(f32[8,64,512]{2,1,0:T(8,128)S(1)} %get-tuple-element.59.ot_ref) | copy-start | bytes 3145732
  92.1 37.0 %copy-start.15 = (bf16[8,256,128]{2,1,0:T(8,128)(2,1)}, bf16[8,256,128]{2,1,0:T(8,128)(2,1)S(1)}, u32[]{:S(2)}) copy-start(bf16[8,256,128]{2,1,0:T(8,128)(2,1)S(1)} %get-tuple-element.53.q_ref) | copy-start | bytes 1572868
  129.9 95.7 %copy-start.1 = (bf16[4,256,128]{2,1,0:T(8,128)(2,1)S(1)}, bf16[4,256,128]{2,1,0:T(8,128)(2,1)}, u32[]{:S(2)}) copy-start(bf16[4,256,128]{2,1,0:T(8,128)(2,1)} %copy-done) | copy-start | bytes 786436
  219.8 9.3 %copy-start.29 = (bf16[256,1024]{1,0:T(8,128)(2,1)S(1)}, bf16[256,1024]{1,0:T(8,128)(2,1)}, u32[]{:S(2)}) copy-start(bf16[256,1024]{1,0:T(8,128)(2,1)} %copy-done.28) | copy-start | bytes 1572868
  220.8 83.9 %collective-permute-start.3 = (bf16[256,1024]{1,0:T(8,128)(2,1)}, bf16[256,1024]{1,0:T(8,128)(2,1)}, u32[]{:S(2)}, u32[]{:S(2)}) collective-permute-start(bf16[256,1024]{1,0:T(8,128)(2,1)} %get-tuple-element.62), channel_id=1, source_target_pairs={{0,2},{1,3},{2,4},{3,5},{4,6},{5,7},{6,0},{7,1},{8,10},{9,11},{10,... | collective-permute-start | bytes 1572872 | tf_op jit(solution)/shard_map/ppermute | solution.py:1080
  220.9 83.9 %collective-permute-start.4 = (bf16[256,1024]{1,0:T(8,128)(2,1)}, bf16[256,1024]{1,0:T(8,128)(2,1)}, u32[]{:S(2)}, u32[]{:S(2)}) collective-permute-start(bf16[256,1024]{1,0:T(8,128)(2,1)} %get-tuple-element.63), channel_id=1, source_target_pairs={{0,4},{1,5},{2,6},{3,7},{4,0},{5,1},{6,2},{7,3},{8,12},{9,13},{10,... | collective-permute-start | bytes 1572872 | tf_op jit(solution)/shard_map/ppermute | solution.py:1080
  225.4 79.4 %collective-permute-start.5 = (bf16[256,1024]{1,0:T(8,128)(2,1)}, bf16[256,1024]{1,0:T(8,128)(2,1)}, u32[]{:S(2)}, u32[]{:S(2)}) collective-permute-start(bf16[256,1024]{1,0:T(8,128)(2,1)} %get-tuple-element.64), channel_id=1, source_target_pairs={{0,6},{1,7},{2,0},{3,1},{4,2},{5,3},{6,4},{7,5},{8,14},{9,15},{10,... | collective-permute-start | bytes 1572872 | tf_op jit(solution)/shard_map/ppermute | solution.py:1080
  229.6 144.3 %all-to-all-start = ((bf16[4,2,256,1536]{3,2,1,0:T(8,128)(2,1)}), bf16[4,2,256,1536]{3,2,1,0:T(8,128)(2,1)}, u32[]{:S(2)}, u32[]{:S(2)}) async-start(bf16[4,2,256,1536]{3,2,1,0:T(8,128)(2,1)} %get-tuple-element.77), calls=%async_computation | async-start | bytes 12582912 | tf_op jit(solution)/shard_map/all_to_all | solution.py:1085
  238.2 44.4 %copy-start.14 = (f32[8,64,512]{2,1,0:T(8,128)S(1)}, f32[8,64,512]{2,1,0:T(8,128)}, u32[]{:S(2)}) copy-start(f32[8,64,512]{2,1,0:T(8,128)} %copy-done.13) | copy-start | bytes 3145732
  238.2 44.4 %copy-start.16 = (bf16[8,256,128]{2,1,0:T(8,128)(2,1)S(1)}, bf16[8,256,128]{2,1,0:T(8,128)(2,1)}, u32[]{:S(2)}) copy-start(bf16[8,256,128]{2,1,0:T(8,128)(2,1)} %copy-done.15) | copy-start | bytes 1572868
  238.2 44.4 %copy-start.18 = (bf16[8,256,128]{2,1,0:T(8,128)(2,1)S(1)}, bf16[8,256,128]{2,1,0:T(8,128)(2,1)}, u32[]{:S(2)}) copy-start(bf16[8,256,128]{2,1,0:T(8,128)(2,1)} %copy-done.17) | copy-start | bytes 1572868
  282.6 22.2 %copy-start.12 = (bf16[8,256,1024]{2,1,0:T(8,128)(2,1)S(1)}, bf16[8,256,1024]{2,1,0:T(8,128)(2,1)}, u32[]{:S(2)}) copy-start(bf16[8,256,1024]{2,1,0:T(8,128)(2,1)} %copy-done.11) | copy-start | bytes 12582916
  342.0 24.2 %copy-start.8 = (bf16[256,2048]{1,0:T(8,128)(2,1)S(1)}, bf16[256,2048]{1,0:T(8,128)(2,1)}, u32[]{:S(2)}) copy-start(bf16[256,2048]{1,0:T(8,128)(2,1)} %copy-done.7) | copy-start | bytes 3145732
  361.3 8.5 %copy-start.30 = (f32[32,512]{1,0:T(8,128)}, f32[32,512]{1,0:T(8,128)S(1)}, u32[]{:S(2)}) copy-start(f32[32,512]{1,0:T(8,128)S(1)} %reshape.154) | copy-start | bytes 196612
  361.5 8.3 %copy-start.31 = (f32[32,512]{1,0:T(8,128)}, f32[32,512]{1,0:T(8,128)S(1)}, u32[]{:S(2)}) copy-start(f32[32,512]{1,0:T(8,128)S(1)} %reshape.155) | copy-start | bytes 196612
  (23 other events, 53.5 us)
Sparse Core Ops, SparseCore 0:
  9.9 59.6 all-gather.5
  71.4 51.8 all-gather.3
  125.1 52.7 all-gather.7

commit v4 on v3

--- a/solution.py
+++ b/solution.py
@@ -27,7 +27,9 @@
         out_spec = pl.BlockSpec(memory_space=pl.ANY)
         extra = []
         lead = (PIECES,) if kind == "gather" and axis == "seq" else ()
-        if kind == "gather":
+        if kind == "share":
+            shape, dtype, copies = (count,) + x.shape, x.dtype, 2 * (count - 1)
+        elif kind == "gather":
             shape, dtype = (count,) + x.shape, x.dtype
             copies = count - 1 if axis == "dp" else 3 + 4 * (count // 2 - 1)
         elif kind == "swap":
@@ -118,6 +120,57 @@
                             axis, x, o.at[frm], send.at[k - 1], recv.at[k - 1], to
                         ).wait_recv
                     )
+            elif kind == "share":
+                seq, half = me["seq"], x.shape[0] // 2
+                core = lax.rem(seq, 2)
+                sibling = seq + 1 - 2 * core
+                own = pltpu.make_async_copy(x, o.at[my], local)
+                own.start()
+                third.append(own.wait)
+
+                def side_of(ref, which, half=half):
+                    return ref.at[pl.ds(which * half, half)]
+
+                def relay(k, axis=axis, x=x, o=o, send=send, recv=recv, count=count, my=my, core=core, sibling=sibling, side_of=side_of):
+                    to = lax.rem(my + k, count)
+                    frm = lax.rem(my + count - k, count)
+                    remote(
+                        axis,
+                        side_of(x, core),
+                        side_of(o.at[frm], core),
+                        send.at[k - 1],
+                        recv.at[k - 1],
+                        to,
+                    ).wait_recv()
+                    slot = count - 2 + k
+                    spot = side_of(o.at[frm], core)
+                    over = remote("seq", spot, spot, send.at[slot], recv.at[slot], sibling)
+                    over.start()
+                    third.append(over.wait_send)
+                    third.append(
+                        remote(
+                            "seq",
+                            spot,
+                            side_of(o.at[frm], 1 - core),
+                            send.at[slot],
+                            recv.at[slot],
+                            sibling,
+                        ).wait_recv
+                    )
+
+                for k in range(1, count):
+                    to = lax.rem(my + k, count)
+                    copy = remote(
+                        axis,
+                        side_of(x, core),
+                        side_of(o.at[my], core),
+                        send.at[k - 1],
+                        recv.at[k - 1],
+                        to,
+                    )
+                    copy.start()
+                    third.append(copy.wait_send)
+                    second.append((k + 0.75, functools.partial(relay, k)))
             elif kind == "gather":
                 chips = count // 2
                 chip, core = my // 2, lax.rem(my, 2)
@@ -974,6 +1027,243 @@
     )(normed, *cots, mask, router, w_in, w_out)
 
 
+def final_exchange(
+    collective_id, qkv_cot, grad_qkv, token_grads, w_full, tokens, mid_cot, gain, mid, branches
+):
+    devices, parts = lax.axis_size("seq"), lax.axis_size("dp")
+    chips = devices // 2
+    _, rows, cols = qkv_cot.shape
+    width = tokens.shape[1]
+    out_rows = grad_qkv.shape[2]
+    count = len(token_grads)
+    wides = [x.shape[3] for x in token_grads]
+    token_grads = [x.reshape(parts, chips, 2, out_rows, x.shape[3]) for x in token_grads]
+
+    def kernel(*refs):
+        qkv_in, gq_in = refs[:2]
+        gt_in = refs[2 : 2 + count]
+        w_in, tok_ref, mid_cot_ref, gain_ref, mid_ref = refs[2 + count : 7 + count]
+        y_refs = refs[7 + count : 7 + count + chips]
+        refs = refs[7 + count + chips :]
+        in_grad, output, gq_out = refs[:3]
+        gt_out = refs[3 : 3 + count]
+        refs = refs[3 + count :]
+        (
+            qkv_tok, w_all, nac, gq_recv, gq_sum,
+            q_send, q_recv, local, w_sem, gq_send, gq_rsem, gqz_send, gqz_recv, gq_local,
+        ) = refs[:14]
+        work = [refs[14 + 11 * i : 25 + 11 * i] for i in range(count)]
+        me, my = lax.axis_index("seq"), lax.axis_index("dp")
+        chip, core = me // 2, lax.rem(me, 2)
+        sibling = me + 1 - 2 * core
+        w_copy = pltpu.make_async_copy(w_in, w_all, w_sem)
+        w_copy.start()
+        barrier = pltpu.get_barrier_semaphore()
+        for axis, index, size in (("seq", me, devices), ("dp", my, parts)):
+            for k in range(1, size):
+                pl.semaphore_signal(
+                    barrier,
+                    inc=1,
+                    device_id={axis: lax.rem(index + k, size)},
+                    device_id_type=MESH,
+                )
+        pl.semaphore_wait(barrier, devices + parts - 2)
+
+        def remote(axis, src, dst, send, recv, to):
+            return pltpu.make_async_remote_copy(
+                src_ref=src,
+                dst_ref=dst,
+                send_sem=send,
+                recv_sem=recv,
+                device_id={axis: to},
+                device_id_type=MESH,
+            )
+
+        sent = []
+
+        def columns(j):
+            return qkv_tok.at[:, pl.ds(pl.multiple_of(j * cols, cols), cols)]
+
+        for x, w in zip(gt_in, work):
+            mine, theirs, far, near, last, sems, dp_send, dp_recv, z_send, z_recv, _ = w
+            copy = remote(
+                "seq", x.at[:, :, 1 - core], theirs, sems.at[0], sems.at[1], sibling
+            )
+            copy.start()
+            sent.append(copy)
+            pltpu.make_async_copy(x.at[:, :, core], mine, sems.at[2]).start()
+        for k in range(1, parts):
+            to = lax.rem(my + k, parts)
+            copy = remote(
+                "dp", gq_in.at[to], gq_recv.at[my], gq_send.at[k - 1], gq_rsem.at[k - 1], to
+            )
+            copy.start()
+            sent.append(copy)
+        own_q = pltpu.make_async_copy(gq_in.at[my], gq_recv.at[my], gq_local)
+        own_q.start()
+        own = pltpu.make_async_copy(qkv_in.at[me], columns(me), local)
+        own.start()
+        for k in range(1, devices):
+            to = lax.rem(me + k, devices)
+            copy = remote(
+                "seq", qkv_in.at[to], columns(me), q_send.at[k - 1], q_recv.at[k - 1], to
+            )
+            copy.start()
+            sent.append(copy)
+
+        for x, w in zip(gt_in, work):
+            mine, theirs, far, near, last, sems, dp_send, dp_recv, z_send, z_recv, _ = w
+            remote("seq", x.at[:, :, core], theirs, sems.at[0], sems.at[1], sibling).wait_recv()
+            pltpu.make_async_copy(x.at[:, :, core], mine, sems.at[2]).wait()
+            mine[...] = (mine[...].astype(f32) + theirs[...].astype(f32)).astype(bf16)
+            for k in range(1, parts):
+                to = lax.rem(my + k, parts)
+                copy = remote(
+                    "dp", mine.at[to], far.at[k - 1], dp_send.at[k - 1], dp_recv.at[k - 1], to
+                )
+                copy.start()
+                sent.append(copy)
+
+        total = y_refs[0][...].astype(f32)
+        for k in range(1, chips):
+            total = total + y_refs[k][...].astype(f32)
+        output[...] = (mid_ref[...] + res_mult * total).astype(bf16)
+
+        own_q.wait()
+        for k in range(1, parts):
+            frm = lax.rem(my + parts - k, parts)
+            remote(
+                "dp", gq_in.at[frm], gq_recv.at[frm], gq_send.at[k - 1], gq_rsem.at[k - 1], frm
+            ).wait_recv()
+        summed = gq_recv[0].astype(f32)
+        for p in range(1, parts):
+            summed = summed + gq_recv[p].astype(f32)
+        gq_sum[...] = summed.astype(bf16)
+        own_z = pltpu.make_async_copy(gq_sum.at[me], gq_out.at[me], gq_local)
+        own_z.start()
+        for k in range(1, devices):
+            to = lax.rem(me + k, devices)
+            copy = remote(
+                "seq", gq_sum.at[to], gq_out.at[me], gqz_send.at[k - 1], gqz_recv.at[k - 1], to
+            )
+            copy.start()
+            sent.append(copy)
+        for w in work:
+            mine, theirs, far, near, last, sems, dp_send, dp_recv, z_send, z_recv, _ = w
+            summed = mine[my].astype(f32)
+            for k in range(1, parts):
+                remote(
+                    "dp", mine.at[0], far.at[k - 1], dp_send.at[k - 1], dp_recv.at[k - 1], my
+                ).wait_recv()
+                summed = summed + far[k - 1].astype(f32)
+            near[...] = summed.astype(bf16)
+            for k in range(1, chips):
+                to = lax.rem(chip + k, chips)
+                copy = remote(
+                    "seq",
+                    near.at[to],
+                    last.at[k - 1],
+                    z_send.at[k - 1],
+                    z_recv.at[k - 1],
+                    2 * to + core,
+                )
+                copy.start()
+                sent.append(copy)
+
+        own.wait()
+        w_copy.wait()
+        for k in range(1, devices):
+            frm = lax.rem(me + devices - k, devices)
+            remote(
+                "seq", qkv_in.at[frm], columns(frm), q_send.at[k - 1], q_recv.at[k - 1], frm
+            ).wait_recv()
+
+        @pl.loop(0, width // 256)
+        def _(j):
+            at = pl.multiple_of(j * 256, 256)
+            nac[:, pl.ds(at, 256)] = dot_nt(qkv_tok[...], w_all[pl.ds(at, 256), :])
+
+        resid = tok_ref[...].astype(f32)
+        scale = lax.rsqrt(jnp.mean(resid * resid, axis=-1, keepdims=True) + norm_eps)
+        weighted = nac[...] * gain_ref[...].astype(f32)
+        in_grad[...] = (
+            mid_cot_ref[...]
+            + scale * weighted
+            - resid
+            * (scale * scale * scale)
+            * jnp.mean(weighted * resid, axis=-1, keepdims=True)
+        ).astype(bf16)
+
+        for o, w in zip(gt_out, work):
+            mine, theirs, far, near, last, sems, dp_send, dp_recv, z_send, z_recv, _ = w
+            summed = near[chip].astype(f32)
+            for k in range(1, chips):
+                remote(
+                    "seq", near.at[0], last.at[k - 1], z_send.at[k - 1], z_recv.at[k - 1], me
+                ).wait_recv()
+                summed = summed + last[k - 1].astype(f32)
+            o[...] = summed
+        own_z.wait()
+        for k in range(1, devices):
+            frm = lax.rem(me + devices - k, devices)
+            remote(
+                "seq", gq_sum.at[frm], gq_out.at[frm], gqz_send.at[k - 1], gqz_recv.at[k - 1], frm
+            ).wait_recv()
+        for copy in sent:
+            copy.wait_send()
+
+    hbm = pl.BlockSpec(memory_space=pl.ANY)
+    vmem = pl.BlockSpec(memory_space=pltpu.VMEM)
+    dma = pltpu.SemaphoreType.DMA
+    scratch = [
+        pltpu.VMEM((rows, devices * cols), bf16),
+        pltpu.VMEM(w_full.shape, bf16),
+        pltpu.VMEM((rows, width), f32),
+        pltpu.VMEM(grad_qkv.shape, bf16),
+        pltpu.VMEM(grad_qkv.shape[1:], bf16),
+        dma((devices - 1,)),
+        dma((devices - 1,)),
+        dma,
+        dma,
+        dma((parts - 1,)),
+        dma((parts - 1,)),
+        dma((devices - 1,)),
+        dma((devices - 1,)),
+        dma,
+    ]
+    for wide in wides:
+        piece = (out_rows, wide)
+        scratch += [
+            pltpu.VMEM((parts, chips) + piece, bf16),
+            pltpu.VMEM((parts, chips) + piece, bf16),
+            pltpu.VMEM((parts - 1, chips) + piece, bf16),
+            pltpu.VMEM((chips,) + piece, bf16),
+            pltpu.VMEM((chips - 1,) + piece, bf16),
+            dma((3,)),
+            dma((parts - 1,)),
+            dma((parts - 1,)),
+            dma((chips - 1,)),
+            dma((chips - 1,)),
+            dma,
+        ]
+    return pl.pallas_call(
+        kernel,
+        name="final_exchange",
+        out_shape=[
+            jax.ShapeDtypeStruct((rows, width), bf16),
+            jax.ShapeDtypeStruct((rows, width), bf16),
+            jax.ShapeDtypeStruct(grad_qkv.shape[1:], bf16),
+        ]
+        + [jax.ShapeDtypeStruct((out_rows, wide), f32) for wide in wides],
+        in_specs=[hbm] * (3 + count) + [vmem] * (4 + chips),
+        out_specs=[vmem] * (3 + count),
+        scratch_shapes=scratch,
+        compiler_params=pltpu.CompilerParams(
+            collective_id=collective_id, has_side_effects=True, vmem_limit_bytes=48 << 20
+        ),
+    )(qkv_cot, grad_qkv, *token_grads, w_full, tokens, mid_cot, gain, mid, *branches)
+
+
 def rms_parts(values):
     return lax.rsqrt(jnp.mean(values * values, axis=-1, keepdims=True) + norm_eps)
 
@@ -1034,6 +1324,13 @@
     expert_out_full = lax.all_gather(expert_out.astype(bf16), "dp", axis=1, tiled=True)
     w_full = lax.all_gather(w_all, "dp", axis=0, tiled=True)
 
+    chips = devices // 2
+
+    def shift(x, k):
+        return lax.ppermute(x, "seq", [(i, (i + 2 * k) % devices) for i in range(devices)])
+
+    held = out_grad[0]
+    early = shift(held, 1)
     tok_all, doc_all, mask_all, w_own_all, wo_full, misc_full = exchange(
         0,
         [
@@ -1041,16 +1338,12 @@
             ("gather", "seq", doc_rows, None),
             ("gather", "seq", mask, None),
             ("gather", "dp", w_own, None),
-            ("gather", "dp", w_out.astype(bf16), None),
-            ("gather", "dp", misc, None),
+            ("share", "dp", w_out.astype(bf16), None),
+            ("share", "dp", misc, None),
         ],
     )
-    held, tok_all = lax.optimization_barrier((out_grad[0], tok_all))
-    chips = devices // 2
-    cots = [held] + [
-        lax.ppermute(held, "seq", [(i, (i + 2 * k) % devices) for i in range(devices)])
-        for k in range(1, chips)
-    ]
+    tok_all, held, early = lax.optimization_barrier((tok_all, held, early))
+    cots = [held, early] + [shift(held, k) for k in range(2, chips)]
     w_own_all = w_own_all.reshape(width, w_cols)
     wo_full = wo_full.reshape(width, width)
     misc_full = misc_full.reshape(width, LANES)
@@ -1076,12 +1369,8 @@
     (_, _, _, moe_sum, gate_cot, e_grads, *branches) = moe_exchange(
         2, normed_m, cots, mask_all, misc_full, expert_in_full, expert_out_full, parts
     )
-    branches = [branches[0]] + [
-        lax.ppermute(
-            branches[k], "seq", [(i, (i + 2 * k) % devices) for i in range(devices)]
-        )
-        for k in range(1, chips)
-    ]
+    middle = chips // 2
+    branches[middle] = shift(branches[middle], middle)
     e_grads = lax.all_to_all(e_grads, "dp", split_axis=0, concat_axis=0)
     gate_cot = gate_cot[:, :own_experts].reshape(experts, rows)
     logits = lax.dot_general(
@@ -1106,6 +1395,10 @@
     (heads_cot,) = exchange(
         4, [("swap", "seq", attended_cot, ("in", q_width) if wide else None)]
     )
+    others = [k for k in range(1, chips) if k != middle]
+    heads_cot, later = lax.optimization_barrier((heads_cot, [branches[k] for k in others]))
+    for k, branch in zip(others, later):
+        branches[k] = shift(branch, k)
     qkv_cot = attend_backward(q_all, kv_all, heads_cot, ot, lse, table, docs, heads)
     qkv_cot, branches = lax.optimization_barrier((qkv_cot, branches))
     grad_qkv = dot_tn(
@@ -1114,44 +1407,25 @@
     router_pack = jnp.concatenate(
         [grad_router, grad_gain_m[:, None], jnp.zeros((width, LANES - experts - 1), f32)], axis=1
     ).astype(bf16)
-    qkv_cot_tok, grad_qkv, grad_wo, router_pack = exchange(
+    out_rows = w_rows // devices
+    input_grad, output, grad_qkv, grad_wo, router_pack = final_exchange(
         5,
+        qkv_cot,
+        grad_qkv.reshape(parts, devices, out_rows, w_cols),
         [
-            ("swap", "seq", qkv_cot, ("out", w_cols)),
-            ("swap", "dp", grad_qkv.reshape(parts, w_rows, w_cols), None),
-            ("swap", "dp", grad_wo.astype(bf16).reshape(parts, w_rows, width), None),
-            ("swap", "dp", router_pack.reshape(parts, w_rows, LANES), None),
+            grad_wo.astype(bf16).reshape(parts, devices, out_rows, width),
+            router_pack.reshape(parts, devices, out_rows, LANES),
         ],
-    )
-    normed_a_cot = dot_nt(qkv_cot_tok, w_full)
-    grad_qkv = jnp.sum(grad_qkv.astype(f32), axis=0).astype(bf16)
-    grad_wo = jnp.sum(grad_wo.astype(f32), axis=0).astype(bf16)
-    router_pack = jnp.sum(router_pack.astype(f32), axis=0).astype(bf16)
-    out_rows = w_rows // devices
-    grad_qkv, grad_wo, router_pack = exchange(
-        6,
-        [
-            ("swap", "seq", grad_qkv.reshape(devices, out_rows, w_cols), None),
-            ("swap", "seq", grad_wo.reshape(devices, out_rows, width), None),
-            ("swap", "seq", router_pack.reshape(devices, out_rows, LANES), None),
-        ],
-    )
-    grad_wo, e_grads = lax.optimization_barrier((grad_wo, e_grads))
-    branch_sum = branches[0].astype(f32)
-    for k in range(1, chips):
-        branch_sum = branch_sum + branches[k].astype(f32)
-    output = (mid + res_mult * branch_sum).astype(bf16)[None]
-    e_grads = jnp.sum(e_grads.astype(f32), axis=0)
-    grad_e_in, grad_e_out = e_grads[:, :, : 2 * FFE], e_grads[:, :, 2 * FFE :]
-    resid_scale = rms_parts(resid)
-    weighted = normed_a_cot * gain_a.astype(f32)
-    input_grad = (
-        mid_cot
-        + resid_scale * weighted
-        - resid
-        * (resid_scale * resid_scale * resid_scale)
-        * jnp.mean(weighted * resid, axis=-1, keepdims=True)
-    ).astype(bf16)[None]
+        w_full,
+        tokens[0],
+        mid_cot,
+        gain_a[None],
+        mid,
+        branches,
+    )
+    input_grad, output = input_grad[None], output[None]
+    grad_e_in = jnp.sum(e_grads[..., : 2 * FFE].astype(f32), axis=0)
+    grad_e_out = jnp.sum(e_grads[..., 2 * FFE :].astype(f32), axis=0)
 
     grad_qkv = grad_qkv.astype(f32)
     grad_wq = grad_qkv[:, :, :q_width].transpose(1, 0, 2).reshape(out_rows, devices * q_width)
@@ -1162,8 +1436,6 @@
 
     grad_wk = per_head(grad_qkv[:, :, HEADS_LANES : HEADS_LANES + HEAD_SIZE])
     grad_wv = per_head(grad_qkv[:, :, HEADS_LANES + HEAD_SIZE :])
-    grad_wo = jnp.sum(grad_wo.astype(f32), axis=0)
-    router_pack = jnp.sum(router_pack.astype(f32), axis=0)
     grad_router = router_pack[:, :experts]
     grad_gain_m = router_pack[:, experts]
 

time: 392 us -> 356 us (0.908)
  Pallas kernels: 306 us -> 255 us
  waiting for transfers between devices: 0.11 us -> 16.6 us
  local copies, waits for them, and re-layouts: 17.1 us -> 21.3 us
    pallas_call x5 -> x3, Pallas kernels: 177 us -> 88 us  [exchange(): pl.pallas_call(kernel, name=f'exchange{collective_id}', out_shape=out_sha...]
    pallas_call x0 -> x1, Pallas kernels: none -> 37.5 us  [final_exchange(): pl.pallas_call(kernel, name='final_exchange', out_shape=[jax.ShapeDtypeSt...]
    ppermute x6, waiting for transfers between devices: 0.02 us -> 16.6 us  [shift(): lax.ppermute(x, 'seq', [(i, (i + 2 * k) % devices) for i in range(devices)])]
    unnamed x80 -> x93, local copies, waits for them, and re-layouts: 10.3 us -> 14.8 us
  transfers between devices with their start and end apart: 10 -> 10, of which waited for: 0 -> 2; matrix products, arithmetic and copies ran while one was open for 9% -> 9% of each run, Pallas kernels for 79% -> 72%
where the time goes in v4:
time: 356 us; the launch traced here: 353 us
  Pallas kernels  255 us (72%)
  local copies, waits for them, and re-layouts  21.3 us (6%)
  other arithmetic  20.5 us (6%)
  waiting for transfers between devices  16.6 us (5%)
  between operations  14.4 us (4%)
  starting transfers between devices  13.8 us (4%)
  matrix products  11.3 us (3%)
    pallas_call x1, Pallas kernels, moe_exchange(): pl.pallas_call(kernel, name='moe_exchange', out_shape=[jax.ShapeDtypeStru...  89.3 us
    pallas_call x3, Pallas kernels, exchange(): pl.pallas_call(kernel, name=f'exchange{collective_id}', out_shape=out_sha...  88 us
    pallas_call x1, Pallas kernels, final_exchange(): pl.pallas_call(kernel, name='final_exchange', out_shape=[jax.ShapeDtypeSt...  37.5 us
    pallas_call x1, Pallas kernels, attend_backward(): pl.pallas_call(kernel, name='attend_backward', grid_spec=grid_spec, out_s...  22.2 us
    pallas_call x1, Pallas kernels, attend_forward(): pl.pallas_call(kernel, name='attend_forward', grid_spec=grid_spec, out_sh...  17.8 us
    ppermute x6, waiting for transfers between devices, shift(): lax.ppermute(x, 'seq', [(i, (i + 2 * k) % devices) for i in range(devices)])  16.6 us
    unnamed x93, local copies, waits for them, and re-layouts  14.8 us
    ppermute x6, starting transfers between devices, shift(): lax.ppermute(x, 'seq', [(i, (i + 2 * k) % devices) for i in range(devices)])  8.14 us
  transfers between devices with their start and end apart: 10, of which 2 were waited for; matrix products, arithmetic and copies ran while one was open for 9% of the time, Pallas kernels for 72%

profile of v4, /device:TPU:13, one launch (start us, length us, event | category | flops | bytes accessed | tf_op | source)
XLA Modules:
  0.0 352.7 jit_solution(8033781840455532575)
XLA Ops:
  7.2 2.2 convert_element_type.109
  16.9 48.3 %exchange0.1 = (bf16[8,256,1024]{2,1,0:T(8,128)(2,1)}, s32[8,8,256]{2,1,0:T(8,128)S(1)}, bf16[8,256,128]{2,1,0:T(8,128)(2,1)S(1)}, bf16[4,256,256]{2,1,0:T(8,128...) custom-call(bf16[256,1024]{1,0:T(8,128)(2,1)S(1)} %bitcast.57, ...), custom_call_target="tpu_custom_call" | custom-call | tf_op jit(solution)/shard_map/exchange0/pallas_call | solution.py:247
  66.0 4.2 %collective-permute-start.1 = (bf16[256,1024]{1,0:T(8,128)(2,1)}, bf16[256,1024]{1,0:T(8,128)(2,1)}, u32[]{:S(2)}, u32[]{:S(2)}) collective-permute-start(bf16[256,1024]{1,0:T(8,128)(2,1)} %bitcast.73), channel_id=1, source_target_pairs={{0,4},{1,5},{2,6},{3,7},{4,0},{5,1},{6,2},{7,3},{8,12},{9,13},{10,... | collective-permute-start | bytes 1572872 | tf_op jit(solution)/shard_map/ppermute | solution.py:1330
  70.2 2.5 copy-done.13
  73.8 17.8 %attend_forward.1 = (bf16[8,256,1024]{2,1,0:T(8,128)(2,1)S(1)}, bf16[8,256,128]{2,1,0:T(8,128)(2,1)S(1)}, bf16[8,256,128]{2,1,0:T(8,128)(2,1)S(1)}, bf16[8,256,1...) custom-call(s32[8]{0:T(128)S(1)} %convert_reduce_fusion.3.first_ref, ...), custom_call_target="tpu_custom_call" | custom-call | flops 3221225472 | bytes 16777216 | tf_op jit(solution)/shard_map/attend_forward/pallas_call | solution.py:425
  91.6 2.1 copy-done.17
  94.4 22.1 %exchange1.1 = bf16[256,1024]{1,0:T(8,128)(2,1)S(1)} custom-call(bf16[8,256,128]{2,1,0:T(8,128)(2,1)S(1)} %get-tuple-element.53.refs_0_), custom_call_target="tpu_custom_call" | custom-call | tf_op jit(solution)/shard_map/exchange1/pallas_call | solution.py:247
  116.5 1.7 multiply_reduce_fusion.2
  118.3 2.2 multiply_convert_fusion.1.refs_0_
  120.5 89.3 %moe_exchange.1 = (bf16[2,8,256,1024]{3,2,1,0:T(8,128)(2,1)}, bf16[2,8,256,1024]{3,2,1,0:T(8,128)(2,1)}, bf16[2,8,256,512]{3,2,1,0:T(8,128)(2,1)}, f32[256,1024]...) custom-call(bf16[256,1024]{1,0:T(8,128)(2,1)} %multiply_convert_fusi, ...), custom_call_target="tpu_custom_call" | custom-call | flops 38654705664 | bytes 41943040 | tf_op jit(solution)/shard_map/moe_exchange/pallas_call | solution.py:967
  209.9 5.5 %all-to-all-start = ((bf16[4,2,256,1536]{3,2,1,0:T(8,128)(2,1)}), bf16[4,2,256,1536]{3,2,1,0:T(8,128)(2,1)}, u32[]{:S(2)}, u32[]{:S(2)}) async-start(bf16[4,2,256,1536]{3,2,1,0:T(8,128)(2,1)} %get-tuple-element.80), calls=%async_computation | async-start | bytes 12582912 | tf_op jit(solution)/shard_map/all_to_all | solution.py:1374
  215.5 1.5 fusion.10
  218.4 1.8 multiply_reduce_fusion
  220.2 2.1 subtract_add_fusion.refs_6_
  223.2 17.6 %exchange4.1.do_ref = bf16[8,256,128]{2,1,0:T(8,128)(2,1)S(1)} custom-call(bf16[256,1024]{1,0:T(8,128)(2,1)S(1)} %convolution_convert_fusion.1.refs_0_), custom_call_target="tpu_custom_call" | custom-call | tf_op jit(solution)/shard_map/exchange4/pallas_call | solution.py:247
  242.7 1.5 collective-permute-start.5
  247.6 2.1 convolution_convert_fusion
  250.1 22.2 %attend_backward.1.refs_0_ = bf16[8,256,256]{2,1,0:T(8,128)(2,1)S(1)} custom-call(s32[8]{0:T(128)S(1)} %convert_reduce_fusion.3.first_ref, bf16[8,256,128]{2,1,0:T(8,128)(2,1)S(1)} %copy-done.22, bf16[8,256,128]{2,1,0:T(8,128)(2,1)S(1)} %copy-done.24, bf16[8,256,128]{2,1,0:T(8,128)(2,1)S(1)} %copy-done.12, f32[8,64,512]{2,1,0:T(8,128)S(1)} %copy-done.20, ...), custom_call_target="tpu_custom_call" | custom-call | flops 5368709120 | bytes 4194304 | tf_op jit(solution)/shard_map/attend_backward/pallas_call | solution.py:540
  272.2 15.1 %collective-permute-done.4.refs_11_ = bf16[256,1024]{1,0:T(8,128)(2,1)} collective-permute-done((bf16[256,1024]{1,0:T(8,128)(2,1)}, bf16[256,1024]{1,0:T(8,128)(2,1)}, u32[]{:S(2)}, u32[]{:S(2)}) %collective-permute-start.4) | collective-permute-done | bytes 524320 | tf_op jit(solution)/shard_map/ppermute | solution.py:1330
  288.8 2.1 fusion.1
  292.0 37.5 %final_exchange.1 = (bf16[256,1024]{1,0:T(8,128)(2,1)S(1)}, bf16[256,1024]{1,0:T(8,128)(2,1)S(1)}, bf16[8,32,256]{2,1,0:T(8,128)(2,1)S(1)}, f32[32,1024]{1,0:T(8,128)S(1)}, f32[32,128]{1,0:T(8,128)S(1)}) custom-call(bf16[8,256,256]{2,1,0:T(8,128)(2,1)S(1)} %attend_backward.1.refs_0_, bf16[4,8,32,256]{3,2,1,0:T(8,128)(2,1)S(1)} %bitcast.59, ...), custom_call_target="tpu_custom_call" | custom-call | tf_op jit(solution)/shard_map/final_exchange/pallas_call | solution.py:1249
  333.9 1.7 multiply_reduce_fusion.3
  336.2 4.6 %convert_reduce_fusion = f32[2,256,1024]{2,1,0:T(8,128)} fusion(bf16[4,2,256,1536]{3,2,1,0:T(8,128)(2,1)} %all-to-all-done), kind=kLoop, calls=%fused_computation | loop fusion | flops 3670016 | bytes 6291456 | tf_op jit(solution)/shard_map/reduce_sum | solution.py:1427
  340.8 3.1 convert_reduce_fusion.1
  (158 shorter events, 27.7 us)
Async XLA Ops:
  7.2 113.3 %all-gather.6.cloned.1.call-start = ((), (), s32[]{:S(2)}) async-start(), calls=%async_computation.2 | async-start | bytes 2621440 | tf_op jit(solution)/shard_map/all_gather | solution.py:1324
  9.5 111.0 %all-gather.4.cloned.1.call-start = ((), (), s32[]{:S(2)}) async-start(), calls=%async_computation.1 | async-start | bytes 5242880 | tf_op jit(solution)/shard_map/all_gather | solution.py:1323
  10.7 280.2 %all-gather.8.cloned.1.call-start = ((), (), s32[]{:S(2)}) async-start(), calls=%async_computation.3 | async-start | bytes 5242880 | tf_op jit(solution)/shard_map/all_gather | solution.py:1325
  10.8 55.2 %collective-permute-start = (bf16[256,1024]{1,0:T(8,128)(2,1)}, bf16[256,1024]{1,0:T(8,128)(2,1)}, u32[]{:S(2)}, u32[]{:S(2)}) collective-permute-start(bf16[256,1024]{1,0:T(8,128)(2,1)} %bitcast.72), channel_id=1, source_target_pairs={{0,2},{1,3},{2,4},{3,5},{4,6},{5,7},{6,0},{7,1},{8,10},{9,11},{10,... | collective-permute-start | bytes 1572872 | tf_op jit(solution)/shard_map/ppermute | solution.py:1330
  65.2 26.4 %copy-start = (bf16[4,256,128]{2,1,0:T(8,128)(2,1)}, bf16[4,256,128]{2,1,0:T(8,128)(2,1)S(1)}, u32[]{:S(2)}) copy-start(bf16[4,256,128]{2,1,0:T(8,128)(2,1)S(1)} %get-tuple-element.50) | copy-start | bytes 786436
  65.2 26.4 %copy-start.14 = (bf16[8,256,128]{2,1,0:T(8,128)(2,1)}, bf16[8,256,128]{2,1,0:T(8,128)(2,1)S(1)}, u32[]{:S(2)}) copy-start(bf16[8,256,128]{2,1,0:T(8,128)(2,1)S(1)} %get-tuple-element.57.refs_5_) | copy-start | bytes 1572868
  65.2 51.3 %copy-start.2 = (bf16[4,256,1024]{2,1,0:T(8,128)(2,1)}, bf16[4,256,1024]{2,1,0:T(8,128)(2,1)S(1)}, u32[]{:S(2)}) copy-start(bf16[4,256,1024]{2,1,0:T(8,128)(2,1)S(1)} %get-tuple-element.54) | copy-start | bytes 6291460
  66.0 54.5 %collective-permute-start.1 = (bf16[256,1024]{1,0:T(8,128)(2,1)}, bf16[256,1024]{1,0:T(8,128)(2,1)}, u32[]{:S(2)}, u32[]{:S(2)}) collective-permute-start(bf16[256,1024]{1,0:T(8,128)(2,1)} %bitcast.73), channel_id=1, source_target_pairs={{0,4},{1,5},{2,6},{3,7},{4,0},{5,1},{6,2},{7,3},{8,12},{9,13},{10,... | collective-permute-start | bytes 1572872 | tf_op jit(solution)/shard_map/ppermute | solution.py:1330
  70.2 50.3 %collective-permute-start.2 = (bf16[256,1024]{1,0:T(8,128)(2,1)}, bf16[256,1024]{1,0:T(8,128)(2,1)}, u32[]{:S(2)}, u32[]{:S(2)}) collective-permute-start(bf16[256,1024]{1,0:T(8,128)(2,1)} %bitcast.74), channel_id=1, source_target_pairs={{0,6},{1,7},{2,0},{3,1},{4,2},{5,3},{6,4},{7,5},{8,14},{9,15},{10,... | collective-permute-start | bytes 1572872 | tf_op jit(solution)/shard_map/ppermute | solution.py:1330
  94.4 23.8 %copy-start.19 = (f32[8,64,512]{2,1,0:T(8,128)}, f32[8,64,512]{2,1,0:T(8,128)S(1)}, u32[]{:S(2)}) copy-start(f32[8,64,512]{2,1,0:T(8,128)S(1)} %get-tuple-element.63.ot_ref) | copy-start | bytes 3145732
  94.4 23.8 %copy-start.23 = (bf16[8,256,128]{2,1,0:T(8,128)(2,1)}, bf16[8,256,128]{2,1,0:T(8,128)(2,1)S(1)}, u32[]{:S(2)}) copy-start(bf16[8,256,128]{2,1,0:T(8,128)(2,1)S(1)} %get-tuple-element.52.kv_ref) | copy-start | bytes 1572868
  209.9 5.6 %copy-start.1 = (bf16[4,256,128]{2,1,0:T(8,128)(2,1)S(1)}, bf16[4,256,128]{2,1,0:T(8,128)(2,1)}, u32[]{:S(2)}) copy-start(bf16[4,256,128]{2,1,0:T(8,128)(2,1)} %copy-done) | copy-start | bytes 786436
  209.9 126.3 %all-to-all-start = ((bf16[4,2,256,1536]{3,2,1,0:T(8,128)(2,1)}), bf16[4,2,256,1536]{3,2,1,0:T(8,128)(2,1)}, u32[]{:S(2)}, u32[]{:S(2)}) async-start(bf16[4,2,256,1536]{3,2,1,0:T(8,128)(2,1)} %get-tuple-element.80), calls=%async_computation | async-start | bytes 12582912 | tf_op jit(solution)/shard_map/all_to_all | solution.py:1374
  215.4 3.0 copy-start.26
  217.1 3.1 copy-start.34
  222.4 25.1 %copy-start.25 = (f32[256,1024]{1,0:T(8,128)}, f32[256,1024]{1,0:T(8,128)S(1)}, u32[]{:S(2)}) copy-start(f32[256,1024]{1,0:T(8,128)S(1)} %subtract_add_fusion.refs_6_) | copy-start | bytes 3145732
  241.6 30.6 %collective-permute-start.3 = (bf16[256,1024]{1,0:T(8,128)(2,1)}, bf16[256,1024]{1,0:T(8,128)(2,1)S(1)}, u32[]{:S(2)}, u32[]{:S(2)}) collective-permute-start(bf16[256,1024]{1,0:T(8,128)(2,1)} %get-tuple-element.66), channel_id=1, source_target_pairs={{0,2},{1,3},{2,4},{3,5},{4,6},{5,7},{6,0},{7,1},{8,10},{9,11},{10,... | collective-permute-start | bytes 1572872 | tf_op jit(solution)/shard_map/ppermute | solution.py:1330
  241.6 45.7 %collective-permute-start.4 = (bf16[256,1024]{1,0:T(8,128)(2,1)}, bf16[256,1024]{1,0:T(8,128)(2,1)}, u32[]{:S(2)}, u32[]{:S(2)}) collective-permute-start(bf16[256,1024]{1,0:T(8,128)(2,1)} %get-tuple-element.67), channel_id=1, source_target_pairs={{0,4},{1,5},{2,6},{3,7},{4,0},{5,1},{6,2},{7,3},{8,12},{9,13},{10,... | collective-permute-start | bytes 1572872 | tf_op jit(solution)/shard_map/ppermute | solution.py:1330
  242.7 46.1 %collective-permute-start.5 = (bf16[256,1024]{1,0:T(8,128)(2,1)}, bf16[256,1024]{1,0:T(8,128)(2,1)}, u32[]{:S(2)}, u32[]{:S(2)}) collective-permute-start(bf16[256,1024]{1,0:T(8,128)(2,1)} %get-tuple-element.68), channel_id=1, source_target_pairs={{0,6},{1,7},{2,0},{3,1},{4,2},{5,3},{6,4},{7,5},{8,14},{9,15},{10,... | collective-permute-start | bytes 1572872 | tf_op jit(solution)/shard_map/ppermute | solution.py:1330
  250.1 38.7 %copy-start.18 = (bf16[8,256,1024]{2,1,0:T(8,128)(2,1)S(1)}, bf16[8,256,1024]{2,1,0:T(8,128)(2,1)}, u32[]{:S(2)}) copy-start(bf16[8,256,1024]{2,1,0:T(8,128)(2,1)} %copy-done.17) | copy-start | bytes 12582916
  331.3 9.5 %copy-start.35 = (f32[32,512]{1,0:T(8,128)}, f32[32,512]{1,0:T(8,128)S(1)}, u32[]{:S(2)}) copy-start(f32[32,512]{1,0:T(8,128)S(1)} %reshape.112) | copy-start | bytes 196612
  331.5 9.3 %copy-start.36 = (f32[32,512]{1,0:T(8,128)}, f32[32,512]{1,0:T(8,128)S(1)}, u32[]{:S(2)}) copy-start(f32[32,512]{1,0:T(8,128)S(1)} %reshape.113) | copy-start | bytes 196612
  340.8 3.1 copy-start.10
  340.8 3.9 %copy-start.8 = (bf16[256,1024]{1,0:T(8,128)(2,1)S(1)}, bf16[256,1024]{1,0:T(8,128)(2,1)}, u32[]{:S(2)}) copy-start(bf16[256,1024]{1,0:T(8,128)(2,1)} %copy-done.7) | copy-start | bytes 1572868
  (28 other events, 57.1 us)
Sparse Core Ops, SparseCore 0:
  9.9 49.4 all-gather.5
  61.2 52.7 all-gather.3
  116.4 52.7 all-gather.7

commit v5 on v4

--- a/solution.py
+++ b/solution.py
@@ -18,7 +18,7 @@
     return ref.at[:, pl.ds(pl.multiple_of(j * cut, cut), cut)]
 
 
-def exchange(collective_id, ops):
+def exchange(collective_id, ops, prepare=None, given=(), work=(), made=None, keep=None):
     axes = tuple(dict.fromkeys(axis for _, axis, _, _ in ops))
     size = {axis: lax.axis_size(axis) for axis in axes}
     out_shapes, out_specs, scratch, places = [], [], [], []
@@ -27,7 +27,9 @@
         out_spec = pl.BlockSpec(memory_space=pl.ANY)
         extra = []
         lead = (PIECES,) if kind == "gather" and axis == "seq" else ()
-        if kind == "share":
+        if kind == "shift":
+            shape, dtype, copies = x.shape, x.dtype, 1
+        elif kind == "share":
             shape, dtype, copies = (count,) + x.shape, x.dtype, 2 * (count - 1)
         elif kind == "gather":
             shape, dtype = (count,) + x.shape, x.dtype
@@ -49,8 +51,17 @@
             pltpu.SemaphoreType.DMA,
         ] + extra
 
+    early = [x for _, _, x, cut in ops if not isinstance(cut, int)]
+    own_scratch = len(scratch)
+
     def kernel(*refs):
-        ins, outs, work = refs[: len(ops)], refs[len(ops) : 2 * len(ops)], refs[2 * len(ops) :]
+        ins, refs = list(refs[: len(early)]), refs[len(early) :]
+        extra_in, refs = refs[: len(given)], refs[len(given) :]
+        outs, refs = refs[: len(ops)], refs[len(ops) :]
+        if keep is not None:
+            kept, refs = refs[0], refs[1:]
+        work, extra_work = refs[:own_scratch], refs[own_scratch:]
+        ins += [None] * (len(ops) - len(early))
         me = {axis: lax.axis_index(axis) for axis in axes}
         barrier = pltpu.get_barrier_semaphore()
         for axis in axes:
@@ -75,6 +86,15 @@
 
         second, third = [], []
         for (kind, axis, _, cut), x, o, (at, extra) in zip(ops, ins, outs, places):
+            if isinstance(cut, int):
+                if x is None and cut == 0:
+                    all_refs = list(extra_in) + list(extra_work[:-1])
+                    prepare(all_refs)
+                    late = made(all_refs)
+                    leave = pltpu.make_async_copy(all_refs[keep[1]], kept, extra_work[-1])
+                    leave.start()
+                    third.append(leave.wait)
+                x, cut = late[cut], None
             send, recv, local = work[at : at + 3]
             count, my = size[axis], me[axis]
             if kind == "swap":
@@ -120,6 +140,12 @@
                             axis, x, o.at[frm], send.at[k - 1], recv.at[k - 1], to
                         ).wait_recv
                     )
+            elif kind == "shift":
+                copy = remote(
+                    axis, x, o, send.at[0], recv.at[0], lax.rem(my + 2 * (count // 4), count)
+                )
+                second.append((count // 4 + 0.9, copy.start))
+                third.append(copy.wait)
             elif kind == "share":
                 seq, half = me["seq"], x.shape[0] // 2
                 core = lax.rem(seq, 2)
@@ -247,14 +273,16 @@
     return pl.pallas_call(
         kernel,
         name=f"exchange{collective_id}",
-        out_shape=out_shapes,
-        in_specs=[pl.BlockSpec(memory_space=pl.ANY)] * len(ops),
-        out_specs=out_specs,
-        scratch_shapes=scratch,
+        out_shape=out_shapes + ([] if keep is None else [keep[0]]),
+        in_specs=[pl.BlockSpec(memory_space=pl.ANY)] * (len(early) + len(given)),
+        out_specs=out_specs + ([] if keep is None else [pl.BlockSpec(memory_space=pl.ANY)]),
+        scratch_shapes=scratch
+        + list(work)
+        + ([] if keep is None else [pltpu.SemaphoreType.DMA]),
         compiler_params=pltpu.CompilerParams(
-            collective_id=collective_id, has_side_effects=True, vmem_limit_bytes=48 << 20
+            collective_id=collective_id, has_side_effects=True, vmem_limit_bytes=60 << 20
         ),
-    )(*[x for _, _, x, _ in ops])
+    )(*early, *given)
 
 QUERY_HEADS = 16
 KEY_VALUE_HEADS = 8
@@ -440,7 +468,7 @@
             transcendentals=length * length,
         ),
         compiler_params=pltpu.CompilerParams(
-            dimension_semantics=("arbitrary",), vmem_limit_bytes=40 << 20
+            dimension_semantics=("arbitrary",), vmem_limit_bytes=60 << 20
         ),
     )(
         first,
@@ -452,17 +480,18 @@
     )
 
 
-def attend_backward(q_all, kv_all, cot, ot, lse, table, docs, heads):
+def attend_backward(q_all, kv_all, cot, ot, lse, table, docs, heads, normed):
     blocks, rows, _ = q_all.shape
     length = blocks * rows
     cols = heads * rows
     first = first_blocks(docs)
 
-    def kernel(first_ref, q_ref, kv_ref, do_ref, ot_ref, lse_ref, table_ref, docs_ref, out_ref, dk_scr, dv_scr, dq_scr, doc_scr):
+    def kernel(first_ref, q_ref, kv_ref, do_ref, ot_ref, lse_ref, table_ref, docs_ref, normed_in, out_ref, grad_ref, dk_scr, dv_scr, dq_scr, doc_scr, normed_all, grad_scr, sem):
         i = pl.program_id(0)
 
         @pl.when(i == 0)
         def _():
+            pltpu.make_async_copy(normed_in, normed_all, sem).start()
             dk_scr[...] = jnp.zeros_like(dk_scr)
             dv_scr[...] = jnp.zeros_like(dv_scr)
 
@@ -502,14 +531,19 @@
 
         @pl.when(i == blocks - 1)
         def _():
+            pltpu.make_async_copy(normed_in, normed_all, sem).wait()
+            grad_scr[...] = jnp.zeros_like(grad_scr)
+
             @pl.loop(0, blocks)
             def _(j):
                 kv = jnp.concatenate([dk_scr[j] * att_mult, dv_scr[j]], axis=1)
                 lane = lax.broadcasted_iota(jnp.int32, kv.shape, 1)
                 c, s = spread_table(table_ref[j])
-                out_ref[j, :, HEADS_LANES:] = jnp.where(
-                    lane < HEAD_SIZE, kv * c - turn(kv) * s, kv
-                ).astype(bf16)
+                kv = jnp.where(lane < HEAD_SIZE, kv * c - turn(kv) * s, kv).astype(bf16)
+                out_ref[j, :, HEADS_LANES:] = kv
+                grad_scr[...] += dot_tn(normed_all[j], out_ref[j])
+
+            grad_ref[...] = grad_scr[...].astype(bf16)
 
     def block(shape):
         return pl.BlockSpec((1,) + shape, lambda i, _: (i, 0, 0))
@@ -528,27 +562,37 @@
             block((1, cols)),
             whole((blocks, HEAD_SIZE, rows)),
             block((1, rows)),
+            pl.BlockSpec(memory_space=pl.ANY),
         ],
-        out_specs=whole((blocks, rows, HEADS_LANES + LANES)),
+        out_specs=[
+            whole((blocks, rows, HEADS_LANES + LANES)),
+            whole((normed.shape[2], HEADS_LANES + LANES)),
+        ],
         scratch_shapes=[
             pltpu.VMEM((blocks, rows, HEAD_SIZE), f32),
             pltpu.VMEM((blocks, rows, HEAD_SIZE), f32),
             pltpu.VMEM((cols, HEAD_SIZE), f32),
             pltpu.VMEM((blocks, rows, LANES), f32),
+            pltpu.VMEM(normed.shape, bf16),
+            pltpu.VMEM((normed.shape[2], HEADS_LANES + LANES), f32),
+            pltpu.SemaphoreType.DMA,
         ],
     )
     return pl.pallas_call(
         kernel,
         name="attend_backward",
         grid_spec=grid_spec,
-        out_shape=jax.ShapeDtypeStruct((blocks, rows, HEADS_LANES + LANES), bf16),
+        out_shape=[
+            jax.ShapeDtypeStruct((blocks, rows, HEADS_LANES + LANES), bf16),
+            jax.ShapeDtypeStruct((normed.shape[2], HEADS_LANES + LANES), bf16),
+        ],
         cost_estimate=pl.CostEstimate(
             flops=5 * length * length * cols // rows * 128,
             bytes_accessed=2 * length * 1024,
             transcendentals=length * length,
         ),
         compiler_params=pltpu.CompilerParams(
-            dimension_semantics=("arbitrary",), vmem_limit_bytes=48 << 20
+            dimension_semantics=("arbitrary",), vmem_limit_bytes=60 << 20
         ),
     )(
         first,
@@ -559,6 +603,7 @@
         lse,
         table,
         docs[:, None],
+        normed,
     )
 
 
@@ -567,6 +612,7 @@
     chips = devices // 2
     rows, width = normed.shape
     own_experts = w_in.shape[0]
+    gate_rows = devices * own_experts
 
     def order(chip, k):
         left = chip < chips - 1 - chip
@@ -578,15 +624,15 @@
         x_in, g_in = refs[0], refs[1 : 1 + chips]
         mask_ref, router_ref, win_in, wout_in = refs[1 + chips : 5 + chips]
         (lin_out, slot_out, hid_out, n_sum, gate_out, g_out) = refs[5 + chips : 11 + chips]
-        y_outs = refs[11 + chips : 11 + 2 * chips]
+        y_outs = refs[11 + chips : 12 + chips + chips // 2]
         (
             x_all, g_all, win, wout, y_acc, n_acc, gate_acc, gate_stage,
-            n_mine, n_far, n_give, n_theirs, y_mine, y_give, y_theirs, y_pre,
+            n_mine, n_far, n_give, n_theirs, y_give, y_theirs, y_pre, y_in,
             lin_st, slot_st, hid_st, gin, gout, hid_ld,
             local, line_send, line_recv, sib_send, sib_recv, g_local, g_send, g_recv,
             n_send, n_recv, y_send, y_recv, far_send, far_recv, gate_send, gate_recv,
-            st_sem, y_sem, ld_sem, w_sem, wg_sem,
-        ) = refs[11 + 2 * chips :]
+            st_sem, y_sem, ld_sem, w_sem, wg_sem, hand_send, hand_recv,
+        ) = refs[12 + chips + chips // 2 :]
         me = lax.axis_index("seq")
         chip, core = me // 2, lax.rem(me, 2)
         sibling = me + 1 - 2 * core
@@ -681,13 +727,23 @@
             )
 
         def n_copy(p):
-            return remote(n_give.at[p], n_theirs.at[p], n_send.at[p], n_recv.at[p], sibling)
+            return remote(n_give, n_theirs.at[p], n_send.at[p], n_recv.at[p], sibling)
 
         def y_copy(p):
-            return remote(y_give.at[p], y_theirs.at[p], y_send.at[p], y_recv.at[p], sibling)
-
-        def y_leave(p, k):
-            return pltpu.make_async_copy(y_pre.at[p], y_outs[k], y_sem.at[p])
+            return remote(y_give, y_theirs.at[p], y_send.at[p], y_recv.at[p], sibling)
+
+        pairs = chips // 2
+        pair = chip // 2
+        mate = chip + 1 - 2 * lax.rem(chip, 2)
+
+        def y_leave(b, k):
+            return pltpu.make_async_copy(y_pre.at[b], y_outs[k], y_sem.at[k])
+
+        def y_hand(b):
+            far = lax.rem(b // 2 + pairs - pair, pairs) - 1
+            return remote(
+                y_pre.at[b], y_in.at[far], hand_send.at[far], hand_recv.at[far], 2 * mate + core
+            )
 
         def stage_copies(e, block):
             return [
@@ -704,7 +760,7 @@
         def fold(k):
             b, p = order(chip, k), lax.rem(k, 2)
             n_copy(p).wait_recv()
-            both = n_mine[b].astype(f32) + n_theirs[p].astype(f32)
+            both = n_acc[...].astype(bf16).astype(f32) + n_theirs[p].astype(f32)
 
             @pl.when(b == chip)
             def _():
@@ -715,18 +771,20 @@
                 n_mine[b] = both.astype(bf16)
                 far_copy(b).start()
 
-            @pl.when(k > 1)
+            y_copy(p).wait_recv()
+            y_pre[b] = (y_acc[...] + y_theirs[p].astype(f32)).astype(bf16)
+
+            @pl.when(b == chip)
             def _():
-                y_leave(p, 0).wait()
-
-            y_copy(p).wait_recv()
-            y_pre[p] = (y_mine[...].astype(f32) + y_theirs[p].astype(f32)).astype(bf16)
-            away = lax.rem(b - chip + chips, chips)
-            for r in range(chips):
-
-                @pl.when(away == r)
-                def _(r=r):
-                    y_leave(p, r).start()
+                y_leave(b, 0).start()
+
+            @pl.when(b == mate)
+            def _():
+                y_leave(b, 1).start()
+
+            @pl.when((b != mate) & (lax.rem(b + chip, 2) == 1))
+            def _():
+                y_hand(b).start()
 
         def compute(block, before):
             x = x_all[block]
@@ -748,7 +806,7 @@
                 )
                 lin = dot_nn(x_all[block], win[e])
                 gate_lin, up_lin = lin[:, :FFE], lin[:, FFE:]
-                sig = 1.0 / (1.0 + jnp.exp(-gate_lin))
+                sig = 0.5 + 0.5 * jnp.tanh(0.5 * gate_lin)
                 silu = gate_lin * sig
                 hidden = (silu * up_lin).astype(bf16)
 
@@ -762,7 +820,7 @@
                 y_acc[...] += gate * res
                 cot = g_all[block].astype(f32) * res_mult
                 gate_acc[...] += jnp.where(
-                    lane == e, jnp.sum(cot * res, axis=1, keepdims=True), 0.0
+                    lane == me * own_experts + e, jnp.sum(cot * res, axis=1, keepdims=True), 0.0
                 )
                 slot = (gate * cot).astype(bf16)
                 slot_st[e] = slot
@@ -779,7 +837,7 @@
                     copy.start()
                 n_acc[...] += dot_nt(lin_cot, win[e]).astype(bf16).astype(f32)
 
-            gate_stage[block] = gate_acc[...].T[:8]
+            gate_stage[block] = gate_acc[...].T[:gate_rows]
 
             @pl.when(block != me)
             def _():
@@ -823,26 +881,17 @@
 
                     @pl.when(k > 0)
                     def _():
-                        fold(k - 1)
-
-                    @pl.when(k > 1)
-                    def _():
-                        n_copy(p).wait_send()
-                        y_copy(p).wait_send()
-
-                    n_give[p] = n_acc[...].astype(bf16)
-                    y_give[p] = y_acc[...].astype(bf16)
+                        n_copy(1 - p).wait_send()
+                        y_copy(1 - p).wait_send()
+
+                    n_give[...] = n_acc[...].astype(bf16)
+                    y_give[...] = y_acc[...].astype(bf16)
                     n_copy(p).start()
                     y_copy(p).start()
 
                 @pl.when(h == 1)
                 def _():
-                    n_mine[b] = n_acc[...].astype(bf16)
-                    y_mine[...] = y_acc[...].astype(bf16)
-
-        @pl.loop(chips - 1, chips)
-        def _(k):
-            fold(k)
+                    fold(k)
 
         for e in range(own_experts):
             for copy in stage_copies(e, 0):
@@ -900,6 +949,15 @@
                             pass_on(away, i, me - 2 * side).wait_send()
 
         own_sends(lambda copy: copy.wait_send())
+
+        def keep_of(j):
+            return 2 * lax.rem(pair + 1 + j, pairs) + lax.rem(chip, 2)
+
+        for j in range(pairs - 1):
+            b = keep_of(j)
+            y_hand(b).wait_recv()
+            y_pre[b] = (y_pre[b].astype(f32) + y_in[j].astype(f32)).astype(bf16)
+            y_leave(b, 2 + j).start()
 
         part_rows = width // parts
         leaving = []
@@ -915,7 +973,9 @@
                     leaving.append(
                         (
                             pltpu.make_async_copy(
-                                x_all.at[i, here], g_out.at[part, e, :, pl.ds(0, 2 * FFE)], wg_sem.at[at]
+                                x_all.at[i, here],
+                                g_out.at[part, e, :, pl.ds(0, 2 * FFE)],
+                                wg_sem.at[at],
                             ),
                             pltpu.make_async_copy(
                                 g_all.at[i, here, pl.ds(0, FFE)],
@@ -948,13 +1008,16 @@
             ).wait_recv()
             gate_copy(block).wait_send()
 
-        for p in range(2):
-            n_copy(p).wait_send()
-            y_copy(p).wait_send()
-            y_leave(p, 0).wait()
-        for pair in leaving:
-            for copy in pair:
+        n_copy((chips - 1) % 2).wait_send()
+        y_copy((chips - 1) % 2).wait_send()
+        for both in leaving:
+            for copy in both:
                 copy.wait()
+        y_leave(chip, 0).wait()
+        y_leave(mate, 1).wait()
+        for j in range(pairs - 1):
+            y_leave(keep_of(j), 2 + j).wait()
+            y_hand(keep_of(j) + mate - chip).wait_send()
 
         for k in range(chips):
             cot_to_sibling(k).wait_send()
@@ -972,12 +1035,12 @@
             jax.ShapeDtypeStruct((own_experts, devices) + block, bf16),
             jax.ShapeDtypeStruct((own_experts, devices, rows, FFE), bf16),
             jax.ShapeDtypeStruct(block, f32),
-            jax.ShapeDtypeStruct((devices, 8, rows), f32),
+            jax.ShapeDtypeStruct((devices, gate_rows, rows), f32),
             jax.ShapeDtypeStruct((parts, own_experts, width // parts, 3 * FFE), bf16),
         ]
-        + [jax.ShapeDtypeStruct(block, bf16)] * chips,
+        + [jax.ShapeDtypeStruct(block, bf16)] * (1 + chips // 2),
         in_specs=[hbm] * (1 + chips) + [vmem] * 2 + [hbm] * 2,
-        out_specs=[hbm] * 3 + [vmem] * 2 + [hbm] * (1 + chips),
+        out_specs=[hbm] * 3 + [vmem] * 2 + [hbm] * (2 + chips // 2),
         scratch_shapes=[
             pltpu.VMEM((devices,) + block, bf16),
             pltpu.VMEM((devices,) + block, bf16),
@@ -986,15 +1049,15 @@
             pltpu.VMEM(block, f32),
             pltpu.VMEM(block, f32),
             pltpu.VMEM((rows, LANES), f32),
-            pltpu.VMEM((devices, 8, rows), f32),
+            pltpu.VMEM((devices, gate_rows, rows), f32),
             pltpu.VMEM((chips,) + block, bf16),
             pltpu.VMEM((chips,) + block, bf16),
-            pltpu.VMEM((2,) + block, bf16),
+            pltpu.VMEM(block, bf16),
             pltpu.VMEM((2,) + block, bf16),
             pltpu.VMEM(block, bf16),
             pltpu.VMEM((2,) + block, bf16),
-            pltpu.VMEM((2,) + block, bf16),
-            pltpu.VMEM((2,) + block, bf16),
+            pltpu.VMEM((chips,) + block, bf16),
+            pltpu.VMEM((chips // 2 - 1,) + block, bf16),
             pltpu.VMEM((own_experts, rows, 2 * FFE), bf16),
             pltpu.VMEM((own_experts,) + block, bf16),
             pltpu.VMEM((own_experts, rows, FFE), bf16),
@@ -1013,18 +1076,363 @@
         ]
         + [
             dma((3, own_experts)),
-            dma((2,)),
+            dma((1 + chips // 2,)),
             dma((3, 2)),
             dma((2,)),
             dma((2 * own_experts * max(parts, width // rows),)),
+            dma((chips // 2 - 1,)),
+            dma((chips // 2 - 1,)),
         ],
         cost_estimate=pl.CostEstimate(
             flops=flops, bytes_accessed=40 << 20, transcendentals=devices * rows * FFE * 2
         ),
         compiler_params=pltpu.CompilerParams(
-            collective_id=collective_id, has_side_effects=True, vmem_limit_bytes=62 << 20
+            collective_id=collective_id, has_side_effects=True, vmem_limit_bytes=63 << 20
         ),
     )(normed, *cots, mask, router, w_in, w_out)
+
+
+class Links:
+    def __init__(self, axes):
+        self.size = {axis: lax.axis_size(axis) for axis in axes}
+        self.me = {axis: lax.axis_index(axis) for axis in axes}
+
+    def barrier(self):
+        sem = pltpu.get_barrier_semaphore()
+        for axis, size in self.size.items():
+            for k in range(1, size):
+                pl.semaphore_signal(
+                    sem,
+                    inc=1,
+                    device_id={axis: lax.rem(self.me[axis] + k, size)},
+                    device_id_type=MESH,
+                )
+        pl.semaphore_wait(sem, sum(size - 1 for size in self.size.values()))
+
+    def copy(self, axis, src, dst, send, recv, to):
+        return pltpu.make_async_remote_copy(
+            src_ref=src,
+            dst_ref=dst,
+            send_sem=send,
+            recv_sem=recv,
+            device_id={axis: to},
+            device_id_type=MESH,
+        )
+
+    def swap_start(self, axis, src, dst, send, recv, local):
+        me, size = self.me[axis], self.size[axis]
+        pltpu.make_async_copy(src.at[me], dst.at[me], local).start()
+        for k in range(1, size):
+            to = lax.rem(me + k, size)
+            self.copy(axis, src.at[to], dst.at[me], send.at[k - 1], recv.at[k - 1], to).start()
+
+    def swap_wait(self, axis, src, dst, send, recv, local):
+        me, size = self.me[axis], self.size[axis]
+        pltpu.make_async_copy(src.at[me], dst.at[me], local).wait()
+        for k in range(1, size):
+            frm = lax.rem(me + size - k, size)
+            self.copy(axis, src.at[frm], dst.at[frm], send.at[k - 1], recv.at[k - 1], frm).wait()
+
+
+def loads(pairs, sems):
+    copies = [
+        pltpu.make_async_copy(src, dst, sems.at[i]) for i, (src, dst) in enumerate(pairs)
+    ]
+    for copy in copies:
+        copy.start()
+    return copies
+
+
+def staged(arrays):
+    return [pltpu.VMEM(x.shape, x.dtype) for x in arrays]
+
+
+def swap_sems(size):
+    dma = pltpu.SemaphoreType.DMA
+    return [dma((size - 1,)), dma((size - 1,)), dma]
+
+
+def attended_exchange(collective_id, attended_own, tokens, w_out, gain):
+    devices, rows, cols = attended_own.shape
+    width = tokens.shape[1]
+
+    ins = [tokens, w_out, gain]
+    outs = [
+        jax.ShapeDtypeStruct((rows, width), bf16),
+        jax.ShapeDtypeStruct((rows, width), f32),
+        jax.ShapeDtypeStruct((rows, width), bf16),
+    ]
+
+    def kernel(att_in, *refs):
+        given, results = refs[:3], refs[3:6]
+        tok, w_all, gain_ref = refs[6:9]
+        att_ref, mid_ref, norm_ref, got, in_sem, out_sem, *sems = refs[9:]
+        links = Links(("seq",))
+        arriving = loads(list(zip(given, (tok, w_all, gain_ref))), in_sem)
+        links.barrier()
+        links.swap_start("seq", att_in, got, *sems)
+        for copy in arriving:
+            copy.wait()
+        links.swap_wait("seq", att_in, got, *sems)
+        attended = jnp.concatenate([got[j] for j in range(devices)], axis=1)
+        att_ref[...] = attended
+        mid = tok[...].astype(f32) + res_mult * dot_nn(attended, w_all[...])
+        mid_ref[...] = mid
+        scale = lax.rsqrt(jnp.mean(mid * mid, axis=-1, keepdims=True) + norm_eps)
+        norm_ref[...] = (mid * scale * gain_ref[...].astype(f32)).astype(bf16)
+        for copy in loads(list(zip((att_ref, mid_ref, norm_ref), results)), out_sem):
+            copy.wait()
+
+    hbm = pl.BlockSpec(memory_space=pl.ANY)
+    dma = pltpu.SemaphoreType.DMA
+    return pl.pallas_call(
+        kernel,
+        name="attended_exchange",
+        out_shape=outs,
+        in_specs=[hbm] * 4,
+        out_specs=[hbm] * 3,
+        scratch_shapes=staged(ins)
+        + staged(outs)
+        + [pltpu.VMEM(attended_own.shape, bf16), dma((3,)), dma((3,))]
+        + swap_sems(devices),
+        compiler_params=pltpu.CompilerParams(
+            collective_id=collective_id, has_side_effects=True, vmem_limit_bytes=60 << 20
+        ),
+    )(attended_own, *ins)
+
+
+def middle_exchange(
+    collective_id, moe_sum, gate_cot, normed, router, mask, mid, out_grad, gain, w_out, attended, cols
+):
+    devices, gate_rows, rows = gate_cot.shape
+    width = normed.shape[1]
+    experts = gate_rows
+
+    ins = [moe_sum, gate_cot, normed, router, mask, mid, out_grad, gain, w_out, attended]
+    outs = [
+        jax.ShapeDtypeStruct((width, LANES), bf16),
+        jax.ShapeDtypeStruct((rows, width), f32),
+        jax.ShapeDtypeStruct((width, width), bf16),
+    ]
+
+    def kernel(*refs):
+        given, heads_out, results, refs = refs[:10], refs[10], refs[11:14], refs[14:]
+        (
+            moe_ref, gate_ref, norm_ref, router_ref, mask_ref, mid_ref, cot_ref, gain_ref, w_all, att_ref,
+            pack_out, mid_cot_out, wo_out, give, in_sem, out_sem, *sems,
+        ) = refs
+        links = Links(("seq",))
+        arriving = loads(list(zip(given, refs[:10])), in_sem)
+        links.barrier()
+        for copy in arriving:
+            copy.wait()
+        there = mask_ref[...] > 0
+        logits = jnp.where(there, dot_nn(norm_ref[...], router_ref[...]), -1e30)
+        gates = jnp.where(
+            there, jnp.exp(logits - jnp.max(logits, axis=1, keepdims=True)), 0.0
+        )
+        gates = gates / jnp.sum(gates, axis=1, keepdims=True)
+        gate = gate_ref[0]
+        for j in range(1, devices):
+            gate = gate + gate_ref[j]
+        gate = jnp.concatenate([gate, jnp.zeros((LANES - gate_rows, rows), f32)], axis=0).T
+        pick_cot = gates * (gate - jnp.sum(gates * gate, axis=1, keepdims=True))
+        logit_cot = pick_cot.astype(bf16)
+        cot = moe_ref[...] + dot_nt(logit_cot, router_ref[...])
+        mid = mid_ref[...]
+        scale = lax.rsqrt(jnp.mean(mid * mid, axis=-1, keepdims=True) + norm_eps)
+        gain_grad = jnp.sum(cot * mid * scale, axis=0, keepdims=True)
+        weighted = cot * gain_ref[...].astype(f32)
+        mid_cot = (
+            cot_ref[...].astype(f32)
+            + scale * weighted
+            - mid * (scale * scale * scale) * jnp.mean(weighted * mid, axis=-1, keepdims=True)
+        )
+        mid_cot_out[...] = mid_cot
+        branch_cot = (res_mult * mid_cot).astype(bf16)
+        attended_cot = dot_nt(branch_cot, w_all[...]).astype(bf16)
+        for j in range(devices):
+            give[j] = attended_cot[:, j * cols : (j + 1) * cols]
+        links.swap_start("seq", give, heads_out, *sems)
+        wo_out[...] = dot_tn(att_ref[...], branch_cot).astype(bf16)
+        pack = dot_tn(norm_ref[...], logit_cot)
+        lane = lax.broadcasted_iota(jnp.int32, pack.shape, 1)
+        pack_out[...] = jnp.where(
+            lane == experts, jnp.broadcast_to(gain_grad, (LANES, width)).T, pack
+        ).astype(bf16)
+        for copy in loads(list(zip((pack_out, mid_cot_out, wo_out), results)), out_sem):
+            copy.wait()
+        links.swap_wait("seq", give, heads_out, *sems)
+
+    hbm = pl.BlockSpec(memory_space=pl.ANY)
+    dma = pltpu.SemaphoreType.DMA
+    return pl.pallas_call(
+        kernel,
+        name="middle_exchange",
+        out_shape=[jax.ShapeDtypeStruct((devices, rows, cols), bf16)] + outs,
+        in_specs=[hbm] * 10,
+        out_specs=[hbm] * 4,
+        scratch_shapes=staged(ins)
+        + staged(outs)
+        + [pltpu.VMEM((devices, rows, cols), bf16), dma((10,)), dma((3,))]
+        + swap_sems(devices),
+        compiler_params=pltpu.CompilerParams(
+            collective_id=collective_id, has_side_effects=True, vmem_limit_bytes=60 << 20
+        ),
+    )(*ins)
+
+
+def finish(e_grads, grad_qkv, grad_wo, pack, input_grad, output, weights, gain, heads, experts):
+    parts, own_experts, e_rows, e_cols = e_grads.shape
+    devices, out_rows, _ = grad_qkv.shape
+    q_width = heads * HEAD_SIZE
+    share = devices // KEY_VALUE_HEADS if devices > KEY_VALUE_HEADS else 1
+    steps = 8
+    chunk = e_rows // steps
+    me = lax.axis_index("seq").astype(jnp.int32).reshape(1)
+
+    def kernel(
+        me_ref, e_ref, qkv_ref, wo_ref, pack_ref, in_ref, out_ref, wq, wk, wv, gain_ref,
+        e_in, e_out, gq, gk, gv, gwo, grouter, ggain_m, ggain_a, in_grad, output_ref,
+    ):
+        total = e_ref[0].astype(f32)
+        for p in range(1, parts):
+            total = total + e_ref[p].astype(f32)
+        e_in[...] = total[:, :, : 2 * FFE]
+        e_out[...] = total[:, :, 2 * FFE :]
+
+        @pl.when(pl.program_id(0) == 0)
+        def _():
+            blocks = [qkv_ref[j].astype(f32) for j in range(devices)]
+
+            def per_head(first):
+                heads_of = []
+                for j in range(KEY_VALUE_HEADS):
+                    part = blocks[j * share][:, first : first + HEAD_SIZE]
+                    for i in range(1, share):
+                        part = part + blocks[j * share + i][:, first : first + HEAD_SIZE]
+                    heads_of.append(part)
+                return jnp.concatenate(heads_of, axis=1)
+
+            grad_q = jnp.concatenate([b[:, :q_width] for b in blocks], axis=1)
+            grad_k = per_head(HEADS_LANES)
+            grad_v = per_head(HEADS_LANES + HEAD_SIZE)
+            gq[...], gk[...], gv[...] = grad_q, grad_k, grad_v
+
+            def rounded(ref):
+                return ref[...].astype(bf16).astype(f32)
+
+            def row(column):
+                return jnp.broadcast_to(column, (out_rows, LANES)).T[:1]
+
+            gain_grad = (
+                jnp.sum(rounded(wq) * grad_q, axis=1, keepdims=True)
+                + jnp.sum(rounded(wk) * grad_k, axis=1, keepdims=True)
+                + jnp.sum(rounded(wv) * grad_v, axis=1, keepdims=True)
+            )
+            own = lax.broadcasted_iota(jnp.int32, (devices, 1), 0) == me_ref[0]
+            own_gain = jnp.sum(jnp.where(own, rounded(gain_ref), 0.0), axis=0, keepdims=True)
+            ggain_a[...] = row(gain_grad) / own_gain
+            gwo[...] = wo_ref[...]
+            grouter[...] = pack_ref[:, :experts]
+            ggain_m[...] = row(pack_ref[:, experts : experts + 1])
+            in_grad[...] = in_ref[...]
+            output_ref[...] = out_ref[...]
+
+    def whole(x):
+        return pl.BlockSpec(x.shape, lambda i, _: (0,) * len(x.shape))
+
+    def own_rows(x):
+        return pl.BlockSpec((out_rows, x.shape[1]), lambda i, me_ref: (me_ref[0], 0))
+
+    def shape(*dims, dtype=f32):
+        return jax.ShapeDtypeStruct(dims, dtype)
+
+    rest = [grad_qkv, grad_wo, pack, input_grad, output]
+    kv_width = KEY_VALUE_HEADS * HEAD_SIZE
+    small = [
+        shape(out_rows, devices * q_width),
+        shape(out_rows, kv_width),
+        shape(out_rows, kv_width),
+        shape(*grad_wo.shape),
+        shape(out_rows, experts),
+        shape(1, out_rows),
+        shape(1, out_rows),
+        shape(*input_grad.shape, dtype=bf16),
+        shape(*output.shape, dtype=bf16),
+    ]
+    return pl.pallas_call(
+        kernel,
+        name="finish",
+        grid_spec=pltpu.PrefetchScalarGridSpec(
+            num_scalar_prefetch=1,
+            grid=(steps,),
+            in_specs=[pl.BlockSpec((parts, own_experts, chunk, e_cols), lambda i, _: (0, 0, i, 0))]
+            + [whole(x) for x in rest]
+            + [own_rows(x) for x in weights]
+            + [whole(gain)],
+            out_specs=[
+                pl.BlockSpec((own_experts, chunk, 2 * FFE), lambda i, _: (0, i, 0)),
+                pl.BlockSpec((own_experts, chunk, FFE), lambda i, _: (0, i, 0)),
+            ]
+            + [whole(x) for x in small],
+        ),
+        out_shape=[
+            shape(own_experts, e_rows, 2 * FFE),
+            shape(own_experts, e_rows, FFE),
+        ]
+        + small,
+        cost_estimate=pl.CostEstimate(flops=0, bytes_accessed=8 << 20, transcendentals=0),
+        compiler_params=pltpu.CompilerParams(
+            dimension_semantics=("arbitrary",), vmem_limit_bytes=48 << 20
+        ),
+    )(me, e_grads, *rest, *weights, gain)
+
+
+def first_exchange(collective_id, tokens, out_grad, docs, mask, misc, w_query, w_key, w_value, w_out):
+    devices, parts = lax.axis_size("seq"), lax.axis_size("dp")
+    w_rows, width = w_out.shape
+    heads = QUERY_HEADS // devices
+    q_width = heads * HEAD_SIZE
+    group = QUERY_HEADS // KEY_VALUE_HEADS
+    w_cols = HEADS_LANES + LANES
+    weights = [w_query, w_key, w_value, w_out]
+
+    def prepare(refs):
+        given, (wq, wk, wv, wo, w_all, wo_low, sem) = refs[:4], refs[4:]
+        for copy in loads(list(zip(given, (wq, wk, wv, wo))), sem):
+            copy.wait()
+        wo_low[...] = wo[...].astype(bf16)
+        for s in range(devices):
+            kv = s * heads // group * HEAD_SIZE
+            pieces = [wq[:, s * q_width : (s + 1) * q_width]]
+            if q_width < HEADS_LANES:
+                pieces.append(jnp.zeros((w_rows, HEADS_LANES - q_width), f32))
+            pieces += [wk[:, kv : kv + HEAD_SIZE], wv[:, kv : kv + HEAD_SIZE]]
+            w_all[s] = jnp.concatenate(pieces, axis=1).astype(bf16)
+
+    return exchange(
+        collective_id,
+        [
+            ("gather", "seq", tokens, None),
+            ("gather", "seq", docs, None),
+            ("gather", "seq", mask, None),
+            ("shift", "seq", out_grad, None),
+            ("share", "dp", misc, None),
+            ("gather", "dp", jax.ShapeDtypeStruct((w_rows, w_cols), bf16), 0),
+            ("share", "dp", jax.ShapeDtypeStruct((w_rows, width), bf16), 1),
+        ],
+        prepare=prepare,
+        given=weights,
+        work=staged(weights)
+        + [
+            pltpu.VMEM((devices, w_rows, w_cols), bf16),
+            pltpu.VMEM((w_rows, width), bf16),
+            pltpu.SemaphoreType.DMA((4,)),
+        ],
+        made=lambda refs: (refs[8].at[lax.axis_index("seq")], refs[9]),
+        keep=(jax.ShapeDtypeStruct((devices, w_rows, w_cols), bf16), 8),
+    )
 
 
 def final_exchange(
@@ -1039,25 +1447,28 @@
     wides = [x.shape[3] for x in token_grads]
     token_grads = [x.reshape(parts, chips, 2, out_rows, x.shape[3]) for x in token_grads]
 
+    ins = [w_full, tokens, mid_cot, gain, mid, *branches]
+
     def kernel(*refs):
         qkv_in, gq_in = refs[:2]
         gt_in = refs[2 : 2 + count]
-        w_in, tok_ref, mid_cot_ref, gain_ref, mid_ref = refs[2 + count : 7 + count]
-        y_refs = refs[7 + count : 7 + count + chips]
-        refs = refs[7 + count + chips :]
-        in_grad, output, gq_out = refs[:3]
+        given = refs[2 + count : 2 + count + len(ins)]
+        refs = refs[2 + count + len(ins) :]
+        in_grad_out, output_out, gq_out = refs[:3]
         gt_out = refs[3 : 3 + count]
         refs = refs[3 + count :]
         (
-            qkv_tok, w_all, nac, gq_recv, gq_sum,
-            q_send, q_recv, local, w_sem, gq_send, gq_rsem, gqz_send, gqz_recv, gq_local,
-        ) = refs[:14]
-        work = [refs[14 + 11 * i : 25 + 11 * i] for i in range(count)]
+            qkv_tok, nac, gq_recv, gq_sum,
+            q_send, q_recv, local, gq_send, gq_rsem, gqz_send, gqz_recv, gq_local,
+        ) = refs[:12]
+        work = [refs[12 + 11 * i : 23 + 11 * i] for i in range(count)]
+        refs = refs[12 + 11 * count :]
+        local_ins, (in_grad, output, in_sem, out_sem) = refs[: len(ins)], refs[len(ins) :]
+        w_all, tok_ref, mid_cot_ref, gain_ref, mid_ref, *y_refs = local_ins
         me, my = lax.axis_index("seq"), lax.axis_index("dp")
         chip, core = me // 2, lax.rem(me, 2)
         sibling = me + 1 - 2 * core
-        w_copy = pltpu.make_async_copy(w_in, w_all, w_sem)
-        w_copy.start()
+        arriving = loads(list(zip(given, local_ins)), in_sem)
         barrier = pltpu.get_barrier_semaphore()
         for axis, index, size in (("seq", me, devices), ("dp", my, parts)):
             for k in range(1, size):
@@ -1124,10 +1535,14 @@
                 copy.start()
                 sent.append(copy)
 
+        for copy in arriving:
+            copy.wait()
         total = y_refs[0][...].astype(f32)
-        for k in range(1, chips):
+        for k in range(1, len(branches)):
             total = total + y_refs[k][...].astype(f32)
         output[...] = (mid_ref[...] + res_mult * total).astype(bf16)
+        leaving = [pltpu.make_async_copy(output, output_out, out_sem.at[0])]
+        leaving[0].start()
 
         own_q.wait()
         for k in range(1, parts):
@@ -1170,18 +1585,16 @@
                 copy.start()
                 sent.append(copy)
 
-        own.wait()
-        w_copy.wait()
-        for k in range(1, devices):
+        for k in range(devices):
             frm = lax.rem(me + devices - k, devices)
-            remote(
-                "seq", qkv_in.at[frm], columns(frm), q_send.at[k - 1], q_recv.at[k - 1], frm
-            ).wait_recv()
-
-        @pl.loop(0, width // 256)
-        def _(j):
-            at = pl.multiple_of(j * 256, 256)
-            nac[:, pl.ds(at, 256)] = dot_nt(qkv_tok[...], w_all[pl.ds(at, 256), :])
+            if k == 0:
+                own.wait()
+            else:
+                remote(
+                    "seq", qkv_in.at[frm], columns(frm), q_send.at[k - 1], q_recv.at[k - 1], frm
+                ).wait_recv()
+            part = dot_nt(columns(frm)[...], w_all[frm])
+            nac[...] = part if k == 0 else nac[...] + part
 
         resid = tok_ref[...].astype(f32)
         scale = lax.rsqrt(jnp.mean(resid * resid, axis=-1, keepdims=True) + norm_eps)
@@ -1194,6 +1607,8 @@
             * jnp.mean(weighted * resid, axis=-1, keepdims=True)
         ).astype(bf16)
 
+        leaving.append(pltpu.make_async_copy(in_grad, in_grad_out, out_sem.at[1]))
+        leaving[1].start()
         for o, w in zip(gt_out, work):
             mine, theirs, far, near, last, sems, dp_send, dp_recv, z_send, z_recv, _ = w
             summed = near[chip].astype(f32)
@@ -1211,19 +1626,19 @@
             ).wait_recv()
         for copy in sent:
             copy.wait_send()
+        for copy in leaving:
+            copy.wait()
 
     hbm = pl.BlockSpec(memory_space=pl.ANY)
     vmem = pl.BlockSpec(memory_space=pltpu.VMEM)
     dma = pltpu.SemaphoreType.DMA
     scratch = [
         pltpu.VMEM((rows, devices * cols), bf16),
-        pltpu.VMEM(w_full.shape, bf16),
         pltpu.VMEM((rows, width), f32),
         pltpu.VMEM(grad_qkv.shape, bf16),
         pltpu.VMEM(grad_qkv.shape[1:], bf16),
         dma((devices - 1,)),
         dma((devices - 1,)),
-        dma,
         dma,
         dma((parts - 1,)),
         dma((parts - 1,)),
@@ -1246,6 +1661,12 @@
             dma((chips - 1,)),
             dma,
         ]
+    scratch += staged(ins) + [
+        pltpu.VMEM((rows, width), bf16),
+        pltpu.VMEM((rows, width), bf16),
+        dma((len(ins),)),
+        dma((2,)),
+    ]
     return pl.pallas_call(
         kernel,
         name="final_exchange",
@@ -1255,25 +1676,13 @@
             jax.ShapeDtypeStruct(grad_qkv.shape[1:], bf16),
         ]
         + [jax.ShapeDtypeStruct((out_rows, wide), f32) for wide in wides],
-        in_specs=[hbm] * (3 + count) + [vmem] * (4 + chips),
-        out_specs=[vmem] * (3 + count),
+        in_specs=[hbm] * (2 + count + len(ins)),
+        out_specs=[hbm] * 3 + [vmem] * count,
         scratch_shapes=scratch,
         compiler_params=pltpu.CompilerParams(
-            collective_id=collective_id, has_side_effects=True, vmem_limit_bytes=48 << 20
+            collective_id=collective_id, has_side_effects=True, vmem_limit_bytes=60 << 20
         ),
-    )(qkv_cot, grad_qkv, *token_grads, w_full, tokens, mid_cot, gain, mid, *branches)
-
-
-def rms_parts(values):
-    return lax.rsqrt(jnp.mean(values * values, axis=-1, keepdims=True) + norm_eps)
-
-
-def rms_pull(values, scale, gain, cot):
-    weighted = cot * gain
-    pulled = scale * weighted - values * (scale * scale * scale) * jnp.mean(
-        weighted * values, axis=-1, keepdims=True
-    )
-    return pulled, jnp.sum(cot * values * scale, axis=0)
+    )(qkv_cot, grad_qkv, *token_grads, *ins)
 
 
 def on_device(
@@ -1296,21 +1705,12 @@
     rows, width = tokens.shape[1:]
     length = rows * devices
     experts = w_router.shape[1]
-    own_experts = expert_in.shape[0]
     heads = QUERY_HEADS // devices
     group = QUERY_HEADS // KEY_VALUE_HEADS
-    share = max(1, group // heads)
     q_width = heads * HEAD_SIZE
     w_rows = w_query.shape[0]
 
-    wq = w_query.astype(bf16).reshape(w_rows, devices, q_width)
-    wq = jnp.pad(wq, ((0, 0), (0, 0), (0, HEADS_LANES - q_width)))
-    wk = key_weight_matrix.astype(bf16).reshape(w_rows, KEY_VALUE_HEADS, HEAD_SIZE)
-    wv = value_weight_matrix.astype(bf16).reshape(w_rows, KEY_VALUE_HEADS, HEAD_SIZE)
-    wkv = jnp.repeat(jnp.concatenate([wk, wv], axis=2), share, axis=1)
     w_cols = HEADS_LANES + LANES
-    w_all = jnp.concatenate([wq, wkv], axis=2).reshape(w_rows, devices * w_cols)
-    w_own = lax.dynamic_slice_in_dim(w_all, me * w_cols, w_cols, 1)
     misc = jnp.concatenate(
         [w_router, gain_attn[:, None], gain_moe[:, None]], axis=1
     ).astype(bf16)
@@ -1322,98 +1722,66 @@
 
     expert_in_full = lax.all_gather(expert_in.astype(bf16), "dp", axis=1, tiled=True)
     expert_out_full = lax.all_gather(expert_out.astype(bf16), "dp", axis=1, tiled=True)
-    w_full = lax.all_gather(w_all, "dp", axis=0, tiled=True)
-
     chips = devices // 2
 
     def shift(x, k):
         return lax.ppermute(x, "seq", [(i, (i + 2 * k) % devices) for i in range(devices)])
 
-    held = out_grad[0]
-    early = shift(held, 1)
-    tok_all, doc_all, mask_all, w_own_all, wo_full, misc_full = exchange(
+    tok_all, doc_all, mask_all, middle_cot, misc_full, w_own_all, wo_full, w_all = first_exchange(
         0,
-        [
-            ("gather", "seq", tokens[0], None),
-            ("gather", "seq", doc_rows, None),
-            ("gather", "seq", mask, None),
-            ("gather", "dp", w_own, None),
-            ("share", "dp", w_out.astype(bf16), None),
-            ("share", "dp", misc, None),
-        ],
-    )
-    tok_all, held, early = lax.optimization_barrier((tok_all, held, early))
-    cots = [held, early] + [shift(held, k) for k in range(2, chips)]
+        tokens[0],
+        out_grad[0],
+        doc_rows,
+        mask,
+        misc,
+        w_query,
+        key_weight_matrix,
+        value_weight_matrix,
+        w_out,
+    )
+    w_full = lax.all_gather(w_all, "dp", axis=1, tiled=True)
+    held, tok_all = lax.optimization_barrier((out_grad[0], tok_all))
+    cots = [held] + [
+        middle_cot if k == chips // 2 else shift(held, k) for k in range(1, chips)
+    ]
     w_own_all = w_own_all.reshape(width, w_cols)
     wo_full = wo_full.reshape(width, width)
     misc_full = misc_full.reshape(width, LANES)
     gain_a = misc_full[:, experts]
-    gain_m = misc_full[:, experts + 1].astype(f32)
+    gain_m = misc_full[:, experts + 1]
     docs = doc_all[:, 0]
     table = rope_table(devices, rows)
 
     normed_a, q_all, kv_all, attended_own, ot, lse = attend_forward(
         tok_all, w_own_all, gain_a[None], table, docs, heads
     )
-    wide = q_width % LANES == 0
-    (attended,) = exchange(
-        1, [("swap", "seq", attended_own, ("out", q_width) if wide else None)]
-    )
-    if not wide:
-        attended = attended.transpose(1, 0, 2).reshape(rows, devices * q_width)
-
-    resid = tokens[0].astype(f32)
-    mid = resid + res_mult * dot_nn(attended, wo_full)
-    mid_scale = rms_parts(mid)
-    normed_m = (mid * mid_scale * gain_m).astype(bf16)
+    attended, mid, normed_m = attended_exchange(
+        1, attended_own, tokens[0], wo_full, gain_m[None]
+    )
     (_, _, _, moe_sum, gate_cot, e_grads, *branches) = moe_exchange(
         2, normed_m, cots, mask_all, misc_full, expert_in_full, expert_out_full, parts
     )
-    middle = chips // 2
-    branches[middle] = shift(branches[middle], middle)
     e_grads = lax.all_to_all(e_grads, "dp", split_axis=0, concat_axis=0)
-    gate_cot = gate_cot[:, :own_experts].reshape(experts, rows)
-    logits = lax.dot_general(
-        misc_full[:, :experts], normed_m, (((0,), (1,)), ((), ())), preferred_element_type=f32
-    )
-    logits = jnp.where(mask[:, :experts].T > 0, logits, -jnp.inf)
-    my_gates = jnp.exp(logits - jnp.max(logits, axis=0, keepdims=True))
-    my_gates = my_gates / jnp.sum(my_gates, axis=0, keepdims=True)
-    pick_cot = my_gates * (gate_cot - jnp.sum(my_gates * gate_cot, axis=0, keepdims=True))
-    logit_cot = pick_cot.astype(bf16)
-    grad_router = dot_nn(logit_cot, normed_m).T
-    normed_m_cot = moe_sum + lax.dot_general(
-        logit_cot, misc_full[:, :experts], (((0,), (1,)), ((), ())), preferred_element_type=f32
-    )
-    pulled, grad_gain_m = rms_pull(mid, mid_scale, gain_m, normed_m_cot)
-    mid_cot = out_grad[0].astype(f32) + pulled
-    branch_cot = (res_mult * mid_cot).astype(bf16)
-    grad_wo = dot_tn(attended, branch_cot)
-    attended_cot = dot_nt(branch_cot, wo_full).astype(bf16)
-    if not wide:
-        attended_cot = attended_cot.reshape(rows, devices, q_width).transpose(1, 0, 2)
-    (heads_cot,) = exchange(
-        4, [("swap", "seq", attended_cot, ("in", q_width) if wide else None)]
-    )
-    others = [k for k in range(1, chips) if k != middle]
-    heads_cot, later = lax.optimization_barrier((heads_cot, [branches[k] for k in others]))
-    for k, branch in zip(others, later):
-        branches[k] = shift(branch, k)
-    qkv_cot = attend_backward(q_all, kv_all, heads_cot, ot, lse, table, docs, heads)
+    heads_cot, router_pack, mid_cot, grad_wo = middle_exchange(
+        4, moe_sum, gate_cot, normed_m, misc_full, mask, mid, out_grad[0], gain_m[None],
+        wo_full, attended, q_width,
+    )
+    heads_cot, branches = lax.optimization_barrier((heads_cot, branches))
+    branches = [
+        branches[0],
+        lax.ppermute(branches[1], "seq", [(i, i ^ 2) for i in range(devices)]),
+    ] + [shift(branches[1 + k], 2 * k) for k in range(1, chips // 2)]
+    qkv_cot, grad_qkv = attend_backward(
+        q_all, kv_all, heads_cot, ot, lse, table, docs, heads, normed_a
+    )
     qkv_cot, branches = lax.optimization_barrier((qkv_cot, branches))
-    grad_qkv = dot_tn(
-        normed_a.reshape(length, width), qkv_cot.reshape(length, w_cols)
-    ).astype(bf16)
-    router_pack = jnp.concatenate(
-        [grad_router, grad_gain_m[:, None], jnp.zeros((width, LANES - experts - 1), f32)], axis=1
-    ).astype(bf16)
     out_rows = w_rows // devices
     input_grad, output, grad_qkv, grad_wo, router_pack = final_exchange(
         5,
         qkv_cot,
         grad_qkv.reshape(parts, devices, out_rows, w_cols),
         [
-            grad_wo.astype(bf16).reshape(parts, devices, out_rows, width),
+            grad_wo.reshape(parts, devices, out_rows, width),
             router_pack.reshape(parts, devices, out_rows, LANES),
         ],
         w_full,
@@ -1423,30 +1791,25 @@
         mid,
         branches,
     )
+
+    (
+        grad_e_in, grad_e_out, grad_wq, grad_wk, grad_wv, grad_wo, grad_router, grad_gain_m,
+        grad_gain_a, input_grad, output,
+    ) = finish(
+        e_grads,
+        grad_qkv,
+        grad_wo,
+        router_pack,
+        input_grad,
+        output,
+        [w_query, key_weight_matrix, value_weight_matrix],
+        gain_attn.reshape(devices, out_rows),
+        heads,
+        experts,
+    )
     input_grad, output = input_grad[None], output[None]
-    grad_e_in = jnp.sum(e_grads[..., : 2 * FFE].astype(f32), axis=0)
-    grad_e_out = jnp.sum(e_grads[..., 2 * FFE :].astype(f32), axis=0)
-
-    grad_qkv = grad_qkv.astype(f32)
-    grad_wq = grad_qkv[:, :, :q_width].transpose(1, 0, 2).reshape(out_rows, devices * q_width)
-
-    def per_head(part):
-        part = part.reshape(devices // share, share, out_rows, HEAD_SIZE).sum(axis=1)
-        return part.transpose(1, 0, 2).reshape(out_rows, KEY_VALUE_HEADS * HEAD_SIZE)
-
-    grad_wk = per_head(grad_qkv[:, :, HEADS_LANES : HEADS_LANES + HEAD_SIZE])
-    grad_wv = per_head(grad_qkv[:, :, HEADS_LANES + HEAD_SIZE :])
-    grad_router = router_pack[:, :experts]
-    grad_gain_m = router_pack[:, experts]
-
-    def own_rows(weight):
-        return lax.dynamic_slice_in_dim(weight, me * out_rows, out_rows, 0).astype(bf16).astype(f32)
-
-    grad_gain_a = (
-        jnp.sum(own_rows(w_query) * grad_wq, axis=1)
-        + jnp.sum(own_rows(key_weight_matrix) * grad_wk, axis=1)
-        + jnp.sum(own_rows(value_weight_matrix) * grad_wv, axis=1)
-    ) / own_rows(gain_attn)
+    grad_gain_a = grad_gain_a.reshape(out_rows)
+    grad_gain_m = grad_gain_m.reshape(out_rows)
     return (
         output,
         input_grad,

time: 356 us -> 337 us (0.947)
  Pallas kernels: 255 us -> 287 us
  waiting for transfers between devices: 16.6 us -> 0.09 us
  other arithmetic: 20.5 us -> 6.57 us
  matrix products: 11.3 us -> 0 us
  local copies, waits for them, and re-layouts: 21.3 us -> 13.1 us
    pallas_call x0 -> x3, Pallas kernels: none -> 44.7 us  [the longest x1 19.7 us: attended_exchange(): pl.pallas_call(kernel, name='attended_exchange', out_shape=outs, in_specs...]
    pallas_call x3 -> x1, Pallas kernels: 88 us -> 54.4 us  [exchange(): pl.pallas_call(kernel, name=f'exchange{collective_id}', out_shape=out_sha...]
    ppermute x6 -> x3, waiting for transfers between devices: 16.6 us -> 0.01 us  [shift(): lax.ppermute(x, 'seq', [(i, (i + 2 * k) % devices) for i in range(devices)])]
    dot_general x7 -> x0, matrix products: 11.3 us -> none  [the longest x2 4.18 us: dot_tn(): lax.dot_general(a, b, (((0,), (0,)), ((), ())), preferred_element_type=f32)]
    reduce_sum x6 -> x0, other arithmetic: 10.8 us -> none  [the longest x1 4.63 us: on_device(): grad_e_in = jnp.sum(e_grads[..., :2 * FFE].astype(f32), axis=0)]
    unnamed x93 -> x44, local copies, waits for them, and re-layouts: 14.8 us -> 7.82 us
    pallas_call x1, Pallas kernels: 89.3 us -> 96 us  [moe_exchange(): pl.pallas_call(kernel, name='moe_exchange', out_shape=[jax.ShapeDtypeStru...]
    pallas_call x1, Pallas kernels: 37.5 us -> 44.1 us  [final_exchange(): pl.pallas_call(kernel, name='final_exchange', out_shape=[jax.ShapeDtypeSt...]
  transfers between devices with their start and end apart: 10 -> 8, of which waited for: 2 -> 0; matrix products, arithmetic and copies ran while one was open for 9% -> 3% of each run, Pallas kernels for 72% -> 84%
where the time goes in v5:
time: 337 us; the launch traced here: 334 us
  Pallas kernels  287 us (85%)
  between operations  14.1 us (4%)
  local copies, waits for them, and re-layouts  13.1 us (4%)
  starting transfers between devices  12.7 us (4%)
  other arithmetic  6.57 us (2%)
    pallas_call x1, Pallas kernels, moe_exchange(): pl.pallas_call(kernel, name='moe_exchange', out_shape=[jax.ShapeDtypeStru...  96 us
    pallas_call x1, Pallas kernels, exchange(): pl.pallas_call(kernel, name=f'exchange{collective_id}', out_shape=out_sha...  54.4 us
    pallas_call x1, Pallas kernels, final_exchange(): pl.pallas_call(kernel, name='final_exchange', out_shape=[jax.ShapeDtypeSt...  44.1 us
    pallas_call x1, Pallas kernels, attend_backward(): pl.pallas_call(kernel, name='attend_backward', grid_spec=grid_spec, out_s...  27.7 us
    pallas_call x1, Pallas kernels, attend_forward(): pl.pallas_call(kernel, name='attend_forward', grid_spec=grid_spec, out_sh...  20.2 us
    pallas_call x1, Pallas kernels, attended_exchange(): pl.pallas_call(kernel, name='attended_exchange', out_shape=outs, in_specs...  19.7 us
    pallas_call x1, Pallas kernels, middle_exchange(): pl.pallas_call(kernel, name='middle_exchange', out_shape=[jax.ShapeDtypeS...  17.3 us
    unnamed x44, local copies, waits for them, and re-layouts  7.82 us
  transfers between devices with their start and end apart: 8, of which 0 were waited for; matrix products, arithmetic and copies ran while one was open for 3% of the time, Pallas kernels for 84%

profile of v5, /device:TPU:13, one launch (start us, length us, event | category | flops | bytes accessed | tf_op | source)
XLA Modules:
  0.0 333.6 jit_solution(17022666643833989904)
XLA Ops:
  7.3 2.1 convert_element_type.19
  9.5 2.8 convert_element_type.18
  15.0 54.4 %exchange0.1 = (bf16[8,256,1024]{2,1,0:T(8,128)(2,1)}, s32[8,8,256]{2,1,0:T(8,128)}, bf16[8,256,128]{2,1,0:T(8,128)(2,1)}, bf16[256,1024]{1,0:T(8,128)(2,1)}, bf...) custom-call(bf16[256,1024]{1,0:T(8,128)(2,1)} %bitcast.20, ...), custom_call_target="tpu_custom_call" | custom-call | tf_op jit(solution)/shard_map/exchange0/pallas_call | solution.py:273
  69.4 2.2 collective-permute-start
  71.6 2.1 collective-permute-start.1
  73.8 0.8 slice.17.docs_ref
  74.6 1.4 slice_reduce_fusion
  78.0 20.2 %attend_forward.1 = (bf16[8,256,1024]{2,1,0:T(8,128)(2,1)}, bf16[8,256,128]{2,1,0:T(8,128)(2,1)}, bf16[8,256,128]{2,1,0:T(8,128)(2,1)}, bf16[8,256,128]{2,1,0:T(...) custom-call(s32[8]{0:T(128)} %convert_reduce_fusion.first_ref, bf16[8,256,1024]{2,1,0:T(8,128)(2,1)} %get-tuple-element.68.tok, ...), custom_call_target="tpu_custom_call" | custom-call | flops 3221225472 | bytes 16777216 | tf_op jit(solution)/shard_map/attend_forward/pallas_call | solution.py:453
  98.2 19.7 %attended_exchange.1 = (bf16[256,1024]{1,0:T(8,128)(2,1)}, f32[256,1024]{1,0:T(8,128)}, bf16[256,1024]{1,0:T(8,128)(2,1)}) custom-call(bf16[8,256,128]{2,1,0:T(8,128)(2,1)} %get-tuple-element.71.att_in, bf16[256,1024]{1,0:T(8,128)(2,1)} %bitcast.21, bf16[1024,1024]{1,0:T(8,128)(2,1)} %bitcast.18, bf16[1,1024]{1,0:T(2,128)(2,1)} %broadcast_in_dim_squeeze.5.refs_2_.refs_7_), custom_call_target="tpu_custom_call" | custom-call | tf_op jit(solution)/shard_map/attended_exchange/pallas_call | solution.py:1188
  118.0 0.8 copy-done.16
  118.7 0.8 copy-done.17
  119.6 96.0 %moe_exchange.1 = (bf16[2,8,256,1024]{3,2,1,0:T(8,128)(2,1)}, bf16[2,8,256,1024]{3,2,1,0:T(8,128)(2,1)}, bf16[2,8,256,512]{3,2,1,0:T(8,128)(2,1)}, f32[256,1024]...) custom-call(bf16[256,1024]{1,0:T(8,128)(2,1)} %get-tuple-element.73., ...), custom_call_target="tpu_custom_call" | custom-call | flops 38654705664 | bytes 41943040 | tf_op jit(solution)/shard_map/moe_exchange/pallas_call | solution.py:1030
  215.6 5.5 %all-to-all-start = ((bf16[4,2,256,1536]{3,2,1,0:T(8,128)(2,1)}), bf16[4,2,256,1536]{3,2,1,0:T(8,128)(2,1)}, u32[]{:S(2)}, u32[]{:S(2)}) async-start(bf16[4,2,256,1536]{3,2,1,0:T(8,128)(2,1)} %get-tuple-element.77), calls=%async_computation | async-start | bytes 12582912 | tf_op jit(solution)/shard_map/all_to_all | solution.py:1764
  221.1 17.3 %middle_exchange.1 = (bf16[8,256,128]{2,1,0:T(8,128)(2,1)}, bf16[1024,128]{1,0:T(8,128)(2,1)}, f32[256,1024]{1,0:T(8,128)}, bf16[1024,1024]{1,0:T(8,128)(2,1)}) custom-call(f32[256,1024]{1,0:T(8,128)} %get-tuple-element.80.refs_0_, f32[8,16,256]{2,1,0:T(8,128)} %get-tuple-element.81.refs_1_, bf16[256,1024]{1,0:T(8,128)(2,1)} %get-tuple-element.73.refs_0_.refs_2_, ...), custom_call_target="tpu_custom_call" | custom-call | tf_op jit(solution)/shard_map/middle_exchange/pallas_call | solution.py:1269
  238.5 2.7 collective-permute-start.3
  241.2 27.7 %attend_backward.1 = (bf16[8,256,256]{2,1,0:T(8,128)(2,1)}, bf16[1024,256]{1,0:T(8,128)(2,1)}) custom-call(s32[8]{0:T(128)} %convert_reduce_fusion.first_ref, bf16[8,256,128]{2,1,0:T(8,128)(2,1)} %get-tuple-element.78.q_ref, bf16[8,256,128]{2,1,0:T(8,128)(2,1)} %get-tuple-element.79.kv_ref, bf16[8,256,128]{2,1,0:T(8,128)(2,1)} %get-tuple-element.88.do_ref, ...), custom_call_target="tpu_custom_call" | custom-call | flops 5368709120 | bytes 4194304 | tf_op jit(solution)/shard_map/attend_backward/pallas_call | solution.py:581
  269.0 0.7 copy-done.9
  269.9 44.1 %final_exchange.1 = (bf16[256,1024]{1,0:T(8,128)(2,1)}, bf16[256,1024]{1,0:T(8,128)(2,1)}, bf16[8,32,256]{2,1,0:T(8,128)(2,1)}, f32[32,1024]{1,0:T(8,128)}, f32[32,128]{1,0:T(8,128)}) custom-call(bf16[8,256,256]{2,1,0:T(8,128)(2,1)} %get-tuple-element.96.refs_0_, bf16[4,8,32,256]{3,2,1,0:T(8,128)(2,1)} %bitcast.32, bf16[4,4,2,32,1024]{4,3,2,1,0:T(8,128)(2,1)} %bitcast.26, ...), custom_call_target="tpu_custom_call" | custom-call | tf_op jit(solution)/shard_map/final_exchange/pallas_call | solution.py:1670
  314.1 1.0 copy-done.3
  315.1 1.0 copy-done.4
  316.2 0.9 copy-done.5
  317.1 0.9 copy-done.6
  318.0 0.7 copy-done.7
  318.7 7.7 %finish.1 = (f32[2,256,1024]{2,1,0:T(8,128)}, f32[2,256,512]{2,1,0:T(8,128)}, f32[32,1024]{1,0:T(8,128)}, f32[32,512]{1,0:T(8,128)}, f32[32,512]{1,0:T(8,128)}, ...) custom-call(s32[1]{0:T(128)} %bitcast.me_ref, ...), custom_call_target="tpu_custom_call" | custom-call | bytes 8388608 | tf_op jit(solution)/shard_map/finish/pallas_call | solution.py:1364
  (68 shorter events, 5.9 us)
Async XLA Ops:
  7.2 5.1 %copy-start.13 = (s32[1,256,8]{1,2,0:T(8,128)S(1)}, s32[1,256,8]{1,2,0:T(8,128)}, u32[]{:S(2)}) copy-start(s32[1,256,8]{1,2,0:T(8,128)} %param.17) | copy-start | bytes 24580
  7.2 6.3 %copy-start.12 = (f32[256,16]{0,1:T(8,128)S(1)}, f32[256,16]{0,1:T(8,128)}, u32[]{:S(2)}) copy-start(f32[256,16]{0,1:T(8,128)} %param.22) | copy-start | bytes 49156
  7.2 6.3 %copy-start.15 = (f32[256]{0:T(256)S(1)}, f32[256]{0:T(256)}, u32[]{:S(2)}) copy-start(f32[256]{0:T(256)} %param.23) | copy-start | bytes 3076
  7.2 6.4 %copy-start.20 = (f32[256]{0:T(256)S(1)}, f32[256]{0:T(256)}, u32[]{:S(2)}) copy-start(f32[256]{0:T(256)} %param.24) | copy-start | bytes 3076
  7.2 7.2 %copy-start.14 = (s32[1,256]{1,0:T(1,128)S(1)}, s32[1,256]{1,0:T(1,128)}, u32[]{:S(2)}) copy-start(s32[1,256]{1,0:T(1,128)} %param.16) | copy-start | bytes 3076
  7.2 111.5 %all-gather.6.cloned.1.call-start = ((), (), s32[]{:S(2)}) async-start(), calls=%async_computation.2 | async-start | bytes 2621440 | tf_op jit(solution)/shard_map/all_gather | solution.py:1724
  9.4 60.0 %copy-start.8 = (bf16[1,256,1024]{2,1,0:T(8,128)(2,1)S(1)}, bf16[1,256,1024]{2,1,0:T(8,128)(2,1)}, u32[]{:S(2)}) copy-start(bf16[1,256,1024]{2,1,0:T(8,128)(2,1)} %param.15) | copy-start | bytes 1572868
  9.4 110.2 %all-gather.4.cloned.1.call-start = ((), (), s32[]{:S(2)}) async-start(), calls=%async_computation.1 | async-start | bytes 5242880 | tf_op jit(solution)/shard_map/all_gather | solution.py:1723
  12.2 256.7 %all-gather.8.cloned.1.call-start = ((), (), s32[]{:S(2)}) async-start(), calls=%async_computation.3 | async-start | bytes 5242880 | tf_op jit(solution)/shard_map/all_gather | solution.py:1742
  69.4 48.5 %collective-permute-start = (bf16[256,1024]{1,0:T(8,128)(2,1)S(1)}, bf16[256,1024]{1,0:T(8,128)(2,1)S(1)}, u32[]{:S(2)}, u32[]{:S(2)}) collective-permute-start(bf16[256,1024]{1,0:T(8,128)(2,1)S(1)} %bitcast.30), channel_id=1, source_target_pairs={{0,2},{1,3},{2,4},{3,5},{4,6},{5,7},{6,0},{7,1},{8,10},{9,11},{10,... | collective-permute-start | bytes 1572872 | tf_op jit(solution)/shard_map/ppermute | solution.py:1728
  71.6 46.4 %collective-permute-start.1 = (bf16[256,1024]{1,0:T(8,128)(2,1)S(1)}, bf16[256,1024]{1,0:T(8,128)(2,1)S(1)}, u32[]{:S(2)}, u32[]{:S(2)}) collective-permute-start(bf16[256,1024]{1,0:T(8,128)(2,1)S(1)} %bitcast.31), channel_id=1, source_target_pairs={{0,6},{1,7},{2,0},{3,1},{4,2},{5,3},{6,4},{7,5},{8,14},{9,15},{10,... | collective-permute-start | bytes 1572872 | tf_op jit(solution)/shard_map/ppermute | solution.py:1728
  74.6 3.4 %copy-start.11 = (s32[8,1,256]{2,1,0:T(1,128)}, s32[8,1,256]{2,1,0:T(1,128)S(1)}, u32[]{:S(2)}) copy-start(s32[8,1,256]{2,1,0:T(1,128)S(1)} %slice.17.docs_ref) | copy-start | bytes 24580
  215.6 98.5 %all-to-all-start = ((bf16[4,2,256,1536]{3,2,1,0:T(8,128)(2,1)}), bf16[4,2,256,1536]{3,2,1,0:T(8,128)(2,1)}, u32[]{:S(2)}, u32[]{:S(2)}) async-start(bf16[4,2,256,1536]{3,2,1,0:T(8,128)(2,1)} %get-tuple-element.77), calls=%async_computation | async-start | bytes 12582912 | tf_op jit(solution)/shard_map/all_to_all | solution.py:1764
  221.1 17.3 %copy-start.19 = (bf16[256,1024]{1,0:T(8,128)(2,1)S(1)}, bf16[256,1024]{1,0:T(8,128)(2,1)}, u32[]{:S(2)}) copy-start(bf16[256,1024]{1,0:T(8,128)(2,1)} %get-tuple-element.94) | copy-start | bytes 1572868
  221.1 17.4 %copy-start.18 = (bf16[256,1024]{1,0:T(8,128)(2,1)S(1)}, bf16[256,1024]{1,0:T(8,128)(2,1)}, u32[]{:S(2)}) copy-start(bf16[256,1024]{1,0:T(8,128)(2,1)} %get-tuple-element.95) | copy-start | bytes 1572868
  238.4 30.5 %collective-permute-start.2 = (bf16[256,1024]{1,0:T(8,128)(2,1)S(1)}, bf16[256,1024]{1,0:T(8,128)(2,1)S(1)}, u32[]{:S(2)}, u32[]{:S(2)}) collective-permute-start(bf16[256,1024]{1,0:T(8,128)(2,1)S(1)} %copy-done.19), channel_id=1, source_target_pairs={{0,2},{1,3},{2,0},{3,1},{4,6},{5,7},{6,4},{7,5},{8,10},{9,11},{10,... | collective-permute-start | bytes 1572872 | tf_op jit(solution)/shard_map/ppermute | solution.py:1772
  238.5 30.4 %collective-permute-start.3 = (bf16[256,1024]{1,0:T(8,128)(2,1)S(1)}, bf16[256,1024]{1,0:T(8,128)(2,1)S(1)}, u32[]{:S(2)}, u32[]{:S(2)}) collective-permute-start(bf16[256,1024]{1,0:T(8,128)(2,1)S(1)} %copy-done.18), channel_id=1, source_target_pairs={{0,4},{1,5},{2,6},{3,7},{4,0},{5,1},{6,2},{7,3},{8,12},{9,13},{10,... | collective-permute-start | bytes 1572872 | tf_op jit(solution)/shard_map/ppermute | solution.py:1728
  268.9 0.9 copy-start.10
  269.9 44.2 %copy-start = (f32[256,1024]{1,0:T(8,128)S(1)}, f32[256,1024]{1,0:T(8,128)}, u32[]{:S(2)}) copy-start(f32[256,1024]{1,0:T(8,128)} %wq.1) | copy-start | bytes 3145732
  269.9 44.2 %copy-start.1 = (f32[256,512]{1,0:T(8,128)S(1)}, f32[256,512]{1,0:T(8,128)}, u32[]{:S(2)}) copy-start(f32[256,512]{1,0:T(8,128)} %wk.1) | copy-start | bytes 1572868
  269.9 44.2 %copy-start.2 = (f32[256,512]{1,0:T(8,128)S(1)}, f32[256,512]{1,0:T(8,128)}, u32[]{:S(2)}) copy-start(f32[256,512]{1,0:T(8,128)} %wv.1) | copy-start | bytes 1572868
  314.1 1.0 copy-start.3
  315.1 1.0 copy-start.4
  316.2 0.9 copy-start.5
  (5 other events, 4.0 us)
Sparse Core Ops, SparseCore 0:
  9.9 49.4 all-gather.5
  61.8 52.7 all-gather.3
  116.5 52.5 all-gather.7

commit v6 on v5

--- a/solution.py
+++ b/solution.py
@@ -347,30 +347,38 @@
     return jnp.broadcast_to(row, (lanes, row.shape[1])).T
 
 
-def first_blocks(docs):
-    return jnp.sum(
-        (docs[:, -1][:, None] < docs[:, 0][None, :]).astype(jnp.int32), axis=0
-    )
+def first_block(docs_ref, i):
+    docs = docs_ref[:, 0, :].astype(f32)
+    own = lax.broadcasted_iota(jnp.int32, docs.shape, 0) == i
+    lane = lax.broadcasted_iota(jnp.int32, docs.shape, 1)
+    start = jnp.sum(jnp.where(own & (lane == 0), docs, 0.0))
+    ends = (lane == docs.shape[1] - 1) & (docs < start)
+    return jnp.sum(jnp.where(ends, 1.0, 0.0)).astype(jnp.int32)
 
 
 def stack_heads(x, heads):
     return jnp.concatenate(
         [x[:, h * HEAD_SIZE : (h + 1) * HEAD_SIZE] for h in range(heads)], axis=0
     )
+
+
+def gain_row(ref, which):
+    return jnp.concatenate(
+        [ref[p, which : which + 1, :] for p in range(ref.shape[0])], axis=1
+    ).astype(f32)
 
 
 def attend_forward(tok_all, w_own, gain, table, docs, heads):
     blocks, rows, width = tok_all.shape
     length = blocks * rows
     cols = heads * rows
-    first = first_blocks(docs)
     out_width = heads * HEAD_SIZE
 
-    def kernel(first_ref, tok, w, gain_ref, table_ref, docs_ref, na_ref, q_ref, kv_ref, att_ref, ot_ref, lse_ref, k_scr, vt_scr, doc_scr):
+    def kernel(tok, w, gain_ref, table_ref, docs_ref, na_ref, q_ref, kv_ref, att_ref, ot_ref, lse_ref, k_scr, vt_scr, doc_scr):
         i = pl.program_id(0)
         x = tok[0].astype(f32)
         scale = lax.rsqrt(jnp.mean(x * x, axis=-1, keepdims=True) + norm_eps)
-        na = (x * scale * gain_ref[...].astype(f32)).astype(bf16)
+        na = (x * scale * gain_row(gain_ref, 0)).astype(bf16)
         na_ref[0] = na
         qkv = dot_nn(na, w[...])
         c, s = spread_table(table_ref[0])
@@ -383,7 +391,7 @@
         k_scr[i] = kv[:, :HEAD_SIZE]
         vt_scr[i] = kv.astype(f32).T[HEAD_SIZE:].astype(bf16)
         q2 = stack_heads(q, heads)
-        doc_row = docs_ref[0].astype(f32)
+        doc_row = docs_ref[i, :1].astype(f32)
         doc_scr[i] = across_lanes(doc_row, LANES)
         doc_query = jnp.concatenate([doc_row] * heads, axis=1)
         query = i * rows + lax.rem(lax.broadcasted_iota(jnp.int32, (1, cols), 1), rows)
@@ -403,7 +411,7 @@
             return new_top, total, ot
 
         top, total, ot = lax.fori_loop(
-            first_ref[i],
+            first_block(docs_ref, i),
             i + 1,
             step,
             (
@@ -421,20 +429,20 @@
         ).astype(bf16)
 
     def block(shape):
-        return pl.BlockSpec((1,) + shape, lambda i, _: (i, 0, 0))
+        return pl.BlockSpec((1,) + shape, lambda i: (i, 0, 0))
 
     def whole(shape):
-        return pl.BlockSpec(shape, lambda i, _: (0,) * len(shape))
+        return pl.BlockSpec(shape, lambda i: (0,) * len(shape))
 
     grid_spec = pltpu.PrefetchScalarGridSpec(
-        num_scalar_prefetch=1,
+        num_scalar_prefetch=0,
         grid=(blocks,),
         in_specs=[
             block((rows, width)),
             whole(w_own.shape),
-            whole((1, width)),
+            whole(gain.shape),
             block((HEAD_SIZE, rows)),
-            block((1, rows)),
+            whole(docs.shape),
         ],
         out_specs=[
             block((rows, width)),
@@ -471,27 +479,24 @@
             dimension_semantics=("arbitrary",), vmem_limit_bytes=60 << 20
         ),
     )(
-        first,
         tok_all,
         w_own,
         gain,
         table,
-        docs[:, None],
-    )
-
-
-def attend_backward(q_all, kv_all, cot, ot, lse, table, docs, heads, normed):
+        docs,
+    )
+
+
+def attend_backward(q_all, kv_all, cot, ot, lse, table, docs, heads):
     blocks, rows, _ = q_all.shape
     length = blocks * rows
     cols = heads * rows
-    first = first_blocks(docs)
-
-    def kernel(first_ref, q_ref, kv_ref, do_ref, ot_ref, lse_ref, table_ref, docs_ref, normed_in, out_ref, grad_ref, dk_scr, dv_scr, dq_scr, doc_scr, normed_all, grad_scr, sem):
+
+    def kernel(q_ref, kv_ref, do_ref, ot_ref, lse_ref, table_ref, docs_ref, out_ref, dk_scr, dv_scr, dq_scr, doc_scr):
         i = pl.program_id(0)
 
         @pl.when(i == 0)
         def _():
-            pltpu.make_async_copy(normed_in, normed_all, sem).start()
             dk_scr[...] = jnp.zeros_like(dk_scr)
             dv_scr[...] = jnp.zeros_like(dv_scr)
 
@@ -499,14 +504,14 @@
         do2 = stack_heads(do_ref[0], heads)
         delta = jnp.sum(do2.astype(f32).T * ot_ref[0], axis=0, keepdims=True)
         log_total = lse_ref[0]
-        doc_row = docs_ref[0].astype(f32)
+        doc_row = docs_ref[i, :1].astype(f32)
         doc_scr[i] = across_lanes(doc_row, LANES)
         doc_query = jnp.concatenate([doc_row] * heads, axis=1)
         query = i * rows + lax.rem(lax.broadcasted_iota(jnp.int32, (1, cols), 1), rows)
         key_iota = lax.broadcasted_iota(jnp.int32, (rows, cols), 0)
         dq_scr[...] = jnp.zeros_like(dq_scr)
 
-        @pl.loop(first_ref[i], i + 1)
+        @pl.loop(first_block(docs_ref, i), i + 1)
         def _(j):
             kv = kv_ref[j]
             k, v = kv[:, :HEAD_SIZE], kv[:, HEAD_SIZE:]
@@ -531,9 +536,6 @@
 
         @pl.when(i == blocks - 1)
         def _():
-            pltpu.make_async_copy(normed_in, normed_all, sem).wait()
-            grad_scr[...] = jnp.zeros_like(grad_scr)
-
             @pl.loop(0, blocks)
             def _(j):
                 kv = jnp.concatenate([dk_scr[j] * att_mult, dv_scr[j]], axis=1)
@@ -541,18 +543,15 @@
                 c, s = spread_table(table_ref[j])
                 kv = jnp.where(lane < HEAD_SIZE, kv * c - turn(kv) * s, kv).astype(bf16)
                 out_ref[j, :, HEADS_LANES:] = kv
-                grad_scr[...] += dot_tn(normed_all[j], out_ref[j])
-
-            grad_ref[...] = grad_scr[...].astype(bf16)
 
     def block(shape):
-        return pl.BlockSpec((1,) + shape, lambda i, _: (i, 0, 0))
+        return pl.BlockSpec((1,) + shape, lambda i: (i, 0, 0))
 
     def whole(shape):
-        return pl.BlockSpec(shape, lambda i, _: (0,) * len(shape))
+        return pl.BlockSpec(shape, lambda i: (0,) * len(shape))
 
     grid_spec = pltpu.PrefetchScalarGridSpec(
-        num_scalar_prefetch=1,
+        num_scalar_prefetch=0,
         grid=(blocks,),
         in_specs=[
             block((rows, HEADS_LANES)),
@@ -561,31 +560,21 @@
             block((HEAD_SIZE, cols)),
             block((1, cols)),
             whole((blocks, HEAD_SIZE, rows)),
-            block((1, rows)),
-            pl.BlockSpec(memory_space=pl.ANY),
+            whole(docs.shape),
         ],
-        out_specs=[
-            whole((blocks, rows, HEADS_LANES + LANES)),
-            whole((normed.shape[2], HEADS_LANES + LANES)),
-        ],
+        out_specs=whole((blocks, rows, HEADS_LANES + LANES)),
         scratch_shapes=[
             pltpu.VMEM((blocks, rows, HEAD_SIZE), f32),
             pltpu.VMEM((blocks, rows, HEAD_SIZE), f32),
             pltpu.VMEM((cols, HEAD_SIZE), f32),
             pltpu.VMEM((blocks, rows, LANES), f32),
-            pltpu.VMEM(normed.shape, bf16),
-            pltpu.VMEM((normed.shape[2], HEADS_LANES + LANES), f32),
-            pltpu.SemaphoreType.DMA,
         ],
     )
     return pl.pallas_call(
         kernel,
         name="attend_backward",
         grid_spec=grid_spec,
-        out_shape=[
-            jax.ShapeDtypeStruct((blocks, rows, HEADS_LANES + LANES), bf16),
-            jax.ShapeDtypeStruct((normed.shape[2], HEADS_LANES + LANES), bf16),
-        ],
+        out_shape=jax.ShapeDtypeStruct((blocks, rows, HEADS_LANES + LANES), bf16),
         cost_estimate=pl.CostEstimate(
             flops=5 * length * length * cols // rows * 128,
             bytes_accessed=2 * length * 1024,
@@ -595,19 +584,17 @@
             dimension_semantics=("arbitrary",), vmem_limit_bytes=60 << 20
         ),
     )(
-        first,
         q_all,
         kv_all,
         cot,
         ot,
         lse,
         table,
-        docs[:, None],
-        normed,
-    )
-
-
-def moe_exchange(collective_id, normed, cots, mask, router, w_in, w_out, parts):
+        docs,
+    )
+
+
+def moe_exchange(collective_id, normed, cots, mask, router, w_in, w_out):
     devices = lax.axis_size("seq")
     chips = devices // 2
     rows, width = normed.shape
@@ -847,24 +834,24 @@
             def _():
                 gate_out[block] = gate_stage[block]
 
+        def hop(k, i):
+            for side in (-1, 1):
+                away = chip + side * k
+
+                @pl.when((k > 0) & (k < chips) & (away >= 0) & (away < chips))
+                def _(side=side, away=away):
+                    pass_on(away, i, me).wait_recv()
+
+                    @pl.when((chip - side >= 0) & (chip - side < chips))
+                    def _():
+                        pass_on(away, i, me - 2 * side).start()
+
+                    to_sibling(away, i).start()
+
         @pl.loop(0, chips)
         def _(k):
             b = order(chip, k)
-
-            for side in (-1, 1):
-                away = chip + side * k
-
-                for i in range(PIECES):
-
-                    @pl.when((k > 0) & (away >= 0) & (away < chips))
-                    def _(side=side, away=away, i=i):
-                        pass_on(away, i, me).wait_recv()
-                        to_sibling(away, i).start()
-
-                        @pl.when((chip - side >= 0) & (chip - side < chips))
-                        def _():
-                            pass_on(away, i, me - 2 * side).start()
-
+            hop(k, 1)
             for i in range(PIECES):
                 across(own_piece(i), b, 1 - core, i).wait_recv()
             remote(
@@ -873,6 +860,10 @@
 
             @pl.loop(0, 2)
             def _(h):
+                @pl.when(h == 1)
+                def _():
+                    hop(k + 1, 0)
+
                 compute(2 * b + lax.rem(core + 1 + h, 2), (k > 0) | (h > 0))
 
                 @pl.when(h == 0)
@@ -959,33 +950,28 @@
             y_pre[b] = (y_pre[b].astype(f32) + y_in[j].astype(f32)).astype(bf16)
             y_leave(b, 2 + j).start()
 
-        part_rows = width // parts
         leaving = []
         for e in range(own_experts):
             for j in range(width // rows):
                 i = e * (width // rows) + j
                 x_all[i] = gin[e, j * rows : (j + 1) * rows].astype(bf16)
                 g_all[i, :, :FFE] = gout[e, j * rows : (j + 1) * rows].astype(bf16)
-                for q in range(rows // part_rows):
-                    here = pl.ds(q * part_rows, part_rows)
-                    part = (j * rows + q * part_rows) // part_rows
-                    at = 2 * len(leaving)
-                    leaving.append(
-                        (
-                            pltpu.make_async_copy(
-                                x_all.at[i, here],
-                                g_out.at[part, e, :, pl.ds(0, 2 * FFE)],
-                                wg_sem.at[at],
-                            ),
-                            pltpu.make_async_copy(
-                                g_all.at[i, here, pl.ds(0, FFE)],
-                                g_out.at[part, e, :, pl.ds(2 * FFE, FFE)],
-                                wg_sem.at[at + 1],
-                            ),
-                        )
+                at = 2 * len(leaving)
+                here = pl.ds(j * rows, rows)
+                leaving.append(
+                    (
+                        pltpu.make_async_copy(
+                            x_all.at[i], g_out.at[e, here, pl.ds(0, 2 * FFE)], wg_sem.at[at]
+                        ),
+                        pltpu.make_async_copy(
+                            g_all.at[i, :, pl.ds(0, FFE)],
+                            g_out.at[e, here, pl.ds(2 * FFE, FFE)],
+                            wg_sem.at[at + 1],
+                        ),
                     )
-                    for copy in leaving[-1]:
-                        copy.start()
+                )
+                for copy in leaving[-1]:
+                    copy.start()
 
         @pl.loop(1, chips)
         def _(k):
@@ -1036,7 +1022,7 @@
             jax.ShapeDtypeStruct((own_experts, devices, rows, FFE), bf16),
             jax.ShapeDtypeStruct(block, f32),
             jax.ShapeDtypeStruct((devices, gate_rows, rows), f32),
-            jax.ShapeDtypeStruct((parts, own_experts, width // parts, 3 * FFE), bf16),
+            jax.ShapeDtypeStruct((own_experts, width, 3 * FFE), bf16),
         ]
         + [jax.ShapeDtypeStruct(block, bf16)] * (1 + chips // 2),
         in_specs=[hbm] * (1 + chips) + [vmem] * 2 + [hbm] * 2,
@@ -1079,7 +1065,7 @@
             dma((1 + chips // 2,)),
             dma((3, 2)),
             dma((2,)),
-            dma((2 * own_experts * max(parts, width // rows),)),
+            dma((2 * own_experts * (width // rows),)),
             dma((chips // 2 - 1,)),
             dma((chips // 2 - 1,)),
         ],
@@ -1179,7 +1165,7 @@
         mid = tok[...].astype(f32) + res_mult * dot_nn(attended, w_all[...])
         mid_ref[...] = mid
         scale = lax.rsqrt(jnp.mean(mid * mid, axis=-1, keepdims=True) + norm_eps)
-        norm_ref[...] = (mid * scale * gain_ref[...].astype(f32)).astype(bf16)
+        norm_ref[...] = (mid * scale * gain_row(gain_ref, 1)).astype(bf16)
         for copy in loads(list(zip((att_ref, mid_ref, norm_ref), results)), out_sem):
             copy.wait()
 
@@ -1242,7 +1228,7 @@
         mid = mid_ref[...]
         scale = lax.rsqrt(jnp.mean(mid * mid, axis=-1, keepdims=True) + norm_eps)
         gain_grad = jnp.sum(cot * mid * scale, axis=0, keepdims=True)
-        weighted = cot * gain_ref[...].astype(f32)
+        weighted = cot * gain_row(gain_ref, 1)
         mid_cot = (
             cot_ref[...].astype(f32)
             + scale * weighted
@@ -1283,11 +1269,11 @@
 
 
 def finish(e_grads, grad_qkv, grad_wo, pack, input_grad, output, weights, gain, heads, experts):
-    parts, own_experts, e_rows, e_cols = e_grads.shape
+    own_experts, e_rows, e_cols = e_grads.shape
     devices, out_rows, _ = grad_qkv.shape
     q_width = heads * HEAD_SIZE
     share = devices // KEY_VALUE_HEADS if devices > KEY_VALUE_HEADS else 1
-    steps = 8
+    steps = 4
     chunk = e_rows // steps
     me = lax.axis_index("seq").astype(jnp.int32).reshape(1)
 
@@ -1295,11 +1281,8 @@
         me_ref, e_ref, qkv_ref, wo_ref, pack_ref, in_ref, out_ref, wq, wk, wv, gain_ref,
         e_in, e_out, gq, gk, gv, gwo, grouter, ggain_m, ggain_a, in_grad, output_ref,
     ):
-        total = e_ref[0].astype(f32)
-        for p in range(1, parts):
-            total = total + e_ref[p].astype(f32)
-        e_in[...] = total[:, :, : 2 * FFE]
-        e_out[...] = total[:, :, 2 * FFE :]
+        e_in[...] = e_ref[:, :, : 2 * FFE].astype(f32)
+        e_out[...] = e_ref[:, :, 2 * FFE :].astype(f32)
 
         @pl.when(pl.program_id(0) == 0)
         def _():
@@ -1367,7 +1350,7 @@
         grid_spec=pltpu.PrefetchScalarGridSpec(
             num_scalar_prefetch=1,
             grid=(steps,),
-            in_specs=[pl.BlockSpec((parts, own_experts, chunk, e_cols), lambda i, _: (0, 0, i, 0))]
+            in_specs=[pl.BlockSpec((own_experts, chunk, e_cols), lambda i, _: (0, i, 0))]
             + [whole(x) for x in rest]
             + [own_rows(x) for x in weights]
             + [whole(gain)],
@@ -1384,12 +1367,12 @@
         + small,
         cost_estimate=pl.CostEstimate(flops=0, bytes_accessed=8 << 20, transcendentals=0),
         compiler_params=pltpu.CompilerParams(
-            dimension_semantics=("arbitrary",), vmem_limit_bytes=48 << 20
+            dimension_semantics=("arbitrary",), vmem_limit_bytes=60 << 20
         ),
     )(me, e_grads, *rest, *weights, gain)
 
 
-def first_exchange(collective_id, tokens, out_grad, docs, mask, misc, w_query, w_key, w_value, w_out):
+def first_exchange(collective_id, tokens, out_grad, docs, mask, misc, gains, w_query, w_key, w_value, w_out):
     devices, parts = lax.axis_size("seq"), lax.axis_size("dp")
     w_rows, width = w_out.shape
     heads = QUERY_HEADS // devices
@@ -1419,6 +1402,7 @@
             ("gather", "seq", mask, None),
             ("shift", "seq", out_grad, None),
             ("share", "dp", misc, None),
+            ("gather", "dp", gains, None),
             ("gather", "dp", jax.ShapeDtypeStruct((w_rows, w_cols), bf16), 0),
             ("share", "dp", jax.ShapeDtypeStruct((w_rows, width), bf16), 1),
         ],
@@ -1435,36 +1419,89 @@
     )
 
 
+def prepare(expert_in, expert_out, picks, docs, w_router, gain_attn, gain_moe):
+    own_experts, w_rows, _ = expert_in.shape
+    rows, experts = picks.shape[0], w_router.shape[1]
+    steps = 4
+    chunk = w_rows // steps
+
+    def kernel(
+        e_in, e_out, picks_ref, docs_ref, router, gain_a, gain_m, in_low, out_low, mask, docs_out, misc, gains
+    ):
+        in_low[...] = e_in[...].astype(bf16)
+        out_low[...] = e_out[...].astype(bf16)
+
+        @pl.when(pl.program_id(0) == 0)
+        def _():
+            lane = lax.broadcasted_iota(jnp.int32, (rows, LANES), 1)
+            chosen = picks_ref[:, :1] == lane
+            for k in range(1, TOP):
+                chosen = chosen | (picks_ref[:, k : k + 1] == lane)
+            mask[...] = jnp.where(chosen, 1.0, 0.0).astype(bf16)
+            docs_out[...] = jnp.broadcast_to(docs_ref[...], docs_out.shape)
+            misc[...] = jnp.concatenate(
+                [router[...], jnp.zeros((w_rows, LANES - experts), f32)], axis=1
+            ).astype(bf16)
+            upper = lax.broadcasted_iota(jnp.int32, (8, w_rows), 0) == 0
+            gains[...] = jnp.where(upper, gain_a[...], gain_m[...]).astype(bf16)
+
+    def whole(shape):
+        return pl.BlockSpec(shape, lambda i: (0,) * len(shape))
+
+    def part(x):
+        return pl.BlockSpec((own_experts, chunk, x.shape[2]), lambda i: (0, i, 0))
+
+    small = [picks, docs, w_router, gain_attn[None], gain_moe[None]]
+    outs = [
+        jax.ShapeDtypeStruct((rows, LANES), bf16),
+        jax.ShapeDtypeStruct((8, rows), jnp.int32),
+        jax.ShapeDtypeStruct((w_rows, LANES), bf16),
+        jax.ShapeDtypeStruct((8, w_rows), bf16),
+    ]
+    return pl.pallas_call(
+        kernel,
+        name="prepare",
+        grid=(steps,),
+        out_shape=[jax.ShapeDtypeStruct(x.shape, bf16) for x in (expert_in, expert_out)] + outs,
+        in_specs=[part(expert_in), part(expert_out)] + [whole(x.shape) for x in small],
+        out_specs=[part(expert_in), part(expert_out)] + [whole(x.shape) for x in outs],
+        compiler_params=pltpu.CompilerParams(
+            dimension_semantics=("arbitrary",), vmem_limit_bytes=60 << 20
+        ),
+    )(expert_in, expert_out, *small)
+
+
 def final_exchange(
-    collective_id, qkv_cot, grad_qkv, token_grads, w_full, tokens, mid_cot, gain, mid, branches
+    collective_id, qkv_cot, normed, token_grads, w_full, tokens, mid_cot, gain, mid, branches
 ):
     devices, parts = lax.axis_size("seq"), lax.axis_size("dp")
     chips = devices // 2
     _, rows, cols = qkv_cot.shape
     width = tokens.shape[1]
-    out_rows = grad_qkv.shape[2]
+    out_rows = token_grads[0].shape[2]
+    gq_shape = (parts, devices, out_rows, cols)
     count = len(token_grads)
     wides = [x.shape[3] for x in token_grads]
     token_grads = [x.reshape(parts, chips, 2, out_rows, x.shape[3]) for x in token_grads]
 
-    ins = [w_full, tokens, mid_cot, gain, mid, *branches]
+    ins = [w_full, normed, qkv_cot, tokens, mid_cot, gain, mid, *branches]
 
     def kernel(*refs):
-        qkv_in, gq_in = refs[:2]
-        gt_in = refs[2 : 2 + count]
-        given = refs[2 + count : 2 + count + len(ins)]
-        refs = refs[2 + count + len(ins) :]
+        qkv_in = refs[0]
+        gt_in = refs[1 : 1 + count]
+        given = refs[1 + count : 1 + count + len(ins)]
+        refs = refs[1 + count + len(ins) :]
         in_grad_out, output_out, gq_out = refs[:3]
         gt_out = refs[3 : 3 + count]
         refs = refs[3 + count :]
         (
-            qkv_tok, nac, gq_recv, gq_sum,
+            qkv_tok, nac, gq_in, grad, gq_recv, gq_sum,
             q_send, q_recv, local, gq_send, gq_rsem, gqz_send, gqz_recv, gq_local,
-        ) = refs[:12]
-        work = [refs[12 + 11 * i : 23 + 11 * i] for i in range(count)]
-        refs = refs[12 + 11 * count :]
+        ) = refs[:14]
+        work = [refs[14 + 11 * i : 25 + 11 * i] for i in range(count)]
+        refs = refs[14 + 11 * count :]
         local_ins, (in_grad, output, in_sem, out_sem) = refs[: len(ins)], refs[len(ins) :]
-        w_all, tok_ref, mid_cot_ref, gain_ref, mid_ref, *y_refs = local_ins
+        w_all, normed_all, qkv_all, tok_ref, mid_cot_ref, gain_ref, mid_ref, *y_refs = local_ins
         me, my = lax.axis_index("seq"), lax.axis_index("dp")
         chip, core = me // 2, lax.rem(me, 2)
         sibling = me + 1 - 2 * core
@@ -1503,15 +1540,6 @@
             copy.start()
             sent.append(copy)
             pltpu.make_async_copy(x.at[:, :, core], mine, sems.at[2]).start()
-        for k in range(1, parts):
-            to = lax.rem(my + k, parts)
-            copy = remote(
-                "dp", gq_in.at[to], gq_recv.at[my], gq_send.at[k - 1], gq_rsem.at[k - 1], to
-            )
-            copy.start()
-            sent.append(copy)
-        own_q = pltpu.make_async_copy(gq_in.at[my], gq_recv.at[my], gq_local)
-        own_q.start()
         own = pltpu.make_async_copy(qkv_in.at[me], columns(me), local)
         own.start()
         for k in range(1, devices):
@@ -1537,6 +1565,22 @@
 
         for copy in arriving:
             copy.wait()
+        grad[...] = jnp.zeros_like(grad)
+
+        @pl.loop(0, devices)
+        def _(j):
+            grad[...] += dot_tn(normed_all[j], qkv_all[j])
+
+        gq_in[...] = grad[...].astype(bf16).reshape(gq_shape)
+        for k in range(1, parts):
+            to = lax.rem(my + k, parts)
+            copy = remote(
+                "dp", gq_in.at[to], gq_recv.at[my], gq_send.at[k - 1], gq_rsem.at[k - 1], to
+            )
+            copy.start()
+            sent.append(copy)
+        own_q = pltpu.make_async_copy(gq_in.at[my], gq_recv.at[my], gq_local)
+        own_q.start()
         total = y_refs[0][...].astype(f32)
         for k in range(1, len(branches)):
             total = total + y_refs[k][...].astype(f32)
@@ -1598,7 +1642,7 @@
 
         resid = tok_ref[...].astype(f32)
         scale = lax.rsqrt(jnp.mean(resid * resid, axis=-1, keepdims=True) + norm_eps)
-        weighted = nac[...] * gain_ref[...].astype(f32)
+        weighted = nac[...] * gain_row(gain_ref, 0)
         in_grad[...] = (
             mid_cot_ref[...]
             + scale * weighted
@@ -1635,8 +1679,10 @@
     scratch = [
         pltpu.VMEM((rows, devices * cols), bf16),
         pltpu.VMEM((rows, width), f32),
-        pltpu.VMEM(grad_qkv.shape, bf16),
-        pltpu.VMEM(grad_qkv.shape[1:], bf16),
+        pltpu.VMEM(gq_shape, bf16),
+        pltpu.VMEM((width, cols), f32),
+        pltpu.VMEM(gq_shape, bf16),
+        pltpu.VMEM(gq_shape[1:], bf16),
         dma((devices - 1,)),
         dma((devices - 1,)),
         dma,
@@ -1673,16 +1719,16 @@
         out_shape=[
             jax.ShapeDtypeStruct((rows, width), bf16),
             jax.ShapeDtypeStruct((rows, width), bf16),
-            jax.ShapeDtypeStruct(grad_qkv.shape[1:], bf16),
+            jax.ShapeDtypeStruct(gq_shape[1:], bf16),
         ]
         + [jax.ShapeDtypeStruct((out_rows, wide), f32) for wide in wides],
-        in_specs=[hbm] * (2 + count + len(ins)),
+        in_specs=[hbm] * (1 + count + len(ins)),
         out_specs=[hbm] * 3 + [vmem] * count,
         scratch_shapes=scratch,
         compiler_params=pltpu.CompilerParams(
             collective_id=collective_id, has_side_effects=True, vmem_limit_bytes=60 << 20
         ),
-    )(qkv_cot, grad_qkv, *token_grads, *ins)
+    )(qkv_cot, *token_grads, *ins)
 
 
 def on_device(
@@ -1711,29 +1757,24 @@
     w_rows = w_query.shape[0]
 
     w_cols = HEADS_LANES + LANES
-    misc = jnp.concatenate(
-        [w_router, gain_attn[:, None], gain_moe[:, None]], axis=1
-    ).astype(bf16)
-    misc = jnp.pad(misc, ((0, 0), (0, LANES - experts - 2)))
-    mask = jnp.any(
-        expert_picks[0][:, :, None] == jnp.arange(LANES, dtype=jnp.int32), axis=1
-    ).astype(bf16)
-    doc_rows = jnp.broadcast_to(doc_ids, (8, rows))
-
-    expert_in_full = lax.all_gather(expert_in.astype(bf16), "dp", axis=1, tiled=True)
-    expert_out_full = lax.all_gather(expert_out.astype(bf16), "dp", axis=1, tiled=True)
+    in_low, out_low, mask, doc_rows, misc, gains = prepare(
+        expert_in, expert_out, expert_picks[0], doc_ids, w_router, gain_attn, gain_moe
+    )
+    expert_in_full = lax.all_gather(in_low, "dp", axis=1, tiled=True)
+    expert_out_full = lax.all_gather(out_low, "dp", axis=1, tiled=True)
     chips = devices // 2
 
     def shift(x, k):
         return lax.ppermute(x, "seq", [(i, (i + 2 * k) % devices) for i in range(devices)])
 
-    tok_all, doc_all, mask_all, middle_cot, misc_full, w_own_all, wo_full, w_all = first_exchange(
+    tok_all, doc_all, mask_all, middle_cot, misc_full, gains_full, w_own_all, wo_full, w_all = first_exchange(
         0,
         tokens[0],
         out_grad[0],
         doc_rows,
         mask,
         misc,
+        gains,
         w_query,
         key_weight_matrix,
         value_weight_matrix,
@@ -1747,23 +1788,20 @@
     w_own_all = w_own_all.reshape(width, w_cols)
     wo_full = wo_full.reshape(width, width)
     misc_full = misc_full.reshape(width, LANES)
-    gain_a = misc_full[:, experts]
-    gain_m = misc_full[:, experts + 1]
-    docs = doc_all[:, 0]
     table = rope_table(devices, rows)
 
     normed_a, q_all, kv_all, attended_own, ot, lse = attend_forward(
-        tok_all, w_own_all, gain_a[None], table, docs, heads
+        tok_all, w_own_all, gains_full, table, doc_all, heads
     )
     attended, mid, normed_m = attended_exchange(
-        1, attended_own, tokens[0], wo_full, gain_m[None]
+        1, attended_own, tokens[0], wo_full, gains_full
     )
     (_, _, _, moe_sum, gate_cot, e_grads, *branches) = moe_exchange(
-        2, normed_m, cots, mask_all, misc_full, expert_in_full, expert_out_full, parts
-    )
-    e_grads = lax.all_to_all(e_grads, "dp", split_axis=0, concat_axis=0)
+        2, normed_m, cots, mask_all, misc_full, expert_in_full, expert_out_full
+    )
+    e_grads = lax.psum_scatter(e_grads, "dp", scatter_dimension=1, tiled=True)
     heads_cot, router_pack, mid_cot, grad_wo = middle_exchange(
-        4, moe_sum, gate_cot, normed_m, misc_full, mask, mid, out_grad[0], gain_m[None],
+        4, moe_sum, gate_cot, normed_m, misc_full, mask, mid, out_grad[0], gains_full,
         wo_full, attended, q_width,
     )
     heads_cot, branches = lax.optimization_barrier((heads_cot, branches))
@@ -1771,15 +1809,13 @@
         branches[0],
         lax.ppermute(branches[1], "seq", [(i, i ^ 2) for i in range(devices)]),
     ] + [shift(branches[1 + k], 2 * k) for k in range(1, chips // 2)]
-    qkv_cot, grad_qkv = attend_backward(
-        q_all, kv_all, heads_cot, ot, lse, table, docs, heads, normed_a
-    )
+    qkv_cot = attend_backward(q_all, kv_all, heads_cot, ot, lse, table, doc_all, heads)
     qkv_cot, branches = lax.optimization_barrier((qkv_cot, branches))
     out_rows = w_rows // devices
     input_grad, output, grad_qkv, grad_wo, router_pack = final_exchange(
         5,
         qkv_cot,
-        grad_qkv.reshape(parts, devices, out_rows, w_cols),
+        normed_a,
         [
             grad_wo.reshape(parts, devices, out_rows, width),
             router_pack.reshape(parts, devices, out_rows, LANES),
@@ -1787,7 +1823,7 @@
         w_full,
         tokens[0],
         mid_cot,
-        gain_a[None],
+        gains_full,
         mid,
         branches,
     )

time: 337 us -> 324 us (0.961)
  starting transfers between devices: 12.7 us -> 5.75 us
  other arithmetic: 6.57 us -> 0 us
  local copies, waits for them, and re-layouts: 13.1 us -> 6.75 us
  Pallas kernels: 287 us -> 293 us
    pallas_call x1, Pallas kernels: 44.1 us -> 51.4 us  [final_exchange(): pl.pallas_call(kernel, name='final_exchange', out_shape=[jax.ShapeDtypeSt...]
    all_to_all x1 -> x0, starting transfers between devices: 5.53 us -> none  [on_device(): e_grads = lax.all_to_all(e_grads, 'dp', split_axis=0, concat_axis=0)]
    convert_element_type x3 -> x0, other arithmetic: 5.51 us -> none  [the longest x1 2.77 us: on_device(): expert_in.astype(bf16)]
    pallas_call x0 -> x1, Pallas kernels: none -> 4.42 us  [prepare(): pl.pallas_call(kernel, name='prepare', grid=(steps,), out_shape=[jax.Shap...]
    unnamed x44 -> x17, local copies, waits for them, and re-layouts: 7.82 us -> 6.08 us
  transfers between devices with their start and end apart: 8 -> 8, of which waited for: 0 -> 1; matrix products, arithmetic and copies ran while one was open for 3% -> 0% of each run, Pallas kernels for 84% -> 88%
where the time goes in v6:
time: 324 us; the launch traced here: 321 us
  Pallas kernels  293 us (90%)
  between operations  13.9 us (4%)
  local copies, waits for them, and re-layouts  6.75 us (2%)
  starting transfers between devices  5.75 us (2%)
    pallas_call x1, Pallas kernels, moe_exchange(): pl.pallas_call(kernel, name='moe_exchange', out_shape=[jax.ShapeDtypeStru...  93.1 us
    pallas_call x1, Pallas kernels, exchange(): pl.pallas_call(kernel, name=f'exchange{collective_id}', out_shape=out_sha...  54.6 us
    pallas_call x1, Pallas kernels, final_exchange(): pl.pallas_call(kernel, name='final_exchange', out_shape=[jax.ShapeDtypeSt...  51.4 us
    pallas_call x1, Pallas kernels, attend_backward(): pl.pallas_call(kernel, name='attend_backward', grid_spec=grid_spec, out_s...  25.1 us
    pallas_call x1, Pallas kernels, attended_exchange(): pl.pallas_call(kernel, name='attended_exchange', out_shape=outs, in_specs...  20.2 us
    pallas_call x1, Pallas kernels, attend_forward(): pl.pallas_call(kernel, name='attend_forward', grid_spec=grid_spec, out_sh...  20.1 us
    pallas_call x1, Pallas kernels, middle_exchange(): pl.pallas_call(kernel, name='middle_exchange', out_shape=[jax.ShapeDtypeS...  18.4 us
  transfers between devices with their start and end apart: 8, of which 1 were waited for; matrix products, arithmetic and copies ran while one was open for 0% of the time, Pallas kernels for 88%

profile of v6, /device:TPU:13, one launch (start us, length us, event | category | flops | bytes accessed | tf_op | source)
XLA Modules:
  0.0 321.1 jit_solution(13454729987901214389)
XLA Ops:
  7.2 1.5 copy.25
  8.7 1.5 copy.26.router
  10.2 4.4 %prepare.1 = (bf16[2,256,1024]{2,1,0:T(8,128)(2,1)}, bf16[2,256,512]{2,1,0:T(8,128)(2,1)}, bf16[256,128]{1,0:T(8,128)(2,1)}, s32[8,256]{1,0:T(8,128)}, bf16[256,128]{1,0:T(8,128)(2,1)}, /*index=5*/bf16[8,256]{1,0:T(8,128)(2,1)}) custom-call(f32[2,256,1024]{2,1,0:T(8,128)} %e_in.1, f32[2,256,512]{2,1,0:T(8,128)} %e_out.1, s32[256,8]{1,0:T(8,128)} %bitcast.26, ...), custom_call_target="tpu_custom_call" | custom-call | tf_op jit(solution)/shard_map/prepare/pallas_call | solution.py:1461
  14.6 0.0 all-gather.4.cloned.1.call-start
  14.7 0.7 all-gather.4.cloned.1.call-update
  15.4 54.6 %exchange0.1 = (bf16[8,256,1024]{2,1,0:T(8,128)(2,1)}, s32[8,8,256]{2,1,0:T(8,128)}, bf16[8,256,128]{2,1,0:T(8,128)(2,1)}, bf16[256,1024]{1,0:T(8,128)(2,1)}, bf...) custom-call(bf16[256,1024]{1,0:T(8,128)(2,1)} %bitcast.17, ...), custom_call_target="tpu_custom_call" | custom-call | tf_op jit(solution)/shard_map/exchange0/pallas_call | solution.py:273
  70.1 0.0 reduce-scatter.2.cloned.1.call-start
  70.1 2.1 collective-permute-start
  72.3 2.1 collective-permute-start.1
  74.4 20.1 %attend_forward.1 = (bf16[8,256,1024]{2,1,0:T(8,128)(2,1)}, bf16[8,256,128]{2,1,0:T(8,128)(2,1)}, bf16[8,256,128]{2,1,0:T(8,128)(2,1)}, bf16[8,256,128]{2,1,0:T(...) custom-call(bf16[8,256,1024]{2,1,0:T(8,128)(2,1)} %get-tuple-element.76.tok, bf16[1024,256]{1,0:T(8,128)(2,1)} %bitcast.32, ...), custom_call_target="tpu_custom_call" | custom-call | flops 3221225472 | bytes 16777216 | tf_op jit(solution)/shard_map/attend_forward/pallas_call | solution.py:461
  94.5 20.2 %attended_exchange.1 = (bf16[256,1024]{1,0:T(8,128)(2,1)}, f32[256,1024]{1,0:T(8,128)}, bf16[256,1024]{1,0:T(8,128)(2,1)}) custom-call(bf16[8,256,128]{2,1,0:T(8,128)(2,1)} %get-tuple-element.80.att_in, bf16[256,1024]{1,0:T(8,128)(2,1)} %bitcast.18, bf16[1024,1024]{1,0:T(8,128)(2,1)} %bitcast.15, ...), custom_call_target="tpu_custom_call" | custom-call | tf_op jit(solution)/shard_map/attended_exchange/pallas_call | solution.py:1174
  114.7 0.8 copy-done.6
  115.5 1.3 all-gather.4.cloned.1.call-done.refs_7_
  116.8 93.1 %moe_exchange.1 = (bf16[2,8,256,1024]{3,2,1,0:T(8,128)(2,1)}, bf16[2,8,256,1024]{3,2,1,0:T(8,128)(2,1)}, bf16[2,8,256,512]{3,2,1,0:T(8,128)(2,1)}, f32[256,1024]...) custom-call(bf16[256,1024]{1,0:T(8,128)(2,1)} %get-tuple-element.82., ...), custom_call_target="tpu_custom_call" | custom-call | flops 38654705664 | bytes 41943040 | tf_op jit(solution)/shard_map/moe_exchange/pallas_call | solution.py:1016
  210.0 18.4 %middle_exchange.1 = (bf16[8,256,128]{2,1,0:T(8,128)(2,1)}, bf16[1024,128]{1,0:T(8,128)(2,1)}, f32[256,1024]{1,0:T(8,128)}, bf16[1024,1024]{1,0:T(8,128)(2,1)}) custom-call(f32[256,1024]{1,0:T(8,128)} %get-tuple-element.92.refs_0_, f32[8,16,256]{2,1,0:T(8,128)} %get-tuple-element.93.refs_1_, bf16[256,1024]{1,0:T(8,128)(2,1)} %get-tuple-element.82.refs_0_.refs_2_, ...), custom_call_target="tpu_custom_call" | custom-call | tf_op jit(solution)/shard_map/middle_exchange/pallas_call | solution.py:1255
  228.4 0.1 collective-permute-start.2
  228.5 1.3 collective-permute-start.3
  229.7 0.7 reshape.47.gain_ref
  230.4 25.1 %attend_backward.1.refs_0_.refs_5_ = bf16[8,256,256]{2,1,0:T(8,128)(2,1)} custom-call(bf16[8,256,128]{2,1,0:T(8,128)(2,1)} %get-tuple-element.90.q_ref, bf16[8,256,128]{2,1,0:T(8,128)(2,1)} %get-tuple-element.91.kv_ref, bf16[8,256,128]{2,1,0:T(8,128)(2,1)} %get-tuple-element.100.do_ref, f32[8,64,512]{2,1,0:T(8,128)} %get-tuple-element.101.ot_ref, ...), custom_call_target="tpu_custom_call" | custom-call | flops 5368709120 | bytes 4194304 | tf_op jit(solution)/shard_map/attend_backward/pallas_call | solution.py:573
  255.6 0.7 copy-done.1
  256.3 0.2 copy-done.2
  256.5 51.4 %final_exchange.1 = (bf16[256,1024]{1,0:T(8,128)(2,1)}, bf16[256,1024]{1,0:T(8,128)(2,1)}, bf16[8,32,256]{2,1,0:T(8,128)(2,1)}, f32[32,1024]{1,0:T(8,128)}, f32[32,128]{1,0:T(8,128)}) custom-call(bf16[8,256,256]{2,1,0:T(8,128)(2,1)} %attend_backward.1.refs_0_.refs_5_, bf16[4,4,2,32,1024]{4,3,2,1,0:T(8,128)(2,1)} %bitcast.20, ...), custom_call_target="tpu_custom_call" | custom-call | tf_op jit(solution)/shard_map/final_exchange/pallas_call | solution.py:1716
  308.0 5.2 %finish.1 = (f32[2,256,1024]{2,1,0:T(8,128)}, f32[2,256,512]{2,1,0:T(8,128)}, f32[32,1024]{1,0:T(8,128)}, f32[32,512]{1,0:T(8,128)}, f32[32,512]{1,0:T(8,128)}, ...) custom-call(s32[1]{0:T(128)} %bitcast.me_ref, ...), custom_call_target="tpu_custom_call" | custom-call | bytes 8388608 | tf_op jit(solution)/shard_map/finish/pallas_call | solution.py:1347
  313.1 1.4 copy.27
  (23 shorter events, 0.2 us)
Async XLA Ops:
  7.2 108.3 %all-gather.6.cloned.1.call-start = ((), (), s32[]{:S(2)}) async-start(), calls=%async_computation.2 | async-start | bytes 2621440 | tf_op jit(solution)/shard_map/all_gather | solution.py:1764
  14.6 55.5 %copy-start = (bf16[1,256,1024]{2,1,0:T(8,128)(2,1)S(1)}, bf16[1,256,1024]{2,1,0:T(8,128)(2,1)}, u32[]{:S(2)}) copy-start(bf16[1,256,1024]{2,1,0:T(8,128)(2,1)} %param.15) | copy-start | bytes 1572868
  14.6 102.2 %all-gather.4.cloned.1.call-start = ((), (), s32[]{:S(2)}) async-start(), calls=%async_computation.1 | async-start | bytes 5242880 | tf_op jit(solution)/shard_map/all_gather | solution.py:1763
  15.4 240.2 %all-gather.8.cloned.1.call-start = ((), (), s32[]{:S(2)}) async-start(), calls=%async_computation.4 | async-start | bytes 5242880 | tf_op jit(solution)/shard_map/all_gather | solution.py:1783
  70.1 237.9 %reduce-scatter.2.cloned.1.call-start = ((), (), s32[]{:S(2)}) async-start(), calls=%async_computation.3 | async-start | bytes 7864320 | tf_op jit(solution)/shard_map/reduce_scatter | solution.py:1802
  70.1 44.5 %collective-permute-start = (bf16[256,1024]{1,0:T(8,128)(2,1)S(1)}, bf16[256,1024]{1,0:T(8,128)(2,1)S(1)}, u32[]{:S(2)}, u32[]{:S(2)}) collective-permute-start(bf16[256,1024]{1,0:T(8,128)(2,1)S(1)} %bitcast.24), channel_id=1, source_target_pairs={{0,2},{1,3},{2,4},{3,5},{4,6},{5,7},{6,0},{7,1},{8,10},{9,11},{10,... | collective-permute-start | bytes 1572872 | tf_op jit(solution)/shard_map/ppermute | solution.py:1768
  72.3 43.2 %collective-permute-start.1 = (bf16[256,1024]{1,0:T(8,128)(2,1)S(1)}, bf16[256,1024]{1,0:T(8,128)(2,1)}, u32[]{:S(2)}, u32[]{:S(2)}) collective-permute-start(bf16[256,1024]{1,0:T(8,128)(2,1)S(1)} %bitcast.25), channel_id=1, source_target_pairs={{0,6},{1,7},{2,0},{3,1},{4,2},{5,3},{6,4},{7,5},{8,14},{9,15},{10,... | collective-permute-start | bytes 1572872 | tf_op jit(solution)/shard_map/ppermute | solution.py:1768
  114.7 0.8 copy-start.6
  210.0 18.4 %copy-start.5 = (bf16[256,1024]{1,0:T(8,128)(2,1)S(1)}, bf16[256,1024]{1,0:T(8,128)(2,1)}, u32[]{:S(2)}) copy-start(bf16[256,1024]{1,0:T(8,128)(2,1)} %get-tuple-element.104) | copy-start | bytes 1572868
  210.0 18.5 %copy-start.4 = (bf16[256,1024]{1,0:T(8,128)(2,1)S(1)}, bf16[256,1024]{1,0:T(8,128)(2,1)}, u32[]{:S(2)}) copy-start(bf16[256,1024]{1,0:T(8,128)(2,1)} %get-tuple-element.105) | copy-start | bytes 1572868
  210.0 19.8 %copy-start.3 = (f32[256]{0:T(256)S(1)}, f32[256]{0:T(256)}, u32[]{:S(2)}) copy-start(f32[256]{0:T(256)} %param.23) | copy-start | bytes 3076
  228.4 27.1 %collective-permute-start.2 = (bf16[256,1024]{1,0:T(8,128)(2,1)S(1)}, bf16[256,1024]{1,0:T(8,128)(2,1)S(1)}, u32[]{:S(2)}, u32[]{:S(2)}) collective-permute-start(bf16[256,1024]{1,0:T(8,128)(2,1)S(1)} %copy-done.5), channel_id=1, source_target_pairs={{0,2},{1,3},{2,0},{3,1},{4,6},{5,7},{6,4},{7,5},{8,10},{9,11},{10,... | collective-permute-start | bytes 1572872 | tf_op jit(solution)/shard_map/ppermute | solution.py:1810
  228.5 27.1 %collective-permute-start.3 = (bf16[256,1024]{1,0:T(8,128)(2,1)S(1)}, bf16[256,1024]{1,0:T(8,128)(2,1)S(1)}, u32[]{:S(2)}, u32[]{:S(2)}) collective-permute-start(bf16[256,1024]{1,0:T(8,128)(2,1)S(1)} %copy-done.4), channel_id=1, source_target_pairs={{0,4},{1,5},{2,6},{3,7},{4,0},{5,1},{6,2},{7,3},{8,12},{9,13},{10,... | collective-permute-start | bytes 1572872 | tf_op jit(solution)/shard_map/ppermute | solution.py:1768
  255.5 0.8 copy-start.1
  255.6 0.9 copy-start.2
Sparse Core Ops, SparseCore 0:
  14.8 46.8 all-gather.5
  64.1 52.7 all-gather.3
  118.7 52.6 all-gather.7
  210.1 85.7 reduce-scatter.1

commit v7 on v6

--- a/solution.py
+++ b/solution.py
@@ -594,11 +594,11 @@
     )
 
 
-def moe_exchange(collective_id, normed, cots, mask, router, w_in, w_out):
+def moe_exchange(collective_id, normed, cots, mask, router, weights):
     devices = lax.axis_size("seq")
     chips = devices // 2
     rows, width = normed.shape
-    own_experts = w_in.shape[0]
+    own_experts = weights.shape[0]
     gate_rows = devices * own_experts
 
     def order(chip, k):
@@ -609,9 +609,9 @@
 
     def kernel(*refs):
         x_in, g_in = refs[0], refs[1 : 1 + chips]
-        mask_ref, router_ref, win_in, wout_in = refs[1 + chips : 5 + chips]
-        (lin_out, slot_out, hid_out, n_sum, gate_out, g_out) = refs[5 + chips : 11 + chips]
-        y_outs = refs[11 + chips : 12 + chips + chips // 2]
+        mask_ref, router_ref, w_given = refs[1 + chips : 4 + chips]
+        (lin_out, slot_out, hid_out, n_sum, gate_out, g_out) = refs[4 + chips : 10 + chips]
+        y_outs = refs[10 + chips : 11 + chips + chips // 2]
         (
             x_all, g_all, win, wout, y_acc, n_acc, gate_acc, gate_stage,
             n_mine, n_far, n_give, n_theirs, y_give, y_theirs, y_pre, y_in,
@@ -619,12 +619,16 @@
             local, line_send, line_recv, sib_send, sib_recv, g_local, g_send, g_recv,
             n_send, n_recv, y_send, y_recv, far_send, far_recv, gate_send, gate_recv,
             st_sem, y_sem, ld_sem, w_sem, wg_sem, hand_send, hand_recv,
-        ) = refs[12 + chips + chips // 2 :]
+        ) = refs[11 + chips + chips // 2 :]
         me = lax.axis_index("seq")
         chip, core = me // 2, lax.rem(me, 2)
         sibling = me + 1 - 2 * core
-        win_copy = pltpu.make_async_copy(win_in, win, w_sem.at[0])
-        wout_copy = pltpu.make_async_copy(wout_in, wout, w_sem.at[1])
+        win_copy = pltpu.make_async_copy(
+            w_given.at[:, :, pl.ds(0, 2 * FFE)], win, w_sem.at[0]
+        )
+        wout_copy = pltpu.make_async_copy(
+            w_given.at[:, :, pl.ds(2 * FFE, FFE)], wout, w_sem.at[1]
+        )
         win_copy.start()
         wout_copy.start()
         barrier = pltpu.get_barrier_semaphore()
@@ -1025,13 +1029,13 @@
             jax.ShapeDtypeStruct((own_experts, width, 3 * FFE), bf16),
         ]
         + [jax.ShapeDtypeStruct(block, bf16)] * (1 + chips // 2),
-        in_specs=[hbm] * (1 + chips) + [vmem] * 2 + [hbm] * 2,
+        in_specs=[hbm] * (1 + chips) + [vmem] * 2 + [hbm],
         out_specs=[hbm] * 3 + [vmem] * 2 + [hbm] * (2 + chips // 2),
         scratch_shapes=[
             pltpu.VMEM((devices,) + block, bf16),
             pltpu.VMEM((devices,) + block, bf16),
-            pltpu.VMEM(w_in.shape, bf16),
-            pltpu.VMEM(w_out.shape, bf16),
+            pltpu.VMEM((own_experts, width, 2 * FFE), bf16),
+            pltpu.VMEM((own_experts, width, FFE), bf16),
             pltpu.VMEM(block, f32),
             pltpu.VMEM(block, f32),
             pltpu.VMEM((rows, LANES), f32),
@@ -1075,7 +1079,7 @@
         compiler_params=pltpu.CompilerParams(
             collective_id=collective_id, has_side_effects=True, vmem_limit_bytes=63 << 20
         ),
-    )(normed, *cots, mask, router, w_in, w_out)
+    )(normed, *cots, mask, router, weights)
 
 
 class Links:
@@ -1317,7 +1321,7 @@
             own_gain = jnp.sum(jnp.where(own, rounded(gain_ref), 0.0), axis=0, keepdims=True)
             ggain_a[...] = row(gain_grad) / own_gain
             gwo[...] = wo_ref[...]
-            grouter[...] = pack_ref[:, :experts]
+            grouter[...] = pack_ref[...].T[:experts]
             ggain_m[...] = row(pack_ref[:, experts : experts + 1])
             in_grad[...] = in_ref[...]
             output_ref[...] = out_ref[...]
@@ -1338,7 +1342,7 @@
         shape(out_rows, kv_width),
         shape(out_rows, kv_width),
         shape(*grad_wo.shape),
-        shape(out_rows, experts),
+        shape(experts, out_rows),
         shape(1, out_rows),
         shape(1, out_rows),
         shape(*input_grad.shape, dtype=bf16),
@@ -1421,27 +1425,27 @@
 
 def prepare(expert_in, expert_out, picks, docs, w_router, gain_attn, gain_moe):
     own_experts, w_rows, _ = expert_in.shape
-    rows, experts = picks.shape[0], w_router.shape[1]
+    rows, experts = picks.shape[1], w_router.shape[0]
     steps = 4
     chunk = w_rows // steps
 
     def kernel(
-        e_in, e_out, picks_ref, docs_ref, router, gain_a, gain_m, in_low, out_low, mask, docs_out, misc, gains
+        e_in, e_out, picks_ref, docs_ref, router, gain_a, gain_m, low, mask, docs_out, misc, gains
     ):
-        in_low[...] = e_in[...].astype(bf16)
-        out_low[...] = e_out[...].astype(bf16)
+        low[:, :, : 2 * FFE] = e_in[...].astype(bf16)
+        low[:, :, 2 * FFE :] = e_out[...].astype(bf16)
 
         @pl.when(pl.program_id(0) == 0)
         def _():
-            lane = lax.broadcasted_iota(jnp.int32, (rows, LANES), 1)
-            chosen = picks_ref[:, :1] == lane
+            expert = lax.broadcasted_iota(jnp.int32, (LANES, rows), 0)
+            chosen = picks_ref[:1] == expert
             for k in range(1, TOP):
-                chosen = chosen | (picks_ref[:, k : k + 1] == lane)
-            mask[...] = jnp.where(chosen, 1.0, 0.0).astype(bf16)
+                chosen = chosen | (picks_ref[k : k + 1] == expert)
+            mask[...] = jnp.where(chosen, 1.0, 0.0).T.astype(bf16)
             docs_out[...] = jnp.broadcast_to(docs_ref[...], docs_out.shape)
             misc[...] = jnp.concatenate(
-                [router[...], jnp.zeros((w_rows, LANES - experts), f32)], axis=1
-            ).astype(bf16)
+                [router[...], jnp.zeros((LANES - experts, w_rows), f32)], axis=0
+            ).T.astype(bf16)
             upper = lax.broadcasted_iota(jnp.int32, (8, w_rows), 0) == 0
             gains[...] = jnp.where(upper, gain_a[...], gain_m[...]).astype(bf16)
 
@@ -1462,9 +1466,10 @@
         kernel,
         name="prepare",
         grid=(steps,),
-        out_shape=[jax.ShapeDtypeStruct(x.shape, bf16) for x in (expert_in, expert_out)] + outs,
+        out_shape=[jax.ShapeDtypeStruct((own_experts, w_rows, 3 * FFE), bf16)] + outs,
         in_specs=[part(expert_in), part(expert_out)] + [whole(x.shape) for x in small],
-        out_specs=[part(expert_in), part(expert_out)] + [whole(x.shape) for x in outs],
+        out_specs=[pl.BlockSpec((own_experts, chunk, 3 * FFE), lambda i: (0, i, 0))]
+        + [whole(x.shape) for x in outs],
         compiler_params=pltpu.CompilerParams(
             dimension_semantics=("arbitrary",), vmem_limit_bytes=60 << 20
         ),
@@ -1588,6 +1593,30 @@
         leaving = [pltpu.make_async_copy(output, output_out, out_sem.at[0])]
         leaving[0].start()
 
+        for k in range(devices):
+            frm = lax.rem(me + devices - k, devices)
+            if k == 0:
+                own.wait()
+            else:
+                remote(
+                    "seq", qkv_in.at[frm], columns(frm), q_send.at[k - 1], q_recv.at[k - 1], frm
+                ).wait_recv()
+            part = dot_nt(columns(frm)[...], w_all[frm])
+            nac[...] = part if k == 0 else nac[...] + part
+
+        resid = tok_ref[...].astype(f32)
+        scale = lax.rsqrt(jnp.mean(resid * resid, axis=-1, keepdims=True) + norm_eps)
+        weighted = nac[...] * gain_row(gain_ref, 0)
+        in_grad[...] = (
+            mid_cot_ref[...]
+            + scale * weighted
+            - resid
+            * (scale * scale * scale)
+            * jnp.mean(weighted * resid, axis=-1, keepdims=True)
+        ).astype(bf16)
+
+        leaving.append(pltpu.make_async_copy(in_grad, in_grad_out, out_sem.at[1]))
+        leaving[1].start()
         own_q.wait()
         for k in range(1, parts):
             frm = lax.rem(my + parts - k, parts)
@@ -1629,30 +1658,6 @@
                 copy.start()
                 sent.append(copy)
 
-        for k in range(devices):
-            frm = lax.rem(me + devices - k, devices)
-            if k == 0:
-                own.wait()
-            else:
-                remote(
-                    "seq", qkv_in.at[frm], columns(frm), q_send.at[k - 1], q_recv.at[k - 1], frm
-                ).wait_recv()
-            part = dot_nt(columns(frm)[...], w_all[frm])
-            nac[...] = part if k == 0 else nac[...] + part
-
-        resid = tok_ref[...].astype(f32)
-        scale = lax.rsqrt(jnp.mean(resid * resid, axis=-1, keepdims=True) + norm_eps)
-        weighted = nac[...] * gain_row(gain_ref, 0)
-        in_grad[...] = (
-            mid_cot_ref[...]
-            + scale * weighted
-            - resid
-            * (scale * scale * scale)
-            * jnp.mean(weighted * resid, axis=-1, keepdims=True)
-        ).astype(bf16)
-
-        leaving.append(pltpu.make_async_copy(in_grad, in_grad_out, out_sem.at[1]))
-        leaving[1].start()
         for o, w in zip(gt_out, work):
             mine, theirs, far, near, last, sems, dp_send, dp_recv, z_send, z_recv, _ = w
             summed = near[chip].astype(f32)
@@ -1757,11 +1762,10 @@
     w_rows = w_query.shape[0]
 
     w_cols = HEADS_LANES + LANES
-    in_low, out_low, mask, doc_rows, misc, gains = prepare(
-        expert_in, expert_out, expert_picks[0], doc_ids, w_router, gain_attn, gain_moe
+    low, mask, doc_rows, misc, gains = prepare(
+        expert_in, expert_out, expert_picks[0].T, doc_ids, w_router.T, gain_attn, gain_moe
     )
-    expert_in_full = lax.all_gather(in_low, "dp", axis=1, tiled=True)
-    expert_out_full = lax.all_gather(out_low, "dp", axis=1, tiled=True)
+    expert_full = lax.all_gather(low, "dp", axis=1, tiled=True)
     chips = devices // 2
 
     def shift(x, k):
@@ -1797,7 +1801,7 @@
         1, attended_own, tokens[0], wo_full, gains_full
     )
     (_, _, _, moe_sum, gate_cot, e_grads, *branches) = moe_exchange(
-        2, normed_m, cots, mask_all, misc_full, expert_in_full, expert_out_full
+        2, normed_m, cots, mask_all, misc_full, expert_full
     )
     e_grads = lax.psum_scatter(e_grads, "dp", scatter_dimension=1, tiled=True)
     heads_cot, router_pack, mid_cot, grad_wo = middle_exchange(
@@ -1844,6 +1848,7 @@
         experts,
     )
     input_grad, output = input_grad[None], output[None]
+    grad_router = grad_router.T
     grad_gain_a = grad_gain_a.reshape(out_rows)
     grad_gain_m = grad_gain_m.reshape(out_rows)
     return (

time: 324 us -> 317 us (0.978)
  local copies, waits for them, and re-layouts: 6.75 us -> 2.4 us
    unnamed x17 -> x14, local copies, waits for them, and re-layouts: 6.08 us -> 1.73 us
  transfers between devices with their start and end apart: 8 -> 7, of which waited for: 1 -> 0; matrix products, arithmetic and copies ran while one was open for 0% -> 0% of each run, Pallas kernels for 88% -> 90%
where the time goes in v7:
time: 317 us; the launch traced here: 313 us
  Pallas kernels  290 us (91%)
  between operations  13.9 us (4%)
  starting transfers between devices  6.67 us (2%)
    pallas_call x1, Pallas kernels, moe_exchange(): pl.pallas_call(kernel, name='moe_exchange', out_shape=[jax.ShapeDtypeStru...  91.8 us
    pallas_call x1, Pallas kernels, exchange(): pl.pallas_call(kernel, name=f'exchange{collective_id}', out_shape=out_sha...  54.6 us
    pallas_call x1, Pallas kernels, final_exchange(): pl.pallas_call(kernel, name='final_exchange', out_shape=[jax.ShapeDtypeSt...  52.1 us
    pallas_call x1, Pallas kernels, attend_backward(): pl.pallas_call(kernel, name='attend_backward', grid_spec=grid_spec, out_s...  24.8 us
    pallas_call x1, Pallas kernels, attended_exchange(): pl.pallas_call(kernel, name='attended_exchange', out_shape=outs, in_specs...  20.1 us
    pallas_call x1, Pallas kernels, attend_forward(): pl.pallas_call(kernel, name='attend_forward', grid_spec=grid_spec, out_sh...  20.1 us
    pallas_call x1, Pallas kernels, middle_exchange(): pl.pallas_call(kernel, name='middle_exchange', out_shape=[jax.ShapeDtypeS...  17.4 us
    ppermute x3, starting transfers between devices, shift(): lax.ppermute(x, 'seq', [(i, (i + 2 * k) % devices) for i in range(devices)])  6.48 us
  transfers between devices with their start and end apart: 7, of which 0 were waited for; matrix products, arithmetic and copies ran while one was open for 0% of the time, Pallas kernels for 90%

profile of v7, /device:TPU:13, one launch (start us, length us, event | category | flops | bytes accessed | tf_op | source)
XLA Modules:
  0.0 313.4 jit_solution(10612138192823523511)
XLA Ops:
  7.2 0.0 all-gather.3.cloned.1.call-start
  7.2 4.1 %prepare.1 = (bf16[2,256,1536]{2,1,0:T(8,128)(2,1)}, bf16[256,128]{1,0:T(8,128)(2,1)}, s32[8,256]{1,0:T(8,128)}, bf16[256,128]{1,0:T(8,128)(2,1)}, bf16[8,256]{1,0:T(8,128)(2,1)}) custom-call(f32[2,256,1024]{2,1,0:T(8,128)} %e_in.1, f32[2,256,512]{2,1,0:T(8,128)} %e_out.1, s32[8,256]{1,0:T(8,128)} %bitcast.34, s32[1,256]{1,0:T(1,128)} %docs_ref.1, ...), custom_call_target="tpu_custom_call" | custom-call | tf_op jit(solution)/shard_map/prepare/pallas_call | solution.py:1465
  11.4 0.0 all-gather.3.cloned.1.call-update
  11.4 0.0 all-gather.5.cloned.1.call-start
  11.4 54.6 %exchange0.1 = (bf16[8,256,1024]{2,1,0:T(8,128)(2,1)}, s32[8,8,256]{2,1,0:T(8,128)}, bf16[8,256,128]{2,1,0:T(8,128)(2,1)}, bf16[256,1024]{1,0:T(8,128)(2,1)}, bf...) custom-call(bf16[256,1024]{1,0:T(8,128)(2,1)} %bitcast.21, ...), custom_call_target="tpu_custom_call" | custom-call | tf_op jit(solution)/shard_map/exchange0/pallas_call | solution.py:273
  66.1 0.0 all-gather.5.cloned.1.call-update
  66.1 0.0 reduce-scatter.2.cloned.1.call-start
  66.1 2.1 collective-permute-start
  68.3 2.1 collective-permute-start.1
  70.4 20.1 %attend_forward.1 = (bf16[8,256,1024]{2,1,0:T(8,128)(2,1)}, bf16[8,256,128]{2,1,0:T(8,128)(2,1)}, bf16[8,256,128]{2,1,0:T(8,128)(2,1)}, bf16[8,256,128]{2,1,0:T(...) custom-call(bf16[8,256,1024]{2,1,0:T(8,128)(2,1)} %get-tuple-element.75.tok, bf16[1024,256]{1,0:T(8,128)(2,1)} %bitcast.37, ...), custom_call_target="tpu_custom_call" | custom-call | flops 3221225472 | bytes 16777216 | tf_op jit(solution)/shard_map/attend_forward/pallas_call | solution.py:461
  90.5 20.1 %attended_exchange.1 = (bf16[256,1024]{1,0:T(8,128)(2,1)}, f32[256,1024]{1,0:T(8,128)}, bf16[256,1024]{1,0:T(8,128)(2,1)}) custom-call(bf16[8,256,128]{2,1,0:T(8,128)(2,1)} %get-tuple-element.79.att_in, bf16[256,1024]{1,0:T(8,128)(2,1)} %bitcast.22, bf16[1024,1024]{1,0:T(8,128)(2,1)} %bitcast.19, ...), custom_call_target="tpu_custom_call" | custom-call | tf_op jit(solution)/shard_map/attended_exchange/pallas_call | solution.py:1178
  110.7 0.8 copy-done.6
  111.5 91.8 %moe_exchange.1 = (bf16[2,8,256,1024]{3,2,1,0:T(8,128)(2,1)}, bf16[2,8,256,1024]{3,2,1,0:T(8,128)(2,1)}, bf16[2,8,256,512]{3,2,1,0:T(8,128)(2,1)}, f32[256,1024]...) custom-call(bf16[256,1024]{1,0:T(8,128)(2,1)} %get-tuple-element.81., ...), custom_call_target="tpu_custom_call" | custom-call | flops 38654705664 | bytes 41943040 | tf_op jit(solution)/shard_map/moe_exchange/pallas_call | solution.py:1020
  203.3 17.4 %middle_exchange.1 = (bf16[8,256,128]{2,1,0:T(8,128)(2,1)}, bf16[1024,128]{1,0:T(8,128)(2,1)}, f32[256,1024]{1,0:T(8,128)}, bf16[1024,1024]{1,0:T(8,128)(2,1)}) custom-call(f32[256,1024]{1,0:T(8,128)} %get-tuple-element.90.refs_0_, f32[8,16,256]{2,1,0:T(8,128)} %get-tuple-element.91.refs_1_, bf16[256,1024]{1,0:T(8,128)(2,1)} %get-tuple-element.81.refs_0_.refs_2_, ...), custom_call_target="tpu_custom_call" | custom-call | tf_op jit(solution)/shard_map/middle_exchange/pallas_call | solution.py:1259
  220.7 0.1 collective-permute-start.2
  220.8 2.2 collective-permute-start.3
  223.0 0.7 reshape.47.gain_ref
  223.7 24.8 %attend_backward.1.refs_0_.refs_5_ = bf16[8,256,256]{2,1,0:T(8,128)(2,1)} custom-call(bf16[8,256,128]{2,1,0:T(8,128)(2,1)} %get-tuple-element.88.q_ref, bf16[8,256,128]{2,1,0:T(8,128)(2,1)} %get-tuple-element.89.kv_ref, bf16[8,256,128]{2,1,0:T(8,128)(2,1)} %get-tuple-element.98.do_ref, f32[8,64,512]{2,1,0:T(8,128)} %get-tuple-element.99.ot_ref, ...), custom_call_target="tpu_custom_call" | custom-call | flops 5368709120 | bytes 4194304 | tf_op jit(solution)/shard_map/attend_backward/pallas_call | solution.py:573
  248.6 0.0 all-gather.5.cloned.1.call-done.refs_3_
  248.6 0.7 copy-done.1
  249.3 0.2 copy-done.2
  249.5 52.1 %final_exchange.1 = (bf16[256,1024]{1,0:T(8,128)(2,1)}, bf16[256,1024]{1,0:T(8,128)(2,1)}, bf16[8,32,256]{2,1,0:T(8,128)(2,1)}, f32[32,1024]{1,0:T(8,128)}, f32[32,128]{1,0:T(8,128)}) custom-call(bf16[8,256,256]{2,1,0:T(8,128)(2,1)} %attend_backward.1.refs_0_.refs_5_, bf16[4,4,2,32,1024]{4,3,2,1,0:T(8,128)(2,1)} %bitcast.24, ...), custom_call_target="tpu_custom_call" | custom-call | tf_op jit(solution)/shard_map/final_exchange/pallas_call | solution.py:1721
  301.7 0.0 reduce-scatter.2.cloned.1.call-done.e_ref
  301.7 5.2 %finish.1 = (f32[2,256,1024]{2,1,0:T(8,128)}, f32[2,256,512]{2,1,0:T(8,128)}, f32[32,1024]{1,0:T(8,128)}, f32[32,512]{1,0:T(8,128)}, f32[32,512]{1,0:T(8,128)}, ...) custom-call(s32[1]{0:T(128)} %bitcast.me_ref, ...), custom_call_target="tpu_custom_call" | custom-call | bytes 8388608 | tf_op jit(solution)/shard_map/finish/pallas_call | solution.py:1351
  (17 shorter events, 0.1 us)
Async XLA Ops:
  7.2 104.3 %all-gather.3.cloned.1.call-start = ((), (), s32[]{:S(2)}) async-start(), calls=%async_computation.1 | async-start | bytes 7864320 | tf_op jit(solution)/shard_map/all_gather | solution.py:1768
  11.3 54.8 %copy-start = (bf16[1,256,1024]{2,1,0:T(8,128)(2,1)S(1)}, bf16[1,256,1024]{2,1,0:T(8,128)(2,1)}, u32[]{:S(2)}) copy-start(bf16[1,256,1024]{2,1,0:T(8,128)(2,1)} %param.15) | copy-start | bytes 1572868
  11.4 237.2 %all-gather.5.cloned.1.call-start = ((), (), s32[]{:S(2)}) async-start(), calls=%async_computation.3 | async-start | bytes 5242880 | tf_op jit(solution)/shard_map/all_gather | solution.py:1787
  66.1 235.6 %reduce-scatter.2.cloned.1.call-start = ((), (), s32[]{:S(2)}) async-start(), calls=%async_computation.2 | async-start | bytes 7864320 | tf_op jit(solution)/shard_map/reduce_scatter | solution.py:1806
  66.1 44.5 %collective-permute-start = (bf16[256,1024]{1,0:T(8,128)(2,1)S(1)}, bf16[256,1024]{1,0:T(8,128)(2,1)S(1)}, u32[]{:S(2)}, u32[]{:S(2)}) collective-permute-start(bf16[256,1024]{1,0:T(8,128)(2,1)S(1)} %bitcast.28), channel_id=1, source_target_pairs={{0,2},{1,3},{2,4},{3,5},{4,6},{5,7},{6,0},{7,1},{8,10},{9,11},{10,... | collective-permute-start | bytes 1572872 | tf_op jit(solution)/shard_map/ppermute | solution.py:1772
  68.3 43.2 %collective-permute-start.1 = (bf16[256,1024]{1,0:T(8,128)(2,1)S(1)}, bf16[256,1024]{1,0:T(8,128)(2,1)}, u32[]{:S(2)}, u32[]{:S(2)}) collective-permute-start(bf16[256,1024]{1,0:T(8,128)(2,1)S(1)} %bitcast.29), channel_id=1, source_target_pairs={{0,6},{1,7},{2,0},{3,1},{4,2},{5,3},{6,4},{7,5},{8,14},{9,15},{10,... | collective-permute-start | bytes 1572872 | tf_op jit(solution)/shard_map/ppermute | solution.py:1772
  110.6 0.8 copy-start.6
  203.2 17.5 %copy-start.5 = (bf16[256,1024]{1,0:T(8,128)(2,1)S(1)}, bf16[256,1024]{1,0:T(8,128)(2,1)}, u32[]{:S(2)}) copy-start(bf16[256,1024]{1,0:T(8,128)(2,1)} %get-tuple-element.102) | copy-start | bytes 1572868
  203.3 17.6 %copy-start.4 = (bf16[256,1024]{1,0:T(8,128)(2,1)S(1)}, bf16[256,1024]{1,0:T(8,128)(2,1)}, u32[]{:S(2)}) copy-start(bf16[256,1024]{1,0:T(8,128)(2,1)} %get-tuple-element.103) | copy-start | bytes 1572868
  203.3 19.8 %copy-start.3 = (f32[256]{0:T(256)S(1)}, f32[256]{0:T(256)}, u32[]{:S(2)}) copy-start(f32[256]{0:T(256)} %param.23) | copy-start | bytes 3076
  220.7 27.8 %collective-permute-start.2 = (bf16[256,1024]{1,0:T(8,128)(2,1)S(1)}, bf16[256,1024]{1,0:T(8,128)(2,1)S(1)}, u32[]{:S(2)}, u32[]{:S(2)}) collective-permute-start(bf16[256,1024]{1,0:T(8,128)(2,1)S(1)} %copy-done.5), channel_id=1, source_target_pairs={{0,2},{1,3},{2,0},{3,1},{4,6},{5,7},{6,4},{7,5},{8,10},{9,11},{10,... | collective-permute-start | bytes 1572872 | tf_op jit(solution)/shard_map/ppermute | solution.py:1814
  220.8 27.7 %collective-permute-start.3 = (bf16[256,1024]{1,0:T(8,128)(2,1)S(1)}, bf16[256,1024]{1,0:T(8,128)(2,1)S(1)}, u32[]{:S(2)}, u32[]{:S(2)}) collective-permute-start(bf16[256,1024]{1,0:T(8,128)(2,1)S(1)} %copy-done.4), channel_id=1, source_target_pairs={{0,4},{1,5},{2,6},{3,7},{4,0},{5,1},{6,2},{7,3},{8,12},{9,13},{10,... | collective-permute-start | bytes 1572872 | tf_op jit(solution)/shard_map/ppermute | solution.py:1772
  248.6 0.8 copy-start.1
  248.6 0.9 copy-start.2
Sparse Core Ops, SparseCore 0:
  11.5 81.5 all-gather.2
  94.9 52.6 all-gather.4
  203.4 86.4 reduce-scatter.1

commit v8 on v7

--- a/solution.py
+++ b/solution.py
@@ -702,6 +702,8 @@
         for k in range(chips):
             cot_to_sibling(k).start()
             cot_local(k).start()
+        gin[...] = jnp.zeros_like(gin)
+        gout[...] = jnp.zeros_like(gout)
         own.wait()
         for k in range(chips):
             cot_local(k).wait()
@@ -730,6 +732,9 @@
         def y_leave(b, k):
             return pltpu.make_async_copy(y_pre.at[b], y_outs[k], y_sem.at[k])
 
+        def keep_of(j):
+            return 2 * lax.rem(pair + 1 + j, pairs) + lax.rem(chip, 2)
+
         def y_hand(b):
             far = lax.rem(b // 2 + pairs - pair, pairs) - 1
             return remote(
@@ -772,10 +777,6 @@
             @pl.when(b == mate)
             def _():
                 y_leave(b, 1).start()
-
-            @pl.when((b != mate) & (lax.rem(b + chip, 2) == 1))
-            def _():
-                y_hand(b).start()
 
         def compute(block, before):
             x = x_all[block]
@@ -888,6 +889,9 @@
                 def _():
                     fold(k)
 
+        for j in range(pairs - 1):
+            y_hand(keep_of(j) + mate - chip).start()
+
         for e in range(own_experts):
             for copy in stage_copies(e, 0):
                 copy.wait()
@@ -907,9 +911,6 @@
 
         for copy in loads(jnp.int32(0), 0):
             copy.start()
-        gin[...] = jnp.zeros_like(gin)
-        gout[...] = jnp.zeros_like(gout)
-
         @pl.loop(0, chips * own_experts)
         def _(t):
             p = lax.rem(t, 2)
@@ -944,9 +945,6 @@
                             pass_on(away, i, me - 2 * side).wait_send()
 
         own_sends(lambda copy: copy.wait_send())
-
-        def keep_of(j):
-            return 2 * lax.rem(pair + 1 + j, pairs) + lax.rem(chip, 2)
 
         for j in range(pairs - 1):
             b = keep_of(j)

time: 317 us -> 331 us (1.044)
  Pallas kernels: 290 us -> 305 us
    pallas_call x1, Pallas kernels: 91.8 us -> 99.8 us  [moe_exchange(): pl.pallas_call(kernel, name='moe_exchange', out_shape=[jax.ShapeDtypeStru...]
    pallas_call x1, Pallas kernels: 17.4 us -> 22.1 us  [middle_exchange(): pl.pallas_call(kernel, name='middle_exchange', out_shape=[jax.ShapeDtypeS...]
where the time goes in v8:
time: 331 us; the launch traced here: 327 us
  Pallas kernels  305 us (92%)
  between operations  13.9 us (4%)
  starting transfers between devices  5.68 us (2%)
    pallas_call x1, Pallas kernels, moe_exchange(): pl.pallas_call(kernel, name='moe_exchange', out_shape=[jax.ShapeDtypeStru...  99.8 us
    pallas_call x1, Pallas kernels, exchange(): pl.pallas_call(kernel, name=f'exchange{collective_id}', out_shape=out_sha...  54.6 us
    pallas_call x1, Pallas kernels, final_exchange(): pl.pallas_call(kernel, name='final_exchange', out_shape=[jax.ShapeDtypeSt...  53.1 us
    pallas_call x1, Pallas kernels, attend_backward(): pl.pallas_call(kernel, name='attend_backward', grid_spec=grid_spec, out_s...  25.5 us
    pallas_call x1, Pallas kernels, middle_exchange(): pl.pallas_call(kernel, name='middle_exchange', out_shape=[jax.ShapeDtypeS...  22.1 us
    pallas_call x1, Pallas kernels, attend_forward(): pl.pallas_call(kernel, name='attend_forward', grid_spec=grid_spec, out_sh...  20.6 us
    pallas_call x1, Pallas kernels, attended_exchange(): pl.pallas_call(kernel, name='attended_exchange', out_shape=outs, in_specs...  20.1 us
  transfers between devices with their start and end apart: 7, of which 0 were waited for; matrix products, arithmetic and copies ran while one was open for 0% of the time, Pallas kernels for 90%

profile of v8, /device:TPU:13, one launch (start us, length us, event | category | flops | bytes accessed | tf_op | source)
XLA Modules:
  0.0 327.4 jit_solution(13936887027549934127)
XLA Ops:
  7.2 0.0 all-gather.3.cloned.1.call-start
  7.2 4.1 %prepare.1 = (bf16[2,256,1536]{2,1,0:T(8,128)(2,1)}, bf16[256,128]{1,0:T(8,128)(2,1)}, s32[8,256]{1,0:T(8,128)}, bf16[256,128]{1,0:T(8,128)(2,1)}, bf16[8,256]{1,0:T(8,128)(2,1)}) custom-call(f32[2,256,1024]{2,1,0:T(8,128)} %e_in.1, f32[2,256,512]{2,1,0:T(8,128)} %e_out.1, s32[8,256]{1,0:T(8,128)} %bitcast.34, s32[1,256]{1,0:T(1,128)} %docs_ref.1, ...), custom_call_target="tpu_custom_call" | custom-call | tf_op jit(solution)/shard_map/prepare/pallas_call | solution.py:1463
  11.4 0.0 all-gather.3.cloned.1.call-update
  11.4 0.0 all-gather.5.cloned.1.call-start
  11.4 54.6 %exchange0.1 = (bf16[8,256,1024]{2,1,0:T(8,128)(2,1)}, s32[8,8,256]{2,1,0:T(8,128)}, bf16[8,256,128]{2,1,0:T(8,128)(2,1)}, bf16[256,1024]{1,0:T(8,128)(2,1)}, bf...) custom-call(bf16[256,1024]{1,0:T(8,128)(2,1)} %bitcast.21, ...), custom_call_target="tpu_custom_call" | custom-call | tf_op jit(solution)/shard_map/exchange0/pallas_call | solution.py:273
  66.1 0.0 all-gather.5.cloned.1.call-update
  66.1 0.0 reduce-scatter.2.cloned.1.call-start
  66.1 2.1 collective-permute-start
  68.3 2.1 collective-permute-start.1
  70.4 20.6 %attend_forward.1 = (bf16[8,256,1024]{2,1,0:T(8,128)(2,1)}, bf16[8,256,128]{2,1,0:T(8,128)(2,1)}, bf16[8,256,128]{2,1,0:T(8,128)(2,1)}, bf16[8,256,128]{2,1,0:T(...) custom-call(bf16[8,256,1024]{2,1,0:T(8,128)(2,1)} %get-tuple-element.75.tok, bf16[1024,256]{1,0:T(8,128)(2,1)} %bitcast.37, ...), custom_call_target="tpu_custom_call" | custom-call | flops 3221225472 | bytes 16777216 | tf_op jit(solution)/shard_map/attend_forward/pallas_call | solution.py:461
  91.0 20.1 %attended_exchange.1 = (bf16[256,1024]{1,0:T(8,128)(2,1)}, f32[256,1024]{1,0:T(8,128)}, bf16[256,1024]{1,0:T(8,128)(2,1)}) custom-call(bf16[8,256,128]{2,1,0:T(8,128)(2,1)} %get-tuple-element.79.att_in, bf16[256,1024]{1,0:T(8,128)(2,1)} %bitcast.22, bf16[1024,1024]{1,0:T(8,128)(2,1)} %bitcast.19, ...), custom_call_target="tpu_custom_call" | custom-call | tf_op jit(solution)/shard_map/attended_exchange/pallas_call | solution.py:1176
  111.1 0.8 copy-done.6
  111.9 99.8 %moe_exchange.1 = (bf16[2,8,256,1024]{3,2,1,0:T(8,128)(2,1)}, bf16[2,8,256,1024]{3,2,1,0:T(8,128)(2,1)}, bf16[2,8,256,512]{3,2,1,0:T(8,128)(2,1)}, f32[256,1024]...) custom-call(bf16[256,1024]{1,0:T(8,128)(2,1)} %get-tuple-element.81., ...), custom_call_target="tpu_custom_call" | custom-call | flops 38654705664 | bytes 41943040 | tf_op jit(solution)/shard_map/moe_exchange/pallas_call | solution.py:1018
  211.9 22.1 %middle_exchange.1 = (bf16[8,256,128]{2,1,0:T(8,128)(2,1)}, bf16[1024,128]{1,0:T(8,128)(2,1)}, f32[256,1024]{1,0:T(8,128)}, bf16[1024,1024]{1,0:T(8,128)(2,1)}) custom-call(f32[256,1024]{1,0:T(8,128)} %get-tuple-element.90.refs_0_, f32[8,16,256]{2,1,0:T(8,128)} %get-tuple-element.91.refs_1_, bf16[256,1024]{1,0:T(8,128)(2,1)} %get-tuple-element.81.refs_0_.refs_2_, ...), custom_call_target="tpu_custom_call" | custom-call | tf_op jit(solution)/shard_map/middle_exchange/pallas_call | solution.py:1257
  234.0 0.1 collective-permute-start.2
  234.1 1.2 collective-permute-start.3
  235.3 0.7 reshape.47.gain_ref
  236.0 25.5 %attend_backward.1.refs_0_.refs_5_ = bf16[8,256,256]{2,1,0:T(8,128)(2,1)} custom-call(bf16[8,256,128]{2,1,0:T(8,128)(2,1)} %get-tuple-element.88.q_ref, bf16[8,256,128]{2,1,0:T(8,128)(2,1)} %get-tuple-element.89.kv_ref, bf16[8,256,128]{2,1,0:T(8,128)(2,1)} %get-tuple-element.98.do_ref, f32[8,64,512]{2,1,0:T(8,128)} %get-tuple-element.99.ot_ref, ...), custom_call_target="tpu_custom_call" | custom-call | flops 5368709120 | bytes 4194304 | tf_op jit(solution)/shard_map/attend_backward/pallas_call | solution.py:573
  261.5 0.0 all-gather.5.cloned.1.call-done.refs_3_
  261.5 0.7 copy-done.1
  262.3 0.2 copy-done.2
  262.4 53.1 %final_exchange.1 = (bf16[256,1024]{1,0:T(8,128)(2,1)}, bf16[256,1024]{1,0:T(8,128)(2,1)}, bf16[8,32,256]{2,1,0:T(8,128)(2,1)}, f32[32,1024]{1,0:T(8,128)}, f32[32,128]{1,0:T(8,128)}) custom-call(bf16[8,256,256]{2,1,0:T(8,128)(2,1)} %attend_backward.1.refs_0_.refs_5_, bf16[4,4,2,32,1024]{4,3,2,1,0:T(8,128)(2,1)} %bitcast.24, ...), custom_call_target="tpu_custom_call" | custom-call | tf_op jit(solution)/shard_map/final_exchange/pallas_call | solution.py:1719
  315.6 0.0 reduce-scatter.2.cloned.1.call-done.e_ref
  315.6 5.2 %finish.1 = (f32[2,256,1024]{2,1,0:T(8,128)}, f32[2,256,512]{2,1,0:T(8,128)}, f32[32,1024]{1,0:T(8,128)}, f32[32,512]{1,0:T(8,128)}, f32[32,512]{1,0:T(8,128)}, ...) custom-call(s32[1]{0:T(128)} %bitcast.me_ref, ...), custom_call_target="tpu_custom_call" | custom-call | bytes 8388608 | tf_op jit(solution)/shard_map/finish/pallas_call | solution.py:1349
  (17 shorter events, 0.1 us)
Async XLA Ops:
  7.2 104.8 %all-gather.3.cloned.1.call-start = ((), (), s32[]{:S(2)}) async-start(), calls=%async_computation.1 | async-start | bytes 7864320 | tf_op jit(solution)/shard_map/all_gather | solution.py:1766
  11.3 54.8 %copy-start = (bf16[1,256,1024]{2,1,0:T(8,128)(2,1)S(1)}, bf16[1,256,1024]{2,1,0:T(8,128)(2,1)}, u32[]{:S(2)}) copy-start(bf16[1,256,1024]{2,1,0:T(8,128)(2,1)} %param.15) | copy-start | bytes 1572868
  11.4 250.1 %all-gather.5.cloned.1.call-start = ((), (), s32[]{:S(2)}) async-start(), calls=%async_computation.3 | async-start | bytes 5242880 | tf_op jit(solution)/shard_map/all_gather | solution.py:1785
  66.1 249.5 %reduce-scatter.2.cloned.1.call-start = ((), (), s32[]{:S(2)}) async-start(), calls=%async_computation.2 | async-start | bytes 7864320 | tf_op jit(solution)/shard_map/reduce_scatter | solution.py:1804
  66.1 45.0 %collective-permute-start = (bf16[256,1024]{1,0:T(8,128)(2,1)S(1)}, bf16[256,1024]{1,0:T(8,128)(2,1)S(1)}, u32[]{:S(2)}, u32[]{:S(2)}) collective-permute-start(bf16[256,1024]{1,0:T(8,128)(2,1)S(1)} %bitcast.28), channel_id=1, source_target_pairs={{0,2},{1,3},{2,4},{3,5},{4,6},{5,7},{6,0},{7,1},{8,10},{9,11},{10,... | collective-permute-start | bytes 1572872 | tf_op jit(solution)/shard_map/ppermute | solution.py:1770
  68.3 43.7 %collective-permute-start.1 = (bf16[256,1024]{1,0:T(8,128)(2,1)S(1)}, bf16[256,1024]{1,0:T(8,128)(2,1)}, u32[]{:S(2)}, u32[]{:S(2)}) collective-permute-start(bf16[256,1024]{1,0:T(8,128)(2,1)S(1)} %bitcast.29), channel_id=1, source_target_pairs={{0,6},{1,7},{2,0},{3,1},{4,2},{5,3},{6,4},{7,5},{8,14},{9,15},{10,... | collective-permute-start | bytes 1572872 | tf_op jit(solution)/shard_map/ppermute | solution.py:1770
  111.1 0.8 copy-start.6
  211.8 22.2 %copy-start.5 = (bf16[256,1024]{1,0:T(8,128)(2,1)S(1)}, bf16[256,1024]{1,0:T(8,128)(2,1)}, u32[]{:S(2)}) copy-start(bf16[256,1024]{1,0:T(8,128)(2,1)} %get-tuple-element.102) | copy-start | bytes 1572868
  211.8 22.3 %copy-start.4 = (bf16[256,1024]{1,0:T(8,128)(2,1)S(1)}, bf16[256,1024]{1,0:T(8,128)(2,1)}, u32[]{:S(2)}) copy-start(bf16[256,1024]{1,0:T(8,128)(2,1)} %get-tuple-element.103) | copy-start | bytes 1572868
  211.8 23.5 %copy-start.3 = (f32[256]{0:T(256)S(1)}, f32[256]{0:T(256)}, u32[]{:S(2)}) copy-start(f32[256]{0:T(256)} %param.23) | copy-start | bytes 3076
  234.0 27.5 %collective-permute-start.2 = (bf16[256,1024]{1,0:T(8,128)(2,1)S(1)}, bf16[256,1024]{1,0:T(8,128)(2,1)S(1)}, u32[]{:S(2)}, u32[]{:S(2)}) collective-permute-start(bf16[256,1024]{1,0:T(8,128)(2,1)S(1)} %copy-done.5), channel_id=1, source_target_pairs={{0,2},{1,3},{2,0},{3,1},{4,6},{5,7},{6,4},{7,5},{8,10},{9,11},{10,... | collective-permute-start | bytes 1572872 | tf_op jit(solution)/shard_map/ppermute | solution.py:1812
  234.1 27.4 %collective-permute-start.3 = (bf16[256,1024]{1,0:T(8,128)(2,1)S(1)}, bf16[256,1024]{1,0:T(8,128)(2,1)S(1)}, u32[]{:S(2)}, u32[]{:S(2)}) collective-permute-start(bf16[256,1024]{1,0:T(8,128)(2,1)S(1)} %copy-done.4), channel_id=1, source_target_pairs={{0,4},{1,5},{2,6},{3,7},{4,0},{5,1},{6,2},{7,3},{8,12},{9,13},{10,... | collective-permute-start | bytes 1572872 | tf_op jit(solution)/shard_map/ppermute | solution.py:1770
  261.5 0.8 copy-start.1
  261.5 0.9 copy-start.2
Sparse Core Ops, SparseCore 0:
  11.5 81.5 all-gather.2
  94.9 52.6 all-gather.4
  211.9 91.5 reduce-scatter.1

commit v9 on v7

--- a/solution.py
+++ b/solution.py
@@ -702,6 +702,8 @@
         for k in range(chips):
             cot_to_sibling(k).start()
             cot_local(k).start()
+        gin[...] = jnp.zeros_like(gin)
+        gout[...] = jnp.zeros_like(gout)
         own.wait()
         for k in range(chips):
             cot_local(k).wait()
@@ -773,7 +775,7 @@
             def _():
                 y_leave(b, 1).start()
 
-            @pl.when((b != mate) & (lax.rem(b + chip, 2) == 1))
+            @pl.when((b != chip) & (lax.rem(b + chip, 2) == 0))
             def _():
                 y_hand(b).start()
 
@@ -907,9 +909,6 @@
 
         for copy in loads(jnp.int32(0), 0):
             copy.start()
-        gin[...] = jnp.zeros_like(gin)
-        gout[...] = jnp.zeros_like(gout)
-
         @pl.loop(0, chips * own_experts)
         def _(t):
             p = lax.rem(t, 2)
@@ -946,13 +945,7 @@
         own_sends(lambda copy: copy.wait_send())
 
         def keep_of(j):
-            return 2 * lax.rem(pair + 1 + j, pairs) + lax.rem(chip, 2)
-
-        for j in range(pairs - 1):
-            b = keep_of(j)
-            y_hand(b).wait_recv()
-            y_pre[b] = (y_pre[b].astype(f32) + y_in[j].astype(f32)).astype(bf16)
-            y_leave(b, 2 + j).start()
+            return 2 * lax.rem(pair + 1 + j, pairs) + 1 - lax.rem(chip, 2)
 
         leaving = []
         for e in range(own_experts):
@@ -977,6 +970,12 @@
                 for copy in leaving[-1]:
                     copy.start()
 
+        for j in range(pairs - 1):
+            b = keep_of(j)
+            y_hand(b).wait_recv()
+            y_pre[b] = (y_pre[b].astype(f32) + y_in[j].astype(f32)).astype(bf16)
+            y_leave(b, 2 + j).start()
+
         @pl.loop(1, chips)
         def _(k):
             b = order(chip, k)
@@ -1007,7 +1006,7 @@
         y_leave(mate, 1).wait()
         for j in range(pairs - 1):
             y_leave(keep_of(j), 2 + j).wait()
-            y_hand(keep_of(j) + mate - chip).wait_send()
+            y_hand(keep_of(j) + chip - mate).wait_send()
 
         for k in range(chips):
             cot_to_sibling(k).wait_send()
@@ -1808,11 +1807,18 @@
         4, moe_sum, gate_cot, normed_m, misc_full, mask, mid, out_grad[0], gains_full,
         wo_full, attended, q_width,
     )
+    def across_pairs(x, k):
+        def there(i):
+            chip = i // 2
+            return 2 * (2 * ((chip // 2 + k) % (chips // 2)) + 1 - chip % 2) + i % 2
+
+        return lax.ppermute(x, "seq", [(i, there(i)) for i in range(devices)])
+
     heads_cot, branches = lax.optimization_barrier((heads_cot, branches))
     branches = [
         branches[0],
         lax.ppermute(branches[1], "seq", [(i, i ^ 2) for i in range(devices)]),
-    ] + [shift(branches[1 + k], 2 * k) for k in range(1, chips // 2)]
+    ] + [across_pairs(branches[1 + k], k) for k in range(1, chips // 2)]
     qkv_cot = attend_backward(q_all, kv_all, heads_cot, ot, lse, table, doc_all, heads)
     qkv_cot, branches = lax.optimization_barrier((qkv_cot, branches))
     out_rows = w_rows // devices

time: 317 us -> 318 us (level)
    ppermute x3 -> x2, starting transfers between devices: 6.48 us -> 4.26 us  [shift(): lax.ppermute(x, 'seq', [(i, (i + 2 * k) % devices) for i in range(devices)])]
where the time goes in v9:
time: 318 us; the launch traced here: 315 us
  Pallas kernels  292 us (92%)
  between operations  13.9 us (4%)
  starting transfers between devices  5.99 us (2%)
    pallas_call x1, Pallas kernels, moe_exchange(): pl.pallas_call(kernel, name='moe_exchange', out_shape=[jax.ShapeDtypeStru...  90.1 us
    pallas_call x1, Pallas kernels, exchange(): pl.pallas_call(kernel, name=f'exchange{collective_id}', out_shape=out_sha...  54.6 us
    pallas_call x1, Pallas kernels, final_exchange(): pl.pallas_call(kernel, name='final_exchange', out_shape=[jax.ShapeDtypeSt...  54 us
    pallas_call x1, Pallas kernels, attend_backward(): pl.pallas_call(kernel, name='attend_backward', grid_spec=grid_spec, out_s...  24.8 us
    pallas_call x1, Pallas kernels, attended_exchange(): pl.pallas_call(kernel, name='attended_exchange', out_shape=outs, in_specs...  20.1 us
    pallas_call x1, Pallas kernels, attend_forward(): pl.pallas_call(kernel, name='attend_forward', grid_spec=grid_spec, out_sh...  20.1 us
    pallas_call x1, Pallas kernels, middle_exchange(): pl.pallas_call(kernel, name='middle_exchange', out_shape=[jax.ShapeDtypeS...  19.2 us
  transfers between devices with their start and end apart: 7, of which 0 were waited for; matrix products, arithmetic and copies ran while one was open for 0% of the time, Pallas kernels for 90%

profile of v9, /device:TPU:13, one launch (start us, length us, event | category | flops | bytes accessed | tf_op | source)
XLA Modules:
  0.0 314.8 jit_solution(13124919536036955090)
XLA Ops:
  7.2 0.0 all-gather.3.cloned.1.call-start
  7.2 4.1 %prepare.1 = (bf16[2,256,1536]{2,1,0:T(8,128)(2,1)}, bf16[256,128]{1,0:T(8,128)(2,1)}, s32[8,256]{1,0:T(8,128)}, bf16[256,128]{1,0:T(8,128)(2,1)}, bf16[8,256]{1,0:T(8,128)(2,1)}) custom-call(f32[2,256,1024]{2,1,0:T(8,128)} %e_in.1, f32[2,256,512]{2,1,0:T(8,128)} %e_out.1, s32[8,256]{1,0:T(8,128)} %bitcast.34, s32[1,256]{1,0:T(1,128)} %docs_ref.1, ...), custom_call_target="tpu_custom_call" | custom-call | tf_op jit(solution)/shard_map/prepare/pallas_call | solution.py:1464
  11.4 0.0 all-gather.3.cloned.1.call-update
  11.4 0.0 all-gather.5.cloned.1.call-start
  11.4 54.6 %exchange0.1 = (bf16[8,256,1024]{2,1,0:T(8,128)(2,1)}, s32[8,8,256]{2,1,0:T(8,128)}, bf16[8,256,128]{2,1,0:T(8,128)(2,1)}, bf16[256,1024]{1,0:T(8,128)(2,1)}, bf...) custom-call(bf16[256,1024]{1,0:T(8,128)(2,1)} %bitcast.21, ...), custom_call_target="tpu_custom_call" | custom-call | tf_op jit(solution)/shard_map/exchange0/pallas_call | solution.py:273
  66.1 0.0 all-gather.5.cloned.1.call-update
  66.1 0.0 reduce-scatter.2.cloned.1.call-start
  66.1 2.1 collective-permute-start
  68.3 2.1 collective-permute-start.1
  70.4 20.1 %attend_forward.1 = (bf16[8,256,1024]{2,1,0:T(8,128)(2,1)}, bf16[8,256,128]{2,1,0:T(8,128)(2,1)}, bf16[8,256,128]{2,1,0:T(8,128)(2,1)}, bf16[8,256,128]{2,1,0:T(...) custom-call(bf16[8,256,1024]{2,1,0:T(8,128)(2,1)} %get-tuple-element.75.tok, bf16[1024,256]{1,0:T(8,128)(2,1)} %bitcast.37, ...), custom_call_target="tpu_custom_call" | custom-call | flops 3221225472 | bytes 16777216 | tf_op jit(solution)/shard_map/attend_forward/pallas_call | solution.py:461
  90.5 20.1 %attended_exchange.1 = (bf16[256,1024]{1,0:T(8,128)(2,1)}, f32[256,1024]{1,0:T(8,128)}, bf16[256,1024]{1,0:T(8,128)(2,1)}) custom-call(bf16[8,256,128]{2,1,0:T(8,128)(2,1)} %get-tuple-element.79.att_in, bf16[256,1024]{1,0:T(8,128)(2,1)} %bitcast.22, bf16[1024,1024]{1,0:T(8,128)(2,1)} %bitcast.19, ...), custom_call_target="tpu_custom_call" | custom-call | tf_op jit(solution)/shard_map/attended_exchange/pallas_call | solution.py:1177
  110.7 0.8 copy-done.6
  111.5 90.1 %moe_exchange.1 = (bf16[2,8,256,1024]{3,2,1,0:T(8,128)(2,1)}, bf16[2,8,256,1024]{3,2,1,0:T(8,128)(2,1)}, bf16[2,8,256,512]{3,2,1,0:T(8,128)(2,1)}, f32[256,1024]...) custom-call(bf16[256,1024]{1,0:T(8,128)(2,1)} %get-tuple-element.81., ...), custom_call_target="tpu_custom_call" | custom-call | flops 38654705664 | bytes 41943040 | tf_op jit(solution)/shard_map/moe_exchange/pallas_call | solution.py:1019
  201.7 19.2 %middle_exchange.1 = (bf16[8,256,128]{2,1,0:T(8,128)(2,1)}, bf16[1024,128]{1,0:T(8,128)(2,1)}, f32[256,1024]{1,0:T(8,128)}, bf16[1024,1024]{1,0:T(8,128)(2,1)}) custom-call(f32[256,1024]{1,0:T(8,128)} %get-tuple-element.90.refs_0_, f32[8,16,256]{2,1,0:T(8,128)} %get-tuple-element.91.refs_1_, bf16[256,1024]{1,0:T(8,128)(2,1)} %get-tuple-element.81.refs_0_.refs_2_, ...), custom_call_target="tpu_custom_call" | custom-call | tf_op jit(solution)/shard_map/middle_exchange/pallas_call | solution.py:1258
  220.9 0.1 collective-permute-start.2
  221.0 1.5 collective-permute-start.3
  222.6 0.7 reshape.47.gain_ref
  223.2 24.8 %attend_backward.1.refs_0_.refs_5_ = bf16[8,256,256]{2,1,0:T(8,128)(2,1)} custom-call(bf16[8,256,128]{2,1,0:T(8,128)(2,1)} %get-tuple-element.88.q_ref, bf16[8,256,128]{2,1,0:T(8,128)(2,1)} %get-tuple-element.89.kv_ref, bf16[8,256,128]{2,1,0:T(8,128)(2,1)} %get-tuple-element.98.do_ref, f32[8,64,512]{2,1,0:T(8,128)} %get-tuple-element.99.ot_ref, ...), custom_call_target="tpu_custom_call" | custom-call | flops 5368709120 | bytes 4194304 | tf_op jit(solution)/shard_map/attend_backward/pallas_call | solution.py:573
  248.1 0.0 all-gather.5.cloned.1.call-done.refs_3_
  248.1 0.7 copy-done.1
  248.9 0.2 copy-done.2
  249.0 54.0 %final_exchange.1 = (bf16[256,1024]{1,0:T(8,128)(2,1)}, bf16[256,1024]{1,0:T(8,128)(2,1)}, bf16[8,32,256]{2,1,0:T(8,128)(2,1)}, f32[32,1024]{1,0:T(8,128)}, f32[32,128]{1,0:T(8,128)}) custom-call(bf16[8,256,256]{2,1,0:T(8,128)(2,1)} %attend_backward.1.refs_0_.refs_5_, bf16[4,4,2,32,1024]{4,3,2,1,0:T(8,128)(2,1)} %bitcast.24, ...), custom_call_target="tpu_custom_call" | custom-call | tf_op jit(solution)/shard_map/final_exchange/pallas_call | solution.py:1720
  303.0 0.0 reduce-scatter.2.cloned.1.call-done.e_ref
  303.0 5.2 %finish.1 = (f32[2,256,1024]{2,1,0:T(8,128)}, f32[2,256,512]{2,1,0:T(8,128)}, f32[32,1024]{1,0:T(8,128)}, f32[32,512]{1,0:T(8,128)}, f32[32,512]{1,0:T(8,128)}, ...) custom-call(s32[1]{0:T(128)} %bitcast.me_ref, ...), custom_call_target="tpu_custom_call" | custom-call | bytes 8388608 | tf_op jit(solution)/shard_map/finish/pallas_call | solution.py:1350
  (17 shorter events, 0.1 us)
Async XLA Ops:
  7.2 104.3 %all-gather.3.cloned.1.call-start = ((), (), s32[]{:S(2)}) async-start(), calls=%async_computation.1 | async-start | bytes 7864320 | tf_op jit(solution)/shard_map/all_gather | solution.py:1767
  11.3 54.8 %copy-start = (bf16[1,256,1024]{2,1,0:T(8,128)(2,1)S(1)}, bf16[1,256,1024]{2,1,0:T(8,128)(2,1)}, u32[]{:S(2)}) copy-start(bf16[1,256,1024]{2,1,0:T(8,128)(2,1)} %param.15) | copy-start | bytes 1572868
  11.4 236.7 %all-gather.5.cloned.1.call-start = ((), (), s32[]{:S(2)}) async-start(), calls=%async_computation.3 | async-start | bytes 5242880 | tf_op jit(solution)/shard_map/all_gather | solution.py:1786
  66.1 236.9 %reduce-scatter.2.cloned.1.call-start = ((), (), s32[]{:S(2)}) async-start(), calls=%async_computation.2 | async-start | bytes 7864320 | tf_op jit(solution)/shard_map/reduce_scatter | solution.py:1805
  66.1 44.5 %collective-permute-start = (bf16[256,1024]{1,0:T(8,128)(2,1)S(1)}, bf16[256,1024]{1,0:T(8,128)(2,1)S(1)}, u32[]{:S(2)}, u32[]{:S(2)}) collective-permute-start(bf16[256,1024]{1,0:T(8,128)(2,1)S(1)} %bitcast.28), channel_id=1, source_target_pairs={{0,2},{1,3},{2,4},{3,5},{4,6},{5,7},{6,0},{7,1},{8,10},{9,11},{10,... | collective-permute-start | bytes 1572872 | tf_op jit(solution)/shard_map/ppermute | solution.py:1771
  68.3 43.2 %collective-permute-start.1 = (bf16[256,1024]{1,0:T(8,128)(2,1)S(1)}, bf16[256,1024]{1,0:T(8,128)(2,1)}, u32[]{:S(2)}, u32[]{:S(2)}) collective-permute-start(bf16[256,1024]{1,0:T(8,128)(2,1)S(1)} %bitcast.29), channel_id=1, source_target_pairs={{0,6},{1,7},{2,0},{3,1},{4,2},{5,3},{6,4},{7,5},{8,14},{9,15},{10,... | collective-permute-start | bytes 1572872 | tf_op jit(solution)/shard_map/ppermute | solution.py:1771
  110.6 0.8 copy-start.6
  201.6 19.3 %copy-start.5 = (bf16[256,1024]{1,0:T(8,128)(2,1)S(1)}, bf16[256,1024]{1,0:T(8,128)(2,1)}, u32[]{:S(2)}) copy-start(bf16[256,1024]{1,0:T(8,128)(2,1)} %get-tuple-element.102) | copy-start | bytes 1572868
  201.6 19.4 %copy-start.4 = (bf16[256,1024]{1,0:T(8,128)(2,1)S(1)}, bf16[256,1024]{1,0:T(8,128)(2,1)}, u32[]{:S(2)}) copy-start(bf16[256,1024]{1,0:T(8,128)(2,1)} %get-tuple-element.103) | copy-start | bytes 1572868
  201.7 20.9 %copy-start.3 = (f32[256]{0:T(256)S(1)}, f32[256]{0:T(256)}, u32[]{:S(2)}) copy-start(f32[256]{0:T(256)} %param.23) | copy-start | bytes 3076
  220.9 27.1 %collective-permute-start.2 = (bf16[256,1024]{1,0:T(8,128)(2,1)S(1)}, bf16[256,1024]{1,0:T(8,128)(2,1)S(1)}, u32[]{:S(2)}, u32[]{:S(2)}) collective-permute-start(bf16[256,1024]{1,0:T(8,128)(2,1)S(1)} %copy-done.5), channel_id=1, source_target_pairs={{0,2},{1,3},{2,0},{3,1},{4,6},{5,7},{6,4},{7,5},{8,10},{9,11},{10,... | collective-permute-start | bytes 1572872 | tf_op jit(solution)/shard_map/ppermute | solution.py:1820
  221.0 27.1 %collective-permute-start.3 = (bf16[256,1024]{1,0:T(8,128)(2,1)S(1)}, bf16[256,1024]{1,0:T(8,128)(2,1)S(1)}, u32[]{:S(2)}, u32[]{:S(2)}) collective-permute-start(bf16[256,1024]{1,0:T(8,128)(2,1)S(1)} %copy-done.4), channel_id=1, source_target_pairs={{0,6},{1,7},{2,4},{3,5},{4,2},{5,3},{6,0},{7,1},{8,14},{9,15},{10,... | collective-permute-start | bytes 1572872 | tf_op jit(solution)/shard_map/ppermute | solution.py:1815
  248.1 0.8 copy-start.1
  248.1 0.9 copy-start.2
Sparse Core Ops, SparseCore 0:
  11.5 81.5 all-gather.2
  94.9 52.6 all-gather.4
  201.8 89.2 reduce-scatter.1

commit v10 on v7

--- a/solution.py
+++ b/solution.py
@@ -594,7 +594,7 @@
     )
 
 
-def moe_exchange(collective_id, normed, cots, mask, router, weights):
+def moe_exchange(collective_id, normed, cots, mask, router, weights, parts):
     devices = lax.axis_size("seq")
     chips = devices // 2
     rows, width = normed.shape
@@ -954,26 +954,30 @@
             y_pre[b] = (y_pre[b].astype(f32) + y_in[j].astype(f32)).astype(bf16)
             y_leave(b, 2 + j).start()
 
+        part_rows = width // parts
         leaving = []
         for e in range(own_experts):
             for j in range(width // rows):
                 i = e * (width // rows) + j
                 x_all[i] = gin[e, j * rows : (j + 1) * rows].astype(bf16)
                 g_all[i, :, :FFE] = gout[e, j * rows : (j + 1) * rows].astype(bf16)
-                at = 2 * len(leaving)
-                here = pl.ds(j * rows, rows)
-                leaving.append(
-                    (
+                copies = []
+                for q in range(rows // part_rows):
+                    here = pl.ds(q * part_rows, part_rows)
+                    part = (j * rows) // part_rows + q
+                    copies += [
                         pltpu.make_async_copy(
-                            x_all.at[i], g_out.at[e, here, pl.ds(0, 2 * FFE)], wg_sem.at[at]
+                            x_all.at[i, here],
+                            g_out.at[part, e, :, pl.ds(0, 2 * FFE)],
+                            wg_sem.at[i, 2 * q],
                         ),
                         pltpu.make_async_copy(
-                            g_all.at[i, :, pl.ds(0, FFE)],
-                            g_out.at[e, here, pl.ds(2 * FFE, FFE)],
-                            wg_sem.at[at + 1],
+                            g_all.at[i, here, pl.ds(0, FFE)],
+                            g_out.at[part, e, :, pl.ds(2 * FFE, FFE)],
+                            wg_sem.at[i, 2 * q + 1],
                         ),
-                    )
-                )
+                    ]
+                leaving.append(copies)
                 for copy in leaving[-1]:
                     copy.start()
 
@@ -1026,7 +1030,7 @@
             jax.ShapeDtypeStruct((own_experts, devices, rows, FFE), bf16),
             jax.ShapeDtypeStruct(block, f32),
             jax.ShapeDtypeStruct((devices, gate_rows, rows), f32),
-            jax.ShapeDtypeStruct((own_experts, width, 3 * FFE), bf16),
+            jax.ShapeDtypeStruct((parts, own_experts, width // parts, 3 * FFE), bf16),
         ]
         + [jax.ShapeDtypeStruct(block, bf16)] * (1 + chips // 2),
         in_specs=[hbm] * (1 + chips) + [vmem] * 2 + [hbm],
@@ -1069,7 +1073,7 @@
             dma((1 + chips // 2,)),
             dma((3, 2)),
             dma((2,)),
-            dma((2 * own_experts * (width // rows),)),
+            dma((own_experts * (width // rows), 2 * rows * parts // width)),
             dma((chips // 2 - 1,)),
             dma((chips // 2 - 1,)),
         ],
@@ -1273,7 +1277,7 @@
 
 
 def finish(e_grads, grad_qkv, grad_wo, pack, input_grad, output, weights, gain, heads, experts):
-    own_experts, e_rows, e_cols = e_grads.shape
+    parts, own_experts, e_rows, e_cols = e_grads.shape
     devices, out_rows, _ = grad_qkv.shape
     q_width = heads * HEAD_SIZE
     share = devices // KEY_VALUE_HEADS if devices > KEY_VALUE_HEADS else 1
@@ -1285,8 +1289,11 @@
         me_ref, e_ref, qkv_ref, wo_ref, pack_ref, in_ref, out_ref, wq, wk, wv, gain_ref,
         e_in, e_out, gq, gk, gv, gwo, grouter, ggain_m, ggain_a, in_grad, output_ref,
     ):
-        e_in[...] = e_ref[:, :, : 2 * FFE].astype(f32)
-        e_out[...] = e_ref[:, :, 2 * FFE :].astype(f32)
+        total = e_ref[0].astype(f32)
+        for p in range(1, parts):
+            total = total + e_ref[p].astype(f32)
+        e_in[...] = total[:, :, : 2 * FFE]
+        e_out[...] = total[:, :, 2 * FFE :]
 
         @pl.when(pl.program_id(0) == 0)
         def _():
@@ -1354,7 +1361,7 @@
         grid_spec=pltpu.PrefetchScalarGridSpec(
             num_scalar_prefetch=1,
             grid=(steps,),
-            in_specs=[pl.BlockSpec((own_experts, chunk, e_cols), lambda i, _: (0, i, 0))]
+            in_specs=[pl.BlockSpec((parts, own_experts, chunk, e_cols), lambda i, _: (0, 0, i, 0))]
             + [whole(x) for x in rest]
             + [own_rows(x) for x in weights]
             + [whole(gain)],
@@ -1801,9 +1808,9 @@
         1, attended_own, tokens[0], wo_full, gains_full
     )
     (_, _, _, moe_sum, gate_cot, e_grads, *branches) = moe_exchange(
-        2, normed_m, cots, mask_all, misc_full, expert_full
+        2, normed_m, cots, mask_all, misc_full, expert_full, parts
     )
-    e_grads = lax.psum_scatter(e_grads, "dp", scatter_dimension=1, tiled=True)
+    e_grads = lax.all_to_all(e_grads, "dp", split_axis=0, concat_axis=0)
     heads_cot, router_pack, mid_cot, grad_wo = middle_exchange(
         4, moe_sum, gate_cot, normed_m, misc_full, mask, mid, out_grad[0], gains_full,
         wo_full, attended, q_width,

time: 317 us -> 324 us (1.022)
  starting transfers between devices: 6.67 us -> 12.2 us
    all_to_all x0 -> x1, starting transfers between devices: none -> 5.44 us  [on_device(): e_grads = lax.all_to_all(e_grads, 'dp', split_axis=0, concat_axis=0)]
  transfers between devices with their start and end apart: 7 -> 7, of which waited for: 0 -> 0; matrix products, arithmetic and copies ran while one was open for 0% -> 0% of each run, Pallas kernels for 90% -> 87%
where the time goes in v10:
time: 324 us; the launch traced here: 321 us
  Pallas kernels  292 us (90%)
  between operations  14.2 us (4%)
  starting transfers between devices  12.2 us (4%)
    pallas_call x1, Pallas kernels, moe_exchange(): pl.pallas_call(kernel, name='moe_exchange', out_shape=[jax.ShapeDtypeStru...  91.8 us
    pallas_call x1, Pallas kernels, exchange(): pl.pallas_call(kernel, name=f'exchange{collective_id}', out_shape=out_sha...  54.6 us
    pallas_call x1, Pallas kernels, final_exchange(): pl.pallas_call(kernel, name='final_exchange', out_shape=[jax.ShapeDtypeSt...  51.9 us
    pallas_call x1, Pallas kernels, attend_backward(): pl.pallas_call(kernel, name='attend_backward', grid_spec=grid_spec, out_s...  24.8 us
    pallas_call x1, Pallas kernels, attended_exchange(): pl.pallas_call(kernel, name='attended_exchange', out_shape=outs, in_specs...  20.3 us
    pallas_call x1, Pallas kernels, attend_forward(): pl.pallas_call(kernel, name='attend_forward', grid_spec=grid_spec, out_sh...  20.1 us
    pallas_call x1, Pallas kernels, middle_exchange(): pl.pallas_call(kernel, name='middle_exchange', out_shape=[jax.ShapeDtypeS...  17.4 us
    ppermute x3, starting transfers between devices, shift(): lax.ppermute(x, 'seq', [(i, (i + 2 * k) % devices) for i in range(devices)])  6.6 us
  transfers between devices with their start and end apart: 7, of which 0 were waited for; matrix products, arithmetic and copies ran while one was open for 0% of the time, Pallas kernels for 87%

profile of v10, /device:TPU:13, one launch (start us, length us, event | category | flops | bytes accessed | tf_op | source)
XLA Modules:
  0.0 321.3 jit_solution(4012913833962611416)
XLA Ops:
  7.2 0.0 all-gather.3.cloned.1.call-start
  7.2 4.2 %prepare.1 = (bf16[2,256,1536]{2,1,0:T(8,128)(2,1)}, bf16[256,128]{1,0:T(8,128)(2,1)}, s32[8,256]{1,0:T(8,128)}, bf16[256,128]{1,0:T(8,128)(2,1)}, bf16[8,256]{1,0:T(8,128)(2,1)}) custom-call(f32[2,256,1024]{2,1,0:T(8,128)} %e_in.1, f32[2,256,512]{2,1,0:T(8,128)} %e_out.1, s32[8,256]{1,0:T(8,128)} %bitcast.34, s32[1,256]{1,0:T(1,128)} %docs_ref.1, ...), custom_call_target="tpu_custom_call" | custom-call | tf_op jit(solution)/shard_map/prepare/pallas_call | solution.py:1472
  11.4 0.0 all-gather.3.cloned.1.call-update
  11.4 0.0 all-gather.5.cloned.1.call-start
  11.5 54.6 %exchange0.1 = (bf16[8,256,1024]{2,1,0:T(8,128)(2,1)}, s32[8,8,256]{2,1,0:T(8,128)}, bf16[8,256,128]{2,1,0:T(8,128)(2,1)}, bf16[256,1024]{1,0:T(8,128)(2,1)}, bf...) custom-call(bf16[256,1024]{1,0:T(8,128)(2,1)} %bitcast.21, ...), custom_call_target="tpu_custom_call" | custom-call | tf_op jit(solution)/shard_map/exchange0/pallas_call | solution.py:273
  66.1 2.1 collective-permute-start
  68.2 2.0 collective-permute-start.1
  70.2 0.0 all-gather.5.cloned.1.call-update
  70.2 20.1 %attend_forward.1 = (bf16[8,256,1024]{2,1,0:T(8,128)(2,1)}, bf16[8,256,128]{2,1,0:T(8,128)(2,1)}, bf16[8,256,128]{2,1,0:T(8,128)(2,1)}, bf16[8,256,128]{2,1,0:T(...) custom-call(bf16[8,256,1024]{2,1,0:T(8,128)(2,1)} %get-tuple-element.75.tok, bf16[1024,256]{1,0:T(8,128)(2,1)} %bitcast.37, ...), custom_call_target="tpu_custom_call" | custom-call | flops 3221225472 | bytes 16777216 | tf_op jit(solution)/shard_map/attend_forward/pallas_call | solution.py:461
  90.3 20.3 %attended_exchange.1 = (bf16[256,1024]{1,0:T(8,128)(2,1)}, f32[256,1024]{1,0:T(8,128)}, bf16[256,1024]{1,0:T(8,128)(2,1)}) custom-call(bf16[8,256,128]{2,1,0:T(8,128)(2,1)} %get-tuple-element.79.att_in, bf16[256,1024]{1,0:T(8,128)(2,1)} %bitcast.22, bf16[1024,1024]{1,0:T(8,128)(2,1)} %bitcast.19, ...), custom_call_target="tpu_custom_call" | custom-call | tf_op jit(solution)/shard_map/attended_exchange/pallas_call | solution.py:1182
  110.7 0.8 copy-done.6
  111.5 0.8 copy-done.7
  112.3 91.8 %moe_exchange.1 = (bf16[2,8,256,1024]{3,2,1,0:T(8,128)(2,1)}, bf16[2,8,256,1024]{3,2,1,0:T(8,128)(2,1)}, bf16[2,8,256,512]{3,2,1,0:T(8,128)(2,1)}, f32[256,1024]...) custom-call(bf16[256,1024]{1,0:T(8,128)(2,1)} %get-tuple-element.81., ...), custom_call_target="tpu_custom_call" | custom-call | flops 38654705664 | bytes 41943040 | tf_op jit(solution)/shard_map/moe_exchange/pallas_call | solution.py:1024
  204.1 5.4 %all-to-all-start = ((bf16[4,2,256,1536]{3,2,1,0:T(8,128)(2,1)}), bf16[4,2,256,1536]{3,2,1,0:T(8,128)(2,1)}, u32[]{:S(2)}, u32[]{:S(2)}) async-start(bf16[4,2,256,1536]{3,2,1,0:T(8,128)(2,1)} %get-tuple-element.87), calls=%async_computation | async-start | bytes 12582912 | tf_op jit(solution)/shard_map/all_to_all | solution.py:1813
  209.6 17.4 %middle_exchange.1 = (bf16[8,256,128]{2,1,0:T(8,128)(2,1)}, bf16[1024,128]{1,0:T(8,128)(2,1)}, f32[256,1024]{1,0:T(8,128)}, bf16[1024,1024]{1,0:T(8,128)(2,1)}) custom-call(f32[256,1024]{1,0:T(8,128)} %get-tuple-element.90.refs_0_, f32[8,16,256]{2,1,0:T(8,128)} %get-tuple-element.91.refs_1_, bf16[256,1024]{1,0:T(8,128)(2,1)} %get-tuple-element.81.refs_0_.refs_2_, ...), custom_call_target="tpu_custom_call" | custom-call | tf_op jit(solution)/shard_map/middle_exchange/pallas_call | solution.py:1263
  227.0 0.1 collective-permute-start.2
  227.1 2.5 collective-permute-start.3
  229.6 0.7 reshape.47.gain_ref
  230.3 24.8 %attend_backward.1.refs_0_.refs_5_ = bf16[8,256,256]{2,1,0:T(8,128)(2,1)} custom-call(bf16[8,256,128]{2,1,0:T(8,128)(2,1)} %get-tuple-element.88.q_ref, bf16[8,256,128]{2,1,0:T(8,128)(2,1)} %get-tuple-element.89.kv_ref, bf16[8,256,128]{2,1,0:T(8,128)(2,1)} %get-tuple-element.98.do_ref, f32[8,64,512]{2,1,0:T(8,128)} %get-tuple-element.99.ot_ref, ...), custom_call_target="tpu_custom_call" | custom-call | flops 5368709120 | bytes 4194304 | tf_op jit(solution)/shard_map/attend_backward/pallas_call | solution.py:573
  255.1 0.0 all-gather.5.cloned.1.call-done.refs_3_
  255.2 0.7 copy-done.1
  255.9 0.2 copy-done.2
  256.1 51.9 %final_exchange.1 = (bf16[256,1024]{1,0:T(8,128)(2,1)}, bf16[256,1024]{1,0:T(8,128)(2,1)}, bf16[8,32,256]{2,1,0:T(8,128)(2,1)}, f32[32,1024]{1,0:T(8,128)}, f32[32,128]{1,0:T(8,128)}) custom-call(bf16[8,256,256]{2,1,0:T(8,128)(2,1)} %attend_backward.1.refs_0_.refs_5_, bf16[4,4,2,32,1024]{4,3,2,1,0:T(8,128)(2,1)} %bitcast.24, ...), custom_call_target="tpu_custom_call" | custom-call | tf_op jit(solution)/shard_map/final_exchange/pallas_call | solution.py:1728
  308.0 6.4 %finish.1 = (f32[2,256,1024]{2,1,0:T(8,128)}, f32[2,256,512]{2,1,0:T(8,128)}, f32[32,1024]{1,0:T(8,128)}, f32[32,512]{1,0:T(8,128)}, f32[32,512]{1,0:T(8,128)}, ...) custom-call(s32[1]{0:T(128)} %bitcast.me_ref, ...), custom_call_target="tpu_custom_call" | custom-call | bytes 8388608 | tf_op jit(solution)/shard_map/finish/pallas_call | solution.py:1358
  (18 shorter events, 0.0 us)
Async XLA Ops:
  7.2 104.3 %all-gather.3.cloned.1.call-start = ((), (), s32[]{:S(2)}) async-start(), calls=%async_computation.1 | async-start | bytes 7864320 | tf_op jit(solution)/shard_map/all_gather | solution.py:1775
  7.2 58.9 %copy-start = (bf16[1,256,1024]{2,1,0:T(8,128)(2,1)S(1)}, bf16[1,256,1024]{2,1,0:T(8,128)(2,1)}, u32[]{:S(2)}) copy-start(bf16[1,256,1024]{2,1,0:T(8,128)(2,1)} %param.15) | copy-start | bytes 1572868
  11.4 243.7 %all-gather.5.cloned.1.call-start = ((), (), s32[]{:S(2)}) async-start(), calls=%async_computation.2 | async-start | bytes 5242880 | tf_op jit(solution)/shard_map/all_gather | solution.py:1794
  66.1 44.6 %collective-permute-start = (bf16[256,1024]{1,0:T(8,128)(2,1)S(1)}, bf16[256,1024]{1,0:T(8,128)(2,1)S(1)}, u32[]{:S(2)}, u32[]{:S(2)}) collective-permute-start(bf16[256,1024]{1,0:T(8,128)(2,1)S(1)} %bitcast.28), channel_id=1, source_target_pairs={{0,2},{1,3},{2,4},{3,5},{4,6},{5,7},{6,0},{7,1},{8,10},{9,11},{10,... | collective-permute-start | bytes 1572872 | tf_op jit(solution)/shard_map/ppermute | solution.py:1779
  68.2 42.5 %collective-permute-start.1 = (bf16[256,1024]{1,0:T(8,128)(2,1)S(1)}, bf16[256,1024]{1,0:T(8,128)(2,1)S(1)}, u32[]{:S(2)}, u32[]{:S(2)}) collective-permute-start(bf16[256,1024]{1,0:T(8,128)(2,1)S(1)} %bitcast.29), channel_id=1, source_target_pairs={{0,6},{1,7},{2,0},{3,1},{4,2},{5,3},{6,4},{7,5},{8,14},{9,15},{10,... | collective-permute-start | bytes 1572872 | tf_op jit(solution)/shard_map/ppermute | solution.py:1779
  110.7 0.8 copy-start.6
  111.5 0.8 copy-start.7
  204.1 103.9 %all-to-all-start = ((bf16[4,2,256,1536]{3,2,1,0:T(8,128)(2,1)}), bf16[4,2,256,1536]{3,2,1,0:T(8,128)(2,1)}, u32[]{:S(2)}, u32[]{:S(2)}) async-start(bf16[4,2,256,1536]{3,2,1,0:T(8,128)(2,1)} %get-tuple-element.87), calls=%async_computation | async-start | bytes 12582912 | tf_op jit(solution)/shard_map/all_to_all | solution.py:1813
  209.5 17.5 %copy-start.5 = (bf16[256,1024]{1,0:T(8,128)(2,1)S(1)}, bf16[256,1024]{1,0:T(8,128)(2,1)}, u32[]{:S(2)}) copy-start(bf16[256,1024]{1,0:T(8,128)(2,1)} %get-tuple-element.102) | copy-start | bytes 1572868
  209.5 17.5 %copy-start.4 = (bf16[256,1024]{1,0:T(8,128)(2,1)S(1)}, bf16[256,1024]{1,0:T(8,128)(2,1)}, u32[]{:S(2)}) copy-start(bf16[256,1024]{1,0:T(8,128)(2,1)} %get-tuple-element.103) | copy-start | bytes 1572868
  209.5 20.1 %copy-start.3 = (f32[256]{0:T(256)S(1)}, f32[256]{0:T(256)}, u32[]{:S(2)}) copy-start(f32[256]{0:T(256)} %param.23) | copy-start | bytes 3076
  227.0 28.1 %collective-permute-start.2 = (bf16[256,1024]{1,0:T(8,128)(2,1)S(1)}, bf16[256,1024]{1,0:T(8,128)(2,1)S(1)}, u32[]{:S(2)}, u32[]{:S(2)}) collective-permute-start(bf16[256,1024]{1,0:T(8,128)(2,1)S(1)} %copy-done.5), channel_id=1, source_target_pairs={{0,2},{1,3},{2,0},{3,1},{4,6},{5,7},{6,4},{7,5},{8,10},{9,11},{10,... | collective-permute-start | bytes 1572872 | tf_op jit(solution)/shard_map/ppermute | solution.py:1821
  227.1 28.0 %collective-permute-start.3 = (bf16[256,1024]{1,0:T(8,128)(2,1)S(1)}, bf16[256,1024]{1,0:T(8,128)(2,1)S(1)}, u32[]{:S(2)}, u32[]{:S(2)}) collective-permute-start(bf16[256,1024]{1,0:T(8,128)(2,1)S(1)} %copy-done.4), channel_id=1, source_target_pairs={{0,4},{1,5},{2,6},{3,7},{4,0},{5,1},{6,2},{7,3},{8,12},{9,13},{10,... | collective-permute-start | bytes 1572872 | tf_op jit(solution)/shard_map/ppermute | solution.py:1779
  255.1 0.8 copy-start.1
  255.1 0.9 copy-start.2
Sparse Core Ops, SparseCore 0:
  11.6 81.5 all-gather.2
  94.9 52.6 all-gather.4

commit v11 on v7

--- a/solution.py
+++ b/solution.py
@@ -390,19 +390,20 @@
         kv_ref[0] = kv
         k_scr[i] = kv[:, :HEAD_SIZE]
         vt_scr[i] = kv.astype(f32).T[HEAD_SIZE:].astype(bf16)
-        q2 = stack_heads(q, heads)
+        q2 = stack_heads(q * jnp.bfloat16(att_mult), heads)
         doc_row = docs_ref[i, :1].astype(f32)
         doc_scr[i] = across_lanes(doc_row, LANES)
         doc_query = jnp.concatenate([doc_row] * heads, axis=1)
         query = i * rows + lax.rem(lax.broadcasted_iota(jnp.int32, (1, cols), 1), rows)
         key_iota = lax.broadcasted_iota(jnp.int32, (rows, cols), 0)
 
-        def step(j, carry):
+        def step(j, carry, diagonal):
             top, total, ot = carry
-            scores = dot_nt(k_scr[j], q2) * att_mult
-            key = key_iota + j * rows
-            same = jnp.concatenate([doc_scr[j]] * (cols // LANES), axis=1) == doc_query
-            scores = jnp.where(same & (key <= query), scores, -1e30)
+            scores = dot_nt(k_scr[j], q2)
+            seen = jnp.concatenate([doc_scr[j]] * (cols // LANES), axis=1) == doc_query
+            if diagonal:
+                seen = seen & (key_iota + j * rows <= query)
+            scores = jnp.where(seen, scores, -1e30)
             new_top = jnp.maximum(top, jnp.max(scores, axis=0, keepdims=True))
             p = jnp.exp(scores - new_top)
             keep = jnp.exp(top - new_top)
@@ -412,14 +413,15 @@
 
         top, total, ot = lax.fori_loop(
             first_block(docs_ref, i),
-            i + 1,
-            step,
+            i,
+            functools.partial(step, diagonal=False),
             (
                 jnp.full((1, cols), -1e30, f32),
                 jnp.zeros((1, cols), f32),
                 jnp.zeros((HEAD_SIZE, cols), f32),
             ),
         )
+        top, total, ot = step(i, (top, total, ot), diagonal=True)
         ot = ot / total
         ot_ref[0] = ot
         lse_ref[0] = top + jnp.log(total)

time: 317 us -> 317 us (level)
  no operation moved by 1% of the time
where the time goes in v11:
time: 317 us; the launch traced here: 313 us
  Pallas kernels  290 us (91%)
  between operations  13.9 us (4%)
  starting transfers between devices  6.67 us (2%)
    pallas_call x1, Pallas kernels, moe_exchange(): pl.pallas_call(kernel, name='moe_exchange', out_shape=[jax.ShapeDtypeStru...  91.8 us
    pallas_call x1, Pallas kernels, exchange(): pl.pallas_call(kernel, name=f'exchange{collective_id}', out_shape=out_sha...  54.6 us
    pallas_call x1, Pallas kernels, final_exchange(): pl.pallas_call(kernel, name='final_exchange', out_shape=[jax.ShapeDtypeSt...  52.1 us
    pallas_call x1, Pallas kernels, attend_backward(): pl.pallas_call(kernel, name='attend_backward', grid_spec=grid_spec, out_s...  24.8 us
    pallas_call x1, Pallas kernels, attended_exchange(): pl.pallas_call(kernel, name='attended_exchange', out_shape=outs, in_specs...  20.2 us
    pallas_call x1, Pallas kernels, attend_forward(): pl.pallas_call(kernel, name='attend_forward', grid_spec=grid_spec, out_sh...  19.8 us
    pallas_call x1, Pallas kernels, middle_exchange(): pl.pallas_call(kernel, name='middle_exchange', out_shape=[jax.ShapeDtypeS...  17.4 us
    ppermute x3, starting transfers between devices, shift(): lax.ppermute(x, 'seq', [(i, (i + 2 * k) % devices) for i in range(devices)])  6.48 us
  transfers between devices with their start and end apart: 7, of which 0 were waited for; matrix products, arithmetic and copies ran while one was open for 0% of the time, Pallas kernels for 90%

profile of v11, /device:TPU:13, one launch (start us, length us, event | category | flops | bytes accessed | tf_op | source)
XLA Modules:
  0.0 313.1 jit_solution(1152125420448673497)
XLA Ops:
  7.2 0.0 all-gather.3.cloned.1.call-start
  7.2 4.1 %prepare.1 = (bf16[2,256,1536]{2,1,0:T(8,128)(2,1)}, bf16[256,128]{1,0:T(8,128)(2,1)}, s32[8,256]{1,0:T(8,128)}, bf16[256,128]{1,0:T(8,128)(2,1)}, bf16[8,256]{1,0:T(8,128)(2,1)}) custom-call(f32[2,256,1024]{2,1,0:T(8,128)} %e_in.1, f32[2,256,512]{2,1,0:T(8,128)} %e_out.1, s32[8,256]{1,0:T(8,128)} %bitcast.34, s32[1,256]{1,0:T(1,128)} %docs_ref.1, ...), custom_call_target="tpu_custom_call" | custom-call | tf_op jit(solution)/shard_map/prepare/pallas_call | solution.py:1467
  11.4 0.0 all-gather.3.cloned.1.call-update
  11.4 0.0 all-gather.5.cloned.1.call-start
  11.4 54.6 %exchange0.1 = (bf16[8,256,1024]{2,1,0:T(8,128)(2,1)}, s32[8,8,256]{2,1,0:T(8,128)}, bf16[8,256,128]{2,1,0:T(8,128)(2,1)}, bf16[256,1024]{1,0:T(8,128)(2,1)}, bf...) custom-call(bf16[256,1024]{1,0:T(8,128)(2,1)} %bitcast.21, ...), custom_call_target="tpu_custom_call" | custom-call | tf_op jit(solution)/shard_map/exchange0/pallas_call | solution.py:273
  66.1 0.0 all-gather.5.cloned.1.call-update
  66.1 0.0 reduce-scatter.2.cloned.1.call-start
  66.1 2.1 collective-permute-start
  68.3 2.1 collective-permute-start.1
  70.4 19.8 %attend_forward.1 = (bf16[8,256,1024]{2,1,0:T(8,128)(2,1)}, bf16[8,256,128]{2,1,0:T(8,128)(2,1)}, bf16[8,256,128]{2,1,0:T(8,128)(2,1)}, bf16[8,256,128]{2,1,0:T(...) custom-call(bf16[8,256,1024]{2,1,0:T(8,128)(2,1)} %get-tuple-element.75.tok, bf16[1024,256]{1,0:T(8,128)(2,1)} %bitcast.37, ...), custom_call_target="tpu_custom_call" | custom-call | flops 3221225472 | bytes 16777216 | tf_op jit(solution)/shard_map/attend_forward/pallas_call | solution.py:463
  90.2 20.2 %attended_exchange.1 = (bf16[256,1024]{1,0:T(8,128)(2,1)}, f32[256,1024]{1,0:T(8,128)}, bf16[256,1024]{1,0:T(8,128)(2,1)}) custom-call(bf16[8,256,128]{2,1,0:T(8,128)(2,1)} %get-tuple-element.79.att_in, bf16[256,1024]{1,0:T(8,128)(2,1)} %bitcast.22, bf16[1024,1024]{1,0:T(8,128)(2,1)} %bitcast.19, ...), custom_call_target="tpu_custom_call" | custom-call | tf_op jit(solution)/shard_map/attended_exchange/pallas_call | solution.py:1180
  110.4 0.8 copy-done.6
  111.2 91.8 %moe_exchange.1 = (bf16[2,8,256,1024]{3,2,1,0:T(8,128)(2,1)}, bf16[2,8,256,1024]{3,2,1,0:T(8,128)(2,1)}, bf16[2,8,256,512]{3,2,1,0:T(8,128)(2,1)}, f32[256,1024]...) custom-call(bf16[256,1024]{1,0:T(8,128)(2,1)} %get-tuple-element.81., ...), custom_call_target="tpu_custom_call" | custom-call | flops 38654705664 | bytes 41943040 | tf_op jit(solution)/shard_map/moe_exchange/pallas_call | solution.py:1022
  203.0 17.4 %middle_exchange.1 = (bf16[8,256,128]{2,1,0:T(8,128)(2,1)}, bf16[1024,128]{1,0:T(8,128)(2,1)}, f32[256,1024]{1,0:T(8,128)}, bf16[1024,1024]{1,0:T(8,128)(2,1)}) custom-call(f32[256,1024]{1,0:T(8,128)} %get-tuple-element.90.refs_0_, f32[8,16,256]{2,1,0:T(8,128)} %get-tuple-element.91.refs_1_, bf16[256,1024]{1,0:T(8,128)(2,1)} %get-tuple-element.81.refs_0_.refs_2_, ...), custom_call_target="tpu_custom_call" | custom-call | tf_op jit(solution)/shard_map/middle_exchange/pallas_call | solution.py:1261
  220.4 0.1 collective-permute-start.2
  220.5 2.2 collective-permute-start.3
  222.7 0.7 reshape.47.gain_ref
  223.4 24.8 %attend_backward.1.refs_0_.refs_5_ = bf16[8,256,256]{2,1,0:T(8,128)(2,1)} custom-call(bf16[8,256,128]{2,1,0:T(8,128)(2,1)} %get-tuple-element.88.q_ref, bf16[8,256,128]{2,1,0:T(8,128)(2,1)} %get-tuple-element.89.kv_ref, bf16[8,256,128]{2,1,0:T(8,128)(2,1)} %get-tuple-element.98.do_ref, f32[8,64,512]{2,1,0:T(8,128)} %get-tuple-element.99.ot_ref, ...), custom_call_target="tpu_custom_call" | custom-call | flops 5368709120 | bytes 4194304 | tf_op jit(solution)/shard_map/attend_backward/pallas_call | solution.py:575
  248.3 0.0 all-gather.5.cloned.1.call-done.refs_3_
  248.3 0.7 copy-done.1
  249.0 0.2 copy-done.2
  249.2 52.1 %final_exchange.1 = (bf16[256,1024]{1,0:T(8,128)(2,1)}, bf16[256,1024]{1,0:T(8,128)(2,1)}, bf16[8,32,256]{2,1,0:T(8,128)(2,1)}, f32[32,1024]{1,0:T(8,128)}, f32[32,128]{1,0:T(8,128)}) custom-call(bf16[8,256,256]{2,1,0:T(8,128)(2,1)} %attend_backward.1.refs_0_.refs_5_, bf16[4,4,2,32,1024]{4,3,2,1,0:T(8,128)(2,1)} %bitcast.24, ...), custom_call_target="tpu_custom_call" | custom-call | tf_op jit(solution)/shard_map/final_exchange/pallas_call | solution.py:1723
  301.4 0.0 reduce-scatter.2.cloned.1.call-done.e_ref
  301.4 5.2 %finish.1 = (f32[2,256,1024]{2,1,0:T(8,128)}, f32[2,256,512]{2,1,0:T(8,128)}, f32[32,1024]{1,0:T(8,128)}, f32[32,512]{1,0:T(8,128)}, f32[32,512]{1,0:T(8,128)}, ...) custom-call(s32[1]{0:T(128)} %bitcast.me_ref, ...), custom_call_target="tpu_custom_call" | custom-call | bytes 8388608 | tf_op jit(solution)/shard_map/finish/pallas_call | solution.py:1353
  (17 shorter events, 0.1 us)
Async XLA Ops:
  7.2 104.0 %all-gather.3.cloned.1.call-start = ((), (), s32[]{:S(2)}) async-start(), calls=%async_computation.1 | async-start | bytes 7864320 | tf_op jit(solution)/shard_map/all_gather | solution.py:1770
  11.3 54.8 %copy-start = (bf16[1,256,1024]{2,1,0:T(8,128)(2,1)S(1)}, bf16[1,256,1024]{2,1,0:T(8,128)(2,1)}, u32[]{:S(2)}) copy-start(bf16[1,256,1024]{2,1,0:T(8,128)(2,1)} %param.15) | copy-start | bytes 1572868
  11.4 236.9 %all-gather.5.cloned.1.call-start = ((), (), s32[]{:S(2)}) async-start(), calls=%async_computation.3 | async-start | bytes 5242880 | tf_op jit(solution)/shard_map/all_gather | solution.py:1789
  66.1 235.3 %reduce-scatter.2.cloned.1.call-start = ((), (), s32[]{:S(2)}) async-start(), calls=%async_computation.2 | async-start | bytes 7864320 | tf_op jit(solution)/shard_map/reduce_scatter | solution.py:1808
  66.1 44.2 %collective-permute-start = (bf16[256,1024]{1,0:T(8,128)(2,1)S(1)}, bf16[256,1024]{1,0:T(8,128)(2,1)S(1)}, u32[]{:S(2)}, u32[]{:S(2)}) collective-permute-start(bf16[256,1024]{1,0:T(8,128)(2,1)S(1)} %bitcast.28), channel_id=1, source_target_pairs={{0,2},{1,3},{2,4},{3,5},{4,6},{5,7},{6,0},{7,1},{8,10},{9,11},{10,... | collective-permute-start | bytes 1572872 | tf_op jit(solution)/shard_map/ppermute | solution.py:1774
  68.3 42.9 %collective-permute-start.1 = (bf16[256,1024]{1,0:T(8,128)(2,1)S(1)}, bf16[256,1024]{1,0:T(8,128)(2,1)}, u32[]{:S(2)}, u32[]{:S(2)}) collective-permute-start(bf16[256,1024]{1,0:T(8,128)(2,1)S(1)} %bitcast.29), channel_id=1, source_target_pairs={{0,6},{1,7},{2,0},{3,1},{4,2},{5,3},{6,4},{7,5},{8,14},{9,15},{10,... | collective-permute-start | bytes 1572872 | tf_op jit(solution)/shard_map/ppermute | solution.py:1774
  110.3 0.8 copy-start.6
  202.9 17.5 %copy-start.5 = (bf16[256,1024]{1,0:T(8,128)(2,1)S(1)}, bf16[256,1024]{1,0:T(8,128)(2,1)}, u32[]{:S(2)}) copy-start(bf16[256,1024]{1,0:T(8,128)(2,1)} %get-tuple-element.102) | copy-start | bytes 1572868
  203.0 17.6 %copy-start.4 = (bf16[256,1024]{1,0:T(8,128)(2,1)S(1)}, bf16[256,1024]{1,0:T(8,128)(2,1)}, u32[]{:S(2)}) copy-start(bf16[256,1024]{1,0:T(8,128)(2,1)} %get-tuple-element.103) | copy-start | bytes 1572868
  203.0 19.8 %copy-start.3 = (f32[256]{0:T(256)S(1)}, f32[256]{0:T(256)}, u32[]{:S(2)}) copy-start(f32[256]{0:T(256)} %param.23) | copy-start | bytes 3076
  220.4 27.8 %collective-permute-start.2 = (bf16[256,1024]{1,0:T(8,128)(2,1)S(1)}, bf16[256,1024]{1,0:T(8,128)(2,1)S(1)}, u32[]{:S(2)}, u32[]{:S(2)}) collective-permute-start(bf16[256,1024]{1,0:T(8,128)(2,1)S(1)} %copy-done.5), channel_id=1, source_target_pairs={{0,2},{1,3},{2,0},{3,1},{4,6},{5,7},{6,4},{7,5},{8,10},{9,11},{10,... | collective-permute-start | bytes 1572872 | tf_op jit(solution)/shard_map/ppermute | solution.py:1816
  220.5 27.7 %collective-permute-start.3 = (bf16[256,1024]{1,0:T(8,128)(2,1)S(1)}, bf16[256,1024]{1,0:T(8,128)(2,1)S(1)}, u32[]{:S(2)}, u32[]{:S(2)}) collective-permute-start(bf16[256,1024]{1,0:T(8,128)(2,1)S(1)} %copy-done.4), channel_id=1, source_target_pairs={{0,4},{1,5},{2,6},{3,7},{4,0},{5,1},{6,2},{7,3},{8,12},{9,13},{10,... | collective-permute-start | bytes 1572872 | tf_op jit(solution)/shard_map/ppermute | solution.py:1774
  248.2 0.8 copy-start.1
  248.3 0.9 copy-start.2
Sparse Core Ops, SparseCore 0:
  11.5 81.5 all-gather.2
  94.9 52.6 all-gather.4
  203.1 86.4 reduce-scatter.1

commit v12 on v11

--- a/solution.py
+++ b/solution.py
@@ -502,7 +502,7 @@
             dk_scr[...] = jnp.zeros_like(dk_scr)
             dv_scr[...] = jnp.zeros_like(dv_scr)
 
-        q2 = stack_heads(q_ref[0], heads)
+        q2 = stack_heads(q_ref[0] * jnp.bfloat16(att_mult), heads)
         do2 = stack_heads(do_ref[0], heads)
         delta = jnp.sum(do2.astype(f32).T * ot_ref[0], axis=0, keepdims=True)
         log_total = lse_ref[0]
@@ -517,7 +517,7 @@
         def _(j):
             kv = kv_ref[j]
             k, v = kv[:, :HEAD_SIZE], kv[:, HEAD_SIZE:]
-            scores = dot_nt(k, q2) * att_mult
+            scores = dot_nt(k, q2)
             key = key_iota + j * rows
             same = jnp.concatenate([doc_scr[j]] * (cols // LANES), axis=1) == doc_query
             p = jnp.where(same & (key <= query), jnp.exp(scores - log_total), 0.0)
@@ -540,7 +540,7 @@
         def _():
             @pl.loop(0, blocks)
             def _(j):
-                kv = jnp.concatenate([dk_scr[j] * att_mult, dv_scr[j]], axis=1)
+                kv = jnp.concatenate([dk_scr[j], dv_scr[j]], axis=1)
                 lane = lax.broadcasted_iota(jnp.int32, kv.shape, 1)
                 c, s = spread_table(table_ref[j])
                 kv = jnp.where(lane < HEAD_SIZE, kv * c - turn(kv) * s, kv).astype(bf16)

time: 317 us -> 317 us (level)
  no operation moved by 1% of the time
where the time goes in v12:
time: 317 us; the launch traced here: 313 us
  Pallas kernels  290 us (91%)
  between operations  13.9 us (4%)
  starting transfers between devices  6.67 us (2%)
    pallas_call x1, Pallas kernels, moe_exchange(): pl.pallas_call(kernel, name='moe_exchange', out_shape=[jax.ShapeDtypeStru...  91.8 us
    pallas_call x1, Pallas kernels, exchange(): pl.pallas_call(kernel, name=f'exchange{collective_id}', out_shape=out_sha...  54.6 us
    pallas_call x1, Pallas kernels, final_exchange(): pl.pallas_call(kernel, name='final_exchange', out_shape=[jax.ShapeDtypeSt...  52.3 us
    pallas_call x1, Pallas kernels, attend_backward(): pl.pallas_call(kernel, name='attend_backward', grid_spec=grid_spec, out_s...  24.7 us
    pallas_call x1, Pallas kernels, attended_exchange(): pl.pallas_call(kernel, name='attended_exchange', out_shape=outs, in_specs...  20.2 us
    pallas_call x1, Pallas kernels, attend_forward(): pl.pallas_call(kernel, name='attend_forward', grid_spec=grid_spec, out_sh...  19.8 us
    pallas_call x1, Pallas kernels, middle_exchange(): pl.pallas_call(kernel, name='middle_exchange', out_shape=[jax.ShapeDtypeS...  17.4 us
    ppermute x3, starting transfers between devices, shift(): lax.ppermute(x, 'seq', [(i, (i + 2 * k) % devices) for i in range(devices)])  6.48 us
  transfers between devices with their start and end apart: 7, of which 0 were waited for; matrix products, arithmetic and copies ran while one was open for 0% of the time, Pallas kernels for 90%

profile of v12, /device:TPU:13, one launch (start us, length us, event | category | flops | bytes accessed | tf_op | source)
XLA Modules:
  0.0 313.1 jit_solution(12134304625219903707)
XLA Ops:
  7.2 0.0 all-gather.3.cloned.1.call-start
  7.2 4.1 %prepare.1 = (bf16[2,256,1536]{2,1,0:T(8,128)(2,1)}, bf16[256,128]{1,0:T(8,128)(2,1)}, s32[8,256]{1,0:T(8,128)}, bf16[256,128]{1,0:T(8,128)(2,1)}, bf16[8,256]{1,0:T(8,128)(2,1)}) custom-call(f32[2,256,1024]{2,1,0:T(8,128)} %e_in.1, f32[2,256,512]{2,1,0:T(8,128)} %e_out.1, s32[8,256]{1,0:T(8,128)} %bitcast.34, s32[1,256]{1,0:T(1,128)} %docs_ref.1, ...), custom_call_target="tpu_custom_call" | custom-call | tf_op jit(solution)/shard_map/prepare/pallas_call | solution.py:1467
  11.4 0.0 all-gather.3.cloned.1.call-update
  11.4 0.0 all-gather.5.cloned.1.call-start
  11.4 54.6 %exchange0.1 = (bf16[8,256,1024]{2,1,0:T(8,128)(2,1)}, s32[8,8,256]{2,1,0:T(8,128)}, bf16[8,256,128]{2,1,0:T(8,128)(2,1)}, bf16[256,1024]{1,0:T(8,128)(2,1)}, bf...) custom-call(bf16[256,1024]{1,0:T(8,128)(2,1)} %bitcast.21, ...), custom_call_target="tpu_custom_call" | custom-call | tf_op jit(solution)/shard_map/exchange0/pallas_call | solution.py:273
  66.1 0.0 all-gather.5.cloned.1.call-update
  66.1 0.0 reduce-scatter.2.cloned.1.call-start
  66.1 2.1 collective-permute-start
  68.3 2.1 collective-permute-start.1
  70.4 19.8 %attend_forward.1 = (bf16[8,256,1024]{2,1,0:T(8,128)(2,1)}, bf16[8,256,128]{2,1,0:T(8,128)(2,1)}, bf16[8,256,128]{2,1,0:T(8,128)(2,1)}, bf16[8,256,128]{2,1,0:T(...) custom-call(bf16[8,256,1024]{2,1,0:T(8,128)(2,1)} %get-tuple-element.75.tok, bf16[1024,256]{1,0:T(8,128)(2,1)} %bitcast.37, ...), custom_call_target="tpu_custom_call" | custom-call | flops 3221225472 | bytes 16777216 | tf_op jit(solution)/shard_map/attend_forward/pallas_call | solution.py:463
  90.2 20.2 %attended_exchange.1 = (bf16[256,1024]{1,0:T(8,128)(2,1)}, f32[256,1024]{1,0:T(8,128)}, bf16[256,1024]{1,0:T(8,128)(2,1)}) custom-call(bf16[8,256,128]{2,1,0:T(8,128)(2,1)} %get-tuple-element.79.att_in, bf16[256,1024]{1,0:T(8,128)(2,1)} %bitcast.22, bf16[1024,1024]{1,0:T(8,128)(2,1)} %bitcast.19, ...), custom_call_target="tpu_custom_call" | custom-call | tf_op jit(solution)/shard_map/attended_exchange/pallas_call | solution.py:1180
  110.4 0.8 copy-done.6
  111.2 91.8 %moe_exchange.1 = (bf16[2,8,256,1024]{3,2,1,0:T(8,128)(2,1)}, bf16[2,8,256,1024]{3,2,1,0:T(8,128)(2,1)}, bf16[2,8,256,512]{3,2,1,0:T(8,128)(2,1)}, f32[256,1024]...) custom-call(bf16[256,1024]{1,0:T(8,128)(2,1)} %get-tuple-element.81., ...), custom_call_target="tpu_custom_call" | custom-call | flops 38654705664 | bytes 41943040 | tf_op jit(solution)/shard_map/moe_exchange/pallas_call | solution.py:1022
  203.0 17.4 %middle_exchange.1 = (bf16[8,256,128]{2,1,0:T(8,128)(2,1)}, bf16[1024,128]{1,0:T(8,128)(2,1)}, f32[256,1024]{1,0:T(8,128)}, bf16[1024,1024]{1,0:T(8,128)(2,1)}) custom-call(f32[256,1024]{1,0:T(8,128)} %get-tuple-element.90.refs_0_, f32[8,16,256]{2,1,0:T(8,128)} %get-tuple-element.91.refs_1_, bf16[256,1024]{1,0:T(8,128)(2,1)} %get-tuple-element.81.refs_0_.refs_2_, ...), custom_call_target="tpu_custom_call" | custom-call | tf_op jit(solution)/shard_map/middle_exchange/pallas_call | solution.py:1261
  220.4 0.1 collective-permute-start.2
  220.5 2.2 collective-permute-start.3
  222.7 0.7 reshape.47.gain_ref
  223.4 24.7 %attend_backward.1.refs_0_.refs_5_ = bf16[8,256,256]{2,1,0:T(8,128)(2,1)} custom-call(bf16[8,256,128]{2,1,0:T(8,128)(2,1)} %get-tuple-element.88.q_ref, bf16[8,256,128]{2,1,0:T(8,128)(2,1)} %get-tuple-element.89.kv_ref, bf16[8,256,128]{2,1,0:T(8,128)(2,1)} %get-tuple-element.98.do_ref, f32[8,64,512]{2,1,0:T(8,128)} %get-tuple-element.99.ot_ref, ...), custom_call_target="tpu_custom_call" | custom-call | flops 5368709120 | bytes 4194304 | tf_op jit(solution)/shard_map/attend_backward/pallas_call | solution.py:575
  248.1 0.0 all-gather.5.cloned.1.call-done.refs_3_
  248.2 0.7 copy-done.1
  248.9 0.2 copy-done.2
  249.1 52.3 %final_exchange.1 = (bf16[256,1024]{1,0:T(8,128)(2,1)}, bf16[256,1024]{1,0:T(8,128)(2,1)}, bf16[8,32,256]{2,1,0:T(8,128)(2,1)}, f32[32,1024]{1,0:T(8,128)}, f32[32,128]{1,0:T(8,128)}) custom-call(bf16[8,256,256]{2,1,0:T(8,128)(2,1)} %attend_backward.1.refs_0_.refs_5_, bf16[4,4,2,32,1024]{4,3,2,1,0:T(8,128)(2,1)} %bitcast.24, ...), custom_call_target="tpu_custom_call" | custom-call | tf_op jit(solution)/shard_map/final_exchange/pallas_call | solution.py:1723
  301.4 0.0 reduce-scatter.2.cloned.1.call-done.e_ref
  301.4 5.2 %finish.1 = (f32[2,256,1024]{2,1,0:T(8,128)}, f32[2,256,512]{2,1,0:T(8,128)}, f32[32,1024]{1,0:T(8,128)}, f32[32,512]{1,0:T(8,128)}, f32[32,512]{1,0:T(8,128)}, ...) custom-call(s32[1]{0:T(128)} %bitcast.me_ref, ...), custom_call_target="tpu_custom_call" | custom-call | bytes 8388608 | tf_op jit(solution)/shard_map/finish/pallas_call | solution.py:1353
  (17 shorter events, 0.1 us)
Async XLA Ops:
  7.2 104.0 %all-gather.3.cloned.1.call-start = ((), (), s32[]{:S(2)}) async-start(), calls=%async_computation.1 | async-start | bytes 7864320 | tf_op jit(solution)/shard_map/all_gather | solution.py:1770
  11.3 54.8 %copy-start = (bf16[1,256,1024]{2,1,0:T(8,128)(2,1)S(1)}, bf16[1,256,1024]{2,1,0:T(8,128)(2,1)}, u32[]{:S(2)}) copy-start(bf16[1,256,1024]{2,1,0:T(8,128)(2,1)} %param.15) | copy-start | bytes 1572868
  11.4 236.8 %all-gather.5.cloned.1.call-start = ((), (), s32[]{:S(2)}) async-start(), calls=%async_computation.3 | async-start | bytes 5242880 | tf_op jit(solution)/shard_map/all_gather | solution.py:1789
  66.1 235.3 %reduce-scatter.2.cloned.1.call-start = ((), (), s32[]{:S(2)}) async-start(), calls=%async_computation.2 | async-start | bytes 7864320 | tf_op jit(solution)/shard_map/reduce_scatter | solution.py:1808
  66.1 44.2 %collective-permute-start = (bf16[256,1024]{1,0:T(8,128)(2,1)S(1)}, bf16[256,1024]{1,0:T(8,128)(2,1)S(1)}, u32[]{:S(2)}, u32[]{:S(2)}) collective-permute-start(bf16[256,1024]{1,0:T(8,128)(2,1)S(1)} %bitcast.28), channel_id=1, source_target_pairs={{0,2},{1,3},{2,4},{3,5},{4,6},{5,7},{6,0},{7,1},{8,10},{9,11},{10,... | collective-permute-start | bytes 1572872 | tf_op jit(solution)/shard_map/ppermute | solution.py:1774
  68.3 42.9 %collective-permute-start.1 = (bf16[256,1024]{1,0:T(8,128)(2,1)S(1)}, bf16[256,1024]{1,0:T(8,128)(2,1)}, u32[]{:S(2)}, u32[]{:S(2)}) collective-permute-start(bf16[256,1024]{1,0:T(8,128)(2,1)S(1)} %bitcast.29), channel_id=1, source_target_pairs={{0,6},{1,7},{2,0},{3,1},{4,2},{5,3},{6,4},{7,5},{8,14},{9,15},{10,... | collective-permute-start | bytes 1572872 | tf_op jit(solution)/shard_map/ppermute | solution.py:1774
  110.3 0.8 copy-start.6
  202.9 17.5 %copy-start.5 = (bf16[256,1024]{1,0:T(8,128)(2,1)S(1)}, bf16[256,1024]{1,0:T(8,128)(2,1)}, u32[]{:S(2)}) copy-start(bf16[256,1024]{1,0:T(8,128)(2,1)} %get-tuple-element.102) | copy-start | bytes 1572868
  203.0 17.6 %copy-start.4 = (bf16[256,1024]{1,0:T(8,128)(2,1)S(1)}, bf16[256,1024]{1,0:T(8,128)(2,1)}, u32[]{:S(2)}) copy-start(bf16[256,1024]{1,0:T(8,128)(2,1)} %get-tuple-element.103) | copy-start | bytes 1572868
  203.0 19.8 %copy-start.3 = (f32[256]{0:T(256)S(1)}, f32[256]{0:T(256)}, u32[]{:S(2)}) copy-start(f32[256]{0:T(256)} %param.23) | copy-start | bytes 3076
  220.4 27.7 %collective-permute-start.2 = (bf16[256,1024]{1,0:T(8,128)(2,1)S(1)}, bf16[256,1024]{1,0:T(8,128)(2,1)S(1)}, u32[]{:S(2)}, u32[]{:S(2)}) collective-permute-start(bf16[256,1024]{1,0:T(8,128)(2,1)S(1)} %copy-done.5), channel_id=1, source_target_pairs={{0,2},{1,3},{2,0},{3,1},{4,6},{5,7},{6,4},{7,5},{8,10},{9,11},{10,... | collective-permute-start | bytes 1572872 | tf_op jit(solution)/shard_map/ppermute | solution.py:1816
  220.5 27.6 %collective-permute-start.3 = (bf16[256,1024]{1,0:T(8,128)(2,1)S(1)}, bf16[256,1024]{1,0:T(8,128)(2,1)S(1)}, u32[]{:S(2)}, u32[]{:S(2)}) collective-permute-start(bf16[256,1024]{1,0:T(8,128)(2,1)S(1)} %copy-done.4), channel_id=1, source_target_pairs={{0,4},{1,5},{2,6},{3,7},{4,0},{5,1},{6,2},{7,3},{8,12},{9,13},{10,... | collective-permute-start | bytes 1572872 | tf_op jit(solution)/shard_map/ppermute | solution.py:1774
  248.1 0.8 copy-start.1
  248.1 0.9 copy-start.2
Sparse Core Ops, SparseCore 0:
  11.5 81.5 all-gather.2
  94.9 52.6 all-gather.4
  203.1 86.4 reduce-scatter.1
